TPU v7x, 32 devices: a whole 2x2x4 slice. The times are simulated.
32 devices in a mesh: gx: 4 (over y, x), gy: 8 (over z, core).
Axes of the slice: x: 2, y: 2, z: 4, core: 2. Of those that a mesh axis runs over, the one named last changes fastest.
Arguments:
- features: bfloat16 [64, 512, 128], P(('gx', 'gy')), may hold values from -11 to 11
- brick_pos: int32 [64], P(('gx', 'gy')), may hold values from 0 to 4, as said below
- cotangent: bfloat16 [64, 512, 128], P(('gx', 'gy')), may hold values from -40 to 40
- first_kernel: bfloat16 [27, 128, 128], replicated, may hold values from -0.109375 to 0.109375
- second_kernel: bfloat16 [27, 128, 128], replicated, may hold values from -0.109375 to 0.109375
- norm_gain: float32 [128], replicated, may hold values from 0.1 to 1.9
Outputs:
- block_out: bfloat16 [64, 512, 128], P(('gx', 'gy'))
- feature_grad: bfloat16 [64, 512, 128], P(('gx', 'gy'))
- kernel_update: float32 [2, 27, 128, 128], replicated
- gain_update: float32 [128], replicated
Inputs may be any that keep to these rules, and one draw needn't show every extreme that they name: `brick_pos`: on each device block the first k slots (k between max(1, 0) and 2, and k = 2 on at least one block) hold distinct positions below 4; the remaining slots hold 4.
All inputs are finite; a program needn't handle non-finite values.
Results may differ from a plain program's by a relative error of at most 0.0029.
Values may be sent and summed in bfloat16 or wider, within the bound.
No kernel may reach another device: no remote copies, remote signals or barrier semaphores. Data moves between devices by JAX's collectives and lax.ppermute only.
A program may use at most 128 MiB of HBM per device.

v0:
```python
import jax
import jax.numpy as jnp
from jax import lax
from jax.sharding import PartitionSpec as P

BX = 2
BY = 2
BZ = 1
POS = 4


clip_level = 0.5


def with_halo(cells, sides, width):
    for axis, dim in sides:
        count = lax.axis_size(axis)
        ends = count - 1
        head = lax.slice_in_dim(cells, 0, width, axis=dim)
        tail = lax.slice_in_dim(cells, cells.shape[dim] - width, cells.shape[dim], axis=dim)
        cells = jnp.concatenate(
            [
                lax.ppermute(tail, axis, [(i, (i + 1) % count) for i in range(ends)]),
                cells,
                lax.ppermute(head, axis, [((i + 1) % count, i) for i in range(ends)]),
            ],
            axis=dim,
        )
    return cells


def brick_coords(position):
    brick_x = position // (BY * BZ)
    brick_y = position // BZ % BY
    brick_z = position % BZ
    return (brick_x, brick_y, brick_z)


def activate(pre, norm_gain):
    average = jnp.mean(pre, axis=-1, keepdims=True)
    center = pre - average
    spread = jnp.mean(center * center, axis=-1, keepdims=True)
    normed = center * lax.rsqrt(spread + 1e-05) * norm_gain
    return normed * jax.nn.sigmoid(normed)


def apply_taps(tile_set, kernel, flipped):
    slot_count, channels = (tile_set.shape[0], tile_set.shape[-1])
    summed = jnp.zeros((slot_count * 512, channels), jnp.float32)
    for step_x in range(3):
        for step_y in range(3):
            for step_z in range(3):
                tap_index = (step_x * 3 + step_y) * 3 + step_z
                if flipped:
                    start_x, start_y, start_z = (2 - step_x, 2 - step_y, 2 - step_z)
                else:
                    start_x, start_y, start_z = (step_x, step_y, step_z)
                window = tile_set[
                    :, start_x : start_x + 8, start_y : start_y + 8, start_z : start_z + 8, :
                ]
                window = window.reshape(slot_count * 512, channels)
                if flipped:
                    summed = summed + lax.dot_general(
                        window,
                        kernel[tap_index],
                        (((1,), (1,)), ((), ())),
                        preferred_element_type=jnp.float32,
                    )
                else:
                    summed = summed + jnp.dot(
                        window, kernel[tap_index], preferred_element_type=jnp.float32
                    )
    return summed.reshape(slot_count, 512, channels)


def tap_grads(tile_set, upstream):
    slot_count, channels = (tile_set.shape[0], tile_set.shape[-1])
    flat_rows = upstream.reshape(slot_count * 512, channels)
    result = []
    for step_x in range(3):
        for step_y in range(3):
            for step_z in range(3):
                window = tile_set[
                    :, step_x : step_x + 8, step_y : step_y + 8, step_z : step_z + 8, :
                ]
                window = window.reshape(slot_count * 512, channels)
                result.append(
                    lax.dot_general(
                        window,
                        flat_rows,
                        (((0,), (0,)), ((), ())),
                        preferred_element_type=jnp.float32,
                    )
                )
    return jnp.stack(result)


def widen_grid(dense_grid):
    widened = with_halo(dense_grid, (("gx", 0), ("gy", 1)), 1)
    return jnp.pad(widened, ((0, 0), (0, 0), (1, 1), (0, 0)))


def clip_factor(squares, channels):
    entries = 54.0 * channels * channels + channels
    return jnp.minimum(1.0, clip_level / jnp.sqrt(squares / entries + 1e-06))


def per_device(features, brick_pos, cotangent, first_kernel, second_kernel, norm_gain):
    slot_count, channels = (features.shape[0], features.shape[2])
    is_live = brick_pos < POS
    brick_x, brick_y, brick_z = brick_coords(jnp.minimum(brick_pos, POS - 1))
    put_x = jnp.where(is_live, brick_x, BX)
    live_mask = is_live[:, None, None]
    given_rows = jnp.where(live_mask, features, jnp.zeros_like(features))
    upstream = jnp.where(live_mask, cotangent, jnp.zeros_like(cotangent))

    def tiles_for(values):
        bricks = jnp.zeros((BX, BY, BZ, 8, 8, 8, channels), values.dtype)
        bricks = bricks.at[put_x, brick_y, brick_z].set(
            values.reshape(slot_count, 8, 8, 8, channels), mode="drop"
        )
        dense_grid = bricks.transpose(0, 3, 1, 4, 2, 5, 6).reshape(BX * 8, BY * 8, BZ * 8, channels)
        padded = widen_grid(dense_grid)

        def take_tile(start_x, start_y, start_z):
            return lax.dynamic_slice(
                padded, (start_x * 8, start_y * 8, start_z * 8, start_x * 0), (10, 10, 10, channels)
            )

        return jax.vmap(take_tile)(brick_x, brick_y, brick_z)

    given_tiles = tiles_for(given_rows)
    first_pre = jnp.where(live_mask, apply_taps(given_tiles, first_kernel, False), 0.0)
    hidden_full, pullback = jax.vjp(activate, first_pre, norm_gain)
    hidden = jnp.where(live_mask, hidden_full, 0.0).astype(jnp.bfloat16)
    hidden_tiles = tiles_for(hidden)
    second_pre = jnp.where(live_mask, apply_taps(hidden_tiles, second_kernel, False), 0.0)
    block_out = (given_rows.astype(jnp.float32) + second_pre).astype(jnp.bfloat16)
    second_grad = tap_grads(hidden_tiles, upstream).reshape(-1)
    hidden_grad = jnp.where(live_mask, apply_taps(tiles_for(upstream), second_kernel, True), 0.0)
    pre_full, gain_grad = pullback(hidden_grad)
    pre_grad = jnp.where(live_mask, pre_full, 0.0).astype(jnp.bfloat16)
    first_grad = tap_grads(given_tiles, pre_grad).reshape(-1)
    back_conv = apply_taps(tiles_for(pre_grad), first_kernel, True)
    feature_grad = jnp.where(live_mask, upstream.astype(jnp.float32) + back_conv, 0.0).astype(
        jnp.bfloat16
    )
    combined, gain_summed = lax.psum(
        (jnp.concatenate([first_grad, second_grad]), gain_grad), ("gx", "gy")
    )
    shrink = clip_factor(
        jnp.sum(combined * combined) + jnp.sum(gain_summed * gain_summed), channels
    )
    updated = shrink * combined
    kernel_update = updated.reshape(2, 27, channels, channels)
    return (block_out, feature_grad, kernel_update, shrink * gain_summed)


def solution(mesh):
    in_specs = (
        P(("gx", "gy"), None, None),
        P(("gx", "gy")),
        P(("gx", "gy"), None, None),
        P(),
        P(),
        P(),
    )
    out_specs = (P(("gx", "gy"), None, None), P(("gx", "gy"), None, None), P(), P())
    return jax.shard_map(
        per_device, mesh=mesh, in_specs=in_specs, out_specs=out_specs, check_vma=False
    )
```

profile of v0, /device:TPU:0, one launch (start us, length us, event | category | flops | bytes accessed | tf_op | source)
XLA Modules:
  0.0 332.0 jit_solution(15290965411382618557)
XLA Ops:
  7.2 0.7 fusion.288
  8.6 0.7 fusion.291
  9.2 1.1 broadcast_select_fusion
  11.2 4.9 %collective-permute-start.8 = (bf16[1,16,8,128]{3,2,1,0:T(8,128)(2,1)S(1)}, bf16[1,16,8,128]{3,2,1,0:T(8,128)(2,1)S(1)}, u32[]{:S(2)}, u32[]{:S(2)}) collective-permute-start(bf16[1,16,8,128]{3,2,1,0:T(8,128)(2,1)S(1)} %get-tuple-element.24), channel_id=1, source_target_pairs={{0,8},{8,16},{16,24},{1,9},{9,17},{17,25},{2,10},{10,18},{18,26},{... | collective-permute-start | bytes 98312 | tf_op jit(solution)/shard_map/ppermute | solution.py:23
  16.1 1.3 collective-permute-start.9
  18.3 4.6 %collective-permute-start = (bf16[1,16,8,128]{3,2,1,0:T(8,128)(2,1)S(1)}, bf16[1,16,8,128]{3,2,1,0:T(8,128)(2,1)S(1)}, u32[]{:S(2)}, u32[]{:S(2)}) collective-permute-start(bf16[1,16,8,128]{3,2,1,0:T(8,128)(2,1)S(1)} %get-tuple-element.28), channel_id=1, source_target_pairs={{0,8},{8,16},{16,24},{1,9},{9,17},{17,25},{2,10},{10,18},{18,26},{... | collective-permute-start | bytes 98312 | tf_op jit(solution)/shard_map/ppermute | solution.py:23
  22.8 1.3 collective-permute-start.1
  24.3 1.3 collective-permute-start.10
  25.6 1.3 collective-permute-start.11
  26.9 2.1 collective-permute-done.1
  29.0 2.7 collective-permute-start.2
  31.7 1.3 collective-permute-start.3
  33.8 2.7 pad_slice_fusion.18
  36.6 1.4 fusion.300
  39.2 1.1 pad_slice_fusion.54
  56.1 2.5 multiply_reduce_fusion.1
  58.8 2.7 fusion.293
  61.6 1.5 select_convert_fusion
  63.3 1.3 fusion.52
  71.9 1.2 copy-done.96
  73.3 2.3 fusion.62
  76.5 4.9 %collective-permute-start.4 = (bf16[1,16,8,128]{3,2,1,0:T(8,128)(2,1)S(1)}, bf16[1,16,8,128]{3,2,1,0:T(8,128)(2,1)S(1)}, u32[]{:S(2)}, u32[]{:S(2)}) collective-permute-start(bf16[1,16,8,128]{3,2,1,0:T(8,128)(2,1)S(1)} %get-tuple-element.26), channel_id=1, source_target_pairs={{0,8},{8,16},{16,24},{1,9},{9,17},{17,25},{2,10},{10,18},{18,26},{... | collective-permute-start | bytes 98312 | tf_op jit(solution)/shard_map/ppermute | solution.py:23
  81.4 1.3 collective-permute-start.5
  82.7 45.0 %psum.15 = f32[128]{0:T(128)S(1)} all-reduce(f32[128]{0:T(128)S(1)} %copy-done.163), channel_id=1, replica_groups=mesh['gx'=4,'gy'=8] {'gx','gy'}, use_global_device_ids=true, to_apply=%region_11.12 | all-reduce | flops 128 | bytes 1024 | tf_op jit(solution)/shard_map/psum | solution.py:148
  128.5 0.8 copy-done.2
  129.3 1.1 copy.13
  131.1 4.2 %collective-permute-start.12 = (bf16[1,16,8,128]{3,2,1,0:T(8,128)(2,1)S(1)}, bf16[1,16,8,128]{3,2,1,0:T(8,128)(2,1)S(1)}, u32[]{:S(2)}, u32[]{:S(2)}) collective-permute-start(bf16[1,16,8,128]{3,2,1,0:T(8,128)(2,1)S(1)} %get-tuple-element.22), channel_id=1, source_target_pairs={{0,8},{8,16},{16,24},{1,9},{9,17},{17,25},{2,10},{10,18},{18,26},{... | collective-permute-start | bytes 98312 | tf_op jit(solution)/shard_map/ppermute | solution.py:23
  135.2 1.3 collective-permute-start.13
  136.6 1.3 collective-permute-start.6
  137.9 1.3 collective-permute-start.7
  139.2 1.8 collective-permute-done.13
  141.7 3.5 %collective-permute-start.14 = (bf16[18,1,8,128]{3,2,1,0:T(8,128)(2,1)}, bf16[18,1,8,128]{3,2,1,0:T(8,128)(2,1)}, u32[]{:S(2)}, u32[]{:S(2)}) collective-permute-start(bf16[18,1,8,128]{3,2,1,0:T(8,128)(2,1)} %get-tuple-element.14), channel_id=1, source_target_pairs={{0,1},{1,2},{2,3},{3,4},{4,5},{5,6},{6,7},{8,9},{9,10},{10,11},{11... | collective-permute-start | bytes 110600 | tf_op jit(solution)/shard_map/ppermute | solution.py:23
  145.2 1.5 collective-permute-start.15
  146.7 1.0 pad_maximum_fusion.2
  147.7 1.8 gather_fusion.1
  149.5 2.7 pad_slice_fusion.36
  152.3 1.3 fusion.301
  153.6 1.8 pad_maximum_fusion.4
  155.3 1.8 gather_fusion.3
  157.2 2.7 pad_slice_fusion
  159.9 1.4 fusion.299
  161.3 1.0 fusion.117
  170.3 2.0 pad_maximum_fusion
  172.4 1.4 convolution_add_fusion.77
  190.8 1.0 select_convert_fusion.1
  191.8 123.9 %all-reduce.6.cloned.1.call-done = f32[884736]{0:T(1024)} async-done(((f32[884736]{0:T(1024)}), f32[884736]{0:T(1024)}) %all-reduce.6.cloned.1.call-update) | async-done | bytes 3538960 | tf_op jit(solution)/shard_map/psum | solution.py:148
  315.7 3.5 %multiply_reduce_fusion = f32[]{:T(128)} fusion(f32[884736]{0:T(1024)} %all-reduce.6.cloned.1.call-done), kind=kLoop, calls=%fused_computation.9 | loop fusion | flops 1769471 | bytes 3538948 | tf_op jit(solution)/shard_map/reduce_sum | solution.py:152
  321.1 4.0 %broadcast_multiply_fusion = f32[884736]{0:T(1024)} fusion(f32[884736]{0:T(1024)} %all-reduce.6.cloned.1.call-done, f32[]{:T(128)S(6)} %min.7), kind=kLoop, calls=%fused_computation.82 | loop fusion | flops 884736 | bytes 7077892 | tf_op jit(solution)/shard_map/mul | solution.py:154
  (539 shorter events, 54.2 us)
Async XLA Ops:
  7.2 308.5 %all-reduce.6.cloned.1.call-start = ((), (), s32[]{:S(2)}) async-start(), calls=%async_computation | async-start | bytes 7077888 | tf_op jit(solution)/shard_map/psum | solution.py:148
  7.9 30.2 %copy-start.155 = (s32[2]{0:T(128)}, s32[2]{0:T(128)S(1)}, u32[]{:S(2)}) copy-start(s32[2]{0:T(128)S(1)} %get-tuple-element.9) | copy-start | bytes 28
  8.6 15.6 %copy-start.156 = (pred[2]{0:T(512)(128)(4,1)}, pred[2]{0:T(512)(128)(4,1)S(1)}, u32[]{:S(2)}) copy-start(pred[2]{0:T(512)(128)(4,1)S(1)} %broadcast_compare_fusion) | copy-start | bytes 10
  11.2 13.0 %collective-permute-start.8 = (bf16[1,16,8,128]{3,2,1,0:T(8,128)(2,1)S(1)}, bf16[1,16,8,128]{3,2,1,0:T(8,128)(2,1)S(1)}, u32[]{:S(2)}, u32[]{:S(2)}) collective-permute-start(bf16[1,16,8,128]{3,2,1,0:T(8,128)(2,1)S(1)} %get-tuple-element.24), channel_id=1, source_target_pairs={{0,8},{8,16},{16,24},{1,9},{9,17},{17,25},{2,10},{10,18},{18,26},{... | collective-permute-start | bytes 98312 | tf_op jit(solution)/shard_map/ppermute | solution.py:23
  16.1 8.1 %collective-permute-start.9 = (bf16[1,16,8,128]{3,2,1,0:T(8,128)(2,1)S(1)}, bf16[1,16,8,128]{3,2,1,0:T(8,128)(2,1)S(1)}, u32[]{:S(2)}, u32[]{:S(2)}) collective-permute-start(bf16[1,16,8,128]{3,2,1,0:T(8,128)(2,1)S(1)} %get-tuple-element.25), channel_id=1, source_target_pairs={{8,0},{16,8},{24,16},{9,1},{17,9},{25,17},{10,2},{18,10},{26,18},{... | collective-permute-start | bytes 98312 | tf_op jit(solution)/shard_map/ppermute | solution.py:25
  18.3 8.6 %collective-permute-start = (bf16[1,16,8,128]{3,2,1,0:T(8,128)(2,1)S(1)}, bf16[1,16,8,128]{3,2,1,0:T(8,128)(2,1)S(1)}, u32[]{:S(2)}, u32[]{:S(2)}) collective-permute-start(bf16[1,16,8,128]{3,2,1,0:T(8,128)(2,1)S(1)} %get-tuple-element.28), channel_id=1, source_target_pairs={{0,8},{8,16},{16,24},{1,9},{9,17},{17,25},{2,10},{10,18},{18,26},{... | collective-permute-start | bytes 98312 | tf_op jit(solution)/shard_map/ppermute | solution.py:23
  22.8 6.2 %collective-permute-start.1 = (bf16[1,16,8,128]{3,2,1,0:T(8,128)(2,1)S(1)}, bf16[1,16,8,128]{3,2,1,0:T(8,128)(2,1)S(1)}, u32[]{:S(2)}, u32[]{:S(2)}) collective-permute-start(bf16[1,16,8,128]{3,2,1,0:T(8,128)(2,1)S(1)} %get-tuple-element.29), channel_id=1, source_target_pairs={{8,0},{16,8},{24,16},{9,1},{17,9},{25,17},{10,2},{18,10},{26,18},{... | collective-permute-start | bytes 98312 | tf_op jit(solution)/shard_map/ppermute | solution.py:25
  24.3 8.8 %collective-permute-start.10 = (bf16[18,1,8,128]{3,2,1,0:T(8,128)(2,1)S(1)}, bf16[18,1,8,128]{3,2,1,0:T(8,128)(2,1)S(1)}, u32[]{:S(2)}, u32[]{:S(2)}) collective-permute-start(bf16[18,1,8,128]{3,2,1,0:T(8,128)(2,1)S(1)} %get-tuple-element.16), channel_id=1, source_target_pairs={{0,1},{1,2},{2,3},{3,4},{4,5},{5,6},{6,7},{8,9},{9,10},{10,11},{11... | collective-permute-start | bytes 110600 | tf_op jit(solution)/shard_map/ppermute | solution.py:23
  25.6 7.5 %collective-permute-start.11 = (bf16[18,1,8,128]{3,2,1,0:T(8,128)(2,1)S(1)}, bf16[18,1,8,128]{3,2,1,0:T(8,128)(2,1)S(1)}, u32[]{:S(2)}, u32[]{:S(2)}) collective-permute-start(bf16[18,1,8,128]{3,2,1,0:T(8,128)(2,1)S(1)} %get-tuple-element.17), channel_id=1, source_target_pairs={{1,0},{2,1},{3,2},{4,3},{5,4},{6,5},{7,6},{9,8},{10,9},{11,10},{12... | collective-permute-start | bytes 110600 | tf_op jit(solution)/shard_map/ppermute | solution.py:25
  29.0 8.9 %collective-permute-start.2 = (bf16[18,1,8,128]{3,2,1,0:T(8,128)(2,1)S(1)}, bf16[18,1,8,128]{3,2,1,0:T(8,128)(2,1)S(1)}, u32[]{:S(2)}, u32[]{:S(2)}) collective-permute-start(bf16[18,1,8,128]{3,2,1,0:T(8,128)(2,1)S(1)} %get-tuple-element.20), channel_id=1, source_target_pairs={{0,1},{1,2},{2,3},{3,4},{4,5},{5,6},{6,7},{8,9},{9,10},{10,11},{11... | collective-permute-start | bytes 110600 | tf_op jit(solution)/shard_map/ppermute | solution.py:23
  31.7 6.2 %collective-permute-start.3 = (bf16[18,1,8,128]{3,2,1,0:T(8,128)(2,1)S(1)}, bf16[18,1,8,128]{3,2,1,0:T(8,128)(2,1)S(1)}, u32[]{:S(2)}, u32[]{:S(2)}) collective-permute-start(bf16[18,1,8,128]{3,2,1,0:T(8,128)(2,1)S(1)} %get-tuple-element.21), channel_id=1, source_target_pairs={{1,0},{2,1},{3,2},{4,3},{5,4},{6,5},{7,6},{9,8},{10,9},{11,10},{12... | collective-permute-start | bytes 110600 | tf_op jit(solution)/shard_map/ppermute | solution.py:25
  39.1 3.3 copy-start.31
  39.1 4.0 %copy-start.25 = (bf16[2,8,8,8,128]{4,3,2,1,0:T(8,128)(2,1)}, bf16[2,8,8,8,128]{4,3,2,1,0:T(8,128)(2,1)S(1)}, u32[]{:S(2)}) copy-start(bf16[2,8,8,8,128]{4,3,2,1,0:T(8,128)(2,1)S(1)} %get-tuple-element.133) | copy-start | bytes 786436
  39.1 4.6 %copy-start.17 = (bf16[2,8,8,8,128]{4,3,2,1,0:T(8,128)(2,1)}, bf16[2,8,8,8,128]{4,3,2,1,0:T(8,128)(2,1)S(1)}, u32[]{:S(2)}) copy-start(bf16[2,8,8,8,128]{4,3,2,1,0:T(8,128)(2,1)S(1)} %get-tuple-element.132) | copy-start | bytes 786436
  39.1 5.3 %copy-start.7 = (bf16[2,8,8,8,128]{4,3,2,1,0:T(8,128)(2,1)}, bf16[2,8,8,8,128]{4,3,2,1,0:T(8,128)(2,1)S(1)}, u32[]{:S(2)}) copy-start(bf16[2,8,8,8,128]{4,3,2,1,0:T(8,128)(2,1)S(1)} %get-tuple-element.131) | copy-start | bytes 786436
  40.3 3.0 copy-start.33
  40.3 3.2 copy-start.29
  40.3 3.7 %copy-start.27 = (bf16[2,8,8,8,128]{4,3,2,1,0:T(8,128)(2,1)}, bf16[2,8,8,8,128]{4,3,2,1,0:T(8,128)(2,1)S(1)}, u32[]{:S(2)}) copy-start(bf16[2,8,8,8,128]{4,3,2,1,0:T(8,128)(2,1)S(1)} %get-tuple-element.120) | copy-start | bytes 786436
  40.3 3.9 %copy-start.23 = (bf16[2,8,8,8,128]{4,3,2,1,0:T(8,128)(2,1)}, bf16[2,8,8,8,128]{4,3,2,1,0:T(8,128)(2,1)S(1)}, u32[]{:S(2)}) copy-start(bf16[2,8,8,8,128]{4,3,2,1,0:T(8,128)(2,1)S(1)} %get-tuple-element.121) | copy-start | bytes 786436
  40.3 4.3 %copy-start.21 = (bf16[2,8,8,8,128]{4,3,2,1,0:T(8,128)(2,1)}, bf16[2,8,8,8,128]{4,3,2,1,0:T(8,128)(2,1)S(1)}, u32[]{:S(2)}) copy-start(bf16[2,8,8,8,128]{4,3,2,1,0:T(8,128)(2,1)S(1)} %get-tuple-element.122) | copy-start | bytes 786436
  40.3 4.6 %copy-start.19 = (bf16[2,8,8,8,128]{4,3,2,1,0:T(8,128)(2,1)}, bf16[2,8,8,8,128]{4,3,2,1,0:T(8,128)(2,1)S(1)}, u32[]{:S(2)}) copy-start(bf16[2,8,8,8,128]{4,3,2,1,0:T(8,128)(2,1)S(1)} %get-tuple-element.123) | copy-start | bytes 786436
  40.3 4.8 %copy-start.15 = (bf16[2,8,8,8,128]{4,3,2,1,0:T(8,128)(2,1)}, bf16[2,8,8,8,128]{4,3,2,1,0:T(8,128)(2,1)S(1)}, u32[]{:S(2)}) copy-start(bf16[2,8,8,8,128]{4,3,2,1,0:T(8,128)(2,1)S(1)} %get-tuple-element.129) | copy-start | bytes 786436
  40.4 5.0 %copy-start.13 = (bf16[2,8,8,8,128]{4,3,2,1,0:T(8,128)(2,1)}, bf16[2,8,8,8,128]{4,3,2,1,0:T(8,128)(2,1)S(1)}, u32[]{:S(2)}) copy-start(bf16[2,8,8,8,128]{4,3,2,1,0:T(8,128)(2,1)S(1)} %get-tuple-element.124) | copy-start | bytes 786436
  40.4 5.2 %copy-start.11 = (bf16[2,8,8,8,128]{4,3,2,1,0:T(8,128)(2,1)}, bf16[2,8,8,8,128]{4,3,2,1,0:T(8,128)(2,1)S(1)}, u32[]{:S(2)}) copy-start(bf16[2,8,8,8,128]{4,3,2,1,0:T(8,128)(2,1)S(1)} %get-tuple-element.125) | copy-start | bytes 786436
  40.4 5.4 %copy-start.9 = (bf16[2,8,8,8,128]{4,3,2,1,0:T(8,128)(2,1)}, bf16[2,8,8,8,128]{4,3,2,1,0:T(8,128)(2,1)S(1)}, u32[]{:S(2)}) copy-start(bf16[2,8,8,8,128]{4,3,2,1,0:T(8,128)(2,1)S(1)} %get-tuple-element.128) | copy-start | bytes 786436
  40.4 5.6 %copy-start.5 = (bf16[2,8,8,8,128]{4,3,2,1,0:T(8,128)(2,1)}, bf16[2,8,8,8,128]{4,3,2,1,0:T(8,128)(2,1)S(1)}, u32[]{:S(2)}) copy-start(bf16[2,8,8,8,128]{4,3,2,1,0:T(8,128)(2,1)S(1)} %get-tuple-element.126) | copy-start | bytes 786436
  40.4 5.9 %copy-start.3 = (bf16[2,8,8,8,128]{4,3,2,1,0:T(8,128)(2,1)}, bf16[2,8,8,8,128]{4,3,2,1,0:T(8,128)(2,1)S(1)}, u32[]{:S(2)}) copy-start(bf16[2,8,8,8,128]{4,3,2,1,0:T(8,128)(2,1)S(1)} %get-tuple-element.127) | copy-start | bytes 786436
  61.5 3.1 copy-start.51
  61.5 3.4 %copy-start.48 = (bf16[2,8,8,8,128]{4,3,2,1,0:T(8,128)(2,1)S(1)}, bf16[2,8,8,8,128]{4,3,2,1,0:T(8,128)(2,1)}, u32[]{:S(2)}) copy-start(bf16[2,8,8,8,128]{4,3,2,1,0:T(8,128)(2,1)} %copy-done.47) | copy-start | bytes 786436
  61.5 3.7 %copy-start.40 = (bf16[2,8,8,8,128]{4,3,2,1,0:T(8,128)(2,1)S(1)}, bf16[2,8,8,8,128]{4,3,2,1,0:T(8,128)(2,1)}, u32[]{:S(2)}) copy-start(bf16[2,8,8,8,128]{4,3,2,1,0:T(8,128)(2,1)} %copy-done.39) | copy-start | bytes 786436
  61.5 3.9 %copy-start.44 = (bf16[2,8,8,8,128]{4,3,2,1,0:T(8,128)(2,1)S(1)}, bf16[2,8,8,8,128]{4,3,2,1,0:T(8,128)(2,1)}, u32[]{:S(2)}) copy-start(bf16[2,8,8,8,128]{4,3,2,1,0:T(8,128)(2,1)} %copy-done.43) | copy-start | bytes 786436
  63.0 2.8 copy-start.42
  63.3 2.8 copy-start.32
  70.5 2.8 copy-start.157
  70.5 2.8 copy-start.160
  73.3 9.4 %copy-start.163 = (f32[128]{0:T(128)S(1)}, f32[128]{0:T(128)}, u32[]{:S(2)}) copy-start(f32[128]{0:T(128)} %get-tuple-element.4) | copy-start | bytes 1540
  75.6 52.2 %copy-start.100 = (bf16[2,8,8,8,128]{4,3,2,1,0:T(8,128)(2,1)S(1)}, bf16[2,8,8,8,128]{4,3,2,1,0:T(8,128)(2,1)}, u32[]{:S(2)}) copy-start(bf16[2,8,8,8,128]{4,3,2,1,0:T(8,128)(2,1)} %get-tuple-element.12) | copy-start | bytes 786436
  76.5 60.1 %collective-permute-start.4 = (bf16[1,16,8,128]{3,2,1,0:T(8,128)(2,1)S(1)}, bf16[1,16,8,128]{3,2,1,0:T(8,128)(2,1)S(1)}, u32[]{:S(2)}, u32[]{:S(2)}) collective-permute-start(bf16[1,16,8,128]{3,2,1,0:T(8,128)(2,1)S(1)} %get-tuple-element.26), channel_id=1, source_target_pairs={{0,8},{8,16},{16,24},{1,9},{9,17},{17,25},{2,10},{10,18},{18,26},{... | collective-permute-start | bytes 98312 | tf_op jit(solution)/shard_map/ppermute | solution.py:23
  81.4 55.2 %collective-permute-start.5 = (bf16[1,16,8,128]{3,2,1,0:T(8,128)(2,1)S(1)}, bf16[1,16,8,128]{3,2,1,0:T(8,128)(2,1)S(1)}, u32[]{:S(2)}, u32[]{:S(2)}) collective-permute-start(bf16[1,16,8,128]{3,2,1,0:T(8,128)(2,1)S(1)} %get-tuple-element.27), channel_id=1, source_target_pairs={{8,0},{16,8},{24,16},{9,1},{17,9},{25,17},{10,2},{18,10},{26,18},{... | collective-permute-start | bytes 98312 | tf_op jit(solution)/shard_map/ppermute | solution.py:25
  127.7 8.9 %copy-start.161 = (f32[128]{0:T(128)}, f32[128]{0:T(128)S(1)}, u32[]{:S(2)}) copy-start(f32[128]{0:T(128)S(1)} %psum.15) | copy-start | bytes 1540
  131.1 8.1 %collective-permute-start.12 = (bf16[1,16,8,128]{3,2,1,0:T(8,128)(2,1)S(1)}, bf16[1,16,8,128]{3,2,1,0:T(8,128)(2,1)S(1)}, u32[]{:S(2)}, u32[]{:S(2)}) collective-permute-start(bf16[1,16,8,128]{3,2,1,0:T(8,128)(2,1)S(1)} %get-tuple-element.22), channel_id=1, source_target_pairs={{0,8},{8,16},{16,24},{1,9},{9,17},{17,25},{2,10},{10,18},{18,26},{... | collective-permute-start | bytes 98312 | tf_op jit(solution)/shard_map/ppermute | solution.py:23
  135.2 5.8 %collective-permute-start.13 = (bf16[1,16,8,128]{3,2,1,0:T(8,128)(2,1)S(1)}, bf16[1,16,8,128]{3,2,1,0:T(8,128)(2,1)S(1)}, u32[]{:S(2)}, u32[]{:S(2)}) collective-permute-start(bf16[1,16,8,128]{3,2,1,0:T(8,128)(2,1)S(1)} %get-tuple-element.23), channel_id=1, source_target_pairs={{8,0},{16,8},{24,16},{9,1},{17,9},{25,17},{10,2},{18,10},{26,18},{... | collective-permute-start | bytes 98312 | tf_op jit(solution)/shard_map/ppermute | solution.py:25
  136.6 10.1 %collective-permute-start.6 = (bf16[18,1,8,128]{3,2,1,0:T(8,128)(2,1)S(1)}, bf16[18,1,8,128]{3,2,1,0:T(8,128)(2,1)S(1)}, u32[]{:S(2)}, u32[]{:S(2)}) collective-permute-start(bf16[18,1,8,128]{3,2,1,0:T(8,128)(2,1)S(1)} %get-tuple-element.18), channel_id=1, source_target_pairs={{0,1},{1,2},{2,3},{3,4},{4,5},{5,6},{6,7},{8,9},{9,10},{10,11},{11... | collective-permute-start | bytes 110600 | tf_op jit(solution)/shard_map/ppermute | solution.py:23
  137.9 8.8 %collective-permute-start.7 = (bf16[18,1,8,128]{3,2,1,0:T(8,128)(2,1)S(1)}, bf16[18,1,8,128]{3,2,1,0:T(8,128)(2,1)S(1)}, u32[]{:S(2)}, u32[]{:S(2)}) collective-permute-start(bf16[18,1,8,128]{3,2,1,0:T(8,128)(2,1)S(1)} %get-tuple-element.19), channel_id=1, source_target_pairs={{1,0},{2,1},{3,2},{4,3},{5,4},{6,5},{7,6},{9,8},{10,9},{11,10},{12... | collective-permute-start | bytes 110600 | tf_op jit(solution)/shard_map/ppermute | solution.py:25
  141.7 11.9 %collective-permute-start.14 = (bf16[18,1,8,128]{3,2,1,0:T(8,128)(2,1)}, bf16[18,1,8,128]{3,2,1,0:T(8,128)(2,1)}, u32[]{:S(2)}, u32[]{:S(2)}) collective-permute-start(bf16[18,1,8,128]{3,2,1,0:T(8,128)(2,1)} %get-tuple-element.14), channel_id=1, source_target_pairs={{0,1},{1,2},{2,3},{3,4},{4,5},{5,6},{6,7},{8,9},{9,10},{10,11},{11... | collective-permute-start | bytes 110600 | tf_op jit(solution)/shard_map/ppermute | solution.py:23
  145.2 8.4 %collective-permute-start.15 = (bf16[18,1,8,128]{3,2,1,0:T(8,128)(2,1)}, bf16[18,1,8,128]{3,2,1,0:T(8,128)(2,1)}, u32[]{:S(2)}, u32[]{:S(2)}) collective-permute-start(bf16[18,1,8,128]{3,2,1,0:T(8,128)(2,1)} %get-tuple-element.15), channel_id=1, source_target_pairs={{1,0},{2,1},{3,2},{4,3},{5,4},{6,5},{7,6},{9,8},{10,9},{11,10},{12... | collective-permute-start | bytes 110600 | tf_op jit(solution)/shard_map/ppermute | solution.py:25
  159.9 2.7 copy-start.95
  191.8 128.7 %copy-start.162 = (f32[128]{0:T(128)S(1)}, f32[128]{0:T(128)}, u32[]{:S(2)}) copy-start(f32[128]{0:T(128)} %copy-done.161) | copy-start | bytes 1540
  (133 other events, 178.6 us)
Sparse Core Ops, SparseCore 0:
  172.5 143.1 all-reduce.5
where the time goes:
time: 333 us; the launch traced here: 332 us
  waiting for transfers between devices  128 us (38%)
  blocking collectives  45 us (14%)
  matrix products  43.2 us (13%)
  starting transfers between devices  37.9 us (11%)
  local copies, waits for them, and re-layouts  33.8 us (10%)
  other arithmetic  25.6 us (8%)
  between operations  18.6 us (6%)
    psum x1, waiting for transfers between devices, per_device(): lax.psum((jnp.concatenate([first_grad, second_grad]), gain_grad), ('gx',...  124 us
    psum x1, blocking collectives, per_device(): lax.psum((jnp.concatenate([first_grad, second_grad]), gain_grad), ('gx',...  45 us
    ppermute x8, starting transfers between devices, with_halo(): lax.ppermute(tail, axis, [(i, (i + 1) % count) for i in range(ends)])  27.3 us
    dot_general x54, matrix products, tap_grads(): lax.dot_general(window, flat_rows, (((0,), (0,)), ((), ())), preferred_el...  15.4 us
    dot_general x54, matrix products, apply_taps(): lax.dot_general(window, kernel[tap_index], (((1,), (1,)), ((), ())), pref...  14.3 us
    slice x8, local copies, waits for them, and re-layouts, apply_taps(): tile_set[:, start_x:start_x + 8, start_y:start_y + 8, start_z:start_z + 8...  13.6 us
    dot_general x54, matrix products, apply_taps(): jnp.dot(window, kernel[tap_index], preferred_element_type=jnp.float32)  13.4 us
    ppermute x8, starting transfers between devices, with_halo(): lax.ppermute(head, axis, [((i + 1) % count, i) for i in range(ends)])  10.5 us
  transfers between devices with their start and end apart: 17, of which 3 were waited for; matrix products, arithmetic and copies ran while one was open for 9% of the time, Pallas kernels for 0%

commit v1 on v0

v1 whole, which is shorter than its diff:
```python
import functools

import jax
import jax.numpy as jnp
from jax import lax
from jax.experimental import pallas as pl
from jax.experimental.pallas import tpu as pltpu
from jax.sharding import PartitionSpec as P

BY = 2
POS = 4
TAPS = 27
P_ROWS = 1040
FACES = (128, 128, 144, 144)
C = 128
clip_level = 0.5
f32, bf16 = jnp.float32, jnp.bfloat16
VMEM = pl.BlockSpec(memory_space=pltpu.VMEM)
SMEM = pl.BlockSpec(memory_space=pltpu.SMEM)
PARAMS = pltpu.CompilerParams(vmem_limit_bytes=56 << 20)


def sds(shape, dtype):
    return jax.ShapeDtypeStruct(shape, dtype)


def place(pos_ref, slot):
    p = pos_ref[slot]
    q = jnp.minimum(p, POS - 1)
    return p < POS, q // BY, q % BY


def call(body, outs, scratch, args, n_smem):
    return pl.pallas_call(
        body,
        out_shape=outs,
        in_specs=[SMEM] * n_smem + [VMEM] * (len(args) - n_smem),
        out_specs=[VMEM] * len(outs),
        scratch_shapes=scratch,
        compiler_params=PARAMS,
    )(*args)


def pack_x_body(pos, a, b, lo, hi):
    lo[...] = jnp.zeros_like(lo)
    hi[...] = jnp.zeros_like(hi)
    for f, src in enumerate((a, b)):
        for s in range(2):
            live, bx, by = place(pos, s)
            rows = pl.ds(pl.multiple_of(by * 64, 64), 64)

            @pl.when(live & (bx == 0))
            def _():
                lo[f, rows, :] = src[s, 0:64, :]

            @pl.when(live & (bx == 1))
            def _():
                hi[f, rows, :] = src[s, 448:512, :]


def pack_y_body(pos, a, b, xl, xr, lo, hi, tmp):
    for f, src in enumerate((a, b)):
        for d, out in enumerate((lo, hi)):
            tmp[...] = jnp.zeros_like(tmp)
            at = 120 * d
            tmp[0] = xl[f, :, :].astype(f32)[at : at + 8]
            tmp[17] = xr[f, :, :].astype(f32)[at : at + 8]
            for s in range(2):
                live, bx, by = place(pos, s)

                @pl.when(live & (by == d))
                def _():
                    cube = src[s].astype(f32).reshape(8, 8, 8, C)
                    tmp[pl.ds(1 + bx * 8, 8)] = cube[:, 7 * d]

            out[f] = tmp[...].reshape(144, C).astype(bf16)


def build(grid, f, pos, src, xl, xr, yl, yr):
    grid[f] = jnp.zeros(grid.shape[1:], f32)
    for s in range(2):
        live, bx, by = place(pos, s)

        @pl.when(live)
        def _():
            grid[f, pl.ds(1 + bx * 8, 8), pl.ds(1 + by * 8, 8)] = (
                src[s].astype(f32).reshape(8, 8, 8, C)
            )

    grid[f, 0, 1:17] = xl[f].astype(f32).reshape(16, 8, C)
    grid[f, 17, 1:17] = xr[f].astype(f32).reshape(16, 8, C)
    grid[f, :, 0] = yl[f].astype(f32).reshape(18, 8, C)
    grid[f, :, 17] = yr[f].astype(f32).reshape(18, 8, C)


def window(grid, f, bx, by, j):
    sx, sy = j // 3, j % 3
    w = grid[f, pl.ds(bx * 8 + sx, 8), pl.ds(by * 8 + sy, 8)]
    return w.reshape(512, C).astype(bf16)


def up_z(v):
    z = lax.broadcasted_iota(jnp.int32, v.shape, 1)
    return jnp.where(z == 7, 0.0, pltpu.roll(v, 7, 1))


def down_z(v):
    z = lax.broadcasted_iota(jnp.int32, v.shape, 1)
    return jnp.where(z == 0, 0.0, pltpu.roll(v, 1, 1))


def fill_weights(w, k, flipped):
    for j in range(9):
        for oz in range(3):
            if flipped:
                w[oz * C : (oz + 1) * C, j * C : (j + 1) * C] = k[3 * (8 - j) + oz]
            else:
                w[j * C : (j + 1) * C, oz * C : (oz + 1) * C] = k[3 * j + oz]


def convolve(grid, f, bx, by, cols, w, flipped):
    for j in range(9):
        cols[:, j * C : (j + 1) * C] = window(grid, f, bx, by, j)
    dims = (((1,), (1,)), ((), ())) if flipped else (((1,), (0,)), ((), ()))
    y = lax.dot_general(cols[...], w[...], dims, preferred_element_type=f32)
    lower, mid, upper = (y[:, i * C : (i + 1) * C].reshape(64, 8, C) for i in range(3))
    if flipped:
        out = mid + up_z(lower) + down_z(upper)
    else:
        out = mid + down_z(lower) + up_z(upper)
    return out.reshape(512, C)


def split3(v):
    hi = v.astype(bf16).astype(f32)
    rest = v - hi
    mid = rest.astype(bf16).astype(f32)
    return hi, mid, rest - mid


def main_body(
    pos, meta, a, b, xl, xr, yl, yr, k1, k2, gain,
    hid, pre, msg, gain_part, grid, cols, w1, w2, hg
):
    core = meta[0]
    for f, src in enumerate((a, b)):
        build(grid, f, pos, src, xl, xr, yl, yr)
    fill_weights(w1, k1, False)
    fill_weights(w2, k2, True)
    at = P_ROWS
    for ref in (xl, xr, yl, yr):
        msg[at : at + ref.shape[1]] = ref[1 - core]
        at += ref.shape[1]
    g = gain[...]
    total = jnp.zeros((1, C), f32)
    for s in range(2):
        live, bx, by = place(pos, s)
        hg[...] = convolve(grid, 1, bx, by, cols, w2, True)
        first = convolve(grid, 0, bx, by, cols, w1, False)
        center = first - jnp.mean(first, axis=1, keepdims=True)
        spread = jnp.mean(center * center, axis=1, keepdims=True)
        inv = lax.rsqrt(spread + 1e-05)
        n = center * inv
        v = n * g
        sig = jax.nn.sigmoid(v)
        on = jnp.where(live, 1.0, 0.0)
        h = jnp.where(live, v * sig, 0.0).astype(bf16)
        grad = jnp.where(live, hg[...], 0.0)
        dv = grad * (sig * (1.0 + v * (1.0 - sig)))
        total = total + jnp.sum(dv * n, axis=0, keepdims=True)
        dn = dv * g
        m1 = jnp.mean(dn, axis=1, keepdims=True)
        m2 = jnp.mean(dn * n, axis=1, keepdims=True)
        p = (inv * (dn - m1 - n * m2)).astype(bf16)
        hid[s] = h
        pre[s] = p
        msg[s * 512 : (s + 1) * 512] = jnp.where(core == 0, h, p)
    gain_part[...] = jnp.broadcast_to(total, (8, C))
    msg[1024:P_ROWS] = pack3(total)


def out_body(pos, src, xl, xr, yl, yr, k, base, out, grid, cols, w, *, field):
    build(grid, 0, pos, src, *(e.at[field : field + 1] for e in (xl, xr, yl, yr)))
    fill_weights(w, k, field == 1)
    for s in range(2):
        live, bx, by = place(pos, s)
        y = convolve(grid, 0, bx, by, cols, w, field == 1)
        out[s] = jnp.where(live, base[s].astype(f32) + y, 0.0).astype(bf16)


def grads_body(
    pos, ppos, meta, a, b, xl, xr, yl, yr, other, hid, pre, msg, gain_part,
    low, out, gsum, grid, cols, pt, acc, *, chunks
):
    core, mine = meta[0], meta[1]

    @pl.when(core == 0)
    def _():
        build(grid, 0, pos, a, xl, xr, yl, yr)

    @pl.when(core != 0)
    def _():
        build(grid, 0, pos, b, *(e.at[1:2] for e in (xl, xr, yl, yr)))

    faces, at = [], P_ROWS
    for rows in FACES:
        faces.append(msg.at[pl.ds(at, rows)].reshape(1, rows, C))
        at += rows
    build(grid.at[1:2], 0, ppos, other, *faces)
    for k in range(4):
        s = k % 2
        _, bx, by = place(pos if k < 2 else ppos, s)
        rows = slice(k * 512, (k + 1) * 512)
        for j in range(9):
            cols[rows, j * C : (j + 1) * C] = window(grid, k // 2, bx, by, j)
        if k < 2:
            v = jnp.where(core == 0, pre[s], hid[s])
        else:
            v = msg[s * 512 : (s + 1) * 512]
        v = v.astype(f32).reshape(64, 8, C)
        for i, t in enumerate((up_z(v), v, down_z(v))):
            pt[i * C : (i + 1) * C, rows] = t.reshape(512, C).T.astype(bf16)
    y = jnp.dot(pt[...], cols[...], preferred_element_type=f32)
    for j in range(9):
        acc[j * 384 : (j + 1) * 384] = y[:, j * C : (j + 1) * C]
    size = acc.shape[0] // chunks
    half = chunks // 2
    for p in range(half):
        at = pl.multiple_of((mine ^ p) * size, 8)
        low[p * size : (p + 1) * size] = acc[pl.ds(at, size)]
    for p in range(0, half, 2):
        at = pl.multiple_of((mine ^ (p + half)) * size, 8)
        nxt = pl.multiple_of((mine ^ (p + half + 1)) * size, 8)
        two = jnp.concatenate([acc[pl.ds(at, size)], acc[pl.ds(nxt, size)]])
        out[p * size : (p + 2) * size] = two.astype(bf16)
    tile = msg[1024:P_ROWS].astype(f32)
    total = gain_part[0:1] + ((tile[2:3] + tile[1:2]) + tile[0:1])
    gsum[...] = jnp.broadcast_to(total, (8, C))
    out[half * size :] = pack3(total)


def pack3(v):
    hi, mid, low = split3(v)
    row = lax.broadcasted_iota(jnp.int32, (16, C), 0)
    return jnp.where(row == 0, hi, jnp.where(row == 1, mid, jnp.where(row == 2, low, 0.0))).astype(bf16)


def step_body(low, got, g, low_out, msg, g_out):
    rows = low.shape[0]
    tile = got[rows : rows + 16].astype(f32)
    total = g[0:1] + ((tile[2:3] + tile[1:2]) + tile[0:1])
    g_out[...] = jnp.broadcast_to(total, (8, C))
    added = low[...] + got[0:rows].astype(f32)
    if low_out is None:
        msg[0:rows] = added.astype(msg.dtype)
    else:
        keep = low_out.shape[0]
        low_out[...] = added[0:keep]
        msg[0 : rows - keep] = added[keep:].astype(msg.dtype)
        rows -= keep
    msg[rows : rows + 16] = pack3(total).astype(msg.dtype)


def final_body(meta, own, part, own_g, part_g, k_out, g_out, first, second, *, chunks):
    core, mine, theirs = meta[0], meta[1], meta[2]
    n = TAPS * C
    size = n // chunks

    def spread(dst, src, me):
        for p in range(chunks):
            at = pl.multiple_of((me ^ p) * size, 8)
            dst[pl.ds(at, size)] = src[p * size : (p + 1) * size].astype(f32)

    @pl.when(core == 0)
    def _():
        spread(first, own, mine)
        spread(second, part, theirs)

    @pl.when(core != 0)
    def _():
        spread(first, part, theirs)
        spread(second, own, mine)

    g = jnp.where(core == 0, own_g[0:1], part_g[0:1])
    total = jnp.sum(g * g)
    for ref in (first, second):
        v = ref[...].reshape(n // 8, 8, C)
        total = total + jnp.sum(jnp.sum(v * v, axis=0))
    entries = 2.0 * n * C + C
    norm = jnp.full((8, C), total / entries + 1e-06, f32)
    shrink = jnp.minimum(1.0, clip_level / jnp.sqrt(norm))[0:1]
    g_out[...] = g * shrink
    for t in range(TAPS):
        k_out[0, t] = first[t * C : (t + 1) * C].T * shrink
        u = TAPS - 1 - t
        k_out[1, t] = second[u * C : (u + 1) * C] * shrink


def shift(lo, hi, axis):
    n = lax.axis_size(axis)
    from_left = lax.ppermute(hi, axis, [(i, i + 1) for i in range(n - 1)])
    from_right = lax.ppermute(lo, axis, [(i + 1, i) for i in range(n - 1)])
    return from_left, from_right


def halos(pos, a, b):
    lo, hi = call(pack_x_body, [sds((2, 128, C), bf16)] * 2, [], (pos, a, b), 1)
    xl, xr = shift(lo, hi, "gx")
    lo, hi = call(
        pack_y_body,
        [sds((2, 144, C), bf16)] * 2,
        [pltpu.VMEM((18, 8, C), f32)],
        (pos, a, b, xl, xr),
        1,
    )
    yl, yr = shift(lo, hi, "gy")
    return xl, xr, yl, yr


def stages():
    nx, ny = lax.axis_size("gx"), lax.axis_size("gy")
    xs = [(1 << i, 0) for i in range(nx.bit_length() - 1)]
    zs = [(0, 1 << i) for i in range(1, ny.bit_length() - 1)]
    orders = (xs + zs, xs[1:] + xs[:1] + zs)
    perms = []
    for step in zip(*orders):
        pairs = []
        for i in range(nx):
            for j in range(ny):
                dx, dy = step[j % 2]
                pairs.append((i * ny + j, (i ^ dx) * ny + (j ^ dy)))
        perms.append(pairs)
    return orders, perms


def chunk_index(order, halvings, ix, iy):
    out = 0
    for s, (dx, dy) in enumerate(order[:halvings]):
        bit = ((ix & dx) | (iy & dy)) != 0
        out = out + bit.astype(jnp.int32) * (1 << (halvings - 1 - s))
    return jnp.asarray(out, jnp.int32)


def after(value, *done):
    return lax.optimization_barrier((value, *done))[0]


def per_device(features, brick_pos, cotangent, first_kernel, second_kernel, norm_gain):
    both = ("gx", "gy")
    ny = lax.axis_size("gy")
    ix, iy = lax.axis_index("gx"), lax.axis_index("gy")
    core = iy % 2
    orders, perms = stages()
    halvings = min(len(perms), 4)
    chunks = 1 << halvings
    me_a = chunk_index(orders[0], halvings, ix, iy)
    me_b = chunk_index(orders[1], halvings, ix, iy)
    meta = jnp.stack([core, jnp.where(core == 0, me_a, me_b), jnp.where(core == 0, me_b, me_a)])
    partner = [(i, i ^ 1) for i in range(ny)]
    n = TAPS * C

    ppos = lax.ppermute(brick_pos, "gy", partner)
    other = lax.ppermute(jnp.where(core == 0, cotangent, features), "gy", partner)
    edge = halos(brick_pos, features, cotangent)
    grid = pltpu.VMEM((2, 18, 18, 8, C), f32)
    cols = pltpu.VMEM((512, 9 * C), bf16)
    straight, turned = pltpu.VMEM((9 * C, 3 * C), bf16), pltpu.VMEM((3 * C, 9 * C), bf16)
    hid, pre, msg, gain_part = call(
        main_body,
        [sds((2, 512, C), bf16)] * 2 + [sds((P_ROWS + sum(FACES), C), bf16), sds((8, C), f32)],
        [grid, cols, straight, turned, pltpu.VMEM((512, C), f32)],
        (brick_pos, meta, features, cotangent, *edge, first_kernel, second_kernel, norm_gain.reshape(1, C)),
        2,
    )
    pmsg = lax.ppermute(msg, "gy", partner)
    low, out, g = call(
        functools.partial(grads_body, chunks=chunks),
        [sds((n // 2, C), f32), sds((n // 2 + 16, C), bf16), sds((8, C), f32)],
        [
            grid,
            pltpu.VMEM((2048, 9 * C), bf16),
            pltpu.VMEM((3 * C, 2048), bf16),
            pltpu.VMEM((n, C), f32),
        ],
        (brick_pos, ppos, meta, features, cotangent, *edge, other, hid, pre, pmsg, gain_part),
        3,
    )

    def work():
        ready = yield
        lo, hi = call(
            pack_x_body, [sds((2, 128, C), bf16)] * 2, [], (brick_pos, after(hid, ready), pre), 1
        )
        xl, xr = shift(lo, hi, "gx")
        ready = yield lo
        lo, hi = call(
            pack_y_body,
            [sds((2, 144, C), bf16)] * 2,
            [pltpu.VMEM((18, 8, C), f32)],
            (brick_pos, after(hid, ready), pre, xl, xr),
            1,
        )
        yl, yr = shift(lo, hi, "gy")
        ready = yield lo
        results = []
        for f, (src, k, base, w) in enumerate(
            ((hid, second_kernel, features, straight), (pre, first_kernel, cotangent, turned))
        ):
            (res,) = call(
                functools.partial(out_body, field=f),
                [sds((2, 512, C), bf16)],
                [pltpu.VMEM((1, 18, 18, 8, C), f32), cols, w],
                (brick_pos, after(src, ready), xl, xr, yl, yr, k, base),
                1,
            )
            results.append(res)
            ready = yield res
        yield results

    side = work()
    next(side)
    rows = n // 2
    for s in range(len(perms)):
        done = side.send(out) if s < 4 else None
        got = lax.ppermute(out, both, perms[s])
        last = s == len(perms) - 1
        wide = s + 2 >= len(perms)
        halve = s + 1 < halvings
        keep = rows // 2 if halve else 0
        outs = [sds((rows - keep + 16, C), bf16 if halve and not wide else f32), sds((8, C), f32)]
        if halve:
            outs = [sds((keep, C), f32)] + outs
            body = step_body
        else:
            body = lambda low, got, g, *rest: step_body(low, got, g, None, *rest)
        res = call(body, outs, [], (low, got, g), 0)
        if halve:
            low, out, g = res
            rows = keep
        else:
            out, g = res
            low = out[:rows]
        if done is not None:
            out = after(out, done)
    results = side.send(out)
    full = out[:rows].astype(bf16)
    for perm in reversed(perms[:halvings]):
        full = jnp.concatenate([full, lax.ppermute(full, both, perm)])
    part = lax.ppermute(full, "gy", partner)
    gain = lax.ppermute(g, "gy", partner)
    k_up, g_up = call(
        functools.partial(final_body, chunks=chunks),
        [sds((2, TAPS, C, C), f32), sds((1, C), f32)],
        [pltpu.VMEM((n, C), f32), pltpu.VMEM((n, C), f32)],
        (meta, full, part, g, gain),
        1,
    )
    return (*results, k_up, g_up.reshape(C))


def solution(mesh):
    rows = P(("gx", "gy"), None, None)
    return jax.shard_map(
        per_device,
        mesh=mesh,
        in_specs=(rows, P(("gx", "gy")), rows, P(), P(), P()),
        out_specs=(rows, rows, P(), P()),
        check_vma=False,
    )
```

time: 333 us -> 130 us (0.39)
  waiting for transfers between devices: 128 us -> 40.3 us
  blocking collectives: 45 us -> 0 us
  matrix products: 43.2 us -> 0 us
  Pallas kernels: 0 us -> 39 us
  local copies, waits for them, and re-layouts: 33.8 us -> 8.68 us
  other arithmetic: 25.6 us -> 0.75 us
  between operations: 18.6 us -> 0.89 us
    psum x1 -> x0, waiting for transfers between devices: 124 us -> none  [per_device(): lax.psum((jnp.concatenate([first_grad, second_grad]), gain_grad), ('gx',...]
    psum x1 -> x0, blocking collectives: 45 us -> none  [per_device(): lax.psum((jnp.concatenate([first_grad, second_grad]), gain_grad), ('gx',...]
    dot_general x162 -> x0, matrix products: 43.2 us -> none  [the longest x54 15.4 us: tap_grads(): lax.dot_general(window, flat_rows, (((0,), (0,)), ((), ())), preferred_el...]
    pallas_call x0 -> x13, Pallas kernels: none -> 39 us  [call(): pl.pallas_call(body, out_shape=outs, in_specs=[SMEM] * n_smem + [VMEM] *...]
    ppermute x16 -> x21, waiting for transfers between devices: 4 us -> 40.3 us  [the longest x4 16.2 us: per_device(): full = jnp.concatenate([full, lax.ppermute(full, both, perm)])]
    slice x12 -> x0, local copies, waits for them, and re-layouts: 13.7 us -> none  [the longest x8 13.6 us: apply_taps(): tile_set[:, start_x:start_x + 8, start_y:start_y + 8, start_z:start_z + 8...]
    reduce_sum x4 -> x0, other arithmetic: 7.32 us -> none  [the longest x1 3.51 us: per_device(): jnp.sum(combined * combined) + jnp.sum(gain_summed * gain_summed)]
    concatenate x7 -> x3, other arithmetic: 6.38 us -> 0.05 us  [per_device(): full = jnp.concatenate([full, lax.ppermute(full, both, perm)])]
  transfers between devices with their start and end apart: 17 -> 21, of which waited for: 3 -> 13; matrix products, arithmetic and copies ran while one was open for 9% -> 1% of each run, Pallas kernels for 0% -> 9%
where the time goes in v1:
time: 130 us; the launch traced here: 128 us
  waiting for transfers between devices  40.3 us (31%)
  Pallas kernels  39 us (30%)
  starting transfers between devices  38.4 us (30%)
  local copies, waits for them, and re-layouts  8.68 us (7%)
    pallas_call x13, Pallas kernels, call(): pl.pallas_call(body, out_shape=outs, in_specs=[SMEM] * n_smem + [VMEM] *...  39 us
    ppermute x4, waiting for transfers between devices, per_device(): full = jnp.concatenate([full, lax.ppermute(full, both, perm)])  16.2 us
    ppermute x4, waiting for transfers between devices, shift(): from_right = lax.ppermute(lo, axis, [(i + 1, i) for i in range(n - 1)])  14.3 us
    ppermute x4, starting transfers between devices, shift(): from_left = lax.ppermute(hi, axis, [(i, i + 1) for i in range(n - 1)])  10.2 us
    ppermute x4, starting transfers between devices, per_device(): full = jnp.concatenate([full, lax.ppermute(full, both, perm)])  9.93 us
    ppermute x4, starting transfers between devices, per_device(): got = lax.ppermute(out, both, perms[s])  8.9 us
    unnamed x46, local copies, waits for them, and re-layouts  8.62 us
    ppermute x4, starting transfers between devices, shift(): from_right = lax.ppermute(lo, axis, [(i + 1, i) for i in range(n - 1)])  5.17 us
  transfers between devices with their start and end apart: 21, of which 13 were waited for; matrix products, arithmetic and copies ran while one was open for 1% of the time, Pallas kernels for 9%

profile of v1, /device:TPU:0, one launch (start us, length us, event | category | flops | bytes accessed | tf_op | source)
XLA Modules:
  0.0 128.0 jit_solution(3688386931931208443)
XLA Ops:
  0.7 1.8 %shard_map.93 = (bf16[2,128,128]{2,1,0:T(8,128)(2,1)}, bf16[2,128,128]{2,1,0:T(8,128)(2,1)}) custom-call(s32[2]{0:T(128)} %pos.15, bf16[2,512,128]{2,1,0:T(8,128)(2,1)} %base.2, bf16[2,512,128]{2,1,0:T(8,128)(2,1)} %base.3), custom_call_target="tpu_custom_call" | custom-call | tf_op jit(solution)/shard_map/pallas_call | solution.py:34
  2.5 4.9 %collective-permute-start = (bf16[2,128,128]{2,1,0:T(8,128)(2,1)}, bf16[2,128,128]{2,1,0:T(8,128)(2,1)S(1)}, u32[]{:S(2)}, u32[]{:S(2)}) collective-permute-start(bf16[2,128,128]{2,1,0:T(8,128)(2,1)} %get-tuple-element.40), channel_id=1, source_target_pairs={{0,8},{8,16},{16,24},{1,9},{9,17},{17,25},{2,10},{10,18},{18,26},{... | collective-permute-start | bytes 196616 | tf_op jit(solution)/shard_map/ppermute | solution.py:301
  7.4 1.3 %collective-permute-start.1 = (bf16[2,128,128]{2,1,0:T(8,128)(2,1)}, bf16[2,128,128]{2,1,0:T(8,128)(2,1)S(1)}, u32[]{:S(2)}, u32[]{:S(2)}) collective-permute-start(bf16[2,128,128]{2,1,0:T(8,128)(2,1)} %get-tuple-element.41), channel_id=1, source_target_pairs={{8,0},{16,8},{24,16},{9,1},{17,9},{25,17},{10,2},{18,10},{26,18},{... | collective-permute-start | bytes 196616 | tf_op jit(solution)/shard_map/ppermute | solution.py:302
  8.7 0.9 collective-permute-done.xl
  9.6 4.2 %collective-permute-done.1.xr = bf16[2,128,128]{2,1,0:T(8,128)(2,1)S(1)} collective-permute-done((bf16[2,128,128]{2,1,0:T(8,128)(2,1)}, bf16[2,128,128]{2,1,0:T(8,128)(2,1)S(1)}, u32[]{:S(2)}, u32[]{:S(2)}) %collective-permute-start.1) | collective-permute-done | bytes 65568 | tf_op jit(solution)/shard_map/ppermute | solution.py:302
  14.4 1.8 %shard_map.94 = (bf16[2,144,128]{2,1,0:T(8,128)(2,1)}, bf16[2,144,128]{2,1,0:T(8,128)(2,1)}) custom-call(s32[2]{0:T(128)} %pos.15, bf16[2,512,128]{2,1,0:T(8,128)(2,1)} %base.2, bf16[2,512,128]{2,1,0:T(8,128)(2,1)} %base.3, bf16[2,128,128]{2,1,0:T(8,128)(2,1)} %copy-done.6, bf16[2,128,128]{2,1,0:T(8,128)(2,1)} %copy-done.7), custom_call_target="tpu_custom_call" | custom-call | tf_op jit(solution)/shard_map/pallas_call | solution.py:34
  16.2 1.3 %collective-permute-start.2 = (bf16[2,144,128]{2,1,0:T(8,128)(2,1)}, bf16[2,144,128]{2,1,0:T(8,128)(2,1)S(1)}, u32[]{:S(2)}, u32[]{:S(2)}) collective-permute-start(bf16[2,144,128]{2,1,0:T(8,128)(2,1)} %get-tuple-element.42), channel_id=1, source_target_pairs={{0,1},{1,2},{2,3},{3,4},{4,5},{5,6},{6,7},{8,9},{9,10},{10,11},{11... | collective-permute-start | bytes 221192 | tf_op jit(solution)/shard_map/ppermute | solution.py:301
  17.5 1.3 %collective-permute-start.3 = (bf16[2,144,128]{2,1,0:T(8,128)(2,1)}, bf16[2,144,128]{2,1,0:T(8,128)(2,1)S(1)}, u32[]{:S(2)}, u32[]{:S(2)}) collective-permute-start(bf16[2,144,128]{2,1,0:T(8,128)(2,1)} %get-tuple-element.43), channel_id=1, source_target_pairs={{1,0},{2,1},{3,2},{4,3},{5,4},{6,5},{7,6},{9,8},{10,9},{11,10},{12... | collective-permute-start | bytes 221192 | tf_op jit(solution)/shard_map/ppermute | solution.py:302
  18.8 0.7 pad_add_fusion.meta
  19.5 3.2 %collective-permute-done.3.yr = bf16[2,144,128]{2,1,0:T(8,128)(2,1)S(1)} collective-permute-done((bf16[2,144,128]{2,1,0:T(8,128)(2,1)}, bf16[2,144,128]{2,1,0:T(8,128)(2,1)S(1)}, u32[]{:S(2)}, u32[]{:S(2)}) %collective-permute-start.3) | collective-permute-done | bytes 73760 | tf_op jit(solution)/shard_map/ppermute | solution.py:302
  23.3 6.4 %shard_map.95 = (bf16[2,512,128]{2,1,0:T(8,128)(2,1)}, bf16[2,512,128]{2,1,0:T(8,128)(2,1)}, bf16[1584,128]{1,0:T(8,128)(2,1)}, f32[8,128]{1,0:T(8,128)}) custom-call(s32[2]{0:T(128)} %pos.15, s32[3]{0:T(128)} %pad_add_fusion.meta, bf16[2,512,128]{2,1,0:T(8,128)(2,1)} %base.2, bf16[2,512,128]{2,1,0:T(8,128)(2,1)} %base.3, bf16[2,128,128]{2,1,0:T(8,128)(2,1)} %copy-done.6, ...), custom_call_target="tpu_custom_call" | custom-call | tf_op jit(solution)/shard_map/pallas_call | solution.py:34
  29.8 3.0 %collective-permute-start.6 = (bf16[1584,128]{1,0:T(8,128)(2,1)}, bf16[1584,128]{1,0:T(8,128)(2,1)S(1)}, u32[]{:S(2)}, u32[]{:S(2)}) collective-permute-start(bf16[1584,128]{1,0:T(8,128)(2,1)} %get-tuple-element.46), channel_id=1, source_target_pairs={{0,1},{1,0},{2,3},{3,2},{4,5},{5,4},{6,7},{7,6},{8,9},{9,8},{10,11... | collective-permute-start | bytes 1216520 | tf_op jit(solution)/shard_map/ppermute | solution.py:375
  33.4 1.3 %collective-permute-done.4.ppos = s32[2]{0:T(128)S(1)} collective-permute-done((s32[2]{0:T(128)S(1)}, s32[2]{0:T(128)S(1)}, u32[]{:S(2)}, u32[]{:S(2)}) %collective-permute-start.4) | collective-permute-done | bytes 40 | tf_op jit(solution)/shard_map/ppermute | solution.py:362
  35.6 5.5 %shard_map.96 = (f32[1728,128]{1,0:T(8,128)}, bf16[1744,128]{1,0:T(8,128)(2,1)}, f32[8,128]{1,0:T(8,128)}) custom-call(s32[2]{0:T(128)} %pos.15, s32[2]{0:T(128)} %copy-done.20, s32[3]{0:T(128)} %pad_add_fusion.meta, bf16[2,512,128]{2,1,0:T(8,128)(2,1)} %base.2, bf16[2,512,128]{2,1,0:T(8,128)(2,1)} %base.3, bf16[2,128,128]{2,1,0:T(8,128)(2,1)} %copy-done.6, ...), custom_call_target="tpu_custom_call" | custom-call | tf_op jit(solution)/shard_map/pallas_call | solution.py:34
  41.0 2.5 %collective-permute-start.7 = (bf16[1744,128]{1,0:T(8,128)(2,1)}, bf16[1744,128]{1,0:T(8,128)(2,1)S(1)}, u32[]{:S(2)}, u32[]{:S(2)}) collective-permute-start(bf16[1744,128]{1,0:T(8,128)(2,1)} %get-tuple-element.49), channel_id=1, source_target_pairs={{0,8},{1,17},{2,10},{3,19},{4,12},{5,21},{6,14},{7,23},{8,0},{9,25... | collective-permute-start | bytes 1339400 | tf_op jit(solution)/shard_map/ppermute | solution.py:425
  43.5 1.8 %shard_map.98 = (bf16[2,128,128]{2,1,0:T(8,128)(2,1)}, bf16[2,128,128]{2,1,0:T(8,128)(2,1)}) custom-call(s32[2]{0:T(128)} %pos.15, bf16[2,512,128]{2,1,0:T(8,128)(2,1)} %get-tuple-element.62.hid.a.src, bf16[2,512,128]{2,1,0:T(8,128)(2,1)} %get-tuple-element.68.pre.b.src), custom_call_target="tpu_custom_call" | custom-call | tf_op jit(solution)/shard_map/pallas_call | solution.py:34
  45.3 4.7 %collective-permute-done.7.got = bf16[1744,128]{1,0:T(8,128)(2,1)S(1)} collective-permute-done((bf16[1744,128]{1,0:T(8,128)(2,1)}, bf16[1744,128]{1,0:T(8,128)(2,1)S(1)}, u32[]{:S(2)}, u32[]{:S(2)}) %collective-permute-start.7) | collective-permute-done | bytes 446496 | tf_op jit(solution)/shard_map/ppermute | solution.py:425
  50.0 0.8 copy-done.8
  50.8 2.2 %shard_map.97 = (f32[864,128]{1,0:T(8,128)}, bf16[880,128]{1,0:T(8,128)(2,1)}, f32[8,128]{1,0:T(8,128)}) custom-call(f32[1728,128]{1,0:T(8,128)} %get-tuple-element.48.low, bf16[1744,128]{1,0:T(8,128)(2,1)} %copy-done.8, f32[8,128]{1,0:T(8,128)} %get-tuple-element.50.g), custom_call_target="tpu_custom_call" | custom-call | tf_op jit(solution)/shard_map/pallas_call | solution.py:34
  53.0 1.1 collective-permute-start.8
  54.1 2.8 %collective-permute-start.9 = (bf16[2,128,128]{2,1,0:T(8,128)(2,1)}, bf16[2,128,128]{2,1,0:T(8,128)(2,1)S(1)}, u32[]{:S(2)}, u32[]{:S(2)}) collective-permute-start(bf16[2,128,128]{2,1,0:T(8,128)(2,1)} %get-tuple-element.59), channel_id=1, source_target_pairs={{0,8},{8,16},{16,24},{1,9},{9,17},{17,25},{2,10},{10,18},{18,26},{... | collective-permute-start | bytes 196616 | tf_op jit(solution)/shard_map/ppermute | solution.py:301
  56.9 1.3 %collective-permute-start.10 = (bf16[2,128,128]{2,1,0:T(8,128)(2,1)}, bf16[2,128,128]{2,1,0:T(8,128)(2,1)S(1)}, u32[]{:S(2)}, u32[]{:S(2)}) collective-permute-start(bf16[2,128,128]{2,1,0:T(8,128)(2,1)} %get-tuple-element.54), channel_id=1, source_target_pairs={{8,0},{16,8},{24,16},{9,1},{17,9},{25,17},{10,2},{18,10},{26,18},{... | collective-permute-start | bytes 196616 | tf_op jit(solution)/shard_map/ppermute | solution.py:302
  58.2 0.9 collective-permute-done.9.xl
  59.2 4.2 %collective-permute-done.10.xr = bf16[2,128,128]{2,1,0:T(8,128)(2,1)S(1)} collective-permute-done((bf16[2,128,128]{2,1,0:T(8,128)(2,1)}, bf16[2,128,128]{2,1,0:T(8,128)(2,1)S(1)}, u32[]{:S(2)}, u32[]{:S(2)}) %collective-permute-start.10) | collective-permute-done | bytes 65568 | tf_op jit(solution)/shard_map/ppermute | solution.py:302
  64.0 1.8 %shard_map.100 = (bf16[2,144,128]{2,1,0:T(8,128)(2,1)}, bf16[2,144,128]{2,1,0:T(8,128)(2,1)}) custom-call(s32[2]{0:T(128)} %pos.15, bf16[2,512,128]{2,1,0:T(8,128)(2,1)} %get-tuple-element.62.hid.a.src, bf16[2,512,128]{2,1,0:T(8,128)(2,1)} %get-tuple-element.68.pre.b.src, bf16[2,128,128]{2,1,0:T(8,128)(2,1)} %copy-done.4, bf16[2,128,128]{2,1,0:T(8,128)(2,1)} %copy-done.5), custom_call_target="tpu_custom_call" | custom-call | tf_op jit(solution)/shard_map/pallas_call | solution.py:34
  65.8 0.7 copy-done.15
  66.5 1.9 %shard_map.99 = (f32[432,128]{1,0:T(8,128)}, bf16[448,128]{1,0:T(8,128)(2,1)}, f32[8,128]{1,0:T(8,128)}) custom-call(f32[864,128]{1,0:T(8,128)} %get-tuple-element.51.low, bf16[880,128]{1,0:T(8,128)(2,1)} %copy-done.15, f32[8,128]{1,0:T(8,128)} %get-tuple-element.56.g), custom_call_target="tpu_custom_call" | custom-call | tf_op jit(solution)/shard_map/pallas_call | solution.py:34
  68.4 1.6 %collective-permute-start.13 = (bf16[448,128]{1,0:T(8,128)(2,1)}, bf16[448,128]{1,0:T(8,128)(2,1)S(1)}, u32[]{:S(2)}, u32[]{:S(2)}) collective-permute-start(bf16[448,128]{1,0:T(8,128)(2,1)} %get-tuple-element.61), channel_id=1, source_target_pairs={{0,2},{1,3},{2,0},{3,1},{4,6},{5,7},{6,4},{7,5},{8,10},{9,11},{10,... | collective-permute-start | bytes 344072 | tf_op jit(solution)/shard_map/ppermute | solution.py:425
  69.9 1.3 %collective-permute-start.11 = (bf16[2,144,128]{2,1,0:T(8,128)(2,1)}, bf16[2,144,128]{2,1,0:T(8,128)(2,1)S(1)}, u32[]{:S(2)}, u32[]{:S(2)}) collective-permute-start(bf16[2,144,128]{2,1,0:T(8,128)(2,1)} %get-tuple-element.63), channel_id=1, source_target_pairs={{0,1},{1,2},{2,3},{3,4},{4,5},{5,6},{6,7},{8,9},{9,10},{10,11},{11... | collective-permute-start | bytes 221192 | tf_op jit(solution)/shard_map/ppermute | solution.py:301
  71.2 1.3 %collective-permute-start.12 = (bf16[2,144,128]{2,1,0:T(8,128)(2,1)}, bf16[2,144,128]{2,1,0:T(8,128)(2,1)S(1)}, u32[]{:S(2)}, u32[]{:S(2)}) collective-permute-start(bf16[2,144,128]{2,1,0:T(8,128)(2,1)} %get-tuple-element.60), channel_id=1, source_target_pairs={{1,0},{2,1},{3,2},{4,3},{5,4},{6,5},{7,6},{9,8},{10,9},{11,10},{12... | collective-permute-start | bytes 221192 | tf_op jit(solution)/shard_map/ppermute | solution.py:302
  72.5 2.8 %collective-permute-done.12.yr = bf16[2,144,128]{2,1,0:T(8,128)(2,1)S(1)} collective-permute-done((bf16[2,144,128]{2,1,0:T(8,128)(2,1)}, bf16[2,144,128]{2,1,0:T(8,128)(2,1)S(1)}, u32[]{:S(2)}, u32[]{:S(2)}) %collective-permute-start.12) | collective-permute-done | bytes 73760 | tf_op jit(solution)/shard_map/ppermute | solution.py:302
  75.9 3.9 %shard_map.101 = bf16[2,512,128]{2,1,0:T(8,128)(2,1)} custom-call(s32[2]{0:T(128)} %pos.15, bf16[2,512,128]{2,1,0:T(8,128)(2,1)} %get-tuple-element.62.hid.a.src, bf16[2,128,128]{2,1,0:T(8,128)(2,1)} %copy-done.4, bf16[2,128,128]{2,1,0:T(8,128)(2,1)} %copy-done.5, bf16[2,144,128]{2,1,0:T(8,128)(2,1)} %copy-done.10, bf16[2,144,128]{2,1,0:T(8,128)(2,1)} %copy-done.11, ...), custom_call_target="tpu_custom_call" | custom-call | tf_op jit(solution)/shard_map/pallas_call | solution.py:34
  80.5 1.7 %shard_map.102 = (f32[216,128]{1,0:T(8,128)}, f32[232,128]{1,0:T(8,128)}, f32[8,128]{1,0:T(8,128)}) custom-call(f32[432,128]{1,0:T(8,128)} %get-tuple-element.64.low, bf16[448,128]{1,0:T(8,128)(2,1)} %copy-done.17, f32[8,128]{1,0:T(8,128)} %get-tuple-element.65.g), custom_call_target="tpu_custom_call" | custom-call | tf_op jit(solution)/shard_map/pallas_call | solution.py:34
  82.2 3.8 %collective-permute-start.14 = (f32[232,128]{1,0:T(8,128)}, f32[232,128]{1,0:T(8,128)S(1)}, u32[]{:S(2)}, u32[]{:S(2)}) collective-permute-start(f32[232,128]{1,0:T(8,128)} %get-tuple-element.67), channel_id=1, source_target_pairs={{0,4},{1,5},{2,6},{3,7},{4,0},{5,1},{6,2},{7,3},{8,12},{9,13},{10,... | collective-permute-start | bytes 356360 | tf_op jit(solution)/shard_map/ppermute | solution.py:425
  86.0 4.1 %shard_map.103 = bf16[2,512,128]{2,1,0:T(8,128)(2,1)} custom-call(s32[2]{0:T(128)} %pos.15, bf16[2,512,128]{2,1,0:T(8,128)(2,1)} %get-tuple-element.68.pre.b.src, bf16[2,128,128]{2,1,0:T(8,128)(2,1)} %copy-done.4, bf16[2,128,128]{2,1,0:T(8,128)(2,1)} %copy-done.5, bf16[2,144,128]{2,1,0:T(8,128)(2,1)} %copy-done.10, bf16[2,144,128]{2,1,0:T(8,128)(2,1)} %copy-done.11, ...), custom_call_target="tpu_custom_call" | custom-call | tf_op jit(solution)/shard_map/pallas_call | solution.py:34
  90.7 1.6 %shard_map.104 = (f32[232,128]{1,0:T(8,128)}, f32[8,128]{1,0:T(8,128)}) custom-call(f32[216,128]{1,0:T(8,128)} %get-tuple-element.69.low, f32[232,128]{1,0:T(8,128)} %copy-done.16, f32[8,128]{1,0:T(8,128)} %get-tuple-element.70.g), custom_call_target="tpu_custom_call" | custom-call | tf_op jit(solution)/shard_map/pallas_call | solution.py:34
  92.4 0.9 constant_dynamic-update-slice_fusion.4
  93.3 2.4 %collective-permute-start.15 = (bf16[216,128]{1,0:T(8,128)(2,1)S(1)}, bf16[216,128]{1,0:T(8,128)(2,1)S(1)}, u32[]{:S(2)}, u32[]{:S(2)}) collective-permute-start(bf16[216,128]{1,0:T(8,128)(2,1)S(1)} %get-tuple-element.77), channel_id=1, source_target_pairs={{0,4},{1,5},{2,6},{3,7},{4,0},{5,1},{6,2},{7,3},{8,12},{9,13},{10,... | collective-permute-start | bytes 165896 | tf_op jit(solution)/shard_map/ppermute | solution.py:448
  95.7 2.7 %collective-permute-done.15 = bf16[216,128]{1,0:T(8,128)(2,1)S(1)} collective-permute-done((bf16[216,128]{1,0:T(8,128)(2,1)S(1)}, bf16[216,128]{1,0:T(8,128)(2,1)S(1)}, u32[]{:S(2)}, u32[]{:S(2)}) %collective-permute-start.15) | collective-permute-done | bytes 55328 | tf_op jit(solution)/shard_map/ppermute | solution.py:448
  98.4 3.0 %collective-permute-start.16 = (bf16[432,128]{1,0:T(8,128)(2,1)S(1)}, bf16[432,128]{1,0:T(8,128)(2,1)S(1)}, u32[]{:S(2)}, u32[]{:S(2)}) collective-permute-start(bf16[432,128]{1,0:T(8,128)(2,1)S(1)} %pad_maximum_fusion.2), channel_id=1, source_target_pairs={{0,2},{1,3},{2,0},{3,1},{4,6},{5,7},{6,4},{7,5},{8,10},{9,11},{10,... | collective-permute-start | bytes 331784 | tf_op jit(solution)/shard_map/ppermute | solution.py:448
  101.4 3.4 %collective-permute-done.16 = bf16[432,128]{1,0:T(8,128)(2,1)S(1)} collective-permute-done((bf16[432,128]{1,0:T(8,128)(2,1)S(1)}, bf16[432,128]{1,0:T(8,128)(2,1)S(1)}, u32[]{:S(2)}, u32[]{:S(2)}) %collective-permute-start.16) | collective-permute-done | bytes 110624 | tf_op jit(solution)/shard_map/ppermute | solution.py:448
  104.9 2.1 %collective-permute-start.17 = (bf16[864,128]{1,0:T(8,128)(2,1)S(1)}, bf16[864,128]{1,0:T(8,128)(2,1)S(1)}, u32[]{:S(2)}, u32[]{:S(2)}) collective-permute-start(bf16[864,128]{1,0:T(8,128)(2,1)S(1)} %pad_maximum_fusion.1), channel_id=1, source_target_pairs={{0,16},{1,9},{2,18},{3,11},{4,20},{5,13},{6,22},{7,15},{8,24},{9,1... | collective-permute-start | bytes 663560 | tf_op jit(solution)/shard_map/ppermute | solution.py:448
  107.0 3.9 %collective-permute-done.17 = bf16[864,128]{1,0:T(8,128)(2,1)S(1)} collective-permute-done((bf16[864,128]{1,0:T(8,128)(2,1)S(1)}, bf16[864,128]{1,0:T(8,128)(2,1)S(1)}, u32[]{:S(2)}, u32[]{:S(2)}) %collective-permute-start.17) | collective-permute-done | bytes 221216 | tf_op jit(solution)/shard_map/ppermute | solution.py:448
  110.9 2.4 %collective-permute-start.18 = (bf16[1728,128]{1,0:T(8,128)(2,1)S(1)}, bf16[1728,128]{1,0:T(8,128)(2,1)S(1)}, u32[]{:S(2)}, u32[]{:S(2)}) collective-permute-start(bf16[1728,128]{1,0:T(8,128)(2,1)S(1)} %pad_maximum_fusion), channel_id=1, source_target_pairs={{0,8},{1,17},{2,10},{3,19},{4,12},{5,21},{6,14},{7,23},{8,0},{9,25... | collective-permute-start | bytes 1327112 | tf_op jit(solution)/shard_map/ppermute | solution.py:448
  113.4 6.2 %collective-permute-done.18 = bf16[1728,128]{1,0:T(8,128)(2,1)S(1)} collective-permute-done((bf16[1728,128]{1,0:T(8,128)(2,1)S(1)}, bf16[1728,128]{1,0:T(8,128)(2,1)S(1)}, u32[]{:S(2)}, u32[]{:S(2)}) %collective-permute-start.18) | collective-permute-done | bytes 442400 | tf_op jit(solution)/shard_map/ppermute | solution.py:448
  120.2 1.9 %collective-permute-done.20.part_g = f32[8,128]{1,0:T(8,128)S(1)} collective-permute-done((f32[8,128]{1,0:T(8,128)}, f32[8,128]{1,0:T(8,128)S(1)}, u32[]{:S(2)}, u32[]{:S(2)}) %collective-permute-start.20) | collective-permute-done | bytes 4128 | tf_op jit(solution)/shard_map/ppermute | solution.py:450
  122.8 0.9 copy-done.3
  123.7 4.3 %shard_map.105 = (f32[2,27,128,128]{3,2,1,0:T(8,128)}, f32[1,128]{1,0:T(1,128)}) custom-call(s32[3]{0:T(128)} %pad_add_fusion.meta, bf16[3456,128]{1,0:T(8,128)(2,1)} %copy-done.2, bf16[3456,128]{1,0:T(8,128)(2,1)} %copy-done.3, f32[8,128]{1,0:T(8,128)} %get-tuple-element.73.own_g, f32[8,128]{1,0:T(8,128)} %copy-done.19), custom_call_target="tpu_custom_call" | custom-call | tf_op jit(solution)/shard_map/pallas_call | solution.py:34
  (59 shorter events, 6.6 us)
Async XLA Ops:
  0.6 32.3 %copy-start.18 = (s32[2]{0:T(128)S(1)}, s32[2]{0:T(128)}, u32[]{:S(2)}) copy-start(s32[2]{0:T(128)} %pos.15) | copy-start | bytes 28
  0.6 32.1 %copy-start.1 = (bf16[2,512,128]{2,1,0:T(8,128)(2,1)S(1)}, bf16[2,512,128]{2,1,0:T(8,128)(2,1)}, u32[]{:S(2)}) copy-start(bf16[2,512,128]{2,1,0:T(8,128)(2,1)} %base.3) | copy-start | bytes 786436
  0.7 32.1 %copy-start = (bf16[2,512,128]{2,1,0:T(8,128)(2,1)S(1)}, bf16[2,512,128]{2,1,0:T(8,128)(2,1)}, u32[]{:S(2)}) copy-start(bf16[2,512,128]{2,1,0:T(8,128)(2,1)} %base.2) | copy-start | bytes 786436
  2.5 7.1 %collective-permute-start = (bf16[2,128,128]{2,1,0:T(8,128)(2,1)}, bf16[2,128,128]{2,1,0:T(8,128)(2,1)S(1)}, u32[]{:S(2)}, u32[]{:S(2)}) collective-permute-start(bf16[2,128,128]{2,1,0:T(8,128)(2,1)} %get-tuple-element.40), channel_id=1, source_target_pairs={{0,8},{8,16},{16,24},{1,9},{9,17},{17,25},{2,10},{10,18},{18,26},{... | collective-permute-start | bytes 196616 | tf_op jit(solution)/shard_map/ppermute | solution.py:301
  7.4 6.4 %collective-permute-start.1 = (bf16[2,128,128]{2,1,0:T(8,128)(2,1)}, bf16[2,128,128]{2,1,0:T(8,128)(2,1)S(1)}, u32[]{:S(2)}, u32[]{:S(2)}) collective-permute-start(bf16[2,128,128]{2,1,0:T(8,128)(2,1)} %get-tuple-element.41), channel_id=1, source_target_pairs={{8,0},{16,8},{24,16},{9,1},{17,9},{25,17},{10,2},{18,10},{26,18},{... | collective-permute-start | bytes 196616 | tf_op jit(solution)/shard_map/ppermute | solution.py:302
  9.6 4.2 %copy-start.6 = (bf16[2,128,128]{2,1,0:T(8,128)(2,1)}, bf16[2,128,128]{2,1,0:T(8,128)(2,1)S(1)}, u32[]{:S(2)}) copy-start(bf16[2,128,128]{2,1,0:T(8,128)(2,1)S(1)} %collective-permute-done.xl) | copy-start | bytes 196612
  13.7 0.6 copy-start.7
  16.2 3.3 %collective-permute-start.2 = (bf16[2,144,128]{2,1,0:T(8,128)(2,1)}, bf16[2,144,128]{2,1,0:T(8,128)(2,1)S(1)}, u32[]{:S(2)}, u32[]{:S(2)}) collective-permute-start(bf16[2,144,128]{2,1,0:T(8,128)(2,1)} %get-tuple-element.42), channel_id=1, source_target_pairs={{0,1},{1,2},{2,3},{3,4},{4,5},{5,6},{6,7},{8,9},{9,10},{10,11},{11... | collective-permute-start | bytes 221192 | tf_op jit(solution)/shard_map/ppermute | solution.py:301
  17.5 5.2 %collective-permute-start.3 = (bf16[2,144,128]{2,1,0:T(8,128)(2,1)}, bf16[2,144,128]{2,1,0:T(8,128)(2,1)S(1)}, u32[]{:S(2)}, u32[]{:S(2)}) collective-permute-start(bf16[2,144,128]{2,1,0:T(8,128)(2,1)} %get-tuple-element.43), channel_id=1, source_target_pairs={{1,0},{2,1},{3,2},{4,3},{5,4},{6,5},{7,6},{9,8},{10,9},{11,10},{12... | collective-permute-start | bytes 221192 | tf_op jit(solution)/shard_map/ppermute | solution.py:302
  19.5 3.2 %copy-start.12 = (bf16[2,144,128]{2,1,0:T(8,128)(2,1)}, bf16[2,144,128]{2,1,0:T(8,128)(2,1)S(1)}, u32[]{:S(2)}) copy-start(bf16[2,144,128]{2,1,0:T(8,128)(2,1)S(1)} %collective-permute-done.2.yl) | copy-start | bytes 221188
  22.7 0.6 copy-start.13
  29.8 5.0 %collective-permute-start.6 = (bf16[1584,128]{1,0:T(8,128)(2,1)}, bf16[1584,128]{1,0:T(8,128)(2,1)S(1)}, u32[]{:S(2)}, u32[]{:S(2)}) collective-permute-start(bf16[1584,128]{1,0:T(8,128)(2,1)} %get-tuple-element.46), channel_id=1, source_target_pairs={{0,1},{1,0},{2,3},{3,2},{4,5},{5,4},{6,7},{7,6},{8,9},{9,8},{10,11... | collective-permute-start | bytes 1216520 | tf_op jit(solution)/shard_map/ppermute | solution.py:375
  32.8 1.9 %collective-permute-start.5 = (bf16[2,512,128]{2,1,0:T(8,128)(2,1)S(1)}, bf16[2,512,128]{2,1,0:T(8,128)(2,1)S(1)}, u32[]{:S(2)}, u32[]{:S(2)}) collective-permute-start(bf16[2,512,128]{2,1,0:T(8,128)(2,1)S(1)} %broadcast_select_fusion), channel_id=1, source_target_pairs={{0,1},{1,0},{2,3},{3,2},{4,5},{5,4},{6,7},{7,6},{8,9},{9,8},{10,11... | collective-permute-start | bytes 786440 | tf_op jit(solution)/shard_map/ppermute | solution.py:363
  32.9 1.8 %collective-permute-start.4 = (s32[2]{0:T(128)S(1)}, s32[2]{0:T(128)S(1)}, u32[]{:S(2)}, u32[]{:S(2)}) collective-permute-start(s32[2]{0:T(128)S(1)} %copy-done.18), channel_id=1, source_target_pairs={{0,1},{1,0},{2,3},{3,2},{4,5},{5,4},{6,7},{7,6},{8,9},{9,8},{10,11... | collective-permute-start | bytes 32 | tf_op jit(solution)/shard_map/ppermute | solution.py:362
  34.7 0.5 copy-start.20
  34.7 0.7 copy-start.14
  34.7 0.8 copy-start.9
  41.0 9.0 %collective-permute-start.7 = (bf16[1744,128]{1,0:T(8,128)(2,1)}, bf16[1744,128]{1,0:T(8,128)(2,1)S(1)}, u32[]{:S(2)}, u32[]{:S(2)}) collective-permute-start(bf16[1744,128]{1,0:T(8,128)(2,1)} %get-tuple-element.49), channel_id=1, source_target_pairs={{0,8},{1,17},{2,10},{3,19},{4,12},{5,21},{6,14},{7,23},{8,0},{9,25... | collective-permute-start | bytes 1339400 | tf_op jit(solution)/shard_map/ppermute | solution.py:425
  50.0 0.8 copy-start.8
  53.0 12.8 %collective-permute-start.8 = (bf16[880,128]{1,0:T(8,128)(2,1)}, bf16[880,128]{1,0:T(8,128)(2,1)S(1)}, u32[]{:S(2)}, u32[]{:S(2)}) collective-permute-start(bf16[880,128]{1,0:T(8,128)(2,1)} %get-tuple-element.55), channel_id=1, source_target_pairs={{0,16},{1,9},{2,18},{3,11},{4,20},{5,13},{6,22},{7,15},{8,24},{9,1... | collective-permute-start | bytes 675848 | tf_op jit(solution)/shard_map/ppermute | solution.py:425
  54.1 5.0 %collective-permute-start.9 = (bf16[2,128,128]{2,1,0:T(8,128)(2,1)}, bf16[2,128,128]{2,1,0:T(8,128)(2,1)S(1)}, u32[]{:S(2)}, u32[]{:S(2)}) collective-permute-start(bf16[2,128,128]{2,1,0:T(8,128)(2,1)} %get-tuple-element.59), channel_id=1, source_target_pairs={{0,8},{8,16},{16,24},{1,9},{9,17},{17,25},{2,10},{10,18},{18,26},{... | collective-permute-start | bytes 196616 | tf_op jit(solution)/shard_map/ppermute | solution.py:301
  56.9 6.4 %collective-permute-start.10 = (bf16[2,128,128]{2,1,0:T(8,128)(2,1)}, bf16[2,128,128]{2,1,0:T(8,128)(2,1)S(1)}, u32[]{:S(2)}, u32[]{:S(2)}) collective-permute-start(bf16[2,128,128]{2,1,0:T(8,128)(2,1)} %get-tuple-element.54), channel_id=1, source_target_pairs={{8,0},{16,8},{24,16},{9,1},{17,9},{25,17},{10,2},{18,10},{26,18},{... | collective-permute-start | bytes 196616 | tf_op jit(solution)/shard_map/ppermute | solution.py:302
  59.1 4.2 %copy-start.4 = (bf16[2,128,128]{2,1,0:T(8,128)(2,1)}, bf16[2,128,128]{2,1,0:T(8,128)(2,1)S(1)}, u32[]{:S(2)}) copy-start(bf16[2,128,128]{2,1,0:T(8,128)(2,1)S(1)} %collective-permute-done.9.xl) | copy-start | bytes 196612
  63.3 0.6 copy-start.5
  65.8 0.7 copy-start.15
  68.4 11.5 %collective-permute-start.13 = (bf16[448,128]{1,0:T(8,128)(2,1)}, bf16[448,128]{1,0:T(8,128)(2,1)S(1)}, u32[]{:S(2)}, u32[]{:S(2)}) collective-permute-start(bf16[448,128]{1,0:T(8,128)(2,1)} %get-tuple-element.61), channel_id=1, source_target_pairs={{0,2},{1,3},{2,0},{3,1},{4,6},{5,7},{6,4},{7,5},{8,10},{9,11},{10,... | collective-permute-start | bytes 344072 | tf_op jit(solution)/shard_map/ppermute | solution.py:425
  69.9 2.6 %collective-permute-start.11 = (bf16[2,144,128]{2,1,0:T(8,128)(2,1)}, bf16[2,144,128]{2,1,0:T(8,128)(2,1)S(1)}, u32[]{:S(2)}, u32[]{:S(2)}) collective-permute-start(bf16[2,144,128]{2,1,0:T(8,128)(2,1)} %get-tuple-element.63), channel_id=1, source_target_pairs={{0,1},{1,2},{2,3},{3,4},{4,5},{5,6},{6,7},{8,9},{9,10},{10,11},{11... | collective-permute-start | bytes 221192 | tf_op jit(solution)/shard_map/ppermute | solution.py:301
  71.2 4.1 %collective-permute-start.12 = (bf16[2,144,128]{2,1,0:T(8,128)(2,1)}, bf16[2,144,128]{2,1,0:T(8,128)(2,1)S(1)}, u32[]{:S(2)}, u32[]{:S(2)}) collective-permute-start(bf16[2,144,128]{2,1,0:T(8,128)(2,1)} %get-tuple-element.60), channel_id=1, source_target_pairs={{1,0},{2,1},{3,2},{4,3},{5,4},{6,5},{7,6},{9,8},{10,9},{11,10},{12... | collective-permute-start | bytes 221192 | tf_op jit(solution)/shard_map/ppermute | solution.py:302
  72.5 2.8 %copy-start.10 = (bf16[2,144,128]{2,1,0:T(8,128)(2,1)}, bf16[2,144,128]{2,1,0:T(8,128)(2,1)S(1)}, u32[]{:S(2)}) copy-start(bf16[2,144,128]{2,1,0:T(8,128)(2,1)S(1)} %collective-permute-done.11.yl) | copy-start | bytes 221188
  75.3 0.6 copy-start.11
  79.9 0.6 copy-start.17
  82.2 7.9 %collective-permute-start.14 = (f32[232,128]{1,0:T(8,128)}, f32[232,128]{1,0:T(8,128)S(1)}, u32[]{:S(2)}, u32[]{:S(2)}) collective-permute-start(f32[232,128]{1,0:T(8,128)} %get-tuple-element.67), channel_id=1, source_target_pairs={{0,4},{1,5},{2,6},{3,7},{4,0},{5,1},{6,2},{7,3},{8,12},{9,13},{10,... | collective-permute-start | bytes 356360 | tf_op jit(solution)/shard_map/ppermute | solution.py:425
  90.1 0.6 copy-start.16
  93.3 5.1 %collective-permute-start.15 = (bf16[216,128]{1,0:T(8,128)(2,1)S(1)}, bf16[216,128]{1,0:T(8,128)(2,1)S(1)}, u32[]{:S(2)}, u32[]{:S(2)}) collective-permute-start(bf16[216,128]{1,0:T(8,128)(2,1)S(1)} %get-tuple-element.77), channel_id=1, source_target_pairs={{0,4},{1,5},{2,6},{3,7},{4,0},{5,1},{6,2},{7,3},{8,12},{9,13},{10,... | collective-permute-start | bytes 165896 | tf_op jit(solution)/shard_map/ppermute | solution.py:448
  98.4 6.4 %collective-permute-start.16 = (bf16[432,128]{1,0:T(8,128)(2,1)S(1)}, bf16[432,128]{1,0:T(8,128)(2,1)S(1)}, u32[]{:S(2)}, u32[]{:S(2)}) collective-permute-start(bf16[432,128]{1,0:T(8,128)(2,1)S(1)} %pad_maximum_fusion.2), channel_id=1, source_target_pairs={{0,2},{1,3},{2,0},{3,1},{4,6},{5,7},{6,4},{7,5},{8,10},{9,11},{10,... | collective-permute-start | bytes 331784 | tf_op jit(solution)/shard_map/ppermute | solution.py:448
  104.9 6.0 %collective-permute-start.17 = (bf16[864,128]{1,0:T(8,128)(2,1)S(1)}, bf16[864,128]{1,0:T(8,128)(2,1)S(1)}, u32[]{:S(2)}, u32[]{:S(2)}) collective-permute-start(bf16[864,128]{1,0:T(8,128)(2,1)S(1)} %pad_maximum_fusion.1), channel_id=1, source_target_pairs={{0,16},{1,9},{2,18},{3,11},{4,20},{5,13},{6,22},{7,15},{8,24},{9,1... | collective-permute-start | bytes 663560 | tf_op jit(solution)/shard_map/ppermute | solution.py:448
  110.9 8.7 %collective-permute-start.18 = (bf16[1728,128]{1,0:T(8,128)(2,1)S(1)}, bf16[1728,128]{1,0:T(8,128)(2,1)S(1)}, u32[]{:S(2)}, u32[]{:S(2)}) collective-permute-start(bf16[1728,128]{1,0:T(8,128)(2,1)S(1)} %pad_maximum_fusion), channel_id=1, source_target_pairs={{0,8},{1,17},{2,10},{3,19},{4,12},{5,21},{6,14},{7,23},{8,0},{9,25... | collective-permute-start | bytes 1327112 | tf_op jit(solution)/shard_map/ppermute | solution.py:448
  119.7 2.5 %copy-start.2 = (bf16[3456,128]{1,0:T(8,128)(2,1)}, bf16[3456,128]{1,0:T(8,128)(2,1)S(1)}, u32[]{:S(2)}) copy-start(bf16[3456,128]{1,0:T(8,128)(2,1)S(1)} %constant_dynamic-update-slice_fusion.own) | copy-start | bytes 2654212
  119.7 2.5 %collective-permute-start.19 = (bf16[3456,128]{1,0:T(8,128)(2,1)S(1)}, bf16[3456,128]{1,0:T(8,128)(2,1)S(1)}, u32[]{:S(2)}, u32[]{:S(2)}) collective-permute-start(bf16[3456,128]{1,0:T(8,128)(2,1)S(1)} %constant_dynamic-update-slice_fusion.own), channel_id=1, source_target_pairs={{0,1},{1,0},{2,3},{3,2},{4,5},{5,4},{6,7},{7,6},{8,9},{9,8},{10,11... | collective-permute-start | bytes 2654216 | tf_op jit(solution)/shard_map/ppermute | solution.py:449
  119.8 2.4 %collective-permute-start.20 = (f32[8,128]{1,0:T(8,128)}, f32[8,128]{1,0:T(8,128)S(1)}, u32[]{:S(2)}, u32[]{:S(2)}) collective-permute-start(f32[8,128]{1,0:T(8,128)} %get-tuple-element.73.own_g), channel_id=1, source_target_pairs={{0,1},{1,0},{2,3},{3,2},{4,5},{5,4},{6,7},{7,6},{8,9},{9,8},{10,11... | collective-permute-start | bytes 12296 | tf_op jit(solution)/shard_map/ppermute | solution.py:450
  122.2 0.6 copy-start.19
  122.8 0.9 copy-start.3

commit v2 on v1

--- a/solution.py
+++ b/solution.py
@@ -6,6 +6,7 @@
 from jax.experimental import pallas as pl
 from jax.experimental.pallas import tpu as pltpu
 from jax.sharding import PartitionSpec as P
+
 
 BY = 2
 POS = 4
@@ -17,7 +18,7 @@
 f32, bf16 = jnp.float32, jnp.bfloat16
 VMEM = pl.BlockSpec(memory_space=pltpu.VMEM)
 SMEM = pl.BlockSpec(memory_space=pltpu.SMEM)
-PARAMS = pltpu.CompilerParams(vmem_limit_bytes=56 << 20)
+PARAMS = pltpu.CompilerParams(vmem_limit_bytes=28 << 20)
 
 
 def sds(shape, dtype):
@@ -41,37 +42,49 @@
     )(*args)
 
 
+def pack_x(pos, src, f, lo, hi):
+    for s in range(2):
+        live, bx, by = place(pos, s)
+        rows = pl.ds(pl.multiple_of(by * 64, 64), 64)
+
+        @pl.when(live & (bx == 0))
+        def _():
+            lo[f, rows] = src[s, 0:64]
+
+        @pl.when(live & (bx == 1))
+        def _():
+            hi[f, rows] = src[s, 448:512]
+
+
 def pack_x_body(pos, a, b, lo, hi):
     lo[...] = jnp.zeros_like(lo)
     hi[...] = jnp.zeros_like(hi)
-    for f, src in enumerate((a, b)):
-        for s in range(2):
-            live, bx, by = place(pos, s)
-            rows = pl.ds(pl.multiple_of(by * 64, 64), 64)
-
-            @pl.when(live & (bx == 0))
-            def _():
-                lo[f, rows, :] = src[s, 0:64, :]
-
-            @pl.when(live & (bx == 1))
-            def _():
-                hi[f, rows, :] = src[s, 448:512, :]
+    pack_x(pos, a, 0, lo, hi)
+    pack_x(pos, b, 1, lo, hi)
+
+
+def load_body(pos, core, a, b, a_out, b_out, sent, lo, hi):
+    pack_x_body(pos, a, b, lo, hi)
+    a_out[...] = a[...]
+    b_out[...] = b[...]
+    sent[...] = jnp.where(core[0] == 0, b[...], a[...])
 
 
 def pack_y_body(pos, a, b, xl, xr, lo, hi, tmp):
     for f, src in enumerate((a, b)):
         for d, out in enumerate((lo, hi)):
             tmp[...] = jnp.zeros_like(tmp)
-            at = 120 * d
-            tmp[0] = xl[f, :, :].astype(f32)[at : at + 8]
-            tmp[17] = xr[f, :, :].astype(f32)[at : at + 8]
+            at = 112 * d
+            tmp[0] = xl[f, at : at + 16].astype(f32)[8 * d : 8 * d + 8]
+            tmp[17] = xr[f, at : at + 16].astype(f32)[8 * d : 8 * d + 8]
             for s in range(2):
                 live, bx, by = place(pos, s)
 
                 @pl.when(live & (by == d))
                 def _():
-                    cube = src[s].astype(f32).reshape(8, 8, 8, C)
-                    tmp[pl.ds(1 + bx * 8, 8)] = cube[:, 7 * d]
+                    for x in range(8):
+                        at = x * 64 + 48 * d
+                        tmp[1 + bx * 8 + x] = src[s, at : at + 16].astype(f32)[8 * d : 8 * d + 8]
 
             out[f] = tmp[...].reshape(144, C).astype(bf16)
 
@@ -109,13 +122,13 @@
     return jnp.where(z == 0, 0.0, pltpu.roll(v, 1, 1))
 
 
-def fill_weights(w, k, flipped):
-    for j in range(9):
-        for oz in range(3):
-            if flipped:
-                w[oz * C : (oz + 1) * C, j * C : (j + 1) * C] = k[3 * (8 - j) + oz]
-            else:
+def prep_body(k1, k2, gain, w1, w2, t1, t2, gain_out):
+    for k, w, t in ((k1, w1, t1), (k2, w2, t2)):
+        for j in range(9):
+            for oz in range(3):
                 w[j * C : (j + 1) * C, oz * C : (oz + 1) * C] = k[3 * j + oz]
+                t[oz * C : (oz + 1) * C, j * C : (j + 1) * C] = k[3 * (8 - j) + oz]
+    gain_out[...] = gain[...]
 
 
 def convolve(grid, f, bx, by, cols, w, flipped):
@@ -139,14 +152,12 @@
 
 
 def main_body(
-    pos, meta, a, b, xl, xr, yl, yr, k1, k2, gain,
-    hid, pre, msg, gain_part, grid, cols, w1, w2, hg
+    pos, meta, a, b, xl, xr, yl, yr, w1, w2, gain,
+    hid, pre, msg, gain_part, grid, cols, hg
 ):
     core = meta[0]
     for f, src in enumerate((a, b)):
         build(grid, f, pos, src, xl, xr, yl, yr)
-    fill_weights(w1, k1, False)
-    fill_weights(w2, k2, True)
     at = P_ROWS
     for ref in (xl, xr, yl, yr):
         msg[at : at + ref.shape[1]] = ref[1 - core]
@@ -179,9 +190,8 @@
     msg[1024:P_ROWS] = pack3(total)
 
 
-def out_body(pos, src, xl, xr, yl, yr, k, base, out, grid, cols, w, *, field):
+def out_body(pos, src, xl, xr, yl, yr, w, base, out, grid, cols, *, field):
     build(grid, 0, pos, src, *(e.at[field : field + 1] for e in (xl, xr, yl, yr)))
-    fill_weights(w, k, field == 1)
     for s in range(2):
         live, bx, by = place(pos, s)
         y = convolve(grid, 0, bx, by, cols, w, field == 1)
@@ -236,7 +246,6 @@
     tile = msg[1024:P_ROWS].astype(f32)
     total = gain_part[0:1] + ((tile[2:3] + tile[1:2]) + tile[0:1])
     gsum[...] = jnp.broadcast_to(total, (8, C))
-    out[half * size :] = pack3(total)
 
 
 def pack3(v):
@@ -245,43 +254,32 @@
     return jnp.where(row == 0, hi, jnp.where(row == 1, mid, jnp.where(row == 2, low, 0.0))).astype(bf16)
 
 
-def step_body(low, got, g, low_out, msg, g_out):
-    rows = low.shape[0]
-    tile = got[rows : rows + 16].astype(f32)
-    total = g[0:1] + ((tile[2:3] + tile[1:2]) + tile[0:1])
-    g_out[...] = jnp.broadcast_to(total, (8, C))
-    added = low[...] + got[0:rows].astype(f32)
-    if low_out is None:
-        msg[0:rows] = added.astype(msg.dtype)
-    else:
-        keep = low_out.shape[0]
-        low_out[...] = added[0:keep]
-        msg[0 : rows - keep] = added[keep:].astype(msg.dtype)
-        rows -= keep
-    msg[rows : rows + 16] = pack3(total).astype(msg.dtype)
-
-
-def final_body(meta, own, part, own_g, part_g, k_out, g_out, first, second, *, chunks):
+def final_body(meta, own0, own1, part0, part1, k_out, g_out, first, second, gains, *, chunks):
     core, mine, theirs = meta[0], meta[1], meta[2]
     n = TAPS * C
     size = n // chunks
-
-    def spread(dst, src, me):
+    half = chunks // 2
+
+    def spread(dst, srcs, me, gain):
         for p in range(chunks):
-            at = pl.multiple_of((me ^ p) * size, 8)
-            dst[pl.ds(at, size)] = src[p * size : (p + 1) * size].astype(f32)
+            src, q = srcs[p // half], p % half
+            piece = src[q * (size + 8) : (q + 1) * (size + 8)].astype(f32)
+            dst[pl.ds(pl.multiple_of((me ^ p) * size, 8), size)] = piece[:size]
+            if gain:
+                t = piece[size:]
+                gains[me ^ p] = jnp.broadcast_to((t[2:3] + t[1:2]) + t[0:1], (8, C))
 
     @pl.when(core == 0)
     def _():
-        spread(first, own, mine)
-        spread(second, part, theirs)
+        spread(first, (own0, own1), mine, True)
+        spread(second, (part0, part1), theirs, False)
 
     @pl.when(core != 0)
     def _():
-        spread(first, part, theirs)
-        spread(second, own, mine)
-
-    g = jnp.where(core == 0, own_g[0:1], part_g[0:1])
+        spread(first, (part0, part1), theirs, True)
+        spread(second, (own0, own1), mine, False)
+
+    g = jnp.sum(gains[...], axis=0)[0:1]
     total = jnp.sum(g * g)
     for ref in (first, second):
         v = ref[...].reshape(n // 8, 8, C)
@@ -303,18 +301,14 @@
     return from_left, from_right
 
 
-def halos(pos, a, b):
-    lo, hi = call(pack_x_body, [sds((2, 128, C), bf16)] * 2, [], (pos, a, b), 1)
-    xl, xr = shift(lo, hi, "gx")
-    lo, hi = call(
+def y_faces(pos, a, b, xl, xr):
+    return call(
         pack_y_body,
         [sds((2, 144, C), bf16)] * 2,
         [pltpu.VMEM((18, 8, C), f32)],
         (pos, a, b, xl, xr),
         1,
     )
-    yl, yr = shift(lo, hi, "gy")
-    return xl, xr, yl, yr
 
 
 def stages():
@@ -341,6 +335,15 @@
     return jnp.asarray(out, jnp.int32)
 
 
+def gain_tile(g):
+    rows, rest = [], g
+    for _ in range(3):
+        part = lax.reduce_precision(rest, 8, 7)
+        rows.append(part)
+        rest = rest - part
+    return jnp.concatenate(rows + [jnp.zeros((5, C), f32)]).astype(bf16)
+
+
 def after(value, *done):
     return lax.optimization_barrier((value, *done))[0]
 
@@ -358,24 +361,43 @@
     meta = jnp.stack([core, jnp.where(core == 0, me_a, me_b), jnp.where(core == 0, me_b, me_a)])
     partner = [(i, i ^ 1) for i in range(ny)]
     n = TAPS * C
-
+    size = n // chunks
+
+    hbm = lambda v: pltpu.with_memory_space_constraint(v, pltpu.HBM)
+    features, cotangent, sent, lo, hi = call(
+        load_body,
+        [sds((2, 512, C), bf16)] * 3 + [sds((2, 128, C), bf16)] * 2,
+        [],
+        (brick_pos, core.reshape(1), hbm(features), hbm(cotangent)),
+        2,
+    )
+    xl, xr = shift(lo, hi, "gx")
     ppos = lax.ppermute(brick_pos, "gy", partner)
-    other = lax.ppermute(jnp.where(core == 0, cotangent, features), "gy", partner)
-    edge = halos(brick_pos, features, cotangent)
+    other = lax.ppermute(sent, "gy", partner)
+    straight, turned = sds((9 * C, 3 * C), bf16), sds((3 * C, 9 * C), bf16)
+    w1, w2, t1, t2, gain = call(
+        prep_body,
+        [straight, straight, turned, turned, sds((1, C), f32)],
+        [],
+        (hbm(first_kernel), hbm(second_kernel), hbm(norm_gain.reshape(1, C))),
+        0,
+    )
+    lo, hi = y_faces(brick_pos, after(features, gain), cotangent, xl, xr)
+    lo = after(lo, ppos, other, meta)
+    edge = xl, xr, *shift(lo, hi, "gy")
     grid = pltpu.VMEM((2, 18, 18, 8, C), f32)
     cols = pltpu.VMEM((512, 9 * C), bf16)
-    straight, turned = pltpu.VMEM((9 * C, 3 * C), bf16), pltpu.VMEM((3 * C, 9 * C), bf16)
     hid, pre, msg, gain_part = call(
         main_body,
         [sds((2, 512, C), bf16)] * 2 + [sds((P_ROWS + sum(FACES), C), bf16), sds((8, C), f32)],
-        [grid, cols, straight, turned, pltpu.VMEM((512, C), f32)],
-        (brick_pos, meta, features, cotangent, *edge, first_kernel, second_kernel, norm_gain.reshape(1, C)),
+        [grid, cols, pltpu.VMEM((512, C), f32)],
+        (brick_pos, meta, features, cotangent, *edge, w1, t2, gain),
         2,
     )
     pmsg = lax.ppermute(msg, "gy", partner)
     low, out, g = call(
         functools.partial(grads_body, chunks=chunks),
-        [sds((n // 2, C), f32), sds((n // 2 + 16, C), bf16), sds((8, C), f32)],
+        [sds((n // 2, C), f32), sds((n // 2, C), bf16), sds((8, C), f32)],
         [
             grid,
             pltpu.VMEM((2048, 9 * C), bf16),
@@ -385,74 +407,47 @@
         (brick_pos, ppos, meta, features, cotangent, *edge, other, hid, pre, pmsg, gain_part),
         3,
     )
-
-    def work():
-        ready = yield
-        lo, hi = call(
-            pack_x_body, [sds((2, 128, C), bf16)] * 2, [], (brick_pos, after(hid, ready), pre), 1
-        )
-        xl, xr = shift(lo, hi, "gx")
-        ready = yield lo
-        lo, hi = call(
-            pack_y_body,
-            [sds((2, 144, C), bf16)] * 2,
-            [pltpu.VMEM((18, 8, C), f32)],
-            (brick_pos, after(hid, ready), pre, xl, xr),
+    g = g[0:1]
+
+    lo, hi = call(pack_x_body, [sds((2, 128, C), bf16)] * 2, [], (brick_pos, after(hid, out), pre), 1)
+    xl, xr = shift(lo, hi, "gx")
+    lo, hi = y_faces(brick_pos, hid, pre, xl, xr)
+    around = xl, xr, *shift(lo, hi, "gy")
+    results = []
+    for f, (src, w, base) in enumerate(((hid, w2, features), (pre, t1, cotangent))):
+        (res,) = call(
+            functools.partial(out_body, field=f),
+            [sds((2, 512, C), bf16)],
+            [pltpu.VMEM((1, 18, 18, 8, C), f32), cols],
+            (brick_pos, src, *around, w, base),
             1,
         )
-        yl, yr = shift(lo, hi, "gy")
-        ready = yield lo
-        results = []
-        for f, (src, k, base, w) in enumerate(
-            ((hid, second_kernel, features, straight), (pre, first_kernel, cotangent, turned))
-        ):
-            (res,) = call(
-                functools.partial(out_body, field=f),
-                [sds((2, 512, C), bf16)],
-                [pltpu.VMEM((1, 18, 18, 8, C), f32), cols, w],
-                (brick_pos, after(src, ready), xl, xr, yl, yr, k, base),
-                1,
-            )
-            results.append(res)
-            ready = yield res
-        yield results
-
-    side = work()
-    next(side)
-    rows = n // 2
-    for s in range(len(perms)):
-        done = side.send(out) if s < 4 else None
+        results.append(res)
+
+    for s in range(halvings):
         got = lax.ppermute(out, both, perms[s])
-        last = s == len(perms) - 1
-        wide = s + 2 >= len(perms)
-        halve = s + 1 < halvings
-        keep = rows // 2 if halve else 0
-        outs = [sds((rows - keep + 16, C), bf16 if halve and not wide else f32), sds((8, C), f32)]
-        if halve:
-            outs = [sds((keep, C), f32)] + outs
-            body = step_body
-        else:
-            body = lambda low, got, g, *rest: step_body(low, got, g, None, *rest)
-        res = call(body, outs, [], (low, got, g), 0)
-        if halve:
-            low, out, g = res
-            rows = keep
-        else:
-            out, g = res
-            low = out[:rows]
-        if done is not None:
-            out = after(out, done)
-    results = side.send(out)
-    full = out[:rows].astype(bf16)
-    for perm in reversed(perms[:halvings]):
-        full = jnp.concatenate([full, lax.ppermute(full, both, perm)])
-    part = lax.ppermute(full, "gy", partner)
-    gain = lax.ppermute(g, "gy", partner)
+        low = low + got.astype(f32)
+        if s + 1 < halvings:
+            half = low.shape[0] // 2
+            low, out = low[:half], low[half:]
+            if s + 2 < halvings:
+                out = out.astype(bf16)
+    for s in range(halvings, len(perms)):
+        got = lax.ppermute(jnp.concatenate([low, jnp.broadcast_to(g, (8, C))]), both, perms[s])
+        low, g = low + got[:size], g + got[size : size + 1]
+
+    full = jnp.concatenate([low.astype(bf16), gain_tile(g)])
+    for s in reversed(range(halvings)):
+        got = lax.ppermute(full, both, perms[s])
+        if s:
+            full = jnp.concatenate([full, got])
+    early = lax.ppermute(full, "gy", partner)
+    late = lax.ppermute(got, "gy", partner)
     k_up, g_up = call(
         functools.partial(final_body, chunks=chunks),
         [sds((2, TAPS, C, C), f32), sds((1, C), f32)],
-        [pltpu.VMEM((n, C), f32), pltpu.VMEM((n, C), f32)],
-        (meta, full, part, g, gain),
+        [pltpu.VMEM((n, C), f32), pltpu.VMEM((n, C), f32), pltpu.VMEM((chunks, 8, C), f32)],
+        (meta, full, got, early, late),
         1,
     )
     return (*results, k_up, g_up.reshape(C))
@@ -460,6 +455,7 @@
 
 def solution(mesh):
     rows = P(("gx", "gy"), None, None)
+
     return jax.shard_map(
         per_device,
         mesh=mesh,

time: 130 us -> 119 us (0.915)
  the two profiles are of different devices: /device:TPU:0 before, /device:TPU:1 now
where the time goes in v2:
time: 119 us; the launch traced here: 118 us
  starting transfers between devices  49.9 us (42%)
  waiting for transfers between devices  42.2 us (35%)
  Pallas kernels  23.7 us (20%)
  local copies, waits for them, and re-layouts  1.32 us (1%)
    pallas_call x10, Pallas kernels, call(): pl.pallas_call(body, out_shape=outs, in_specs=[SMEM] * n_smem + [VMEM] *...  23.7 us
    ppermute x4, starting transfers between devices, shift(): from_left = lax.ppermute(hi, axis, [(i, i + 1) for i in range(n - 1)])  15.9 us
    ppermute x4, waiting for transfers between devices, per_device(): got = lax.ppermute(out, both, perms[s])  15.5 us
    ppermute x4, waiting for transfers between devices, shift(): from_right = lax.ppermute(lo, axis, [(i + 1, i) for i in range(n - 1)])  12.6 us
    ppermute x4, waiting for transfers between devices, per_device(): got = lax.ppermute(full, both, perms[s])  12.2 us
    ppermute x1, starting transfers between devices, per_device(): early = lax.ppermute(full, 'gy', partner)  11.3 us
    ppermute x4, starting transfers between devices, per_device(): got = lax.ppermute(out, both, perms[s])  7.13 us
    ppermute x1, starting transfers between devices, per_device(): late = lax.ppermute(got, 'gy', partner)  6.46 us
  transfers between devices with their start and end apart: 21, of which 13 were waited for; matrix products, arithmetic and copies ran while one was open for 0% of the time, Pallas kernels for 9%

profile of v2, /device:TPU:1, one launch (start us, length us, event | category | flops | bytes accessed | tf_op | source)
XLA Modules:
  0.0 118.3 jit_solution(3516679578077062086)
XLA Ops:
  0.6 1.3 %shard_map.93 = (bf16[2,512,128]{2,1,0:T(8,128)(2,1)S(1)}, bf16[2,512,128]{2,1,0:T(8,128)(2,1)S(1)}, bf16[2,512,128]{2,1,0:T(8,128)(2,1)S(1)}, bf16[2,128,128]{2,1,0:T(8,128)(2,1)S(1)}, bf16[2,128,128]{2,1,0:T(8,128)(2,1)S(1)}) custom-call(s32[2]{0:T(128)} %pos.15, s32[1]{0:T(128)} %bitcast.core, bf16[2,512,128]{2,1,0:T(8,128)(2,1)} %a.1, bf16[2,512,128]{2,1,0:T(8,128)(2,1)} %b.1), custom_call_target="tpu_custom_call" | custom-call | tf_op jit(solution)/shard_map/pallas_call | solution.py:35
  1.9 0.1 collective-permute-start.4
  2.0 0.5 collective-permute-start.3
  2.5 4.2 %collective-permute-start = (bf16[2,128,128]{2,1,0:T(8,128)(2,1)S(1)}, bf16[2,128,128]{2,1,0:T(8,128)(2,1)S(1)}, u32[]{:S(2)}, u32[]{:S(2)}) collective-permute-start(bf16[2,128,128]{2,1,0:T(8,128)(2,1)S(1)} %get-tuple-element.34), channel_id=1, source_target_pairs={{0,8},{8,16},{16,24},{1,9},{9,17},{17,25},{2,10},{10,18},{18,26},{... | collective-permute-start | bytes 196616 | tf_op jit(solution)/shard_map/ppermute | solution.py:299
  6.7 1.3 %collective-permute-start.1 = (bf16[2,128,128]{2,1,0:T(8,128)(2,1)S(1)}, bf16[2,128,128]{2,1,0:T(8,128)(2,1)S(1)}, u32[]{:S(2)}, u32[]{:S(2)}) collective-permute-start(bf16[2,128,128]{2,1,0:T(8,128)(2,1)S(1)} %get-tuple-element.35), channel_id=1, source_target_pairs={{8,0},{16,8},{24,16},{9,1},{17,9},{25,17},{10,2},{18,10},{26,18},{... | collective-permute-start | bytes 196616 | tf_op jit(solution)/shard_map/ppermute | solution.py:300
  8.0 2.0 %shard_map.94 = (bf16[1152,384]{1,0:T(8,128)(2,1)S(1)}, bf16[1152,384]{1,0:T(8,128)(2,1)S(1)}, bf16[384,1152]{1,0:T(8,128)(2,1)S(1)}, bf16[384,1152]{1,0:T(8,128)(2,1)S(1)}, f32[1,128]{1,0:T(1,128)S(1)}) custom-call(bf16[27,128,128]{2,1,0:T(8,128)(2,1)} %k1.1, bf16[27,128,128]{2,1,0:T(8,128)(2,1)} %k2.1, f32[1,128]{1,0:T(1,128)} %bitcast.5), custom_call_target="tpu_custom_call" | custom-call | tf_op jit(solution)/shard_map/pallas_call | solution.py:35
  10.0 0.1 pad_add_fusion.meta
  10.1 1.6 %collective-permute-done.1.xr = bf16[2,128,128]{2,1,0:T(8,128)(2,1)S(1)} collective-permute-done((bf16[2,128,128]{2,1,0:T(8,128)(2,1)S(1)}, bf16[2,128,128]{2,1,0:T(8,128)(2,1)S(1)}, u32[]{:S(2)}, u32[]{:S(2)}) %collective-permute-start.1) | collective-permute-done | bytes 65568 | tf_op jit(solution)/shard_map/ppermute | solution.py:300
  11.7 0.8 shard_map.95
  12.5 5.0 %collective-permute-start.2 = (bf16[2,144,128]{2,1,0:T(8,128)(2,1)S(1)}, bf16[2,144,128]{2,1,0:T(8,128)(2,1)S(1)}, u32[]{:S(2)}, u32[]{:S(2)}) collective-permute-start(bf16[2,144,128]{2,1,0:T(8,128)(2,1)S(1)} %get-tuple-element.38), channel_id=1, source_target_pairs={{0,1},{1,2},{2,3},{3,4},{4,5},{5,6},{6,7},{8,9},{9,10},{10,11},{11... | collective-permute-start | bytes 221192 | tf_op jit(solution)/shard_map/ppermute | solution.py:299
  17.5 1.9 %collective-permute-start.5 = (bf16[2,144,128]{2,1,0:T(8,128)(2,1)S(1)}, bf16[2,144,128]{2,1,0:T(8,128)(2,1)S(1)}, u32[]{:S(2)}, u32[]{:S(2)}) collective-permute-start(bf16[2,144,128]{2,1,0:T(8,128)(2,1)S(1)} %get-tuple-element.41), channel_id=1, source_target_pairs={{1,0},{2,1},{3,2},{4,3},{5,4},{6,5},{7,6},{9,8},{10,9},{11,10},{12... | collective-permute-start | bytes 221192 | tf_op jit(solution)/shard_map/ppermute | solution.py:300
  19.4 3.7 %collective-permute-done.5.yr = bf16[2,144,128]{2,1,0:T(8,128)(2,1)S(1)} collective-permute-done((bf16[2,144,128]{2,1,0:T(8,128)(2,1)S(1)}, bf16[2,144,128]{2,1,0:T(8,128)(2,1)S(1)}, u32[]{:S(2)}, u32[]{:S(2)}) %collective-permute-start.5) | collective-permute-done | bytes 73760 | tf_op jit(solution)/shard_map/ppermute | solution.py:300
  23.1 4.5 %shard_map.96 = (bf16[2,512,128]{2,1,0:T(8,128)(2,1)S(1)}, bf16[2,512,128]{2,1,0:T(8,128)(2,1)S(1)}, bf16[1584,128]{1,0:T(8,128)(2,1)S(1)}, f32[8,128]{1,0:T(8,128)S(1)}) custom-call(s32[2]{0:T(128)} %pos.15, s32[3]{0:T(128)S(1)} %pad_add_fusion.meta, bf16[2,512,128]{2,1,0:T(8,128)(2,1)S(1)} %get-tuple-element.37.a.base, ...), custom_call_target="tpu_custom_call" | custom-call | tf_op jit(solution)/shard_map/pallas_call | solution.py:35
  27.7 0.1 collective-permute-start.6
  27.7 1.7 %collective-permute-done.6.msg = bf16[1584,128]{1,0:T(8,128)(2,1)S(1)} collective-permute-done((bf16[1584,128]{1,0:T(8,128)(2,1)S(1)}, bf16[1584,128]{1,0:T(8,128)(2,1)S(1)}, u32[]{:S(2)}, u32[]{:S(2)}) %collective-permute-start.6) | collective-permute-done | bytes 405536 | tf_op jit(solution)/shard_map/ppermute | solution.py:397
  29.5 3.7 %shard_map.97 = (f32[1728,128]{1,0:T(8,128)S(1)}, bf16[1728,128]{1,0:T(8,128)(2,1)S(1)}, f32[8,128]{1,0:T(8,128)S(1)}) custom-call(s32[2]{0:T(128)} %pos.15, s32[2]{0:T(128)S(1)} %collective-permute-done.3.ppos, s32[3]{0:T(128)S(1)} %pad_add_fusion.meta, bf16[2,512,128]{2,1,0:T(8,128)(2,1)S(1)} %get-tuple-element.37.a.base, ...), custom_call_target="tpu_custom_call" | custom-call | tf_op jit(solution)/shard_map/pallas_call | solution.py:35
  33.2 1.3 %collective-permute-start.11 = (bf16[1728,128]{1,0:T(8,128)(2,1)S(1)}, bf16[1728,128]{1,0:T(8,128)(2,1)S(1)}, u32[]{:S(2)}, u32[]{:S(2)}) collective-permute-start(bf16[1728,128]{1,0:T(8,128)(2,1)S(1)} %get-tuple-element.48), channel_id=1, source_target_pairs={{0,8},{1,17},{2,10},{3,19},{4,12},{5,21},{6,14},{7,23},{8,0},{9,25... | collective-permute-start | bytes 1327112 | tf_op jit(solution)/shard_map/ppermute | solution.py:428
  34.4 6.3 %collective-permute-done.11 = bf16[1728,128]{1,0:T(8,128)(2,1)S(1)} collective-permute-done((bf16[1728,128]{1,0:T(8,128)(2,1)S(1)}, bf16[1728,128]{1,0:T(8,128)(2,1)S(1)}, u32[]{:S(2)}, u32[]{:S(2)}) %collective-permute-start.11) | collective-permute-done | bytes 442400 | tf_op jit(solution)/shard_map/ppermute | solution.py:428
  40.7 0.1 convert_add_fusion
  40.8 2.1 %collective-permute-start.12 = (bf16[864,128]{1,0:T(8,128)(2,1)S(1)}, bf16[864,128]{1,0:T(8,128)(2,1)S(1)}, u32[]{:S(2)}, u32[]{:S(2)}) collective-permute-start(bf16[864,128]{1,0:T(8,128)(2,1)S(1)} %slice.49), channel_id=1, source_target_pairs={{0,16},{1,9},{2,18},{3,11},{4,20},{5,13},{6,22},{7,15},{8,24},{9,1... | collective-permute-start | bytes 663560 | tf_op jit(solution)/shard_map/ppermute | solution.py:428
  42.9 3.6 %collective-permute-done.12 = bf16[864,128]{1,0:T(8,128)(2,1)S(1)} collective-permute-done((bf16[864,128]{1,0:T(8,128)(2,1)S(1)}, bf16[864,128]{1,0:T(8,128)(2,1)S(1)}, u32[]{:S(2)}, u32[]{:S(2)}) %collective-permute-start.12) | collective-permute-done | bytes 221216 | tf_op jit(solution)/shard_map/ppermute | solution.py:428
  46.6 1.4 %collective-permute-start.13 = (bf16[432,128]{1,0:T(8,128)(2,1)S(1)}, bf16[432,128]{1,0:T(8,128)(2,1)S(1)}, u32[]{:S(2)}, u32[]{:S(2)}) collective-permute-start(bf16[432,128]{1,0:T(8,128)(2,1)S(1)} %slice.50), channel_id=1, source_target_pairs={{0,2},{1,3},{2,0},{3,1},{4,6},{5,7},{6,4},{7,5},{8,10},{9,11},{10,... | collective-permute-start | bytes 331784 | tf_op jit(solution)/shard_map/ppermute | solution.py:428
  48.0 2.3 %collective-permute-done.13 = bf16[432,128]{1,0:T(8,128)(2,1)S(1)} collective-permute-done((bf16[432,128]{1,0:T(8,128)(2,1)S(1)}, bf16[432,128]{1,0:T(8,128)(2,1)S(1)}, u32[]{:S(2)}, u32[]{:S(2)}) %collective-permute-start.13) | collective-permute-done | bytes 110624 | tf_op jit(solution)/shard_map/ppermute | solution.py:428
  50.3 2.4 %collective-permute-start.14 = (f32[216,128]{1,0:T(8,128)S(1)}, f32[216,128]{1,0:T(8,128)S(1)}, u32[]{:S(2)}, u32[]{:S(2)}) collective-permute-start(f32[216,128]{1,0:T(8,128)S(1)} %slice.35), channel_id=1, source_target_pairs={{0,4},{1,5},{2,6},{3,7},{4,0},{5,1},{6,2},{7,3},{8,12},{9,13},{10,... | collective-permute-start | bytes 331784 | tf_op jit(solution)/shard_map/ppermute | solution.py:428
  52.7 3.3 %collective-permute-done.14 = f32[216,128]{1,0:T(8,128)S(1)} collective-permute-done((f32[216,128]{1,0:T(8,128)S(1)}, f32[216,128]{1,0:T(8,128)S(1)}, u32[]{:S(2)}, u32[]{:S(2)}) %collective-permute-start.14) | collective-permute-done | bytes 110624 | tf_op jit(solution)/shard_map/ppermute | solution.py:428
  56.1 1.2 %collective-permute-start.15 = (bf16[224,128]{1,0:T(8,128)(2,1)S(1)}, bf16[224,128]{1,0:T(8,128)(2,1)S(1)}, u32[]{:S(2)}, u32[]{:S(2)}) collective-permute-start(bf16[224,128]{1,0:T(8,128)(2,1)S(1)} %concatenate.21), channel_id=1, source_target_pairs={{0,4},{1,5},{2,6},{3,7},{4,0},{5,1},{6,2},{7,3},{8,12},{9,13},{10,... | collective-permute-start | bytes 172040 | tf_op jit(solution)/shard_map/ppermute | solution.py:441
  57.3 3.3 %collective-permute-done.15 = bf16[224,128]{1,0:T(8,128)(2,1)S(1)} collective-permute-done((bf16[224,128]{1,0:T(8,128)(2,1)S(1)}, bf16[224,128]{1,0:T(8,128)(2,1)S(1)}, u32[]{:S(2)}, u32[]{:S(2)}) %collective-permute-start.15) | collective-permute-done | bytes 57376 | tf_op jit(solution)/shard_map/ppermute | solution.py:441
  60.7 0.1 collective-permute-start.16
  60.8 4.5 %collective-permute-done.16 = bf16[448,128]{1,0:T(8,128)(2,1)S(1)} collective-permute-done((bf16[448,128]{1,0:T(8,128)(2,1)S(1)}, bf16[448,128]{1,0:T(8,128)(2,1)S(1)}, u32[]{:S(2)}, u32[]{:S(2)}) %collective-permute-start.16) | collective-permute-done | bytes 114720 | tf_op jit(solution)/shard_map/ppermute | solution.py:441
  65.3 0.1 concatenate.23
  65.4 0.7 collective-permute-start.17
  66.1 4.3 %collective-permute-done.17 = bf16[896,128]{1,0:T(8,128)(2,1)} collective-permute-done((bf16[896,128]{1,0:T(8,128)(2,1)S(1)}, bf16[896,128]{1,0:T(8,128)(2,1)}, u32[]{:S(2)}, u32[]{:S(2)}) %collective-permute-start.17) | collective-permute-done | bytes 229408 | tf_op jit(solution)/shard_map/ppermute | solution.py:441
  70.5 1.1 concatenate.24.own0
  71.5 0.1 collective-permute-start.18
  71.6 11.3 %collective-permute-start.19 = (bf16[1792,128]{1,0:T(8,128)(2,1)S(1)}, bf16[1792,128]{1,0:T(8,128)(2,1)S(1)}, u32[]{:S(2)}, u32[]{:S(2)}) collective-permute-start(bf16[1792,128]{1,0:T(8,128)(2,1)S(1)} %concatenate.24.own0), channel_id=1, source_target_pairs={{0,1},{1,0},{2,3},{3,2},{4,5},{5,4},{6,7},{7,6},{8,9},{9,8},{10,11... | collective-permute-start | bytes 1376264 | tf_op jit(solution)/shard_map/ppermute | solution.py:444
  82.9 6.5 %collective-permute-start.20 = (bf16[1792,128]{1,0:T(8,128)(2,1)S(1)}, bf16[1792,128]{1,0:T(8,128)(2,1)S(1)}, u32[]{:S(2)}, u32[]{:S(2)}) collective-permute-start(bf16[1792,128]{1,0:T(8,128)(2,1)S(1)} %collective-permute-done.18.own1), channel_id=1, source_target_pairs={{0,1},{1,0},{2,3},{3,2},{4,5},{5,4},{6,7},{7,6},{8,9},{9,8},{10,11... | collective-permute-start | bytes 1376264 | tf_op jit(solution)/shard_map/ppermute | solution.py:445
  89.3 0.7 shard_map.98
  90.1 3.6 %collective-permute-start.7 = (bf16[2,128,128]{2,1,0:T(8,128)(2,1)S(1)}, bf16[2,128,128]{2,1,0:T(8,128)(2,1)S(1)}, u32[]{:S(2)}, u32[]{:S(2)}) collective-permute-start(bf16[2,128,128]{2,1,0:T(8,128)(2,1)S(1)} %get-tuple-element.50), channel_id=1, source_target_pairs={{0,8},{8,16},{16,24},{1,9},{9,17},{17,25},{2,10},{10,18},{18,26},{... | collective-permute-start | bytes 196616 | tf_op jit(solution)/shard_map/ppermute | solution.py:299
  93.8 1.3 %collective-permute-start.8 = (bf16[2,128,128]{2,1,0:T(8,128)(2,1)S(1)}, bf16[2,128,128]{2,1,0:T(8,128)(2,1)S(1)}, u32[]{:S(2)}, u32[]{:S(2)}) collective-permute-start(bf16[2,128,128]{2,1,0:T(8,128)(2,1)S(1)} %get-tuple-element.51), channel_id=1, source_target_pairs={{8,0},{16,8},{24,16},{9,1},{17,9},{25,17},{10,2},{18,10},{26,18},{... | collective-permute-start | bytes 196616 | tf_op jit(solution)/shard_map/ppermute | solution.py:300
  95.1 0.1 collective-permute-done.7.xl
  95.2 3.6 %collective-permute-done.8.xr = bf16[2,128,128]{2,1,0:T(8,128)(2,1)S(1)} collective-permute-done((bf16[2,128,128]{2,1,0:T(8,128)(2,1)S(1)}, bf16[2,128,128]{2,1,0:T(8,128)(2,1)S(1)}, u32[]{:S(2)}, u32[]{:S(2)}) %collective-permute-start.8) | collective-permute-done | bytes 65568 | tf_op jit(solution)/shard_map/ppermute | solution.py:300
  98.8 0.8 shard_map.99
  99.6 3.1 %collective-permute-start.9 = (bf16[2,144,128]{2,1,0:T(8,128)(2,1)S(1)}, bf16[2,144,128]{2,1,0:T(8,128)(2,1)S(1)}, u32[]{:S(2)}, u32[]{:S(2)}) collective-permute-start(bf16[2,144,128]{2,1,0:T(8,128)(2,1)S(1)} %get-tuple-element.52), channel_id=1, source_target_pairs={{0,1},{1,2},{2,3},{3,4},{4,5},{5,6},{6,7},{8,9},{9,10},{10,11},{11... | collective-permute-start | bytes 221192 | tf_op jit(solution)/shard_map/ppermute | solution.py:299
  102.7 1.9 %collective-permute-start.10 = (bf16[2,144,128]{2,1,0:T(8,128)(2,1)S(1)}, bf16[2,144,128]{2,1,0:T(8,128)(2,1)S(1)}, u32[]{:S(2)}, u32[]{:S(2)}) collective-permute-start(bf16[2,144,128]{2,1,0:T(8,128)(2,1)S(1)} %get-tuple-element.53), channel_id=1, source_target_pairs={{1,0},{2,1},{3,2},{4,3},{5,4},{6,5},{7,6},{9,8},{10,9},{11,10},{12... | collective-permute-start | bytes 221192 | tf_op jit(solution)/shard_map/ppermute | solution.py:300
  104.7 3.7 %collective-permute-done.10.yr = bf16[2,144,128]{2,1,0:T(8,128)(2,1)S(1)} collective-permute-done((bf16[2,144,128]{2,1,0:T(8,128)(2,1)S(1)}, bf16[2,144,128]{2,1,0:T(8,128)(2,1)S(1)}, u32[]{:S(2)}, u32[]{:S(2)}) %collective-permute-start.10) | collective-permute-done | bytes 73760 | tf_op jit(solution)/shard_map/ppermute | solution.py:300
  108.4 3.1 %shard_map.101 = bf16[2,512,128]{2,1,0:T(8,128)(2,1)} custom-call(s32[2]{0:T(128)} %pos.15, bf16[2,512,128]{2,1,0:T(8,128)(2,1)S(1)} %get-tuple-element.45.pre.b.src, bf16[2,128,128]{2,1,0:T(8,128)(2,1)S(1)} %collective-permute-done.7.xl, bf16[2,128,128]{2,1,0:T(8,128)(2,1)S(1)} %collective-permute-done.8.xr, ...), custom_call_target="tpu_custom_call" | custom-call | tf_op jit(solution)/shard_map/pallas_call | solution.py:35
  111.5 3.3 %shard_map.100 = bf16[2,512,128]{2,1,0:T(8,128)(2,1)} custom-call(s32[2]{0:T(128)} %pos.15, bf16[2,512,128]{2,1,0:T(8,128)(2,1)S(1)} %get-tuple-element.49.hid.a.src, bf16[2,128,128]{2,1,0:T(8,128)(2,1)S(1)} %collective-permute-done.7.xl, bf16[2,128,128]{2,1,0:T(8,128)(2,1)S(1)} %collective-permute-done.8.xr, ...), custom_call_target="tpu_custom_call" | custom-call | tf_op jit(solution)/shard_map/pallas_call | solution.py:35
  114.9 3.4 %shard_map.102 = (f32[2,27,128,128]{3,2,1,0:T(8,128)}, f32[1,128]{1,0:T(1,128)}) custom-call(s32[3]{0:T(128)S(1)} %pad_add_fusion.meta, bf16[1792,128]{1,0:T(8,128)(2,1)S(1)} %concatenate.24.own0, bf16[1792,128]{1,0:T(8,128)(2,1)S(1)} %collective-permute-done.18.own1, bf16[1792,128]{1,0:T(8,128)(2,1)S(1)} %collective-permute-done.19.part0, ...), custom_call_target="tpu_custom_call" | custom-call | tf_op jit(solution)/shard_map/pallas_call | solution.py:35
  (18 shorter events, 0.3 us)
Async XLA Ops:
  1.9 15.5 %collective-permute-start.4 = (bf16[2,512,128]{2,1,0:T(8,128)(2,1)S(1)}, bf16[2,512,128]{2,1,0:T(8,128)(2,1)S(1)}, u32[]{:S(2)}, u32[]{:S(2)}) collective-permute-start(bf16[2,512,128]{2,1,0:T(8,128)(2,1)S(1)} %get-tuple-element.40), channel_id=1, source_target_pairs={{0,1},{1,0},{2,3},{3,2},{4,5},{5,4},{6,7},{7,6},{8,9},{9,8},{10,11... | collective-permute-start | bytes 786440 | tf_op jit(solution)/shard_map/ppermute | solution.py:376
  2.0 15.4 %collective-permute-start.3 = (s32[2]{0:T(128)}, s32[2]{0:T(128)S(1)}, u32[]{:S(2)}, u32[]{:S(2)}) collective-permute-start(s32[2]{0:T(128)} %pos.15), channel_id=1, source_target_pairs={{0,1},{1,0},{2,3},{3,2},{4,5},{5,4},{6,7},{7,6},{8,9},{9,8},{10,11... | collective-permute-start | bytes 32 | tf_op jit(solution)/shard_map/ppermute | solution.py:375
  2.5 7.6 %collective-permute-start = (bf16[2,128,128]{2,1,0:T(8,128)(2,1)S(1)}, bf16[2,128,128]{2,1,0:T(8,128)(2,1)S(1)}, u32[]{:S(2)}, u32[]{:S(2)}) collective-permute-start(bf16[2,128,128]{2,1,0:T(8,128)(2,1)S(1)} %get-tuple-element.34), channel_id=1, source_target_pairs={{0,8},{8,16},{16,24},{1,9},{9,17},{17,25},{2,10},{10,18},{18,26},{... | collective-permute-start | bytes 196616 | tf_op jit(solution)/shard_map/ppermute | solution.py:299
  6.7 5.0 %collective-permute-start.1 = (bf16[2,128,128]{2,1,0:T(8,128)(2,1)S(1)}, bf16[2,128,128]{2,1,0:T(8,128)(2,1)S(1)}, u32[]{:S(2)}, u32[]{:S(2)}) collective-permute-start(bf16[2,128,128]{2,1,0:T(8,128)(2,1)S(1)} %get-tuple-element.35), channel_id=1, source_target_pairs={{8,0},{16,8},{24,16},{9,1},{17,9},{25,17},{10,2},{18,10},{26,18},{... | collective-permute-start | bytes 196616 | tf_op jit(solution)/shard_map/ppermute | solution.py:300
  12.5 6.9 %collective-permute-start.2 = (bf16[2,144,128]{2,1,0:T(8,128)(2,1)S(1)}, bf16[2,144,128]{2,1,0:T(8,128)(2,1)S(1)}, u32[]{:S(2)}, u32[]{:S(2)}) collective-permute-start(bf16[2,144,128]{2,1,0:T(8,128)(2,1)S(1)} %get-tuple-element.38), channel_id=1, source_target_pairs={{0,1},{1,2},{2,3},{3,4},{4,5},{5,6},{6,7},{8,9},{9,10},{10,11},{11... | collective-permute-start | bytes 221192 | tf_op jit(solution)/shard_map/ppermute | solution.py:299
  17.5 5.7 %collective-permute-start.5 = (bf16[2,144,128]{2,1,0:T(8,128)(2,1)S(1)}, bf16[2,144,128]{2,1,0:T(8,128)(2,1)S(1)}, u32[]{:S(2)}, u32[]{:S(2)}) collective-permute-start(bf16[2,144,128]{2,1,0:T(8,128)(2,1)S(1)} %get-tuple-element.41), channel_id=1, source_target_pairs={{1,0},{2,1},{3,2},{4,3},{5,4},{6,5},{7,6},{9,8},{10,9},{11,10},{12... | collective-permute-start | bytes 221192 | tf_op jit(solution)/shard_map/ppermute | solution.py:300
  27.7 1.8 %collective-permute-start.6 = (bf16[1584,128]{1,0:T(8,128)(2,1)S(1)}, bf16[1584,128]{1,0:T(8,128)(2,1)S(1)}, u32[]{:S(2)}, u32[]{:S(2)}) collective-permute-start(bf16[1584,128]{1,0:T(8,128)(2,1)S(1)} %get-tuple-element.46), channel_id=1, source_target_pairs={{0,1},{1,0},{2,3},{3,2},{4,5},{5,4},{6,7},{7,6},{8,9},{9,8},{10,11... | collective-permute-start | bytes 1216520 | tf_op jit(solution)/shard_map/ppermute | solution.py:397
  33.2 7.5 %collective-permute-start.11 = (bf16[1728,128]{1,0:T(8,128)(2,1)S(1)}, bf16[1728,128]{1,0:T(8,128)(2,1)S(1)}, u32[]{:S(2)}, u32[]{:S(2)}) collective-permute-start(bf16[1728,128]{1,0:T(8,128)(2,1)S(1)} %get-tuple-element.48), channel_id=1, source_target_pairs={{0,8},{1,17},{2,10},{3,19},{4,12},{5,21},{6,14},{7,23},{8,0},{9,25... | collective-permute-start | bytes 1327112 | tf_op jit(solution)/shard_map/ppermute | solution.py:428
  40.8 5.7 %collective-permute-start.12 = (bf16[864,128]{1,0:T(8,128)(2,1)S(1)}, bf16[864,128]{1,0:T(8,128)(2,1)S(1)}, u32[]{:S(2)}, u32[]{:S(2)}) collective-permute-start(bf16[864,128]{1,0:T(8,128)(2,1)S(1)} %slice.49), channel_id=1, source_target_pairs={{0,16},{1,9},{2,18},{3,11},{4,20},{5,13},{6,22},{7,15},{8,24},{9,1... | collective-permute-start | bytes 663560 | tf_op jit(solution)/shard_map/ppermute | solution.py:428
  46.6 3.7 %collective-permute-start.13 = (bf16[432,128]{1,0:T(8,128)(2,1)S(1)}, bf16[432,128]{1,0:T(8,128)(2,1)S(1)}, u32[]{:S(2)}, u32[]{:S(2)}) collective-permute-start(bf16[432,128]{1,0:T(8,128)(2,1)S(1)} %slice.50), channel_id=1, source_target_pairs={{0,2},{1,3},{2,0},{3,1},{4,6},{5,7},{6,4},{7,5},{8,10},{9,11},{10,... | collective-permute-start | bytes 331784 | tf_op jit(solution)/shard_map/ppermute | solution.py:428
  50.3 5.7 %collective-permute-start.14 = (f32[216,128]{1,0:T(8,128)S(1)}, f32[216,128]{1,0:T(8,128)S(1)}, u32[]{:S(2)}, u32[]{:S(2)}) collective-permute-start(f32[216,128]{1,0:T(8,128)S(1)} %slice.35), channel_id=1, source_target_pairs={{0,4},{1,5},{2,6},{3,7},{4,0},{5,1},{6,2},{7,3},{8,12},{9,13},{10,... | collective-permute-start | bytes 331784 | tf_op jit(solution)/shard_map/ppermute | solution.py:428
  56.1 4.5 %collective-permute-start.15 = (bf16[224,128]{1,0:T(8,128)(2,1)S(1)}, bf16[224,128]{1,0:T(8,128)(2,1)S(1)}, u32[]{:S(2)}, u32[]{:S(2)}) collective-permute-start(bf16[224,128]{1,0:T(8,128)(2,1)S(1)} %concatenate.21), channel_id=1, source_target_pairs={{0,4},{1,5},{2,6},{3,7},{4,0},{5,1},{6,2},{7,3},{8,12},{9,13},{10,... | collective-permute-start | bytes 172040 | tf_op jit(solution)/shard_map/ppermute | solution.py:441
  60.7 4.6 %collective-permute-start.16 = (bf16[448,128]{1,0:T(8,128)(2,1)S(1)}, bf16[448,128]{1,0:T(8,128)(2,1)S(1)}, u32[]{:S(2)}, u32[]{:S(2)}) collective-permute-start(bf16[448,128]{1,0:T(8,128)(2,1)S(1)} %concatenate.22), channel_id=1, source_target_pairs={{0,2},{1,3},{2,0},{3,1},{4,6},{5,7},{6,4},{7,5},{8,10},{9,11},{10,... | collective-permute-start | bytes 344072 | tf_op jit(solution)/shard_map/ppermute | solution.py:441
  65.4 5.0 %collective-permute-start.17 = (bf16[896,128]{1,0:T(8,128)(2,1)S(1)}, bf16[896,128]{1,0:T(8,128)(2,1)}, u32[]{:S(2)}, u32[]{:S(2)}) collective-permute-start(bf16[896,128]{1,0:T(8,128)(2,1)S(1)} %concatenate.23), channel_id=1, source_target_pairs={{0,16},{1,9},{2,18},{3,11},{4,20},{5,13},{6,22},{7,15},{8,24},{9,1... | collective-permute-start | bytes 688136 | tf_op jit(solution)/shard_map/ppermute | solution.py:441
  71.5 11.4 %collective-permute-start.18 = (bf16[1792,128]{1,0:T(8,128)(2,1)S(1)}, bf16[1792,128]{1,0:T(8,128)(2,1)S(1)}, u32[]{:S(2)}, u32[]{:S(2)}) collective-permute-start(bf16[1792,128]{1,0:T(8,128)(2,1)S(1)} %concatenate.24.own0), channel_id=1, source_target_pairs={{0,8},{1,17},{2,10},{3,19},{4,12},{5,21},{6,14},{7,23},{8,0},{9,25... | collective-permute-start | bytes 1376264 | tf_op jit(solution)/shard_map/ppermute | solution.py:441
  71.6 43.2 %collective-permute-start.19 = (bf16[1792,128]{1,0:T(8,128)(2,1)S(1)}, bf16[1792,128]{1,0:T(8,128)(2,1)S(1)}, u32[]{:S(2)}, u32[]{:S(2)}) collective-permute-start(bf16[1792,128]{1,0:T(8,128)(2,1)S(1)} %concatenate.24.own0), channel_id=1, source_target_pairs={{0,1},{1,0},{2,3},{3,2},{4,5},{5,4},{6,7},{7,6},{8,9},{9,8},{10,11... | collective-permute-start | bytes 1376264 | tf_op jit(solution)/shard_map/ppermute | solution.py:444
  82.9 32.0 %collective-permute-start.20 = (bf16[1792,128]{1,0:T(8,128)(2,1)S(1)}, bf16[1792,128]{1,0:T(8,128)(2,1)S(1)}, u32[]{:S(2)}, u32[]{:S(2)}) collective-permute-start(bf16[1792,128]{1,0:T(8,128)(2,1)S(1)} %collective-permute-done.18.own1), channel_id=1, source_target_pairs={{0,1},{1,0},{2,3},{3,2},{4,5},{5,4},{6,7},{7,6},{8,9},{9,8},{10,11... | collective-permute-start | bytes 1376264 | tf_op jit(solution)/shard_map/ppermute | solution.py:445
  90.1 5.1 %collective-permute-start.7 = (bf16[2,128,128]{2,1,0:T(8,128)(2,1)S(1)}, bf16[2,128,128]{2,1,0:T(8,128)(2,1)S(1)}, u32[]{:S(2)}, u32[]{:S(2)}) collective-permute-start(bf16[2,128,128]{2,1,0:T(8,128)(2,1)S(1)} %get-tuple-element.50), channel_id=1, source_target_pairs={{0,8},{8,16},{16,24},{1,9},{9,17},{17,25},{2,10},{10,18},{18,26},{... | collective-permute-start | bytes 196616 | tf_op jit(solution)/shard_map/ppermute | solution.py:299
  93.8 5.0 %collective-permute-start.8 = (bf16[2,128,128]{2,1,0:T(8,128)(2,1)S(1)}, bf16[2,128,128]{2,1,0:T(8,128)(2,1)S(1)}, u32[]{:S(2)}, u32[]{:S(2)}) collective-permute-start(bf16[2,128,128]{2,1,0:T(8,128)(2,1)S(1)} %get-tuple-element.51), channel_id=1, source_target_pairs={{8,0},{16,8},{24,16},{9,1},{17,9},{25,17},{10,2},{18,10},{26,18},{... | collective-permute-start | bytes 196616 | tf_op jit(solution)/shard_map/ppermute | solution.py:300
  99.6 5.1 %collective-permute-start.9 = (bf16[2,144,128]{2,1,0:T(8,128)(2,1)S(1)}, bf16[2,144,128]{2,1,0:T(8,128)(2,1)S(1)}, u32[]{:S(2)}, u32[]{:S(2)}) collective-permute-start(bf16[2,144,128]{2,1,0:T(8,128)(2,1)S(1)} %get-tuple-element.52), channel_id=1, source_target_pairs={{0,1},{1,2},{2,3},{3,4},{4,5},{5,6},{6,7},{8,9},{9,10},{10,11},{11... | collective-permute-start | bytes 221192 | tf_op jit(solution)/shard_map/ppermute | solution.py:299
  102.7 5.7 %collective-permute-start.10 = (bf16[2,144,128]{2,1,0:T(8,128)(2,1)S(1)}, bf16[2,144,128]{2,1,0:T(8,128)(2,1)S(1)}, u32[]{:S(2)}, u32[]{:S(2)}) collective-permute-start(bf16[2,144,128]{2,1,0:T(8,128)(2,1)S(1)} %get-tuple-element.53), channel_id=1, source_target_pairs={{1,0},{2,1},{3,2},{4,3},{5,4},{6,5},{7,6},{9,8},{10,9},{11,10},{12... | collective-permute-start | bytes 221192 | tf_op jit(solution)/shard_map/ppermute | solution.py:300

commit v3 on v2

--- a/solution.py
+++ b/solution.py
@@ -18,7 +18,6 @@
 f32, bf16 = jnp.float32, jnp.bfloat16
 VMEM = pl.BlockSpec(memory_space=pltpu.VMEM)
 SMEM = pl.BlockSpec(memory_space=pltpu.SMEM)
-PARAMS = pltpu.CompilerParams(vmem_limit_bytes=28 << 20)
 
 
 def sds(shape, dtype):
@@ -31,14 +30,14 @@
     return p < POS, q // BY, q % BY
 
 
-def call(body, outs, scratch, args, n_smem):
+def call(body, outs, scratch, args, n_smem, mib=4):
     return pl.pallas_call(
         body,
         out_shape=outs,
         in_specs=[SMEM] * n_smem + [VMEM] * (len(args) - n_smem),
         out_specs=[VMEM] * len(outs),
         scratch_shapes=scratch,
-        compiler_params=PARAMS,
+        compiler_params=pltpu.CompilerParams(vmem_limit_bytes=mib << 20),
     )(*args)
 
 
@@ -200,7 +199,7 @@
 
 def grads_body(
     pos, ppos, meta, a, b, xl, xr, yl, yr, other, hid, pre, msg, gain_part,
-    low, out, gsum, grid, cols, pt, acc, *, chunks
+    keep_b, keep_a, out_b, out_a, gsum, grid, cols, pt, acc, *, chunks
 ):
     core, mine = meta[0], meta[1]
 
@@ -234,15 +233,12 @@
     for j in range(9):
         acc[j * 384 : (j + 1) * 384] = y[:, j * C : (j + 1) * C]
     size = acc.shape[0] // chunks
-    half = chunks // 2
-    for p in range(half):
-        at = pl.multiple_of((mine ^ p) * size, 8)
-        low[p * size : (p + 1) * size] = acc[pl.ds(at, size)]
-    for p in range(0, half, 2):
-        at = pl.multiple_of((mine ^ (p + half)) * size, 8)
-        nxt = pl.multiple_of((mine ^ (p + half + 1)) * size, 8)
-        two = jnp.concatenate([acc[pl.ds(at, size)], acc[pl.ds(nxt, size)]])
-        out[p * size : (p + 2) * size] = two.astype(bf16)
+    quarter = chunks // 4
+    for k, dst in enumerate((keep_b, keep_a, out_b, out_a)):
+        for p in range(0, quarter, 2):
+            at = [pl.multiple_of((mine ^ (k * quarter + p + i)) * size, 8) for i in range(2)]
+            two = jnp.concatenate([acc[pl.ds(a, size)] for a in at])
+            dst[p * size : (p + 2) * size] = two.astype(dst.dtype)
     tile = msg[1024:P_ROWS].astype(f32)
     total = gain_part[0:1] + ((tile[2:3] + tile[1:2]) + tile[0:1])
     gsum[...] = jnp.broadcast_to(total, (8, C))
@@ -254,15 +250,34 @@
     return jnp.where(row == 0, hi, jnp.where(row == 1, mid, jnp.where(row == 2, low, 0.0))).astype(bf16)
 
 
-def final_body(meta, own0, own1, part0, part1, k_out, g_out, first, second, gains, *, chunks):
+def seal_body(low, g, out):
+    hi, mid, rest = split3(g[0:1])
+    row = lax.broadcasted_iota(jnp.int32, (8, C), 0)
+    tile = jnp.where(row == 0, hi, jnp.where(row == 1, mid, jnp.where(row == 2, rest, 0.0)))
+    out[...] = jnp.concatenate([low[...], tile]).astype(bf16)
+
+
+def join_body(a, b, out):
+    n = a.shape[0]
+    out[0:n] = a[...]
+    out[n:] = b[...]
+
+
+def join(a, b):
+    (out,) = call(join_body, [sds((a.shape[0] + b.shape[0], C), bf16)], [], (a, b), 0)
+    return out
+
+
+def final_body(meta, o0, o1, o2, o3, p0, p1, p2, p3, k_out, g_out, first, second, gains, *, chunks):
+    own, part = (o0, o1, o2, o3), (p0, p1, p2, p3)
     core, mine, theirs = meta[0], meta[1], meta[2]
     n = TAPS * C
     size = n // chunks
-    half = chunks // 2
+    quarter = chunks // 4
 
     def spread(dst, srcs, me, gain):
         for p in range(chunks):
-            src, q = srcs[p // half], p % half
+            src, q = srcs[p // quarter], p % quarter
             piece = src[q * (size + 8) : (q + 1) * (size + 8)].astype(f32)
             dst[pl.ds(pl.multiple_of((me ^ p) * size, 8), size)] = piece[:size]
             if gain:
@@ -271,13 +286,13 @@
 
     @pl.when(core == 0)
     def _():
-        spread(first, (own0, own1), mine, True)
-        spread(second, (part0, part1), theirs, False)
+        spread(first, own, mine, True)
+        spread(second, part, theirs, False)
 
     @pl.when(core != 0)
     def _():
-        spread(first, (part0, part1), theirs, True)
-        spread(second, (own0, own1), mine, False)
+        spread(first, part, theirs, True)
+        spread(second, own, mine, False)
 
     g = jnp.sum(gains[...], axis=0)[0:1]
     total = jnp.sum(g * g)
@@ -335,15 +350,6 @@
     return jnp.asarray(out, jnp.int32)
 
 
-def gain_tile(g):
-    rows, rest = [], g
-    for _ in range(3):
-        part = lax.reduce_precision(rest, 8, 7)
-        rows.append(part)
-        rest = rest - part
-    return jnp.concatenate(rows + [jnp.zeros((5, C), f32)]).astype(bf16)
-
-
 def after(value, *done):
     return lax.optimization_barrier((value, *done))[0]
 
@@ -393,11 +399,12 @@
         [grid, cols, pltpu.VMEM((512, C), f32)],
         (brick_pos, meta, features, cotangent, *edge, w1, t2, gain),
         2,
+        14,
     )
     pmsg = lax.ppermute(msg, "gy", partner)
-    low, out, g = call(
+    keep_b, keep_a, out_b, out_a, g = call(
         functools.partial(grads_body, chunks=chunks),
-        [sds((n // 2, C), f32), sds((n // 2, C), bf16), sds((8, C), f32)],
+        [sds((n // 4, C), f32)] * 2 + [sds((n // 4, C), bf16)] * 2 + [sds((8, C), f32)],
         [
             grid,
             pltpu.VMEM((2048, 9 * C), bf16),
@@ -406,10 +413,11 @@
         ],
         (brick_pos, ppos, meta, features, cotangent, *edge, other, hid, pre, pmsg, gain_part),
         3,
+        20,
     )
     g = g[0:1]
 
-    lo, hi = call(pack_x_body, [sds((2, 128, C), bf16)] * 2, [], (brick_pos, after(hid, out), pre), 1)
+    lo, hi = call(pack_x_body, [sds((2, 128, C), bf16)] * 2, [], (brick_pos, after(hid, out_a), pre), 1)
     xl, xr = shift(lo, hi, "gx")
     lo, hi = y_faces(brick_pos, hid, pre, xl, xr)
     around = xl, xr, *shift(lo, hi, "gy")
@@ -421,34 +429,42 @@
             [pltpu.VMEM((1, 18, 18, 8, C), f32), cols],
             (brick_pos, src, *around, w, base),
             1,
+            10,
         )
         results.append(res)
 
-    for s in range(halvings):
-        got = lax.ppermute(out, both, perms[s])
-        low = low + got.astype(f32)
+    swap = lambda v, s: lax.ppermute(v, both, perms[s])
+    got_a, got_b = swap(out_a, 0), swap(out_b, 0)
+    out = (keep_a + got_a.astype(f32)).astype(bf16)
+    got = swap(out, 1)
+    low = keep_b + got_b.astype(f32) + got.astype(f32)
+    for s in range(2, halvings):
+        half = low.shape[0] // 2
+        out = low[half:]
         if s + 1 < halvings:
-            half = low.shape[0] // 2
-            low, out = low[:half], low[half:]
-            if s + 2 < halvings:
-                out = out.astype(bf16)
+            out = out.astype(bf16)
+        got = swap(out, s)
+        low = low[:half] + got.astype(f32)
     for s in range(halvings, len(perms)):
-        got = lax.ppermute(jnp.concatenate([low, jnp.broadcast_to(g, (8, C))]), both, perms[s])
+        got = swap(jnp.concatenate([low, jnp.broadcast_to(g, (8, C))]), s)
         low, g = low + got[:size], g + got[size : size + 1]
 
-    full = jnp.concatenate([low.astype(bf16), gain_tile(g)])
-    for s in reversed(range(halvings)):
-        got = lax.ppermute(full, both, perms[s])
-        if s:
-            full = jnp.concatenate([full, got])
-    early = lax.ppermute(full, "gy", partner)
-    late = lax.ppermute(got, "gy", partner)
+    (full,) = call(seal_body, [sds((size + 8, C), bf16)], [], (low, g), 0)
+    for s in reversed(range(2, halvings)):
+        got = swap(full, s)
+        full = join(full, got)
+    own = [full]
+    own.append(swap(full, 1))
+    own.append(swap(full, 0))
+    own.append(swap(own[1], 0))
+    part = [lax.ppermute(v, "gy", partner) for v in own]
     k_up, g_up = call(
         functools.partial(final_body, chunks=chunks),
         [sds((2, TAPS, C, C), f32), sds((1, C), f32)],
         [pltpu.VMEM((n, C), f32), pltpu.VMEM((n, C), f32), pltpu.VMEM((chunks, 8, C), f32)],
-        (meta, full, got, early, late),
+        (meta, *own, *part),
         1,
+        14,
     )
     return (*results, k_up, g_up.reshape(C))
 

time: 119 us -> 110 us (0.924)
  the two profiles are of different devices: /device:TPU:1 before, /device:TPU:11 now
where the time goes in v3:
time: 110 us
  starting transfers between devices  43.2 us (39%)
  waiting for transfers between devices  41.6 us (38%)
  Pallas kernels  23.6 us (21%)
    ppermute x10, waiting for transfers between devices, per_device(): swap = lambda v, s: lax.ppermute(v, both, perms[s])  25.9 us
    pallas_call x13, Pallas kernels, call(): pl.pallas_call(body, out_shape=outs, in_specs=[SMEM] * n_smem + [VMEM] *...  23.6 us
    ppermute x4, starting transfers between devices, shift(): from_left = lax.ppermute(hi, axis, [(i, i + 1) for i in range(n - 1)])  16.7 us
    ppermute x4, waiting for transfers between devices, shift(): from_right = lax.ppermute(lo, axis, [(i + 1, i) for i in range(n - 1)])  12.6 us
    ppermute x4, starting transfers between devices, per_device(): part = [lax.ppermute(v, 'gy', partner) for v in own]  10.1 us
    ppermute x4, starting transfers between devices, shift(): from_right = lax.ppermute(lo, axis, [(i + 1, i) for i in range(n - 1)])  9.04 us
    ppermute x10, starting transfers between devices, per_device(): swap = lambda v, s: lax.ppermute(v, both, perms[s])  6.5 us
  transfers between devices with their start and end apart: 25, of which 14 were waited for; matrix products, arithmetic and copies ran while one was open for 0% of the time, Pallas kernels for 10%

profile of v3, /device:TPU:11, one launch (start us, length us, event | category | flops | bytes accessed | tf_op | source)
XLA Modules:
  0.0 109.7 jit_solution(760199152671590590)
XLA Ops:
  0.6 1.3 %shard_map.93 = (bf16[2,512,128]{2,1,0:T(8,128)(2,1)S(1)}, bf16[2,512,128]{2,1,0:T(8,128)(2,1)S(1)}, bf16[2,512,128]{2,1,0:T(8,128)(2,1)S(1)}, bf16[2,128,128]{2,1,0:T(8,128)(2,1)S(1)}, bf16[2,128,128]{2,1,0:T(8,128)(2,1)S(1)}) custom-call(s32[2]{0:T(128)} %pos.15, s32[1]{0:T(128)} %bitcast.core, bf16[2,512,128]{2,1,0:T(8,128)(2,1)} %a.1, bf16[2,512,128]{2,1,0:T(8,128)(2,1)} %b.1), custom_call_target="tpu_custom_call" | custom-call | tf_op jit(solution)/shard_map/pallas_call | solution.py:34
  1.9 0.7 collective-permute-start.4
  2.7 0.1 collective-permute-start.3
  2.7 3.1 %collective-permute-start = (bf16[2,128,128]{2,1,0:T(8,128)(2,1)S(1)}, bf16[2,128,128]{2,1,0:T(8,128)(2,1)S(1)}, u32[]{:S(2)}, u32[]{:S(2)}) collective-permute-start(bf16[2,128,128]{2,1,0:T(8,128)(2,1)S(1)} %get-tuple-element.36), channel_id=1, source_target_pairs={{0,8},{8,16},{16,24},{1,9},{9,17},{17,25},{2,10},{10,18},{18,26},{... | collective-permute-start | bytes 196616 | tf_op jit(solution)/shard_map/ppermute | solution.py:314
  5.8 2.2 %collective-permute-start.1 = (bf16[2,128,128]{2,1,0:T(8,128)(2,1)S(1)}, bf16[2,128,128]{2,1,0:T(8,128)(2,1)S(1)}, u32[]{:S(2)}, u32[]{:S(2)}) collective-permute-start(bf16[2,128,128]{2,1,0:T(8,128)(2,1)S(1)} %get-tuple-element.37), channel_id=1, source_target_pairs={{8,0},{16,8},{24,16},{9,1},{17,9},{25,17},{10,2},{18,10},{26,18},{... | collective-permute-start | bytes 196616 | tf_op jit(solution)/shard_map/ppermute | solution.py:315
  8.1 2.0 %shard_map.94 = (bf16[1152,384]{1,0:T(8,128)(2,1)S(1)}, bf16[1152,384]{1,0:T(8,128)(2,1)S(1)}, bf16[384,1152]{1,0:T(8,128)(2,1)S(1)}, bf16[384,1152]{1,0:T(8,128)(2,1)S(1)}, f32[1,128]{1,0:T(1,128)S(1)}) custom-call(bf16[27,128,128]{2,1,0:T(8,128)(2,1)} %k1.1, bf16[27,128,128]{2,1,0:T(8,128)(2,1)} %k2.1, f32[1,128]{1,0:T(1,128)} %bitcast.5), custom_call_target="tpu_custom_call" | custom-call | tf_op jit(solution)/shard_map/pallas_call | solution.py:34
  10.1 0.1 pad_add_fusion.meta
  10.1 1.6 %collective-permute-done.1.xr = bf16[2,128,128]{2,1,0:T(8,128)(2,1)S(1)} collective-permute-done((bf16[2,128,128]{2,1,0:T(8,128)(2,1)S(1)}, bf16[2,128,128]{2,1,0:T(8,128)(2,1)S(1)}, u32[]{:S(2)}, u32[]{:S(2)}) %collective-permute-start.1) | collective-permute-done | bytes 65568 | tf_op jit(solution)/shard_map/ppermute | solution.py:315
  11.8 0.8 shard_map.95
  12.6 5.0 %collective-permute-start.2 = (bf16[2,144,128]{2,1,0:T(8,128)(2,1)S(1)}, bf16[2,144,128]{2,1,0:T(8,128)(2,1)S(1)}, u32[]{:S(2)}, u32[]{:S(2)}) collective-permute-start(bf16[2,144,128]{2,1,0:T(8,128)(2,1)S(1)} %get-tuple-element.40), channel_id=1, source_target_pairs={{0,1},{1,2},{2,3},{3,4},{4,5},{5,6},{6,7},{8,9},{9,10},{10,11},{11... | collective-permute-start | bytes 221192 | tf_op jit(solution)/shard_map/ppermute | solution.py:314
  17.5 1.9 %collective-permute-start.5 = (bf16[2,144,128]{2,1,0:T(8,128)(2,1)S(1)}, bf16[2,144,128]{2,1,0:T(8,128)(2,1)S(1)}, u32[]{:S(2)}, u32[]{:S(2)}) collective-permute-start(bf16[2,144,128]{2,1,0:T(8,128)(2,1)S(1)} %get-tuple-element.43), channel_id=1, source_target_pairs={{1,0},{2,1},{3,2},{4,3},{5,4},{6,5},{7,6},{9,8},{10,9},{11,10},{12... | collective-permute-start | bytes 221192 | tf_op jit(solution)/shard_map/ppermute | solution.py:315
  19.5 3.7 %collective-permute-done.5.yr = bf16[2,144,128]{2,1,0:T(8,128)(2,1)S(1)} collective-permute-done((bf16[2,144,128]{2,1,0:T(8,128)(2,1)S(1)}, bf16[2,144,128]{2,1,0:T(8,128)(2,1)S(1)}, u32[]{:S(2)}, u32[]{:S(2)}) %collective-permute-start.5) | collective-permute-done | bytes 73760 | tf_op jit(solution)/shard_map/ppermute | solution.py:315
  23.2 4.5 %shard_map.96 = (bf16[2,512,128]{2,1,0:T(8,128)(2,1)S(1)}, bf16[2,512,128]{2,1,0:T(8,128)(2,1)S(1)}, bf16[1584,128]{1,0:T(8,128)(2,1)S(1)}, f32[8,128]{1,0:T(8,128)S(1)}) custom-call(s32[2]{0:T(128)} %pos.15, s32[3]{0:T(128)S(1)} %pad_add_fusion.meta, bf16[2,512,128]{2,1,0:T(8,128)(2,1)S(1)} %get-tuple-element.39.a.base, ...), custom_call_target="tpu_custom_call" | custom-call | tf_op jit(solution)/shard_map/pallas_call | solution.py:34
  27.7 0.1 collective-permute-start.6
  27.8 1.7 %collective-permute-done.6.msg = bf16[1584,128]{1,0:T(8,128)(2,1)S(1)} collective-permute-done((bf16[1584,128]{1,0:T(8,128)(2,1)S(1)}, bf16[1584,128]{1,0:T(8,128)(2,1)S(1)}, u32[]{:S(2)}, u32[]{:S(2)}) %collective-permute-start.6) | collective-permute-done | bytes 405536 | tf_op jit(solution)/shard_map/ppermute | solution.py:404
  29.5 3.7 %shard_map.97 = (f32[864,128]{1,0:T(8,128)S(1)}, f32[864,128]{1,0:T(8,128)S(1)}, bf16[864,128]{1,0:T(8,128)(2,1)S(1)}, bf16[864,128]{1,0:T(8,128)(2,1)S(1)}, f32[8,128]{1,0:T(8,128)S(1)}) custom-call(s32[2]{0:T(128)} %pos.15, s32[2]{0:T(128)S(1)} %collective-permute-done.3.ppos, s32[3]{0:T(128)S(1)} %pad_add_fusion.meta, ...), custom_call_target="tpu_custom_call" | custom-call | tf_op jit(solution)/shard_map/pallas_call | solution.py:34
  33.3 1.5 %collective-permute-start.11 = (bf16[864,128]{1,0:T(8,128)(2,1)S(1)}, bf16[864,128]{1,0:T(8,128)(2,1)S(1)}, u32[]{:S(2)}, u32[]{:S(2)}) collective-permute-start(bf16[864,128]{1,0:T(8,128)(2,1)S(1)} %get-tuple-element.59), channel_id=1, source_target_pairs={{0,8},{1,17},{2,10},{3,19},{4,12},{5,21},{6,14},{7,23},{8,0},{9,25... | collective-permute-start | bytes 663560 | tf_op jit(solution)/shard_map/ppermute | solution.py:436
  34.7 3.6 %collective-permute-done.12 = bf16[864,128]{1,0:T(8,128)(2,1)S(1)} collective-permute-done((bf16[864,128]{1,0:T(8,128)(2,1)S(1)}, bf16[864,128]{1,0:T(8,128)(2,1)S(1)}, u32[]{:S(2)}, u32[]{:S(2)}) %collective-permute-start.12) | collective-permute-done | bytes 221216 | tf_op jit(solution)/shard_map/ppermute | solution.py:436
  38.5 2.2 %collective-permute-done.11 = bf16[864,128]{1,0:T(8,128)(2,1)S(1)} collective-permute-done((bf16[864,128]{1,0:T(8,128)(2,1)S(1)}, bf16[864,128]{1,0:T(8,128)(2,1)S(1)}, u32[]{:S(2)}, u32[]{:S(2)}) %collective-permute-start.11) | collective-permute-done | bytes 221216 | tf_op jit(solution)/shard_map/ppermute | solution.py:436
  40.7 3.0 %collective-permute-done.13 = bf16[864,128]{1,0:T(8,128)(2,1)S(1)} collective-permute-done((bf16[864,128]{1,0:T(8,128)(2,1)S(1)}, bf16[864,128]{1,0:T(8,128)(2,1)S(1)}, u32[]{:S(2)}, u32[]{:S(2)}) %collective-permute-start.13) | collective-permute-done | bytes 221216 | tf_op jit(solution)/shard_map/ppermute | solution.py:436
  43.7 0.1 convert_add_fusion
  43.8 0.2 collective-permute-start.14
  44.0 3.4 %collective-permute-done.14 = bf16[432,128]{1,0:T(8,128)(2,1)S(1)} collective-permute-done((bf16[432,128]{1,0:T(8,128)(2,1)S(1)}, bf16[432,128]{1,0:T(8,128)(2,1)S(1)}, u32[]{:S(2)}, u32[]{:S(2)}) %collective-permute-start.14) | collective-permute-done | bytes 110624 | tf_op jit(solution)/shard_map/ppermute | solution.py:436
  47.5 1.1 %collective-permute-start.15 = (f32[216,128]{1,0:T(8,128)S(1)}, f32[216,128]{1,0:T(8,128)S(1)}, u32[]{:S(2)}, u32[]{:S(2)}) collective-permute-start(f32[216,128]{1,0:T(8,128)S(1)} %slice.24), channel_id=1, source_target_pairs={{0,4},{1,5},{2,6},{3,7},{4,0},{5,1},{6,2},{7,3},{8,12},{9,13},{10,... | collective-permute-start | bytes 331784 | tf_op jit(solution)/shard_map/ppermute | solution.py:436
  48.6 3.6 %collective-permute-done.15 = f32[216,128]{1,0:T(8,128)S(1)} collective-permute-done((f32[216,128]{1,0:T(8,128)S(1)}, f32[216,128]{1,0:T(8,128)S(1)}, u32[]{:S(2)}, u32[]{:S(2)}) %collective-permute-start.15) | collective-permute-done | bytes 110624 | tf_op jit(solution)/shard_map/ppermute | solution.py:436
  52.2 1.0 collective-permute-start.16
  53.2 3.0 %collective-permute-done.16.b = bf16[224,128]{1,0:T(8,128)(2,1)S(1)} collective-permute-done((bf16[224,128]{1,0:T(8,128)(2,1)S(1)}, bf16[224,128]{1,0:T(8,128)(2,1)S(1)}, u32[]{:S(2)}, u32[]{:S(2)}) %collective-permute-start.16) | collective-permute-done | bytes 57376 | tf_op jit(solution)/shard_map/ppermute | solution.py:436
  56.2 1.9 %collective-permute-start.17 = (bf16[448,128]{1,0:T(8,128)(2,1)S(1)}, bf16[448,128]{1,0:T(8,128)(2,1)S(1)}, u32[]{:S(2)}, u32[]{:S(2)}) collective-permute-start(bf16[448,128]{1,0:T(8,128)(2,1)S(1)} %shard_map.103.a), channel_id=1, source_target_pairs={{0,2},{1,3},{2,0},{3,1},{4,6},{5,7},{6,4},{7,5},{8,10},{9,11},{10,... | collective-permute-start | bytes 344072 | tf_op jit(solution)/shard_map/ppermute | solution.py:436
  58.0 2.5 %collective-permute-done.17.b = bf16[448,128]{1,0:T(8,128)(2,1)S(1)} collective-permute-done((bf16[448,128]{1,0:T(8,128)(2,1)S(1)}, bf16[448,128]{1,0:T(8,128)(2,1)S(1)}, u32[]{:S(2)}, u32[]{:S(2)}) %collective-permute-start.17) | collective-permute-done | bytes 114720 | tf_op jit(solution)/shard_map/ppermute | solution.py:436
  60.6 0.1 collective-permute-start.18
  60.7 0.6 collective-permute-start.19
  61.3 4.6 %collective-permute-done.18.o1 = bf16[896,128]{1,0:T(8,128)(2,1)S(1)} collective-permute-done((bf16[896,128]{1,0:T(8,128)(2,1)S(1)}, bf16[896,128]{1,0:T(8,128)(2,1)S(1)}, u32[]{:S(2)}, u32[]{:S(2)}) %collective-permute-start.18) | collective-permute-done | bytes 229408 | tf_op jit(solution)/shard_map/ppermute | solution.py:436
  65.9 0.7 shard_map.98
  66.6 3.1 %collective-permute-start.7 = (bf16[2,128,128]{2,1,0:T(8,128)(2,1)S(1)}, bf16[2,128,128]{2,1,0:T(8,128)(2,1)S(1)}, u32[]{:S(2)}, u32[]{:S(2)}) collective-permute-start(bf16[2,128,128]{2,1,0:T(8,128)(2,1)S(1)} %get-tuple-element.52), channel_id=1, source_target_pairs={{0,8},{8,16},{16,24},{1,9},{9,17},{17,25},{2,10},{10,18},{18,26},{... | collective-permute-start | bytes 196616 | tf_op jit(solution)/shard_map/ppermute | solution.py:314
  69.7 8.6 %collective-permute-start.21 = (bf16[896,128]{1,0:T(8,128)(2,1)S(1)}, bf16[896,128]{1,0:T(8,128)(2,1)S(1)}, u32[]{:S(2)}, u32[]{:S(2)}) collective-permute-start(bf16[896,128]{1,0:T(8,128)(2,1)S(1)} %shard_map.104.o0), channel_id=1, source_target_pairs={{0,1},{1,0},{2,3},{3,2},{4,5},{5,4},{6,7},{7,6},{8,9},{9,8},{10,11... | collective-permute-start | bytes 688136 | tf_op jit(solution)/shard_map/ppermute | solution.py:460
  78.4 0.1 collective-permute-start.22
  78.4 0.4 collective-permute-start.23
  78.9 1.0 collective-permute-start.24
  79.9 1.9 %collective-permute-start.8 = (bf16[2,128,128]{2,1,0:T(8,128)(2,1)S(1)}, bf16[2,128,128]{2,1,0:T(8,128)(2,1)S(1)}, u32[]{:S(2)}, u32[]{:S(2)}) collective-permute-start(bf16[2,128,128]{2,1,0:T(8,128)(2,1)S(1)} %get-tuple-element.53), channel_id=1, source_target_pairs={{8,0},{16,8},{24,16},{9,1},{17,9},{25,17},{10,2},{18,10},{26,18},{... | collective-permute-start | bytes 196616 | tf_op jit(solution)/shard_map/ppermute | solution.py:315
  81.8 4.0 %collective-permute-done.8.xr = bf16[2,128,128]{2,1,0:T(8,128)(2,1)S(1)} collective-permute-done((bf16[2,128,128]{2,1,0:T(8,128)(2,1)S(1)}, bf16[2,128,128]{2,1,0:T(8,128)(2,1)S(1)}, u32[]{:S(2)}, u32[]{:S(2)}) %collective-permute-start.8) | collective-permute-done | bytes 65568 | tf_op jit(solution)/shard_map/ppermute | solution.py:315
  85.8 0.8 shard_map.99
  86.6 5.5 %collective-permute-start.9 = (bf16[2,144,128]{2,1,0:T(8,128)(2,1)S(1)}, bf16[2,144,128]{2,1,0:T(8,128)(2,1)S(1)}, u32[]{:S(2)}, u32[]{:S(2)}) collective-permute-start(bf16[2,144,128]{2,1,0:T(8,128)(2,1)S(1)} %get-tuple-element.54), channel_id=1, source_target_pairs={{0,1},{1,2},{2,3},{3,4},{4,5},{5,6},{6,7},{8,9},{9,10},{10,11},{11... | collective-permute-start | bytes 221192 | tf_op jit(solution)/shard_map/ppermute | solution.py:314
  92.1 1.4 %collective-permute-done.9.yl = bf16[2,144,128]{2,1,0:T(8,128)(2,1)S(1)} collective-permute-done((bf16[2,144,128]{2,1,0:T(8,128)(2,1)S(1)}, bf16[2,144,128]{2,1,0:T(8,128)(2,1)S(1)}, u32[]{:S(2)}, u32[]{:S(2)}) %collective-permute-start.9) | collective-permute-done | bytes 73760 | tf_op jit(solution)/shard_map/ppermute | solution.py:314
  93.5 3.0 %collective-permute-start.10 = (bf16[2,144,128]{2,1,0:T(8,128)(2,1)S(1)}, bf16[2,144,128]{2,1,0:T(8,128)(2,1)S(1)}, u32[]{:S(2)}, u32[]{:S(2)}) collective-permute-start(bf16[2,144,128]{2,1,0:T(8,128)(2,1)S(1)} %get-tuple-element.55), channel_id=1, source_target_pairs={{1,0},{2,1},{3,2},{4,3},{5,4},{6,5},{7,6},{9,8},{10,9},{11,10},{12... | collective-permute-start | bytes 221192 | tf_op jit(solution)/shard_map/ppermute | solution.py:315
  96.5 3.3 %collective-permute-done.10.yr = bf16[2,144,128]{2,1,0:T(8,128)(2,1)S(1)} collective-permute-done((bf16[2,144,128]{2,1,0:T(8,128)(2,1)S(1)}, bf16[2,144,128]{2,1,0:T(8,128)(2,1)S(1)}, u32[]{:S(2)}, u32[]{:S(2)}) %collective-permute-start.10) | collective-permute-done | bytes 73760 | tf_op jit(solution)/shard_map/ppermute | solution.py:315
  99.8 3.1 %shard_map.101 = bf16[2,512,128]{2,1,0:T(8,128)(2,1)} custom-call(s32[2]{0:T(128)} %pos.15, bf16[2,512,128]{2,1,0:T(8,128)(2,1)S(1)} %get-tuple-element.47.pre.b.src, bf16[2,128,128]{2,1,0:T(8,128)(2,1)S(1)} %collective-permute-done.7.xl, bf16[2,128,128]{2,1,0:T(8,128)(2,1)S(1)} %collective-permute-done.8.xr, ...), custom_call_target="tpu_custom_call" | custom-call | tf_op jit(solution)/shard_map/pallas_call | solution.py:34
  102.9 3.3 %shard_map.100 = bf16[2,512,128]{2,1,0:T(8,128)(2,1)} custom-call(s32[2]{0:T(128)} %pos.15, bf16[2,512,128]{2,1,0:T(8,128)(2,1)S(1)} %get-tuple-element.51.hid.a.src, bf16[2,128,128]{2,1,0:T(8,128)(2,1)S(1)} %collective-permute-done.7.xl, bf16[2,128,128]{2,1,0:T(8,128)(2,1)S(1)} %collective-permute-done.8.xr, ...), custom_call_target="tpu_custom_call" | custom-call | tf_op jit(solution)/shard_map/pallas_call | solution.py:34
  106.2 3.4 %shard_map.105 = (f32[2,27,128,128]{3,2,1,0:T(8,128)}, f32[1,128]{1,0:T(1,128)}) custom-call(s32[3]{0:T(128)S(1)} %pad_add_fusion.meta, bf16[896,128]{1,0:T(8,128)(2,1)S(1)} %shard_map.104.o0, bf16[896,128]{1,0:T(8,128)(2,1)S(1)} %collective-permute-done.18.o1, bf16[896,128]{1,0:T(8,128)(2,1)S(1)} %collective-permute-done.19.o2, ...), custom_call_target="tpu_custom_call" | custom-call | tf_op jit(solution)/shard_map/pallas_call | solution.py:34
  (23 shorter events, 0.4 us)
Async XLA Ops:
  1.9 15.6 %collective-permute-start.4 = (bf16[2,512,128]{2,1,0:T(8,128)(2,1)S(1)}, bf16[2,512,128]{2,1,0:T(8,128)(2,1)S(1)}, u32[]{:S(2)}, u32[]{:S(2)}) collective-permute-start(bf16[2,512,128]{2,1,0:T(8,128)(2,1)S(1)} %get-tuple-element.42), channel_id=1, source_target_pairs={{0,1},{1,0},{2,3},{3,2},{4,5},{5,4},{6,7},{7,6},{8,9},{9,8},{10,11... | collective-permute-start | bytes 786440 | tf_op jit(solution)/shard_map/ppermute | solution.py:382
  2.7 14.9 %collective-permute-start.3 = (s32[2]{0:T(128)}, s32[2]{0:T(128)S(1)}, u32[]{:S(2)}, u32[]{:S(2)}) collective-permute-start(s32[2]{0:T(128)} %pos.15), channel_id=1, source_target_pairs={{0,1},{1,0},{2,3},{3,2},{4,5},{5,4},{6,7},{7,6},{8,9},{9,8},{10,11... | collective-permute-start | bytes 32 | tf_op jit(solution)/shard_map/ppermute | solution.py:381
  2.7 7.4 %collective-permute-start = (bf16[2,128,128]{2,1,0:T(8,128)(2,1)S(1)}, bf16[2,128,128]{2,1,0:T(8,128)(2,1)S(1)}, u32[]{:S(2)}, u32[]{:S(2)}) collective-permute-start(bf16[2,128,128]{2,1,0:T(8,128)(2,1)S(1)} %get-tuple-element.36), channel_id=1, source_target_pairs={{0,8},{8,16},{16,24},{1,9},{9,17},{17,25},{2,10},{10,18},{18,26},{... | collective-permute-start | bytes 196616 | tf_op jit(solution)/shard_map/ppermute | solution.py:314
  5.8 5.9 %collective-permute-start.1 = (bf16[2,128,128]{2,1,0:T(8,128)(2,1)S(1)}, bf16[2,128,128]{2,1,0:T(8,128)(2,1)S(1)}, u32[]{:S(2)}, u32[]{:S(2)}) collective-permute-start(bf16[2,128,128]{2,1,0:T(8,128)(2,1)S(1)} %get-tuple-element.37), channel_id=1, source_target_pairs={{8,0},{16,8},{24,16},{9,1},{17,9},{25,17},{10,2},{18,10},{26,18},{... | collective-permute-start | bytes 196616 | tf_op jit(solution)/shard_map/ppermute | solution.py:315
  12.6 6.9 %collective-permute-start.2 = (bf16[2,144,128]{2,1,0:T(8,128)(2,1)S(1)}, bf16[2,144,128]{2,1,0:T(8,128)(2,1)S(1)}, u32[]{:S(2)}, u32[]{:S(2)}) collective-permute-start(bf16[2,144,128]{2,1,0:T(8,128)(2,1)S(1)} %get-tuple-element.40), channel_id=1, source_target_pairs={{0,1},{1,2},{2,3},{3,4},{4,5},{5,6},{6,7},{8,9},{9,10},{10,11},{11... | collective-permute-start | bytes 221192 | tf_op jit(solution)/shard_map/ppermute | solution.py:314
  17.5 5.7 %collective-permute-start.5 = (bf16[2,144,128]{2,1,0:T(8,128)(2,1)S(1)}, bf16[2,144,128]{2,1,0:T(8,128)(2,1)S(1)}, u32[]{:S(2)}, u32[]{:S(2)}) collective-permute-start(bf16[2,144,128]{2,1,0:T(8,128)(2,1)S(1)} %get-tuple-element.43), channel_id=1, source_target_pairs={{1,0},{2,1},{3,2},{4,3},{5,4},{6,5},{7,6},{9,8},{10,9},{11,10},{12... | collective-permute-start | bytes 221192 | tf_op jit(solution)/shard_map/ppermute | solution.py:315
  27.7 1.8 %collective-permute-start.6 = (bf16[1584,128]{1,0:T(8,128)(2,1)S(1)}, bf16[1584,128]{1,0:T(8,128)(2,1)S(1)}, u32[]{:S(2)}, u32[]{:S(2)}) collective-permute-start(bf16[1584,128]{1,0:T(8,128)(2,1)S(1)} %get-tuple-element.48), channel_id=1, source_target_pairs={{0,1},{1,0},{2,3},{3,2},{4,5},{5,4},{6,7},{7,6},{8,9},{9,8},{10,11... | collective-permute-start | bytes 1216520 | tf_op jit(solution)/shard_map/ppermute | solution.py:404
  33.2 5.1 %collective-permute-start.12 = (bf16[864,128]{1,0:T(8,128)(2,1)S(1)}, bf16[864,128]{1,0:T(8,128)(2,1)S(1)}, u32[]{:S(2)}, u32[]{:S(2)}) collective-permute-start(bf16[864,128]{1,0:T(8,128)(2,1)S(1)} %get-tuple-element.50), channel_id=1, source_target_pairs={{0,8},{1,17},{2,10},{3,19},{4,12},{5,21},{6,14},{7,23},{8,0},{9,25... | collective-permute-start | bytes 663560 | tf_op jit(solution)/shard_map/ppermute | solution.py:436
  33.3 7.4 %collective-permute-start.11 = (bf16[864,128]{1,0:T(8,128)(2,1)S(1)}, bf16[864,128]{1,0:T(8,128)(2,1)S(1)}, u32[]{:S(2)}, u32[]{:S(2)}) collective-permute-start(bf16[864,128]{1,0:T(8,128)(2,1)S(1)} %get-tuple-element.59), channel_id=1, source_target_pairs={{0,8},{1,17},{2,10},{3,19},{4,12},{5,21},{6,14},{7,23},{8,0},{9,25... | collective-permute-start | bytes 663560 | tf_op jit(solution)/shard_map/ppermute | solution.py:436
  38.4 5.3 %collective-permute-start.13 = (bf16[864,128]{1,0:T(8,128)(2,1)S(1)}, bf16[864,128]{1,0:T(8,128)(2,1)S(1)}, u32[]{:S(2)}, u32[]{:S(2)}) collective-permute-start(bf16[864,128]{1,0:T(8,128)(2,1)S(1)} %add_convert_fusion), channel_id=1, source_target_pairs={{0,16},{1,9},{2,18},{3,11},{4,20},{5,13},{6,22},{7,15},{8,24},{9,1... | collective-permute-start | bytes 663560 | tf_op jit(solution)/shard_map/ppermute | solution.py:436
  43.8 3.7 %collective-permute-start.14 = (bf16[432,128]{1,0:T(8,128)(2,1)S(1)}, bf16[432,128]{1,0:T(8,128)(2,1)S(1)}, u32[]{:S(2)}, u32[]{:S(2)}) collective-permute-start(bf16[432,128]{1,0:T(8,128)(2,1)S(1)} %slice.28), channel_id=1, source_target_pairs={{0,2},{1,3},{2,0},{3,1},{4,6},{5,7},{6,4},{7,5},{8,10},{9,11},{10,... | collective-permute-start | bytes 331784 | tf_op jit(solution)/shard_map/ppermute | solution.py:436
  47.5 4.7 %collective-permute-start.15 = (f32[216,128]{1,0:T(8,128)S(1)}, f32[216,128]{1,0:T(8,128)S(1)}, u32[]{:S(2)}, u32[]{:S(2)}) collective-permute-start(f32[216,128]{1,0:T(8,128)S(1)} %slice.24), channel_id=1, source_target_pairs={{0,4},{1,5},{2,6},{3,7},{4,0},{5,1},{6,2},{7,3},{8,12},{9,13},{10,... | collective-permute-start | bytes 331784 | tf_op jit(solution)/shard_map/ppermute | solution.py:436
  52.2 4.0 %collective-permute-start.16 = (bf16[224,128]{1,0:T(8,128)(2,1)S(1)}, bf16[224,128]{1,0:T(8,128)(2,1)S(1)}, u32[]{:S(2)}, u32[]{:S(2)}) collective-permute-start(bf16[224,128]{1,0:T(8,128)(2,1)S(1)} %shard_map.102.a), channel_id=1, source_target_pairs={{0,4},{1,5},{2,6},{3,7},{4,0},{5,1},{6,2},{7,3},{8,12},{9,13},{10,... | collective-permute-start | bytes 172040 | tf_op jit(solution)/shard_map/ppermute | solution.py:436
  56.2 4.4 %collective-permute-start.17 = (bf16[448,128]{1,0:T(8,128)(2,1)S(1)}, bf16[448,128]{1,0:T(8,128)(2,1)S(1)}, u32[]{:S(2)}, u32[]{:S(2)}) collective-permute-start(bf16[448,128]{1,0:T(8,128)(2,1)S(1)} %shard_map.103.a), channel_id=1, source_target_pairs={{0,2},{1,3},{2,0},{3,1},{4,6},{5,7},{6,4},{7,5},{8,10},{9,11},{10,... | collective-permute-start | bytes 344072 | tf_op jit(solution)/shard_map/ppermute | solution.py:436
  60.6 5.2 %collective-permute-start.18 = (bf16[896,128]{1,0:T(8,128)(2,1)S(1)}, bf16[896,128]{1,0:T(8,128)(2,1)S(1)}, u32[]{:S(2)}, u32[]{:S(2)}) collective-permute-start(bf16[896,128]{1,0:T(8,128)(2,1)S(1)} %shard_map.104.o0), channel_id=1, source_target_pairs={{0,16},{1,9},{2,18},{3,11},{4,20},{5,13},{6,22},{7,15},{8,24},{9,1... | collective-permute-start | bytes 688136 | tf_op jit(solution)/shard_map/ppermute | solution.py:436
  60.7 17.8 %collective-permute-start.19 = (bf16[896,128]{1,0:T(8,128)(2,1)S(1)}, bf16[896,128]{1,0:T(8,128)(2,1)S(1)}, u32[]{:S(2)}, u32[]{:S(2)}) collective-permute-start(bf16[896,128]{1,0:T(8,128)(2,1)S(1)} %shard_map.104.o0), channel_id=1, source_target_pairs={{0,8},{1,17},{2,10},{3,19},{4,12},{5,21},{6,14},{7,23},{8,0},{9,25... | collective-permute-start | bytes 688136 | tf_op jit(solution)/shard_map/ppermute | solution.py:436
  65.8 13.1 %collective-permute-start.20 = (bf16[896,128]{1,0:T(8,128)(2,1)S(1)}, bf16[896,128]{1,0:T(8,128)(2,1)S(1)}, u32[]{:S(2)}, u32[]{:S(2)}) collective-permute-start(bf16[896,128]{1,0:T(8,128)(2,1)S(1)} %collective-permute-done.18.o1), channel_id=1, source_target_pairs={{0,8},{1,17},{2,10},{3,19},{4,12},{5,21},{6,14},{7,23},{8,0},{9,25... | collective-permute-start | bytes 688136 | tf_op jit(solution)/shard_map/ppermute | solution.py:436
  66.6 13.2 %collective-permute-start.7 = (bf16[2,128,128]{2,1,0:T(8,128)(2,1)S(1)}, bf16[2,128,128]{2,1,0:T(8,128)(2,1)S(1)}, u32[]{:S(2)}, u32[]{:S(2)}) collective-permute-start(bf16[2,128,128]{2,1,0:T(8,128)(2,1)S(1)} %get-tuple-element.52), channel_id=1, source_target_pairs={{0,8},{8,16},{16,24},{1,9},{9,17},{17,25},{2,10},{10,18},{18,26},{... | collective-permute-start | bytes 196616 | tf_op jit(solution)/shard_map/ppermute | solution.py:314
  69.7 36.5 %collective-permute-start.21 = (bf16[896,128]{1,0:T(8,128)(2,1)S(1)}, bf16[896,128]{1,0:T(8,128)(2,1)S(1)}, u32[]{:S(2)}, u32[]{:S(2)}) collective-permute-start(bf16[896,128]{1,0:T(8,128)(2,1)S(1)} %shard_map.104.o0), channel_id=1, source_target_pairs={{0,1},{1,0},{2,3},{3,2},{4,5},{5,4},{6,7},{7,6},{8,9},{9,8},{10,11... | collective-permute-start | bytes 688136 | tf_op jit(solution)/shard_map/ppermute | solution.py:460
  78.4 27.9 %collective-permute-start.22 = (bf16[896,128]{1,0:T(8,128)(2,1)S(1)}, bf16[896,128]{1,0:T(8,128)(2,1)S(1)}, u32[]{:S(2)}, u32[]{:S(2)}) collective-permute-start(bf16[896,128]{1,0:T(8,128)(2,1)S(1)} %collective-permute-done.18.o1), channel_id=1, source_target_pairs={{0,1},{1,0},{2,3},{3,2},{4,5},{5,4},{6,7},{7,6},{8,9},{9,8},{10,11... | collective-permute-start | bytes 688136 | tf_op jit(solution)/shard_map/ppermute | solution.py:460
  78.4 27.8 %collective-permute-start.23 = (bf16[896,128]{1,0:T(8,128)(2,1)S(1)}, bf16[896,128]{1,0:T(8,128)(2,1)S(1)}, u32[]{:S(2)}, u32[]{:S(2)}) collective-permute-start(bf16[896,128]{1,0:T(8,128)(2,1)S(1)} %collective-permute-done.19.o2), channel_id=1, source_target_pairs={{0,1},{1,0},{2,3},{3,2},{4,5},{5,4},{6,7},{7,6},{8,9},{9,8},{10,11... | collective-permute-start | bytes 688136 | tf_op jit(solution)/shard_map/ppermute | solution.py:460
  78.9 27.3 %collective-permute-start.24 = (bf16[896,128]{1,0:T(8,128)(2,1)S(1)}, bf16[896,128]{1,0:T(8,128)(2,1)S(1)}, u32[]{:S(2)}, u32[]{:S(2)}) collective-permute-start(bf16[896,128]{1,0:T(8,128)(2,1)S(1)} %collective-permute-done.20.o3), channel_id=1, source_target_pairs={{0,1},{1,0},{2,3},{3,2},{4,5},{5,4},{6,7},{7,6},{8,9},{9,8},{10,11... | collective-permute-start | bytes 688136 | tf_op jit(solution)/shard_map/ppermute | solution.py:460
  79.9 5.9 %collective-permute-start.8 = (bf16[2,128,128]{2,1,0:T(8,128)(2,1)S(1)}, bf16[2,128,128]{2,1,0:T(8,128)(2,1)S(1)}, u32[]{:S(2)}, u32[]{:S(2)}) collective-permute-start(bf16[2,128,128]{2,1,0:T(8,128)(2,1)S(1)} %get-tuple-element.53), channel_id=1, source_target_pairs={{8,0},{16,8},{24,16},{9,1},{17,9},{25,17},{10,2},{18,10},{26,18},{... | collective-permute-start | bytes 196616 | tf_op jit(solution)/shard_map/ppermute | solution.py:315
  86.6 6.9 %collective-permute-start.9 = (bf16[2,144,128]{2,1,0:T(8,128)(2,1)S(1)}, bf16[2,144,128]{2,1,0:T(8,128)(2,1)S(1)}, u32[]{:S(2)}, u32[]{:S(2)}) collective-permute-start(bf16[2,144,128]{2,1,0:T(8,128)(2,1)S(1)} %get-tuple-element.54), channel_id=1, source_target_pairs={{0,1},{1,2},{2,3},{3,4},{4,5},{5,6},{6,7},{8,9},{9,10},{10,11},{11... | collective-permute-start | bytes 221192 | tf_op jit(solution)/shard_map/ppermute | solution.py:314
  93.5 6.3 %collective-permute-start.10 = (bf16[2,144,128]{2,1,0:T(8,128)(2,1)S(1)}, bf16[2,144,128]{2,1,0:T(8,128)(2,1)S(1)}, u32[]{:S(2)}, u32[]{:S(2)}) collective-permute-start(bf16[2,144,128]{2,1,0:T(8,128)(2,1)S(1)} %get-tuple-element.55), channel_id=1, source_target_pairs={{1,0},{2,1},{3,2},{4,3},{5,4},{6,5},{7,6},{9,8},{10,9},{11,10},{12... | collective-permute-start | bytes 221192 | tf_op jit(solution)/shard_map/ppermute | solution.py:315

commit v4 on v3

--- a/solution.py
+++ b/solution.py
@@ -41,49 +41,54 @@
     )(*args)
 
 
-def pack_x(pos, src, f, lo, hi):
-    for s in range(2):
-        live, bx, by = place(pos, s)
-        rows = pl.ds(pl.multiple_of(by * 64, 64), 64)
-
-        @pl.when(live & (bx == 0))
-        def _():
-            lo[f, rows] = src[s, 0:64]
-
-        @pl.when(live & (bx == 1))
-        def _():
-            hi[f, rows] = src[s, 448:512]
-
-
-def pack_x_body(pos, a, b, lo, hi):
-    lo[...] = jnp.zeros_like(lo)
-    hi[...] = jnp.zeros_like(hi)
-    pack_x(pos, a, 0, lo, hi)
-    pack_x(pos, b, 1, lo, hi)
-
-
-def load_body(pos, core, a, b, a_out, b_out, sent, lo, hi):
-    pack_x_body(pos, a, b, lo, hi)
+def sides(odd, a, b):
+    return jnp.where(odd == 0, b, a), jnp.where(odd == 0, a, b)
+
+
+def pack_x(pos, odd, srcs, outs):
+    for f, src in enumerate(srcs):
+        for out, d in zip(outs, (1 - odd, odd)):
+            out[f] = jnp.zeros(out.shape[1:], bf16)
+            at = pl.multiple_of(d * 448, 64)
+            for s in range(2):
+                live, bx, by = place(pos, s)
+
+                @pl.when(live & (bx == d))
+                def _():
+                    out[f, pl.ds(pl.multiple_of(by * 64, 64), 64)] = src[s, pl.ds(at, 64)]
+
+
+def pack_x_body(pos, odd, a, b, *outs):
+    pack_x(pos, odd[0], (a, b), outs)
+
+
+def load_body(pos, core, odd, a, b, a_out, b_out, sent, *outs):
+    pack_x(pos, odd[0], (a, b), outs)
     a_out[...] = a[...]
     b_out[...] = b[...]
     sent[...] = jnp.where(core[0] == 0, b[...], a[...])
 
 
-def pack_y_body(pos, a, b, xl, xr, lo, hi, tmp):
+def pack_y_body(pos, meta, a, b, xa, xb, ya, yb, tmp):
+    def edge_rows(v, d):
+        v = v.astype(f32)
+        return jnp.where(d == 0, v[0:8], v[8:16])
+
     for f, src in enumerate((a, b)):
-        for d, out in enumerate((lo, hi)):
+        for out, d in ((ya, 1 - meta[0]), (yb, meta[0])):
             tmp[...] = jnp.zeros_like(tmp)
-            at = 112 * d
-            tmp[0] = xl[f, at : at + 16].astype(f32)[8 * d : 8 * d + 8]
-            tmp[17] = xr[f, at : at + 16].astype(f32)[8 * d : 8 * d + 8]
+            rows = pl.ds(pl.multiple_of(d * 112, 16), 16)
+            xl, xr = sides(meta[3], xa[f, rows], xb[f, rows])
+            tmp[0] = edge_rows(xl, d)
+            tmp[17] = edge_rows(xr, d)
             for s in range(2):
                 live, bx, by = place(pos, s)
 
                 @pl.when(live & (by == d))
                 def _():
                     for x in range(8):
-                        at = x * 64 + 48 * d
-                        tmp[1 + bx * 8 + x] = src[s, at : at + 16].astype(f32)[8 * d : 8 * d + 8]
+                        at = pl.multiple_of(x * 64 + d * 48, 16)
+                        tmp[1 + bx * 8 + x] = edge_rows(src[s, pl.ds(at, 16)], d)
 
             out[f] = tmp[...].reshape(144, C).astype(bf16)
 
@@ -99,10 +104,14 @@
                 src[s].astype(f32).reshape(8, 8, 8, C)
             )
 
-    grid[f, 0, 1:17] = xl[f].astype(f32).reshape(16, 8, C)
-    grid[f, 17, 1:17] = xr[f].astype(f32).reshape(16, 8, C)
-    grid[f, :, 0] = yl[f].astype(f32).reshape(18, 8, C)
-    grid[f, :, 17] = yr[f].astype(f32).reshape(18, 8, C)
+    grid[f, 0, 1:17] = xl.astype(f32).reshape(16, 8, C)
+    grid[f, 17, 1:17] = xr.astype(f32).reshape(16, 8, C)
+    grid[f, :, 0] = yl.astype(f32).reshape(18, 8, C)
+    grid[f, :, 17] = yr.astype(f32).reshape(18, 8, C)
+
+
+def faces(meta, f, xa, xb, ya, yb):
+    return *sides(meta[3], xa[f], xb[f]), *sides(meta[0], ya[f], yb[f])
 
 
 def window(grid, f, bx, by, j):
@@ -151,16 +160,16 @@
 
 
 def main_body(
-    pos, meta, a, b, xl, xr, yl, yr, w1, w2, gain,
+    pos, meta, a, b, xa, xb, ya, yb, w1, w2, gain,
     hid, pre, msg, gain_part, grid, cols, hg
 ):
     core = meta[0]
     for f, src in enumerate((a, b)):
-        build(grid, f, pos, src, xl, xr, yl, yr)
+        build(grid, f, pos, src, *faces(meta, f, xa, xb, ya, yb))
     at = P_ROWS
-    for ref in (xl, xr, yl, yr):
-        msg[at : at + ref.shape[1]] = ref[1 - core]
-        at += ref.shape[1]
+    for face in faces(meta, 1 - core, xa, xb, ya, yb):
+        msg[at : at + face.shape[0]] = face
+        at += face.shape[0]
     g = gain[...]
     total = jnp.zeros((1, C), f32)
     for s in range(2):
@@ -189,8 +198,8 @@
     msg[1024:P_ROWS] = pack3(total)
 
 
-def out_body(pos, src, xl, xr, yl, yr, w, base, out, grid, cols, *, field):
-    build(grid, 0, pos, src, *(e.at[field : field + 1] for e in (xl, xr, yl, yr)))
+def out_body(pos, meta, src, xa, xb, ya, yb, w, base, out, grid, cols, *, field):
+    build(grid, 0, pos, src, *faces(meta, field, xa, xb, ya, yb))
     for s in range(2):
         live, bx, by = place(pos, s)
         y = convolve(grid, 0, bx, by, cols, w, field == 1)
@@ -198,24 +207,22 @@
 
 
 def grads_body(
-    pos, ppos, meta, a, b, xl, xr, yl, yr, other, hid, pre, msg, gain_part,
+    pos, ppos, meta, a, b, xa, xb, ya, yb, other, hid, pre, msg, gain_part,
     keep_b, keep_a, out_b, out_a, gsum, grid, cols, pt, acc, *, chunks
 ):
     core, mine = meta[0], meta[1]
 
-    @pl.when(core == 0)
-    def _():
-        build(grid, 0, pos, a, xl, xr, yl, yr)
-
-    @pl.when(core != 0)
-    def _():
-        build(grid, 0, pos, b, *(e.at[1:2] for e in (xl, xr, yl, yr)))
-
-    faces, at = [], P_ROWS
+    for f, src in enumerate((a, b)):
+
+        @pl.when(core == f)
+        def _():
+            build(grid, 0, pos, src, *faces(meta, f, xa, xb, ya, yb))
+
+    theirs, at = [], P_ROWS
     for rows in FACES:
-        faces.append(msg.at[pl.ds(at, rows)].reshape(1, rows, C))
+        theirs.append(msg[at : at + rows])
         at += rows
-    build(grid.at[1:2], 0, ppos, other, *faces)
+    build(grid, 1, ppos, other, *theirs)
     for k in range(4):
         s = k % 2
         _, bx, by = place(pos if k < 2 else ppos, s)
@@ -257,14 +264,16 @@
     out[...] = jnp.concatenate([low[...], tile]).astype(bf16)
 
 
-def join_body(a, b, out):
-    n = a.shape[0]
-    out[0:n] = a[...]
-    out[n:] = b[...]
-
-
-def join(a, b):
-    (out,) = call(join_body, [sds((a.shape[0] + b.shape[0], C), bf16)], [], (a, b), 0)
+def join_body(*refs):
+    out, at = refs[-1], 0
+    for ref in refs[:-1]:
+        out[at : at + ref.shape[0]] = ref[...]
+        at += ref.shape[0]
+
+
+def join(*parts):
+    rows = sum(p.shape[0] for p in parts)
+    (out,) = call(join_body, [sds((rows, C), bf16)], [], parts, 0)
     return out
 
 
@@ -309,37 +318,39 @@
         k_out[1, t] = second[u * C : (u + 1) * C] * shrink
 
 
-def shift(lo, hi, axis):
+def across(a, b, axis):
     n = lax.axis_size(axis)
-    from_left = lax.ppermute(hi, axis, [(i, i + 1) for i in range(n - 1)])
-    from_right = lax.ppermute(lo, axis, [(i + 1, i) for i in range(n - 1)])
-    return from_left, from_right
-
-
-def y_faces(pos, a, b, xl, xr):
+    even, odd = (
+        [p for i in range(first, n - 1, 2) for p in ((i, i + 1), (i + 1, i))] for first in (0, 1)
+    )
+    return lax.ppermute(a, axis, even), lax.ppermute(b, axis, odd)
+
+
+def y_faces(pos, meta, a, b, xa, xb):
     return call(
         pack_y_body,
         [sds((2, 144, C), bf16)] * 2,
         [pltpu.VMEM((18, 8, C), f32)],
-        (pos, a, b, xl, xr),
-        1,
-    )
-
-
-def stages():
+        (pos, meta, a, b, xa, xb),
+        2,
+    )
+
+
+def plan():
     nx, ny = lax.axis_size("gx"), lax.axis_size("gy")
     xs = [(1 << i, 0) for i in range(nx.bit_length() - 1)]
     zs = [(0, 1 << i) for i in range(1, ny.bit_length() - 1)]
-    orders = (xs + zs, xs[1:] + xs[:1] + zs)
-    perms = []
-    for step in zip(*orders):
-        pairs = []
-        for i in range(nx):
-            for j in range(ny):
-                dx, dy = step[j % 2]
-                pairs.append((i * ny + j, (i ^ dx) * ny + (j ^ dy)))
-        perms.append(pairs)
-    return orders, perms
+    k = min(len(zs), 4 - len(xs))
+    orders = (xs + zs[:k], xs[1:] + xs[:1] + zs[:k])
+    group = []
+    for m in range(1, 1 << k):
+        group.append(sum(zs[i][1] for i in range(k) if m >> (k - 1 - i) & 1))
+    return orders, len(xs), group, [z for _, z in zs[k:]]
+
+
+def pairs(dx, dy):
+    nx, ny = lax.axis_size("gx"), lax.axis_size("gy")
+    return [(i * ny + j, (i ^ dx[j % 2]) * ny + (j ^ dy)) for i in range(nx) for j in range(ny)]
 
 
 def chunk_index(order, halvings, ix, iy):
@@ -359,25 +370,24 @@
     ny = lax.axis_size("gy")
     ix, iy = lax.axis_index("gx"), lax.axis_index("gy")
     core = iy % 2
-    orders, perms = stages()
-    halvings = min(len(perms), 4)
-    chunks = 1 << halvings
-    me_a = chunk_index(orders[0], halvings, ix, iy)
-    me_b = chunk_index(orders[1], halvings, ix, iy)
-    meta = jnp.stack([core, jnp.where(core == 0, me_a, me_b), jnp.where(core == 0, me_b, me_a)])
+    orders, halvings, group, copies = plan()
+    chunks = 1 << len(orders[0])
+    me_a = chunk_index(orders[0], len(orders[0]), ix, iy)
+    me_b = chunk_index(orders[1], len(orders[1]), ix, iy)
+    meta = jnp.stack([core, jnp.where(core == 0, me_a, me_b), jnp.where(core == 0, me_b, me_a), ix % 2])
     partner = [(i, i ^ 1) for i in range(ny)]
     n = TAPS * C
     size = n // chunks
 
     hbm = lambda v: pltpu.with_memory_space_constraint(v, pltpu.HBM)
-    features, cotangent, sent, lo, hi = call(
+    features, cotangent, sent, fa, fb = call(
         load_body,
         [sds((2, 512, C), bf16)] * 3 + [sds((2, 128, C), bf16)] * 2,
         [],
-        (brick_pos, core.reshape(1), hbm(features), hbm(cotangent)),
-        2,
-    )
-    xl, xr = shift(lo, hi, "gx")
+        (brick_pos, core.reshape(1), (ix % 2).reshape(1), hbm(features), hbm(cotangent)),
+        3,
+    )
+    xa, xb = across(fa, fb, "gx")
     ppos = lax.ppermute(brick_pos, "gy", partner)
     other = lax.ppermute(sent, "gy", partner)
     straight, turned = sds((9 * C, 3 * C), bf16), sds((3 * C, 9 * C), bf16)
@@ -388,9 +398,9 @@
         (hbm(first_kernel), hbm(second_kernel), hbm(norm_gain.reshape(1, C))),
         0,
     )
-    lo, hi = y_faces(brick_pos, after(features, gain), cotangent, xl, xr)
-    lo = after(lo, ppos, other, meta)
-    edge = xl, xr, *shift(lo, hi, "gy")
+    fa, fb = y_faces(brick_pos, meta, after(features, gain), cotangent, xa, xb)
+    fa = after(fa, ppos, other)
+    edge = xa, xb, *across(fa, fb, "gy")
     grid = pltpu.VMEM((2, 18, 18, 8, C), f32)
     cols = pltpu.VMEM((512, 9 * C), bf16)
     hid, pre, msg, gain_part = call(
@@ -417,46 +427,57 @@
     )
     g = g[0:1]
 
-    lo, hi = call(pack_x_body, [sds((2, 128, C), bf16)] * 2, [], (brick_pos, after(hid, out_a), pre), 1)
-    xl, xr = shift(lo, hi, "gx")
-    lo, hi = y_faces(brick_pos, hid, pre, xl, xr)
-    around = xl, xr, *shift(lo, hi, "gy")
+    fa, fb = call(
+        pack_x_body,
+        [sds((2, 128, C), bf16)] * 2,
+        [],
+        (brick_pos, (ix % 2).reshape(1), after(hid, out_a), pre),
+        2,
+    )
+    xa, xb = across(fa, fb, "gx")
+    fa, fb = y_faces(brick_pos, meta, hid, pre, xa, xb)
+    around = xa, xb, *across(fa, fb, "gy")
     results = []
     for f, (src, w, base) in enumerate(((hid, w2, features), (pre, t1, cotangent))):
         (res,) = call(
             functools.partial(out_body, field=f),
             [sds((2, 512, C), bf16)],
             [pltpu.VMEM((1, 18, 18, 8, C), f32), cols],
-            (brick_pos, src, *around, w, base),
-            1,
+            (brick_pos, meta, src, *around, w, base),
+            2,
             10,
         )
         results.append(res)
 
-    swap = lambda v, s: lax.ppermute(v, both, perms[s])
-    got_a, got_b = swap(out_a, 0), swap(out_b, 0)
+    swap = lambda v, dx, dy=0: lax.ppermute(v, both, pairs(dx, dy))
+    steps = [(a[0], b[0]) for a, b in zip(*orders)][:halvings]
+    got_a, got_b = swap(out_a, steps[0]), swap(out_b, steps[0])
     out = (keep_a + got_a.astype(f32)).astype(bf16)
-    got = swap(out, 1)
+    got = swap(out, steps[1])
     low = keep_b + got_b.astype(f32) + got.astype(f32)
-    for s in range(2, halvings):
+    for step in steps[2:]:
         half = low.shape[0] // 2
-        out = low[half:]
-        if s + 1 < halvings:
-            out = out.astype(bf16)
-        got = swap(out, s)
+        got = swap(low[half:].astype(bf16), step)
         low = low[:half] + got.astype(f32)
-    for s in range(halvings, len(perms)):
-        got = swap(jnp.concatenate([low, jnp.broadcast_to(g, (8, C))]), s)
+    got = []
+    for m, dy in enumerate(group, 1):
+        out = low[m * size : (m + 1) * size]
+        got.append(swap(out if dy == 2 else out.astype(bf16), (0, 0), dy))
+    low = low[:size]
+    for v in got:
+        low = low + v.astype(f32)
+    for dy in copies:
+        got = swap(jnp.concatenate([low, jnp.broadcast_to(g, (8, C))]), (0, 0), dy)
         low, g = low + got[:size], g + got[size : size + 1]
 
     (full,) = call(seal_body, [sds((size + 8, C), bf16)], [], (low, g), 0)
-    for s in reversed(range(2, halvings)):
-        got = swap(full, s)
-        full = join(full, got)
+    full = join(full, *(swap(full, (0, 0), dy) for dy in group))
+    for step in reversed(steps[2:]):
+        full = join(full, swap(full, step))
     own = [full]
-    own.append(swap(full, 1))
-    own.append(swap(full, 0))
-    own.append(swap(own[1], 0))
+    own.append(swap(full, steps[1]))
+    own.append(swap(full, steps[0]))
+    own.append(swap(own[1], steps[0]))
     part = [lax.ppermute(v, "gy", partner) for v in own]
     k_up, g_up = call(
         functools.partial(final_body, chunks=chunks),

time: 110 us -> 97.3 us (0.88)
  the two profiles are of different devices: /device:TPU:11 before, /device:TPU:21 now
where the time goes in v4:
time: 97.3 us; the launch traced here: 97 us
  starting transfers between devices  37.5 us (39%)
  waiting for transfers between devices  34.4 us (35%)
  Pallas kernels  24 us (25%)
    pallas_call x12, Pallas kernels, call(): pl.pallas_call(body, out_shape=outs, in_specs=[SMEM] * n_smem + [VMEM] *...  24 us
    ppermute x12, waiting for transfers between devices, per_device(): swap = lambda v, dx, dy=0: lax.ppermute(v, both, pairs(dx, dy))  21 us
    ppermute x8, starting transfers between devices, across(): return (lax.ppermute(a, axis, even), lax.ppermute(b, axis, odd))  14.9 us
    ppermute x8, waiting for transfers between devices, across(): return (lax.ppermute(a, axis, even), lax.ppermute(b, axis, odd))  12.1 us
    ppermute x4, starting transfers between devices, per_device(): part = [lax.ppermute(v, 'gy', partner) for v in own]  11.9 us
    ppermute x12, starting transfers between devices, per_device(): swap = lambda v, dx, dy=0: lax.ppermute(v, both, pairs(dx, dy))  9.44 us
  transfers between devices with their start and end apart: 27, of which 13 were waited for; matrix products, arithmetic and copies ran while one was open for 0% of the time, Pallas kernels for 11%

profile of v4, /device:TPU:21, one launch (start us, length us, event | category | flops | bytes accessed | tf_op | source)
XLA Modules:
  0.0 97.0 jit_solution(2758364700861335892)
XLA Ops:
  0.7 1.3 %shard_map.93 = (bf16[2,512,128]{2,1,0:T(8,128)(2,1)S(1)}, bf16[2,512,128]{2,1,0:T(8,128)(2,1)S(1)}, bf16[2,512,128]{2,1,0:T(8,128)(2,1)S(1)}, bf16[2,128,128]{2,1,0:T(8,128)(2,1)S(1)}, bf16[2,128,128]{2,1,0:T(8,128)(2,1)S(1)}) custom-call(s32[2]{0:T(128)} %pos.15, s32[1]{0:T(128)} %bitcast.core, s32[1]{0:T(128)} %bitcast.3.odd, bf16[2,512,128]{2,1,0:T(8,128)(2,1)} %a.1, ...), custom_call_target="tpu_custom_call" | custom-call | tf_op jit(solution)/shard_map/pallas_call | solution.py:34
  2.0 0.7 collective-permute-start.3
  2.7 0.1 collective-permute-start.2
  2.8 1.2 %collective-permute-start = (bf16[2,128,128]{2,1,0:T(8,128)(2,1)S(1)}, bf16[2,128,128]{2,1,0:T(8,128)(2,1)S(1)}, u32[]{:S(2)}, u32[]{:S(2)}) collective-permute-start(bf16[2,128,128]{2,1,0:T(8,128)(2,1)S(1)} %get-tuple-element.36), channel_id=1, source_target_pairs={{0,8},{8,0},{16,24},{24,16},{1,9},{9,1},{17,25},{25,17},{2,10},{10... | collective-permute-start | bytes 196616 | tf_op jit(solution)/shard_map/ppermute | solution.py:326
  4.0 2.1 %collective-permute-start.1 = (bf16[2,128,128]{2,1,0:T(8,128)(2,1)S(1)}, bf16[2,128,128]{2,1,0:T(8,128)(2,1)S(1)}, u32[]{:S(2)}, u32[]{:S(2)}) collective-permute-start(bf16[2,128,128]{2,1,0:T(8,128)(2,1)S(1)} %get-tuple-element.37), channel_id=1, source_target_pairs={{8,16},{16,8},{9,17},{17,9},{10,18},{18,10},{11,19},{19,11},{12,20... | collective-permute-start | bytes 196616 | tf_op jit(solution)/shard_map/ppermute | solution.py:326
  6.1 2.0 %shard_map.94 = (bf16[1152,384]{1,0:T(8,128)(2,1)S(1)}, bf16[1152,384]{1,0:T(8,128)(2,1)S(1)}, bf16[384,1152]{1,0:T(8,128)(2,1)S(1)}, bf16[384,1152]{1,0:T(8,128)(2,1)S(1)}, f32[1,128]{1,0:T(1,128)S(1)}) custom-call(bf16[27,128,128]{2,1,0:T(8,128)(2,1)} %k1.1, bf16[27,128,128]{2,1,0:T(8,128)(2,1)} %k2.1, f32[1,128]{1,0:T(1,128)} %bitcast.6), custom_call_target="tpu_custom_call" | custom-call | tf_op jit(solution)/shard_map/pallas_call | solution.py:34
  8.1 0.1 pad_add_fusion.meta
  8.2 1.7 %collective-permute-done.1.xb = bf16[2,128,128]{2,1,0:T(8,128)(2,1)S(1)} collective-permute-done((bf16[2,128,128]{2,1,0:T(8,128)(2,1)S(1)}, bf16[2,128,128]{2,1,0:T(8,128)(2,1)S(1)}, u32[]{:S(2)}, u32[]{:S(2)}) %collective-permute-start.1) | collective-permute-done | bytes 65568 | tf_op jit(solution)/shard_map/ppermute | solution.py:326
  9.9 0.8 shard_map.95
  10.7 4.9 %collective-permute-start.5 = (bf16[2,144,128]{2,1,0:T(8,128)(2,1)S(1)}, bf16[2,144,128]{2,1,0:T(8,128)(2,1)S(1)}, u32[]{:S(2)}, u32[]{:S(2)}) collective-permute-start(bf16[2,144,128]{2,1,0:T(8,128)(2,1)S(1)} %get-tuple-element.43), channel_id=1, source_target_pairs={{1,2},{2,1},{3,4},{4,3},{5,6},{6,5},{9,10},{10,9},{11,12},{12,11},... | collective-permute-start | bytes 221192 | tf_op jit(solution)/shard_map/ppermute | solution.py:326
  15.7 0.1 collective-permute-start.4
  15.8 2.1 %collective-permute-done.5.yb = bf16[2,144,128]{2,1,0:T(8,128)(2,1)S(1)} collective-permute-done((bf16[2,144,128]{2,1,0:T(8,128)(2,1)S(1)}, bf16[2,144,128]{2,1,0:T(8,128)(2,1)S(1)}, u32[]{:S(2)}, u32[]{:S(2)}) %collective-permute-start.5) | collective-permute-done | bytes 73760 | tf_op jit(solution)/shard_map/ppermute | solution.py:326
  17.9 4.6 %shard_map.96 = (bf16[2,512,128]{2,1,0:T(8,128)(2,1)S(1)}, bf16[2,512,128]{2,1,0:T(8,128)(2,1)S(1)}, bf16[1584,128]{1,0:T(8,128)(2,1)S(1)}, f32[8,128]{1,0:T(8,128)S(1)}) custom-call(s32[2]{0:T(128)} %pos.15, s32[4]{0:T(128)S(1)} %pad_add_fusion.meta, bf16[2,512,128]{2,1,0:T(8,128)(2,1)S(1)} %get-tuple-element.39.a.base, ...), custom_call_target="tpu_custom_call" | custom-call | tf_op jit(solution)/shard_map/pallas_call | solution.py:34
  22.4 0.4 collective-permute-start.6
  22.9 1.4 %collective-permute-done.6.msg = bf16[1584,128]{1,0:T(8,128)(2,1)S(1)} collective-permute-done((bf16[1584,128]{1,0:T(8,128)(2,1)S(1)}, bf16[1584,128]{1,0:T(8,128)(2,1)S(1)}, u32[]{:S(2)}, u32[]{:S(2)}) %collective-permute-start.6) | collective-permute-done | bytes 405536 | tf_op jit(solution)/shard_map/ppermute | solution.py:414
  24.2 3.7 %shard_map.97 = (f32[864,128]{1,0:T(8,128)S(1)}, f32[864,128]{1,0:T(8,128)S(1)}, bf16[864,128]{1,0:T(8,128)(2,1)S(1)}, bf16[864,128]{1,0:T(8,128)(2,1)S(1)}, f32[8,128]{1,0:T(8,128)S(1)}) custom-call(s32[2]{0:T(128)} %pos.15, s32[2]{0:T(128)S(1)} %collective-permute-done.2.ppos, s32[4]{0:T(128)S(1)} %pad_add_fusion.meta, ...), custom_call_target="tpu_custom_call" | custom-call | tf_op jit(solution)/shard_map/pallas_call | solution.py:34
  27.9 0.1 collective-permute-start.12
  28.0 1.5 %collective-permute-start.11 = (bf16[864,128]{1,0:T(8,128)(2,1)S(1)}, bf16[864,128]{1,0:T(8,128)(2,1)S(1)}, u32[]{:S(2)}, u32[]{:S(2)}) collective-permute-start(bf16[864,128]{1,0:T(8,128)(2,1)S(1)} %get-tuple-element.59), channel_id=1, source_target_pairs={{0,8},{1,17},{2,10},{3,19},{4,12},{5,21},{6,14},{7,23},{8,0},{9,25... | collective-permute-start | bytes 663560 | tf_op jit(solution)/shard_map/ppermute | solution.py:452
  29.4 3.6 %collective-permute-done.12 = bf16[864,128]{1,0:T(8,128)(2,1)S(1)} collective-permute-done((bf16[864,128]{1,0:T(8,128)(2,1)S(1)}, bf16[864,128]{1,0:T(8,128)(2,1)S(1)}, u32[]{:S(2)}, u32[]{:S(2)}) %collective-permute-start.12) | collective-permute-done | bytes 221216 | tf_op jit(solution)/shard_map/ppermute | solution.py:452
  33.1 0.1 collective-permute-start.13
  33.2 2.2 %collective-permute-done.11 = bf16[864,128]{1,0:T(8,128)(2,1)S(1)} collective-permute-done((bf16[864,128]{1,0:T(8,128)(2,1)S(1)}, bf16[864,128]{1,0:T(8,128)(2,1)S(1)}, u32[]{:S(2)}, u32[]{:S(2)}) %collective-permute-start.11) | collective-permute-done | bytes 221216 | tf_op jit(solution)/shard_map/ppermute | solution.py:452
  35.4 3.2 %collective-permute-done.13 = bf16[864,128]{1,0:T(8,128)(2,1)S(1)} collective-permute-done((bf16[864,128]{1,0:T(8,128)(2,1)S(1)}, bf16[864,128]{1,0:T(8,128)(2,1)S(1)}, u32[]{:S(2)}, u32[]{:S(2)}) %collective-permute-start.13) | collective-permute-done | bytes 221216 | tf_op jit(solution)/shard_map/ppermute | solution.py:452
  38.6 0.1 fusion.2
  38.7 1.3 %collective-permute-start.15 = (f32[216,128]{1,0:T(8,128)S(1)}, f32[216,128]{1,0:T(8,128)S(1)}, u32[]{:S(2)}, u32[]{:S(2)}) collective-permute-start(f32[216,128]{1,0:T(8,128)S(1)} %slice.24), channel_id=1, source_target_pairs={{0,2},{1,3},{2,0},{3,1},{4,6},{5,7},{6,4},{7,5},{8,10},{9,11},{10,... | collective-permute-start | bytes 331784 | tf_op jit(solution)/shard_map/ppermute | solution.py:452
  40.1 0.2 collective-permute-start.14
  40.3 1.2 %collective-permute-start.16 = (bf16[216,128]{1,0:T(8,128)(2,1)S(1)}, bf16[216,128]{1,0:T(8,128)(2,1)S(1)}, u32[]{:S(2)}, u32[]{:S(2)}) collective-permute-start(bf16[216,128]{1,0:T(8,128)(2,1)S(1)} %get-tuple-element.67), channel_id=1, source_target_pairs={{0,6},{1,7},{2,4},{3,5},{4,2},{5,3},{6,0},{7,1},{8,14},{9,15},{10,... | collective-permute-start | bytes 165896 | tf_op jit(solution)/shard_map/ppermute | solution.py:452
  41.5 3.1 %collective-permute-done.14 = bf16[216,128]{1,0:T(8,128)(2,1)S(1)} collective-permute-done((bf16[216,128]{1,0:T(8,128)(2,1)S(1)}, bf16[216,128]{1,0:T(8,128)(2,1)S(1)}, u32[]{:S(2)}, u32[]{:S(2)}) %collective-permute-start.14) | collective-permute-done | bytes 55328 | tf_op jit(solution)/shard_map/ppermute | solution.py:452
  44.7 0.5 collective-permute-start.19
  45.2 4.0 %collective-permute-start.18 = (bf16[224,128]{1,0:T(8,128)(2,1)S(1)}, bf16[224,128]{1,0:T(8,128)(2,1)S(1)}, u32[]{:S(2)}, u32[]{:S(2)}) collective-permute-start(bf16[224,128]{1,0:T(8,128)(2,1)S(1)} %shard_map.102.refs_0_), channel_id=1, source_target_pairs={{0,2},{1,3},{2,0},{3,1},{4,6},{5,7},{6,4},{7,5},{8,10},{9,11},{10,... | collective-permute-start | bytes 172040 | tf_op jit(solution)/shard_map/ppermute | solution.py:452
  49.2 2.2 %collective-permute-done.18.refs_2_ = bf16[224,128]{1,0:T(8,128)(2,1)S(1)} collective-permute-done((bf16[224,128]{1,0:T(8,128)(2,1)S(1)}, bf16[224,128]{1,0:T(8,128)(2,1)S(1)}, u32[]{:S(2)}, u32[]{:S(2)}) %collective-permute-start.18) | collective-permute-done | bytes 57376 | tf_op jit(solution)/shard_map/ppermute | solution.py:452
  51.3 2.3 %collective-permute-done.17.refs_1_ = bf16[224,128]{1,0:T(8,128)(2,1)S(1)} collective-permute-done((bf16[224,128]{1,0:T(8,128)(2,1)S(1)}, bf16[224,128]{1,0:T(8,128)(2,1)S(1)}, u32[]{:S(2)}, u32[]{:S(2)}) %collective-permute-start.17) | collective-permute-done | bytes 57376 | tf_op jit(solution)/shard_map/ppermute | solution.py:452
  53.7 0.5 collective-permute-start.21
  54.2 4.3 %collective-permute-done.20.o1 = bf16[896,128]{1,0:T(8,128)(2,1)S(1)} collective-permute-done((bf16[896,128]{1,0:T(8,128)(2,1)S(1)}, bf16[896,128]{1,0:T(8,128)(2,1)S(1)}, u32[]{:S(2)}, u32[]{:S(2)}) %collective-permute-start.20) | collective-permute-done | bytes 229408 | tf_op jit(solution)/shard_map/ppermute | solution.py:452
  58.6 0.8 shard_map.98
  59.4 0.6 collective-permute-start.7
  60.0 8.8 %collective-permute-start.23 = (bf16[896,128]{1,0:T(8,128)(2,1)S(1)}, bf16[896,128]{1,0:T(8,128)(2,1)S(1)}, u32[]{:S(2)}, u32[]{:S(2)}) collective-permute-start(bf16[896,128]{1,0:T(8,128)(2,1)S(1)} %shard_map.103.o0), channel_id=1, source_target_pairs={{0,1},{1,0},{2,3},{3,2},{4,5},{5,4},{6,7},{7,6},{8,9},{9,8},{10,11... | collective-permute-start | bytes 688136 | tf_op jit(solution)/shard_map/ppermute | solution.py:481
  68.8 0.5 collective-permute-start.25
  69.3 2.6 %collective-permute-start.26 = (bf16[896,128]{1,0:T(8,128)(2,1)S(1)}, bf16[896,128]{1,0:T(8,128)(2,1)S(1)}, u32[]{:S(2)}, u32[]{:S(2)}) collective-permute-start(bf16[896,128]{1,0:T(8,128)(2,1)S(1)} %collective-permute-done.22.o3), channel_id=1, source_target_pairs={{0,1},{1,0},{2,3},{3,2},{4,5},{5,4},{6,7},{7,6},{8,9},{9,8},{10,11... | collective-permute-start | bytes 688136 | tf_op jit(solution)/shard_map/ppermute | solution.py:481
  71.9 2.1 %collective-permute-start.8 = (bf16[2,128,128]{2,1,0:T(8,128)(2,1)S(1)}, bf16[2,128,128]{2,1,0:T(8,128)(2,1)S(1)}, u32[]{:S(2)}, u32[]{:S(2)}) collective-permute-start(bf16[2,128,128]{2,1,0:T(8,128)(2,1)S(1)} %get-tuple-element.53), channel_id=1, source_target_pairs={{8,16},{16,8},{9,17},{17,9},{10,18},{18,10},{11,19},{19,11},{12,20... | collective-permute-start | bytes 196616 | tf_op jit(solution)/shard_map/ppermute | solution.py:326
  73.9 3.8 %collective-permute-done.8.xb = bf16[2,128,128]{2,1,0:T(8,128)(2,1)S(1)} collective-permute-done((bf16[2,128,128]{2,1,0:T(8,128)(2,1)S(1)}, bf16[2,128,128]{2,1,0:T(8,128)(2,1)S(1)}, u32[]{:S(2)}, u32[]{:S(2)}) %collective-permute-start.8) | collective-permute-done | bytes 65568 | tf_op jit(solution)/shard_map/ppermute | solution.py:326
  77.8 0.8 shard_map.99
  78.6 1.9 %collective-permute-start.9 = (bf16[2,144,128]{2,1,0:T(8,128)(2,1)S(1)}, bf16[2,144,128]{2,1,0:T(8,128)(2,1)S(1)}, u32[]{:S(2)}, u32[]{:S(2)}) collective-permute-start(bf16[2,144,128]{2,1,0:T(8,128)(2,1)S(1)} %get-tuple-element.54), channel_id=1, source_target_pairs={{0,1},{1,0},{2,3},{3,2},{4,5},{5,4},{6,7},{7,6},{8,9},{9,8},{10,11... | collective-permute-start | bytes 221192 | tf_op jit(solution)/shard_map/ppermute | solution.py:326
  80.5 0.9 collective-permute-done.9.ya
  81.4 2.1 %collective-permute-start.10 = (bf16[2,144,128]{2,1,0:T(8,128)(2,1)S(1)}, bf16[2,144,128]{2,1,0:T(8,128)(2,1)S(1)}, u32[]{:S(2)}, u32[]{:S(2)}) collective-permute-start(bf16[2,144,128]{2,1,0:T(8,128)(2,1)S(1)} %get-tuple-element.55), channel_id=1, source_target_pairs={{1,2},{2,1},{3,4},{4,3},{5,6},{6,5},{9,10},{10,9},{11,12},{12,11},... | collective-permute-start | bytes 221192 | tf_op jit(solution)/shard_map/ppermute | solution.py:326
  83.5 3.6 %collective-permute-done.10.yb = bf16[2,144,128]{2,1,0:T(8,128)(2,1)S(1)} collective-permute-done((bf16[2,144,128]{2,1,0:T(8,128)(2,1)S(1)}, bf16[2,144,128]{2,1,0:T(8,128)(2,1)S(1)}, u32[]{:S(2)}, u32[]{:S(2)}) %collective-permute-start.10) | collective-permute-done | bytes 73760 | tf_op jit(solution)/shard_map/ppermute | solution.py:326
  87.1 3.2 %shard_map.101 = bf16[2,512,128]{2,1,0:T(8,128)(2,1)} custom-call(s32[2]{0:T(128)} %pos.15, s32[4]{0:T(128)S(1)} %pad_add_fusion.meta, bf16[2,512,128]{2,1,0:T(8,128)(2,1)S(1)} %get-tuple-element.47.pre.b.src, bf16[2,128,128]{2,1,0:T(8,128)(2,1)S(1)} %collective-permute-done.7.xa, bf16[2,128,128]{2,1,0:T(8,128)(2,1)S(1)} %collective-permute-done.8.xb, ...), custom_call_target="tpu_custom_call" | custom-call | tf_op jit(solution)/shard_map/pallas_call | solution.py:34
  90.3 3.3 %shard_map.100 = bf16[2,512,128]{2,1,0:T(8,128)(2,1)} custom-call(s32[2]{0:T(128)} %pos.15, s32[4]{0:T(128)S(1)} %pad_add_fusion.meta, bf16[2,512,128]{2,1,0:T(8,128)(2,1)S(1)} %get-tuple-element.51.hid.a.src, bf16[2,128,128]{2,1,0:T(8,128)(2,1)S(1)} %collective-permute-done.7.xa, bf16[2,128,128]{2,1,0:T(8,128)(2,1)S(1)} %collective-permute-done.8.xb, ...), custom_call_target="tpu_custom_call" | custom-call | tf_op jit(solution)/shard_map/pallas_call | solution.py:34
  93.6 3.4 %shard_map.104 = (f32[2,27,128,128]{3,2,1,0:T(8,128)}, f32[1,128]{1,0:T(1,128)}) custom-call(s32[4]{0:T(128)S(1)} %pad_add_fusion.meta, bf16[896,128]{1,0:T(8,128)(2,1)S(1)} %shard_map.103.o0, bf16[896,128]{1,0:T(8,128)(2,1)S(1)} %collective-permute-done.20.o1, bf16[896,128]{1,0:T(8,128)(2,1)S(1)} %collective-permute-done.21.o2, ...), custom_call_target="tpu_custom_call" | custom-call | tf_op jit(solution)/shard_map/pallas_call | solution.py:34
  (25 shorter events, 0.3 us)
Async XLA Ops:
  2.0 13.7 %collective-permute-start.3 = (bf16[2,512,128]{2,1,0:T(8,128)(2,1)S(1)}, bf16[2,512,128]{2,1,0:T(8,128)(2,1)S(1)}, u32[]{:S(2)}, u32[]{:S(2)}) collective-permute-start(bf16[2,512,128]{2,1,0:T(8,128)(2,1)S(1)} %get-tuple-element.41), channel_id=1, source_target_pairs={{0,1},{1,0},{2,3},{3,2},{4,5},{5,4},{6,7},{7,6},{8,9},{9,8},{10,11... | collective-permute-start | bytes 786440 | tf_op jit(solution)/shard_map/ppermute | solution.py:392
  2.7 13.0 %collective-permute-start.2 = (s32[2]{0:T(128)}, s32[2]{0:T(128)S(1)}, u32[]{:S(2)}, u32[]{:S(2)}) collective-permute-start(s32[2]{0:T(128)} %pos.15), channel_id=1, source_target_pairs={{0,1},{1,0},{2,3},{3,2},{4,5},{5,4},{6,7},{7,6},{8,9},{9,8},{10,11... | collective-permute-start | bytes 32 | tf_op jit(solution)/shard_map/ppermute | solution.py:391
  2.8 5.4 %collective-permute-start = (bf16[2,128,128]{2,1,0:T(8,128)(2,1)S(1)}, bf16[2,128,128]{2,1,0:T(8,128)(2,1)S(1)}, u32[]{:S(2)}, u32[]{:S(2)}) collective-permute-start(bf16[2,128,128]{2,1,0:T(8,128)(2,1)S(1)} %get-tuple-element.36), channel_id=1, source_target_pairs={{0,8},{8,0},{16,24},{24,16},{1,9},{9,1},{17,25},{25,17},{2,10},{10... | collective-permute-start | bytes 196616 | tf_op jit(solution)/shard_map/ppermute | solution.py:326
  4.0 5.9 %collective-permute-start.1 = (bf16[2,128,128]{2,1,0:T(8,128)(2,1)S(1)}, bf16[2,128,128]{2,1,0:T(8,128)(2,1)S(1)}, u32[]{:S(2)}, u32[]{:S(2)}) collective-permute-start(bf16[2,128,128]{2,1,0:T(8,128)(2,1)S(1)} %get-tuple-element.37), channel_id=1, source_target_pairs={{8,16},{16,8},{9,17},{17,9},{10,18},{18,10},{11,19},{19,11},{12,20... | collective-permute-start | bytes 196616 | tf_op jit(solution)/shard_map/ppermute | solution.py:326
  10.7 7.1 %collective-permute-start.5 = (bf16[2,144,128]{2,1,0:T(8,128)(2,1)S(1)}, bf16[2,144,128]{2,1,0:T(8,128)(2,1)S(1)}, u32[]{:S(2)}, u32[]{:S(2)}) collective-permute-start(bf16[2,144,128]{2,1,0:T(8,128)(2,1)S(1)} %get-tuple-element.43), channel_id=1, source_target_pairs={{1,2},{2,1},{3,4},{4,3},{5,6},{6,5},{9,10},{10,9},{11,12},{12,11},... | collective-permute-start | bytes 221192 | tf_op jit(solution)/shard_map/ppermute | solution.py:326
  15.7 2.2 %collective-permute-start.4 = (bf16[2,144,128]{2,1,0:T(8,128)(2,1)S(1)}, bf16[2,144,128]{2,1,0:T(8,128)(2,1)S(1)}, u32[]{:S(2)}, u32[]{:S(2)}) collective-permute-start(bf16[2,144,128]{2,1,0:T(8,128)(2,1)S(1)} %get-tuple-element.42), channel_id=1, source_target_pairs={{0,1},{1,0},{2,3},{3,2},{4,5},{5,4},{6,7},{7,6},{8,9},{9,8},{10,11... | collective-permute-start | bytes 221192 | tf_op jit(solution)/shard_map/ppermute | solution.py:326
  22.4 1.8 %collective-permute-start.6 = (bf16[1584,128]{1,0:T(8,128)(2,1)S(1)}, bf16[1584,128]{1,0:T(8,128)(2,1)S(1)}, u32[]{:S(2)}, u32[]{:S(2)}) collective-permute-start(bf16[1584,128]{1,0:T(8,128)(2,1)S(1)} %get-tuple-element.48), channel_id=1, source_target_pairs={{0,1},{1,0},{2,3},{3,2},{4,5},{5,4},{6,7},{7,6},{8,9},{9,8},{10,11... | collective-permute-start | bytes 1216520 | tf_op jit(solution)/shard_map/ppermute | solution.py:414
  27.9 5.1 %collective-permute-start.12 = (bf16[864,128]{1,0:T(8,128)(2,1)S(1)}, bf16[864,128]{1,0:T(8,128)(2,1)S(1)}, u32[]{:S(2)}, u32[]{:S(2)}) collective-permute-start(bf16[864,128]{1,0:T(8,128)(2,1)S(1)} %get-tuple-element.50), channel_id=1, source_target_pairs={{0,8},{1,17},{2,10},{3,19},{4,12},{5,21},{6,14},{7,23},{8,0},{9,25... | collective-permute-start | bytes 663560 | tf_op jit(solution)/shard_map/ppermute | solution.py:452
  28.0 7.4 %collective-permute-start.11 = (bf16[864,128]{1,0:T(8,128)(2,1)S(1)}, bf16[864,128]{1,0:T(8,128)(2,1)S(1)}, u32[]{:S(2)}, u32[]{:S(2)}) collective-permute-start(bf16[864,128]{1,0:T(8,128)(2,1)S(1)} %get-tuple-element.59), channel_id=1, source_target_pairs={{0,8},{1,17},{2,10},{3,19},{4,12},{5,21},{6,14},{7,23},{8,0},{9,25... | collective-permute-start | bytes 663560 | tf_op jit(solution)/shard_map/ppermute | solution.py:452
  33.1 5.5 %collective-permute-start.13 = (bf16[864,128]{1,0:T(8,128)(2,1)S(1)}, bf16[864,128]{1,0:T(8,128)(2,1)S(1)}, u32[]{:S(2)}, u32[]{:S(2)}) collective-permute-start(bf16[864,128]{1,0:T(8,128)(2,1)S(1)} %add_convert_fusion), channel_id=1, source_target_pairs={{0,16},{1,9},{2,18},{3,11},{4,20},{5,13},{6,22},{7,15},{8,24},{9,1... | collective-permute-start | bytes 663560 | tf_op jit(solution)/shard_map/ppermute | solution.py:452
  38.7 5.9 %collective-permute-start.15 = (f32[216,128]{1,0:T(8,128)S(1)}, f32[216,128]{1,0:T(8,128)S(1)}, u32[]{:S(2)}, u32[]{:S(2)}) collective-permute-start(f32[216,128]{1,0:T(8,128)S(1)} %slice.24), channel_id=1, source_target_pairs={{0,2},{1,3},{2,0},{3,1},{4,6},{5,7},{6,4},{7,5},{8,10},{9,11},{10,... | collective-permute-start | bytes 331784 | tf_op jit(solution)/shard_map/ppermute | solution.py:452
  40.1 4.6 %collective-permute-start.14 = (bf16[216,128]{1,0:T(8,128)(2,1)S(1)}, bf16[216,128]{1,0:T(8,128)(2,1)S(1)}, u32[]{:S(2)}, u32[]{:S(2)}) collective-permute-start(bf16[216,128]{1,0:T(8,128)(2,1)S(1)} %get-tuple-element.66), channel_id=1, source_target_pairs={{0,4},{1,5},{2,6},{3,7},{4,0},{5,1},{6,2},{7,3},{8,12},{9,13},{10,... | collective-permute-start | bytes 165896 | tf_op jit(solution)/shard_map/ppermute | solution.py:452
  40.3 4.4 %collective-permute-start.16 = (bf16[216,128]{1,0:T(8,128)(2,1)S(1)}, bf16[216,128]{1,0:T(8,128)(2,1)S(1)}, u32[]{:S(2)}, u32[]{:S(2)}) collective-permute-start(bf16[216,128]{1,0:T(8,128)(2,1)S(1)} %get-tuple-element.67), channel_id=1, source_target_pairs={{0,6},{1,7},{2,4},{3,5},{4,2},{5,3},{6,0},{7,1},{8,14},{9,15},{10,... | collective-permute-start | bytes 165896 | tf_op jit(solution)/shard_map/ppermute | solution.py:452
  44.7 4.5 %collective-permute-start.19 = (bf16[224,128]{1,0:T(8,128)(2,1)S(1)}, bf16[224,128]{1,0:T(8,128)(2,1)S(1)}, u32[]{:S(2)}, u32[]{:S(2)}) collective-permute-start(bf16[224,128]{1,0:T(8,128)(2,1)S(1)} %shard_map.102.refs_0_), channel_id=1, source_target_pairs={{0,6},{1,7},{2,4},{3,5},{4,2},{5,3},{6,0},{7,1},{8,14},{9,15},{10,... | collective-permute-start | bytes 172040 | tf_op jit(solution)/shard_map/ppermute | solution.py:452
  45.2 6.2 %collective-permute-start.18 = (bf16[224,128]{1,0:T(8,128)(2,1)S(1)}, bf16[224,128]{1,0:T(8,128)(2,1)S(1)}, u32[]{:S(2)}, u32[]{:S(2)}) collective-permute-start(bf16[224,128]{1,0:T(8,128)(2,1)S(1)} %shard_map.102.refs_0_), channel_id=1, source_target_pairs={{0,2},{1,3},{2,0},{3,1},{4,6},{5,7},{6,4},{7,5},{8,10},{9,11},{10,... | collective-permute-start | bytes 172040 | tf_op jit(solution)/shard_map/ppermute | solution.py:452
  49.1 4.5 %collective-permute-start.17 = (bf16[224,128]{1,0:T(8,128)(2,1)S(1)}, bf16[224,128]{1,0:T(8,128)(2,1)S(1)}, u32[]{:S(2)}, u32[]{:S(2)}) collective-permute-start(bf16[224,128]{1,0:T(8,128)(2,1)S(1)} %shard_map.102.refs_0_), channel_id=1, source_target_pairs={{0,4},{1,5},{2,6},{3,7},{4,0},{5,1},{6,2},{7,3},{8,12},{9,13},{10,... | collective-permute-start | bytes 172040 | tf_op jit(solution)/shard_map/ppermute | solution.py:452
  53.6 4.9 %collective-permute-start.20 = (bf16[896,128]{1,0:T(8,128)(2,1)S(1)}, bf16[896,128]{1,0:T(8,128)(2,1)S(1)}, u32[]{:S(2)}, u32[]{:S(2)}) collective-permute-start(bf16[896,128]{1,0:T(8,128)(2,1)S(1)} %shard_map.103.o0), channel_id=1, source_target_pairs={{0,16},{1,9},{2,18},{3,11},{4,20},{5,13},{6,22},{7,15},{8,24},{9,1... | collective-permute-start | bytes 688136 | tf_op jit(solution)/shard_map/ppermute | solution.py:452
  53.7 15.0 %collective-permute-start.21 = (bf16[896,128]{1,0:T(8,128)(2,1)S(1)}, bf16[896,128]{1,0:T(8,128)(2,1)S(1)}, u32[]{:S(2)}, u32[]{:S(2)}) collective-permute-start(bf16[896,128]{1,0:T(8,128)(2,1)S(1)} %shard_map.103.o0), channel_id=1, source_target_pairs={{0,8},{1,17},{2,10},{3,19},{4,12},{5,21},{6,14},{7,23},{8,0},{9,25... | collective-permute-start | bytes 688136 | tf_op jit(solution)/shard_map/ppermute | solution.py:452
  58.6 10.7 %collective-permute-start.22 = (bf16[896,128]{1,0:T(8,128)(2,1)S(1)}, bf16[896,128]{1,0:T(8,128)(2,1)S(1)}, u32[]{:S(2)}, u32[]{:S(2)}) collective-permute-start(bf16[896,128]{1,0:T(8,128)(2,1)S(1)} %collective-permute-done.20.o1), channel_id=1, source_target_pairs={{0,8},{1,17},{2,10},{3,19},{4,12},{5,21},{6,14},{7,23},{8,0},{9,25... | collective-permute-start | bytes 688136 | tf_op jit(solution)/shard_map/ppermute | solution.py:452
  59.4 12.5 %collective-permute-start.7 = (bf16[2,128,128]{2,1,0:T(8,128)(2,1)S(1)}, bf16[2,128,128]{2,1,0:T(8,128)(2,1)S(1)}, u32[]{:S(2)}, u32[]{:S(2)}) collective-permute-start(bf16[2,128,128]{2,1,0:T(8,128)(2,1)S(1)} %get-tuple-element.52), channel_id=1, source_target_pairs={{0,8},{8,0},{16,24},{24,16},{1,9},{9,1},{17,25},{25,17},{2,10},{10... | collective-permute-start | bytes 196616 | tf_op jit(solution)/shard_map/ppermute | solution.py:326
  60.0 33.6 %collective-permute-start.23 = (bf16[896,128]{1,0:T(8,128)(2,1)S(1)}, bf16[896,128]{1,0:T(8,128)(2,1)S(1)}, u32[]{:S(2)}, u32[]{:S(2)}) collective-permute-start(bf16[896,128]{1,0:T(8,128)(2,1)S(1)} %shard_map.103.o0), channel_id=1, source_target_pairs={{0,1},{1,0},{2,3},{3,2},{4,5},{5,4},{6,7},{7,6},{8,9},{9,8},{10,11... | collective-permute-start | bytes 688136 | tf_op jit(solution)/shard_map/ppermute | solution.py:481
  68.7 24.9 %collective-permute-start.24 = (bf16[896,128]{1,0:T(8,128)(2,1)S(1)}, bf16[896,128]{1,0:T(8,128)(2,1)S(1)}, u32[]{:S(2)}, u32[]{:S(2)}) collective-permute-start(bf16[896,128]{1,0:T(8,128)(2,1)S(1)} %collective-permute-done.20.o1), channel_id=1, source_target_pairs={{0,1},{1,0},{2,3},{3,2},{4,5},{5,4},{6,7},{7,6},{8,9},{9,8},{10,11... | collective-permute-start | bytes 688136 | tf_op jit(solution)/shard_map/ppermute | solution.py:481
  68.8 24.8 %collective-permute-start.25 = (bf16[896,128]{1,0:T(8,128)(2,1)S(1)}, bf16[896,128]{1,0:T(8,128)(2,1)S(1)}, u32[]{:S(2)}, u32[]{:S(2)}) collective-permute-start(bf16[896,128]{1,0:T(8,128)(2,1)S(1)} %collective-permute-done.21.o2), channel_id=1, source_target_pairs={{0,1},{1,0},{2,3},{3,2},{4,5},{5,4},{6,7},{7,6},{8,9},{9,8},{10,11... | collective-permute-start | bytes 688136 | tf_op jit(solution)/shard_map/ppermute | solution.py:481
  69.3 24.3 %collective-permute-start.26 = (bf16[896,128]{1,0:T(8,128)(2,1)S(1)}, bf16[896,128]{1,0:T(8,128)(2,1)S(1)}, u32[]{:S(2)}, u32[]{:S(2)}) collective-permute-start(bf16[896,128]{1,0:T(8,128)(2,1)S(1)} %collective-permute-done.22.o3), channel_id=1, source_target_pairs={{0,1},{1,0},{2,3},{3,2},{4,5},{5,4},{6,7},{7,6},{8,9},{9,8},{10,11... | collective-permute-start | bytes 688136 | tf_op jit(solution)/shard_map/ppermute | solution.py:481
  71.9 5.9 %collective-permute-start.8 = (bf16[2,128,128]{2,1,0:T(8,128)(2,1)S(1)}, bf16[2,128,128]{2,1,0:T(8,128)(2,1)S(1)}, u32[]{:S(2)}, u32[]{:S(2)}) collective-permute-start(bf16[2,128,128]{2,1,0:T(8,128)(2,1)S(1)} %get-tuple-element.53), channel_id=1, source_target_pairs={{8,16},{16,8},{9,17},{17,9},{10,18},{18,10},{11,19},{19,11},{12,20... | collective-permute-start | bytes 196616 | tf_op jit(solution)/shard_map/ppermute | solution.py:326
  78.6 2.8 %collective-permute-start.9 = (bf16[2,144,128]{2,1,0:T(8,128)(2,1)S(1)}, bf16[2,144,128]{2,1,0:T(8,128)(2,1)S(1)}, u32[]{:S(2)}, u32[]{:S(2)}) collective-permute-start(bf16[2,144,128]{2,1,0:T(8,128)(2,1)S(1)} %get-tuple-element.54), channel_id=1, source_target_pairs={{0,1},{1,0},{2,3},{3,2},{4,5},{5,4},{6,7},{7,6},{8,9},{9,8},{10,11... | collective-permute-start | bytes 221192 | tf_op jit(solution)/shard_map/ppermute | solution.py:326
  81.4 5.7 %collective-permute-start.10 = (bf16[2,144,128]{2,1,0:T(8,128)(2,1)S(1)}, bf16[2,144,128]{2,1,0:T(8,128)(2,1)S(1)}, u32[]{:S(2)}, u32[]{:S(2)}) collective-permute-start(bf16[2,144,128]{2,1,0:T(8,128)(2,1)S(1)} %get-tuple-element.55), channel_id=1, source_target_pairs={{1,2},{2,1},{3,4},{4,3},{5,6},{6,5},{9,10},{10,9},{11,12},{12,11},... | collective-permute-start | bytes 221192 | tf_op jit(solution)/shard_map/ppermute | solution.py:326

commit v5 on v4

--- a/solution.py
+++ b/solution.py
@@ -94,20 +94,19 @@
 
 
 def build(grid, f, pos, src, xl, xr, yl, yr):
-    grid[f] = jnp.zeros(grid.shape[1:], f32)
+    grid = grid.at[f] if isinstance(f, int) else grid
+    grid[...] = jnp.zeros(grid.shape, f32)
     for s in range(2):
         live, bx, by = place(pos, s)
 
         @pl.when(live)
         def _():
-            grid[f, pl.ds(1 + bx * 8, 8), pl.ds(1 + by * 8, 8)] = (
-                src[s].astype(f32).reshape(8, 8, 8, C)
-            )
-
-    grid[f, 0, 1:17] = xl.astype(f32).reshape(16, 8, C)
-    grid[f, 17, 1:17] = xr.astype(f32).reshape(16, 8, C)
-    grid[f, :, 0] = yl.astype(f32).reshape(18, 8, C)
-    grid[f, :, 17] = yr.astype(f32).reshape(18, 8, C)
+            grid[pl.ds(1 + bx * 8, 8), pl.ds(1 + by * 8, 8)] = src[s].astype(f32).reshape(8, 8, 8, C)
+
+    grid[0, 1:17] = xl.astype(f32).reshape(16, 8, C)
+    grid[17, 1:17] = xr.astype(f32).reshape(16, 8, C)
+    grid[:, 0] = yl.astype(f32).reshape(18, 8, C)
+    grid[:, 17] = yr.astype(f32).reshape(18, 8, C)
 
 
 def faces(meta, f, xa, xb, ya, yb):
@@ -206,49 +205,79 @@
         out[s] = jnp.where(live, base[s].astype(f32) + y, 0.0).astype(bf16)
 
 
-def grads_body(
-    pos, ppos, meta, a, b, xa, xb, ya, yb, other, hid, pre, msg, gain_part,
-    keep_b, keep_a, out_b, out_a, gsum, grid, cols, pt, acc, *, chunks
-):
-    core, mine = meta[0], meta[1]
-
+JS = 5
+
+
+def shifted(pt, slot, v):
+    v = v.astype(f32).reshape(64, 8, C)
+    for i, t in enumerate((up_z(v), v, down_z(v))):
+        pt[i * C : (i + 1) * C, slot * 512 : (slot + 1) * 512] = t.reshape(512, C).T.astype(bf16)
+
+
+def product(grid, pos, pt, upper, cols):
+    for s in range(2):
+        _, bx, by = place(pos, s)
+        for i in range(JS):
+            sx = jnp.where(upper, (i + 9 - JS) // 3, i // 3)
+            sy = jnp.where(upper, (i + 9 - JS) % 3, i % 3)
+            w = grid[pl.ds(bx * 8 + sx, 8), pl.ds(by * 8 + sy, 8)]
+            cols[s * 512 : (s + 1) * 512, i * C : (i + 1) * C] = w.reshape(512, C).astype(bf16)
+    return jnp.dot(pt[...], cols[...], preferred_element_type=f32)
+
+
+def pieces(y, acc, dsts, mine, upper, first, chunks):
+    for i in range(JS):
+        acc[i * 3 * C : (i + 1) * 3 * C] = y[:, i * C : (i + 1) * C]
+    size = TAPS * C // chunks
+    skip = jnp.where(upper, (9 - JS) * 3 * C, 0)
+    p = first
+    for dst in dsts:
+        for q in range(0, dst.shape[0] // size, 2):
+            starts = [pl.multiple_of((mine ^ (p + i)) * size - skip, 8) for i in range(2)]
+            two = jnp.concatenate([acc[pl.ds(a, size)] for a in starts])
+            dst[q * size : (q + 2) * size] = two.astype(dst.dtype)
+            p += 2
+
+
+def sends_upper(mine, chunks):
+    return mine < chunks // 2
+
+
+def own_body(pos, meta, a, b, xa, xb, ya, yb, hid, pre, grid, pt, part, cols, *, chunks):
+    core = meta[0]
     for f, src in enumerate((a, b)):
 
         @pl.when(core == f)
         def _():
-            build(grid, 0, pos, src, *faces(meta, f, xa, xb, ya, yb))
-
+            build(grid, None, pos, src, *faces(meta, f, xa, xb, ya, yb))
+
+    for s in range(2):
+        shifted(pt, s, jnp.where(core == 0, pre[s], hid[s]))
+    part[...] = product(grid, pos, pt, sends_upper(meta[1], chunks), cols)
+
+
+def send_body(
+    ppos, meta, other, msg, gain_part, part, grid, pt, out_b, out_a, gsum, cols, acc, *, chunks
+):
     theirs, at = [], P_ROWS
     for rows in FACES:
         theirs.append(msg[at : at + rows])
         at += rows
-    build(grid, 1, ppos, other, *theirs)
-    for k in range(4):
-        s = k % 2
-        _, bx, by = place(pos if k < 2 else ppos, s)
-        rows = slice(k * 512, (k + 1) * 512)
-        for j in range(9):
-            cols[rows, j * C : (j + 1) * C] = window(grid, k // 2, bx, by, j)
-        if k < 2:
-            v = jnp.where(core == 0, pre[s], hid[s])
-        else:
-            v = msg[s * 512 : (s + 1) * 512]
-        v = v.astype(f32).reshape(64, 8, C)
-        for i, t in enumerate((up_z(v), v, down_z(v))):
-            pt[i * C : (i + 1) * C, rows] = t.reshape(512, C).T.astype(bf16)
-    y = jnp.dot(pt[...], cols[...], preferred_element_type=f32)
-    for j in range(9):
-        acc[j * 384 : (j + 1) * 384] = y[:, j * C : (j + 1) * C]
-    size = acc.shape[0] // chunks
-    quarter = chunks // 4
-    for k, dst in enumerate((keep_b, keep_a, out_b, out_a)):
-        for p in range(0, quarter, 2):
-            at = [pl.multiple_of((mine ^ (k * quarter + p + i)) * size, 8) for i in range(2)]
-            two = jnp.concatenate([acc[pl.ds(a, size)] for a in at])
-            dst[p * size : (p + 2) * size] = two.astype(dst.dtype)
+    build(grid, None, ppos, other, *theirs)
+    for s in range(2):
+        shifted(pt, s, msg[s * 512 : (s + 1) * 512])
+    upper = sends_upper(meta[1], chunks)
+    y = part[...] + product(grid, ppos, pt, upper, cols)
+    pieces(y, acc, (out_b, out_a), meta[1], upper, chunks // 2, chunks)
     tile = msg[1024:P_ROWS].astype(f32)
     total = gain_part[0:1] + ((tile[2:3] + tile[1:2]) + tile[0:1])
     gsum[...] = jnp.broadcast_to(total, (8, C))
+
+
+def keep_body(pos, ppos, meta, grid_a, grid_b, pt_a, pt_b, keep_b, keep_a, cols_a, cols_b, acc, *, chunks):
+    upper = jnp.logical_not(sends_upper(meta[1], chunks))
+    y = product(grid_a, pos, pt_a, upper, cols_a) + product(grid_b, ppos, pt_b, upper, cols_b)
+    pieces(y, acc, (keep_b, keep_a), meta[1], upper, 0, chunks)
 
 
 def pack3(v):
@@ -277,45 +306,74 @@
     return out
 
 
-def final_body(meta, o0, o1, o2, o3, p0, p1, p2, p3, k_out, g_out, first, second, gains, *, chunks):
-    own, part = (o0, o1, o2, o3), (p0, p1, p2, p3)
+def collect(core, sources, mine, theirs, joined, squares, gains, first_piece, chunks):
+    size = TAPS * C // chunks
+    for own in (0, 1):
+
+        @pl.when(core == own)
+        def _():
+            for k in (0, 1):
+                srcs, me = (sources[0], mine) if k == own else (sources[1], theirs)
+                p = first_piece
+                for src in srcs:
+                    joined[k][p * (size + 8) : p * (size + 8) + src.shape[0]] = src[...]
+                    for q in range(src.shape[0] // (size + 8)):
+                        v = src[q * (size + 8) : (q + 1) * (size + 8)].astype(f32)
+                        cube = v[:size].reshape(size // 8, 8, C)
+                        squares[k, me ^ p] = jnp.sum(cube * cube, axis=0)
+                        if k == 0:
+                            t = v[size:]
+                            gains[me ^ p] = jnp.broadcast_to((t[2:3] + t[1:2]) + t[0:1], (8, C))
+                        p += 1
+
+
+def gathered_body(meta, o0, o1, o2, p0, p1, p2, first, second, squares, gains, *, chunks):
+    collect(
+        meta[0], ((o0, o1, o2), (p0, p1, p2)), meta[1], meta[2], (first, second), squares, gains, 0, chunks
+    )
+
+
+def final_body(
+    meta, o3, p3, first_in, second_in, squares_in, gains_in,
+    k_out, g_out, first, second, squares, gains, stage, sems, *, chunks
+):
     core, mine, theirs = meta[0], meta[1], meta[2]
     n = TAPS * C
     size = n // chunks
-    quarter = chunks // 4
-
-    def spread(dst, srcs, me, gain):
-        for p in range(chunks):
-            src, q = srcs[p // quarter], p % quarter
-            piece = src[q * (size + 8) : (q + 1) * (size + 8)].astype(f32)
-            dst[pl.ds(pl.multiple_of((me ^ p) * size, 8), size)] = piece[:size]
-            if gain:
-                t = piece[size:]
-                gains[me ^ p] = jnp.broadcast_to((t[2:3] + t[1:2]) + t[0:1], (8, C))
-
-    @pl.when(core == 0)
-    def _():
-        spread(first, own, mine, True)
-        spread(second, part, theirs, False)
-
-    @pl.when(core != 0)
-    def _():
-        spread(first, part, theirs, True)
-        spread(second, own, mine, False)
-
+    collect(
+        core, ((o3,), (p3,)), mine, theirs, (first, second), squares, gains, chunks // 4 * 3, chunks
+    )
     g = jnp.sum(gains[...], axis=0)[0:1]
-    total = jnp.sum(g * g)
-    for ref in (first, second):
-        v = ref[...].reshape(n // 8, 8, C)
-        total = total + jnp.sum(jnp.sum(v * v, axis=0))
+    total = jnp.sum(g * g) + jnp.sum(jnp.sum(squares[...].reshape(2 * chunks, 8, C), axis=0))
     entries = 2.0 * n * C + C
     norm = jnp.full((8, C), total / entries + 1e-06, f32)
     shrink = jnp.minimum(1.0, clip_level / jnp.sqrt(norm))[0:1]
     g_out[...] = g * shrink
-    for t in range(TAPS):
-        k_out[0, t] = first[t * C : (t + 1) * C].T * shrink
-        u = TAPS - 1 - t
-        k_out[1, t] = second[u * C : (u + 1) * C] * shrink
+
+    def tap(joined, me, t):
+        parts, row = [], t * C
+        while row < (t + 1) * C:
+            chunk, at = row // size, row % size
+            rows = min(size - at, (t + 1) * C - row)
+            start = pl.multiple_of((me ^ chunk) * (size + 8) + at, 8)
+            parts.append(joined[pl.ds(start, rows)].astype(f32))
+            row += rows
+        return jnp.concatenate(parts) if len(parts) > 1 else parts[0]
+
+    copies = []
+    for k, joined in ((1, second), (0, first)):
+        me = jnp.where(core == k, mine, theirs)
+        for part in range(3):
+            for t in range(part * 9, part * 9 + 9):
+                v = tap(joined, me, t if k == 0 else TAPS - 1 - t)
+                stage[k, t] = (v.T if k == 0 else v) * shrink
+            block = (k, pl.ds(part * 9, 9))
+            copies.append(
+                pltpu.make_async_copy(stage.at[block], k_out.at[block], sems.at[len(copies)])
+            )
+            copies[-1].start()
+    for copy in copies:
+        copy.wait()
 
 
 def across(a, b, axis):
@@ -323,7 +381,9 @@
     even, odd = (
         [p for i in range(first, n - 1, 2) for p in ((i, i + 1), (i + 1, i))] for first in (0, 1)
     )
-    return lax.ppermute(a, axis, even), lax.ppermute(b, axis, odd)
+    b = lax.ppermute(b, axis, odd)
+    a = lax.ppermute(a, axis, even)
+    return a, b
 
 
 def y_faces(pos, meta, a, b, xa, xb):
@@ -412,18 +472,33 @@
         14,
     )
     pmsg = lax.ppermute(msg, "gy", partner)
-    keep_b, keep_a, out_b, out_a, g = call(
-        functools.partial(grads_body, chunks=chunks),
-        [sds((n // 4, C), f32)] * 2 + [sds((n // 4, C), bf16)] * 2 + [sds((8, C), f32)],
-        [
-            grid,
-            pltpu.VMEM((2048, 9 * C), bf16),
-            pltpu.VMEM((3 * C, 2048), bf16),
-            pltpu.VMEM((n, C), f32),
-        ],
-        (brick_pos, ppos, meta, features, cotangent, *edge, other, hid, pre, pmsg, gain_part),
+    held = [sds((18, 18, 8, C), f32), sds((3 * C, 1024), bf16)]
+    wide = pltpu.VMEM((1024, JS * C), bf16)
+    acc = pltpu.VMEM((JS * 3 * C, C), f32)
+    grid_a, pt_a, part = call(
+        functools.partial(own_body, chunks=chunks),
+        held + [sds((3 * C, JS * C), f32)],
+        [wide],
+        (brick_pos, meta, features, cotangent, *edge, hid, pre),
+        2,
+        10,
+    )
+    quarter = [sds((n // 4, C), bf16)] * 2
+    grid_b, pt_b, out_b, out_a, g = call(
+        functools.partial(send_body, chunks=chunks),
+        held + quarter + [sds((8, C), f32)],
+        [wide, acc],
+        (ppos, meta, other, pmsg, gain_part, part),
+        2,
+        10,
+    )
+    keep_b, keep_a = call(
+        functools.partial(keep_body, chunks=chunks),
+        [sds((n // 4, C), f32)] * 2,
+        [wide, wide, acc],
+        (brick_pos, ppos, meta, grid_a, grid_b, pt_a, pt_b),
         3,
-        20,
+        12,
     )
     g = g[0:1]
 
@@ -451,7 +526,8 @@
 
     swap = lambda v, dx, dy=0: lax.ppermute(v, both, pairs(dx, dy))
     steps = [(a[0], b[0]) for a, b in zip(*orders)][:halvings]
-    got_a, got_b = swap(out_a, steps[0]), swap(out_b, steps[0])
+    got_a = swap(out_a, steps[0])
+    got_b = swap(out_b, steps[0])
     out = (keep_a + got_a.astype(f32)).astype(bf16)
     got = swap(out, steps[1])
     low = keep_b + got_b.astype(f32) + got.astype(f32)
@@ -479,14 +555,26 @@
     own.append(swap(full, steps[0]))
     own.append(swap(own[1], steps[0]))
     part = [lax.ppermute(v, "gy", partner) for v in own]
-    k_up, g_up = call(
+    rows = chunks * (size + 8)
+    gathered = [
+        sds((rows, C), bf16), sds((rows, C), bf16), sds((2, chunks, 8, C), f32), sds((chunks, 8, C), f32)
+    ]
+    held = call(
+        functools.partial(gathered_body, chunks=chunks),
+        gathered,
+        [],
+        (meta, *own[:3], *part[:3]),
+        1,
+    )
+    k_up, g_up = pl.pallas_call(
         functools.partial(final_body, chunks=chunks),
-        [sds((2, TAPS, C, C), f32), sds((1, C), f32)],
-        [pltpu.VMEM((n, C), f32), pltpu.VMEM((n, C), f32), pltpu.VMEM((chunks, 8, C), f32)],
-        (meta, *own, *part),
-        1,
-        14,
-    )
+        out_shape=[sds((2, TAPS, C, C), f32), sds((1, C), f32), *gathered],
+        in_specs=[SMEM] + [VMEM] * 6,
+        out_specs=[pl.BlockSpec(memory_space=pl.ANY)] + [VMEM] * 5,
+        scratch_shapes=[pltpu.VMEM((2, TAPS, C, C), f32), pltpu.SemaphoreType.DMA((6,))],
+        input_output_aliases={3: 2, 4: 3, 5: 4, 6: 5},
+        compiler_params=pltpu.CompilerParams(vmem_limit_bytes=10 << 20),
+    )(meta, own[3], part[3], *held)[:2]
     return (*results, k_up, g_up.reshape(C))
 
 

time: 97.3 us -> 96.4 us (level)
  waiting for transfers between devices: 34.4 us -> 30.4 us
  Pallas kernels: 24 us -> 26.9 us
    pallas_call x0 -> x1, Pallas kernels: none -> 3.27 us  [per_device(): pl.pallas_call(functools.partial(final_body, chunks=chunks), out_shape=[s...]
    ppermute x12, waiting for transfers between devices: 21 us -> 18.3 us  [per_device(): swap = lambda v, dx, dy=0: lax.ppermute(v, both, pairs(dx, dy))]
    ppermute x1, waiting for transfers between devices: 1.38 us -> 0.01 us  [per_device(): pmsg = lax.ppermute(msg, 'gy', partner)]
    pallas_call x12 -> x14, Pallas kernels: 24 us -> 23.6 us  [call(): pl.pallas_call(body, out_shape=outs, in_specs=[SMEM] * n_smem + [VMEM] *...]
  transfers between devices with their start and end apart: 27 -> 27, of which waited for: 13 -> 12; matrix products, arithmetic and copies ran while one was open for 0% -> 0% of each run, Pallas kernels for 11% -> 17%
where the time goes in v5:
time: 96.4 us; the launch traced here: 96 us
  starting transfers between devices  37.5 us (39%)
  waiting for transfers between devices  30.4 us (32%)
  Pallas kernels  26.9 us (28%)
  between operations  1.06 us (1%)
    pallas_call x14, Pallas kernels, call(): pl.pallas_call(body, out_shape=outs, in_specs=[SMEM] * n_smem + [VMEM] *...  23.6 us
    ppermute x12, waiting for transfers between devices, per_device(): swap = lambda v, dx, dy=0: lax.ppermute(v, both, pairs(dx, dy))  18.3 us
    ppermute x4, starting transfers between devices, per_device(): part = [lax.ppermute(v, 'gy', partner) for v in own]  11.8 us
    ppermute x4, starting transfers between devices, across(): b = lax.ppermute(b, axis, odd)  11.2 us
    ppermute x4, waiting for transfers between devices, across(): b = lax.ppermute(b, axis, odd)  11.1 us
    ppermute x12, starting transfers between devices, per_device(): swap = lambda v, dx, dy=0: lax.ppermute(v, both, pairs(dx, dy))  9.49 us
    ppermute x4, starting transfers between devices, across(): a = lax.ppermute(a, axis, even)  3.76 us
    pallas_call x1, Pallas kernels, per_device(): pl.pallas_call(functools.partial(final_body, chunks=chunks), out_shape=[s...  3.27 us
  transfers between devices with their start and end apart: 27, of which 12 were waited for; matrix products, arithmetic and copies ran while one was open for 0% of the time, Pallas kernels for 17%

profile of v5, /device:TPU:21, one launch (start us, length us, event | category | flops | bytes accessed | tf_op | source)
XLA Modules:
  0.0 96.0 jit_solution(17536164788674016498)
XLA Ops:
  0.7 1.3 %shard_map.93 = (bf16[2,512,128]{2,1,0:T(8,128)(2,1)S(1)}, bf16[2,512,128]{2,1,0:T(8,128)(2,1)S(1)}, bf16[2,512,128]{2,1,0:T(8,128)(2,1)S(1)}, bf16[2,128,128]{2,1,0:T(8,128)(2,1)S(1)}, bf16[2,128,128]{2,1,0:T(8,128)(2,1)S(1)}) custom-call(s32[2]{0:T(128)} %pos.17, s32[1]{0:T(128)} %bitcast.core, s32[1]{0:T(128)} %bitcast.3.odd, bf16[2,512,128]{2,1,0:T(8,128)(2,1)} %a.1, ...), custom_call_target="tpu_custom_call" | custom-call | tf_op jit(solution)/shard_map/pallas_call | solution.py:34
  2.0 0.7 collective-permute-start.3
  2.7 0.1 collective-permute-start.2
  2.8 1.2 %collective-permute-start = (bf16[2,128,128]{2,1,0:T(8,128)(2,1)S(1)}, bf16[2,128,128]{2,1,0:T(8,128)(2,1)S(1)}, u32[]{:S(2)}, u32[]{:S(2)}) collective-permute-start(bf16[2,128,128]{2,1,0:T(8,128)(2,1)S(1)} %get-tuple-element.45), channel_id=1, source_target_pairs={{0,8},{8,0},{16,24},{24,16},{1,9},{9,1},{17,25},{25,17},{2,10},{10... | collective-permute-start | bytes 196616 | tf_op jit(solution)/shard_map/ppermute | solution.py:385
  4.0 2.1 %collective-permute-start.1 = (bf16[2,128,128]{2,1,0:T(8,128)(2,1)S(1)}, bf16[2,128,128]{2,1,0:T(8,128)(2,1)S(1)}, u32[]{:S(2)}, u32[]{:S(2)}) collective-permute-start(bf16[2,128,128]{2,1,0:T(8,128)(2,1)S(1)} %get-tuple-element.46), channel_id=1, source_target_pairs={{8,16},{16,8},{9,17},{17,9},{10,18},{18,10},{11,19},{19,11},{12,20... | collective-permute-start | bytes 196616 | tf_op jit(solution)/shard_map/ppermute | solution.py:384
  6.1 2.0 %shard_map.94 = (bf16[1152,384]{1,0:T(8,128)(2,1)S(1)}, bf16[1152,384]{1,0:T(8,128)(2,1)S(1)}, bf16[384,1152]{1,0:T(8,128)(2,1)S(1)}, bf16[384,1152]{1,0:T(8,128)(2,1)S(1)}, f32[1,128]{1,0:T(1,128)S(1)}) custom-call(bf16[27,128,128]{2,1,0:T(8,128)(2,1)} %k1.1, bf16[27,128,128]{2,1,0:T(8,128)(2,1)} %k2.1, f32[1,128]{1,0:T(1,128)} %bitcast.6), custom_call_target="tpu_custom_call" | custom-call | tf_op jit(solution)/shard_map/pallas_call | solution.py:34
  8.1 0.1 pad_add_fusion.meta
  8.2 1.7 %collective-permute-done.1.xb = bf16[2,128,128]{2,1,0:T(8,128)(2,1)S(1)} collective-permute-done((bf16[2,128,128]{2,1,0:T(8,128)(2,1)S(1)}, bf16[2,128,128]{2,1,0:T(8,128)(2,1)S(1)}, u32[]{:S(2)}, u32[]{:S(2)}) %collective-permute-start.1) | collective-permute-done | bytes 65568 | tf_op jit(solution)/shard_map/ppermute | solution.py:384
  9.9 0.8 shard_map.95
  10.7 4.9 %collective-permute-start.5 = (bf16[2,144,128]{2,1,0:T(8,128)(2,1)S(1)}, bf16[2,144,128]{2,1,0:T(8,128)(2,1)S(1)}, u32[]{:S(2)}, u32[]{:S(2)}) collective-permute-start(bf16[2,144,128]{2,1,0:T(8,128)(2,1)S(1)} %get-tuple-element.52), channel_id=1, source_target_pairs={{1,2},{2,1},{3,4},{4,3},{5,6},{6,5},{9,10},{10,9},{11,12},{12,11},... | collective-permute-start | bytes 221192 | tf_op jit(solution)/shard_map/ppermute | solution.py:384
  15.8 2.1 %collective-permute-done.5.yb = bf16[2,144,128]{2,1,0:T(8,128)(2,1)S(1)} collective-permute-done((bf16[2,144,128]{2,1,0:T(8,128)(2,1)S(1)}, bf16[2,144,128]{2,1,0:T(8,128)(2,1)S(1)}, u32[]{:S(2)}, u32[]{:S(2)}) %collective-permute-start.5) | collective-permute-done | bytes 73760 | tf_op jit(solution)/shard_map/ppermute | solution.py:384
  17.9 4.6 %shard_map.96 = (bf16[2,512,128]{2,1,0:T(8,128)(2,1)S(1)}, bf16[2,512,128]{2,1,0:T(8,128)(2,1)S(1)}, bf16[1584,128]{1,0:T(8,128)(2,1)S(1)}, f32[8,128]{1,0:T(8,128)S(1)}) custom-call(s32[2]{0:T(128)} %pos.17, s32[4]{0:T(128)S(1)} %pad_add_fusion.meta, bf16[2,512,128]{2,1,0:T(8,128)(2,1)S(1)} %get-tuple-element.48.a.base, ...), custom_call_target="tpu_custom_call" | custom-call | tf_op jit(solution)/shard_map/pallas_call | solution.py:34
  22.4 0.4 collective-permute-start.6
  22.9 1.9 %shard_map.97 = (f32[18,18,8,128]{3,2,1,0:T(8,128)S(1)}, bf16[384,1024]{1,0:T(8,128)(2,1)S(1)}, f32[384,640]{1,0:T(8,128)S(1)}) custom-call(s32[2]{0:T(128)} %pos.17, s32[4]{0:T(128)S(1)} %pad_add_fusion.meta, bf16[2,512,128]{2,1,0:T(8,128)(2,1)S(1)} %get-tuple-element.48.a.base, bf16[2,512,128]{2,1,0:T(8,128)(2,1)S(1)} %get-tuple-element.44.b.base, ...), custom_call_target="tpu_custom_call" | custom-call | tf_op jit(solution)/shard_map/pallas_call | solution.py:34
  24.7 1.6 %shard_map.98 = (f32[18,18,8,128]{3,2,1,0:T(8,128)S(1)}, bf16[384,1024]{1,0:T(8,128)(2,1)S(1)}, bf16[864,128]{1,0:T(8,128)(2,1)S(1)}, bf16[864,128]{1,0:T(8,128)(2,1)S(1)}, f32[8,128]{1,0:T(8,128)S(1)}) custom-call(s32[2]{0:T(128)S(1)} %collective-permute-done.2.ppos, s32[4]{0:T(128)S(1)} %pad_add_fusion.meta, ...), custom_call_target="tpu_custom_call" | custom-call | tf_op jit(solution)/shard_map/pallas_call | solution.py:34
  26.4 0.1 collective-permute-start.12
  26.5 1.5 %collective-permute-start.11 = (bf16[864,128]{1,0:T(8,128)(2,1)S(1)}, bf16[864,128]{1,0:T(8,128)(2,1)S(1)}, u32[]{:S(2)}, u32[]{:S(2)}) collective-permute-start(bf16[864,128]{1,0:T(8,128)(2,1)S(1)} %get-tuple-element.73), channel_id=1, source_target_pairs={{0,8},{1,17},{2,10},{3,19},{4,12},{5,21},{6,14},{7,23},{8,0},{9,25... | collective-permute-start | bytes 663560 | tf_op jit(solution)/shard_map/ppermute | solution.py:527
  27.9 2.3 %shard_map.103 = (f32[864,128]{1,0:T(8,128)S(1)}, f32[864,128]{1,0:T(8,128)S(1)}) custom-call(s32[2]{0:T(128)} %pos.17, s32[2]{0:T(128)S(1)} %collective-permute-done.2.ppos, s32[4]{0:T(128)S(1)} %pad_add_fusion.meta, f32[18,18,8,128]{3,2,1,0:T(8,128)S(1)} %get-tuple-element.68.grid_a, f32[18,18,8,128]{3,2,1,0:T(8,128)S(1)} %get-tuple-element.69.grid_b, ...), custom_call_target="tpu_custom_call" | custom-call | tf_op jit(solution)/shard_map/pallas_call | solution.py:34
  30.3 1.3 %collective-permute-done.12 = bf16[864,128]{1,0:T(8,128)(2,1)S(1)} collective-permute-done((bf16[864,128]{1,0:T(8,128)(2,1)S(1)}, bf16[864,128]{1,0:T(8,128)(2,1)S(1)}, u32[]{:S(2)}, u32[]{:S(2)}) %collective-permute-start.12) | collective-permute-done | bytes 221216 | tf_op jit(solution)/shard_map/ppermute | solution.py:527
  31.7 2.2 %collective-permute-done.11 = bf16[864,128]{1,0:T(8,128)(2,1)S(1)} collective-permute-done((bf16[864,128]{1,0:T(8,128)(2,1)S(1)}, bf16[864,128]{1,0:T(8,128)(2,1)S(1)}, u32[]{:S(2)}, u32[]{:S(2)}) %collective-permute-start.11) | collective-permute-done | bytes 221216 | tf_op jit(solution)/shard_map/ppermute | solution.py:527
  33.9 3.0 %collective-permute-done.13 = bf16[864,128]{1,0:T(8,128)(2,1)S(1)} collective-permute-done((bf16[864,128]{1,0:T(8,128)(2,1)S(1)}, bf16[864,128]{1,0:T(8,128)(2,1)S(1)}, u32[]{:S(2)}, u32[]{:S(2)}) %collective-permute-start.13) | collective-permute-done | bytes 221216 | tf_op jit(solution)/shard_map/ppermute | solution.py:527
  36.9 0.1 fusion.2
  37.0 1.2 %collective-permute-start.15 = (f32[216,128]{1,0:T(8,128)S(1)}, f32[216,128]{1,0:T(8,128)S(1)}, u32[]{:S(2)}, u32[]{:S(2)}) collective-permute-start(f32[216,128]{1,0:T(8,128)S(1)} %slice.24), channel_id=1, source_target_pairs={{0,2},{1,3},{2,0},{3,1},{4,6},{5,7},{6,4},{7,5},{8,10},{9,11},{10,... | collective-permute-start | bytes 331784 | tf_op jit(solution)/shard_map/ppermute | solution.py:527
  38.2 0.2 collective-permute-start.14
  38.5 1.3 %collective-permute-start.16 = (bf16[216,128]{1,0:T(8,128)(2,1)S(1)}, bf16[216,128]{1,0:T(8,128)(2,1)S(1)}, u32[]{:S(2)}, u32[]{:S(2)}) collective-permute-start(bf16[216,128]{1,0:T(8,128)(2,1)S(1)} %get-tuple-element.85), channel_id=1, source_target_pairs={{0,6},{1,7},{2,4},{3,5},{4,2},{5,3},{6,0},{7,1},{8,14},{9,15},{10,... | collective-permute-start | bytes 165896 | tf_op jit(solution)/shard_map/ppermute | solution.py:527
  39.8 3.0 %collective-permute-done.14 = bf16[216,128]{1,0:T(8,128)(2,1)S(1)} collective-permute-done((bf16[216,128]{1,0:T(8,128)(2,1)S(1)}, bf16[216,128]{1,0:T(8,128)(2,1)S(1)}, u32[]{:S(2)}, u32[]{:S(2)}) %collective-permute-start.14) | collective-permute-done | bytes 55328 | tf_op jit(solution)/shard_map/ppermute | solution.py:527
  42.8 0.6 collective-permute-start.19
  43.4 3.9 %collective-permute-start.18 = (bf16[224,128]{1,0:T(8,128)(2,1)S(1)}, bf16[224,128]{1,0:T(8,128)(2,1)S(1)}, u32[]{:S(2)}, u32[]{:S(2)}) collective-permute-start(bf16[224,128]{1,0:T(8,128)(2,1)S(1)} %shard_map.104.refs_0_), channel_id=1, source_target_pairs={{0,2},{1,3},{2,0},{3,1},{4,6},{5,7},{6,4},{7,5},{8,10},{9,11},{10,... | collective-permute-start | bytes 172040 | tf_op jit(solution)/shard_map/ppermute | solution.py:527
  47.4 2.2 %collective-permute-done.18.refs_2_ = bf16[224,128]{1,0:T(8,128)(2,1)S(1)} collective-permute-done((bf16[224,128]{1,0:T(8,128)(2,1)S(1)}, bf16[224,128]{1,0:T(8,128)(2,1)S(1)}, u32[]{:S(2)}, u32[]{:S(2)}) %collective-permute-start.18) | collective-permute-done | bytes 57376 | tf_op jit(solution)/shard_map/ppermute | solution.py:527
  49.5 2.3 %collective-permute-done.17.refs_1_ = bf16[224,128]{1,0:T(8,128)(2,1)S(1)} collective-permute-done((bf16[224,128]{1,0:T(8,128)(2,1)S(1)}, bf16[224,128]{1,0:T(8,128)(2,1)S(1)}, u32[]{:S(2)}, u32[]{:S(2)}) %collective-permute-start.17) | collective-permute-done | bytes 57376 | tf_op jit(solution)/shard_map/ppermute | solution.py:527
  51.9 0.5 collective-permute-start.23
  52.4 4.3 %collective-permute-done.20.o1 = bf16[896,128]{1,0:T(8,128)(2,1)S(1)} collective-permute-done((bf16[896,128]{1,0:T(8,128)(2,1)S(1)}, bf16[896,128]{1,0:T(8,128)(2,1)S(1)}, u32[]{:S(2)}, u32[]{:S(2)}) %collective-permute-start.20) | collective-permute-done | bytes 229408 | tf_op jit(solution)/shard_map/ppermute | solution.py:527
  56.8 0.8 shard_map.99
  57.6 0.6 collective-permute-start.7
  58.2 8.7 %collective-permute-start.24 = (bf16[896,128]{1,0:T(8,128)(2,1)S(1)}, bf16[896,128]{1,0:T(8,128)(2,1)S(1)}, u32[]{:S(2)}, u32[]{:S(2)}) collective-permute-start(bf16[896,128]{1,0:T(8,128)(2,1)S(1)} %shard_map.105.o0), channel_id=1, source_target_pairs={{0,1},{1,0},{2,3},{3,2},{4,5},{5,4},{6,7},{7,6},{8,9},{9,8},{10,11... | collective-permute-start | bytes 688136 | tf_op jit(solution)/shard_map/ppermute | solution.py:557
  66.9 0.5 collective-permute-start.25
  67.4 2.6 %collective-permute-start.22 = (bf16[896,128]{1,0:T(8,128)(2,1)S(1)}, bf16[896,128]{1,0:T(8,128)(2,1)S(1)}, u32[]{:S(2)}, u32[]{:S(2)}) collective-permute-start(bf16[896,128]{1,0:T(8,128)(2,1)S(1)} %collective-permute-done.21.o3), channel_id=1, source_target_pairs={{0,1},{1,0},{2,3},{3,2},{4,5},{5,4},{6,7},{7,6},{8,9},{9,8},{10,11... | collective-permute-start | bytes 688136 | tf_op jit(solution)/shard_map/ppermute | solution.py:557
  70.0 2.1 %collective-permute-start.8 = (bf16[2,128,128]{2,1,0:T(8,128)(2,1)S(1)}, bf16[2,128,128]{2,1,0:T(8,128)(2,1)S(1)}, u32[]{:S(2)}, u32[]{:S(2)}) collective-permute-start(bf16[2,128,128]{2,1,0:T(8,128)(2,1)S(1)} %get-tuple-element.63), channel_id=1, source_target_pairs={{8,16},{16,8},{9,17},{17,9},{10,18},{18,10},{11,19},{19,11},{12,20... | collective-permute-start | bytes 196616 | tf_op jit(solution)/shard_map/ppermute | solution.py:384
  72.1 3.8 %collective-permute-done.8.xb = bf16[2,128,128]{2,1,0:T(8,128)(2,1)S(1)} collective-permute-done((bf16[2,128,128]{2,1,0:T(8,128)(2,1)S(1)}, bf16[2,128,128]{2,1,0:T(8,128)(2,1)S(1)}, u32[]{:S(2)}, u32[]{:S(2)}) %collective-permute-start.8) | collective-permute-done | bytes 65568 | tf_op jit(solution)/shard_map/ppermute | solution.py:384
  75.9 0.8 shard_map.100
  76.7 1.9 %collective-permute-start.9 = (bf16[2,144,128]{2,1,0:T(8,128)(2,1)S(1)}, bf16[2,144,128]{2,1,0:T(8,128)(2,1)S(1)}, u32[]{:S(2)}, u32[]{:S(2)}) collective-permute-start(bf16[2,144,128]{2,1,0:T(8,128)(2,1)S(1)} %get-tuple-element.64), channel_id=1, source_target_pairs={{0,1},{1,0},{2,3},{3,2},{4,5},{5,4},{6,7},{7,6},{8,9},{9,8},{10,11... | collective-permute-start | bytes 221192 | tf_op jit(solution)/shard_map/ppermute | solution.py:385
  78.6 0.9 collective-permute-done.9.ya
  79.5 2.1 %collective-permute-start.10 = (bf16[2,144,128]{2,1,0:T(8,128)(2,1)S(1)}, bf16[2,144,128]{2,1,0:T(8,128)(2,1)S(1)}, u32[]{:S(2)}, u32[]{:S(2)}) collective-permute-start(bf16[2,144,128]{2,1,0:T(8,128)(2,1)S(1)} %get-tuple-element.65), channel_id=1, source_target_pairs={{1,2},{2,1},{3,4},{4,3},{5,6},{6,5},{9,10},{10,9},{11,12},{12,11},... | collective-permute-start | bytes 221192 | tf_op jit(solution)/shard_map/ppermute | solution.py:384
  81.6 3.6 %collective-permute-done.10.yb = bf16[2,144,128]{2,1,0:T(8,128)(2,1)S(1)} collective-permute-done((bf16[2,144,128]{2,1,0:T(8,128)(2,1)S(1)}, bf16[2,144,128]{2,1,0:T(8,128)(2,1)S(1)}, u32[]{:S(2)}, u32[]{:S(2)}) %collective-permute-start.10) | collective-permute-done | bytes 73760 | tf_op jit(solution)/shard_map/ppermute | solution.py:384
  85.2 3.4 %shard_map.102 = bf16[2,512,128]{2,1,0:T(8,128)(2,1)} custom-call(s32[2]{0:T(128)} %pos.17, s32[4]{0:T(128)S(1)} %pad_add_fusion.meta, bf16[2,512,128]{2,1,0:T(8,128)(2,1)S(1)} %get-tuple-element.58.pre.b.src, bf16[2,128,128]{2,1,0:T(8,128)(2,1)S(1)} %collective-permute-done.7.xa, bf16[2,128,128]{2,1,0:T(8,128)(2,1)S(1)} %collective-permute-done.8.xb, ...), custom_call_target="tpu_custom_call" | custom-call | tf_op jit(solution)/shard_map/pallas_call | solution.py:34
  88.6 3.2 %shard_map.101 = bf16[2,512,128]{2,1,0:T(8,128)(2,1)} custom-call(s32[2]{0:T(128)} %pos.17, s32[4]{0:T(128)S(1)} %pad_add_fusion.meta, bf16[2,512,128]{2,1,0:T(8,128)(2,1)S(1)} %get-tuple-element.61.hid.a.src, bf16[2,128,128]{2,1,0:T(8,128)(2,1)S(1)} %collective-permute-done.7.xa, bf16[2,128,128]{2,1,0:T(8,128)(2,1)S(1)} %collective-permute-done.8.xb, ...), custom_call_target="tpu_custom_call" | custom-call | tf_op jit(solution)/shard_map/pallas_call | solution.py:34
  91.7 0.9 shard_map.106
  92.6 3.3 %shard_map.107 = (f32[2,27,128,128]{3,2,1,0:T(8,128)}, f32[1,128]{1,0:T(1,128)}, bf16[3584,128]{1,0:T(8,128)(2,1)S(1)}, bf16[3584,128]{1,0:T(8,128)(2,1)S(1)}, f...) custom-call(s32[4]{0:T(128)S(1)} %pad_add_fusion.meta, ...), custom_call_target="tpu_custom_call", output_to_operand_aliasing={{2}: (3, {}), {3}: (4, {}), {4}: (5, {}), {5}: (6, {})} | custom-call | tf_op jit(solution)/shard_map/pallas_call | solution.py:569
  (28 shorter events, 0.4 us)
Async XLA Ops:
  2.0 13.7 %collective-permute-start.3 = (bf16[2,512,128]{2,1,0:T(8,128)(2,1)S(1)}, bf16[2,512,128]{2,1,0:T(8,128)(2,1)S(1)}, u32[]{:S(2)}, u32[]{:S(2)}) collective-permute-start(bf16[2,512,128]{2,1,0:T(8,128)(2,1)S(1)} %get-tuple-element.50), channel_id=1, source_target_pairs={{0,1},{1,0},{2,3},{3,2},{4,5},{5,4},{6,7},{7,6},{8,9},{9,8},{10,11... | collective-permute-start | bytes 786440 | tf_op jit(solution)/shard_map/ppermute | solution.py:452
  2.7 13.0 %collective-permute-start.2 = (s32[2]{0:T(128)}, s32[2]{0:T(128)S(1)}, u32[]{:S(2)}, u32[]{:S(2)}) collective-permute-start(s32[2]{0:T(128)} %pos.17), channel_id=1, source_target_pairs={{0,1},{1,0},{2,3},{3,2},{4,5},{5,4},{6,7},{7,6},{8,9},{9,8},{10,11... | collective-permute-start | bytes 32 | tf_op jit(solution)/shard_map/ppermute | solution.py:451
  2.8 5.4 %collective-permute-start = (bf16[2,128,128]{2,1,0:T(8,128)(2,1)S(1)}, bf16[2,128,128]{2,1,0:T(8,128)(2,1)S(1)}, u32[]{:S(2)}, u32[]{:S(2)}) collective-permute-start(bf16[2,128,128]{2,1,0:T(8,128)(2,1)S(1)} %get-tuple-element.45), channel_id=1, source_target_pairs={{0,8},{8,0},{16,24},{24,16},{1,9},{9,1},{17,25},{25,17},{2,10},{10... | collective-permute-start | bytes 196616 | tf_op jit(solution)/shard_map/ppermute | solution.py:385
  4.0 5.9 %collective-permute-start.1 = (bf16[2,128,128]{2,1,0:T(8,128)(2,1)S(1)}, bf16[2,128,128]{2,1,0:T(8,128)(2,1)S(1)}, u32[]{:S(2)}, u32[]{:S(2)}) collective-permute-start(bf16[2,128,128]{2,1,0:T(8,128)(2,1)S(1)} %get-tuple-element.46), channel_id=1, source_target_pairs={{8,16},{16,8},{9,17},{17,9},{10,18},{18,10},{11,19},{19,11},{12,20... | collective-permute-start | bytes 196616 | tf_op jit(solution)/shard_map/ppermute | solution.py:384
  10.7 7.1 %collective-permute-start.5 = (bf16[2,144,128]{2,1,0:T(8,128)(2,1)S(1)}, bf16[2,144,128]{2,1,0:T(8,128)(2,1)S(1)}, u32[]{:S(2)}, u32[]{:S(2)}) collective-permute-start(bf16[2,144,128]{2,1,0:T(8,128)(2,1)S(1)} %get-tuple-element.52), channel_id=1, source_target_pairs={{1,2},{2,1},{3,4},{4,3},{5,6},{6,5},{9,10},{10,9},{11,12},{12,11},... | collective-permute-start | bytes 221192 | tf_op jit(solution)/shard_map/ppermute | solution.py:384
  15.7 2.2 %collective-permute-start.4 = (bf16[2,144,128]{2,1,0:T(8,128)(2,1)S(1)}, bf16[2,144,128]{2,1,0:T(8,128)(2,1)S(1)}, u32[]{:S(2)}, u32[]{:S(2)}) collective-permute-start(bf16[2,144,128]{2,1,0:T(8,128)(2,1)S(1)} %get-tuple-element.51), channel_id=1, source_target_pairs={{0,1},{1,0},{2,3},{3,2},{4,5},{5,4},{6,7},{7,6},{8,9},{9,8},{10,11... | collective-permute-start | bytes 221192 | tf_op jit(solution)/shard_map/ppermute | solution.py:385
  22.4 2.3 %collective-permute-start.6 = (bf16[1584,128]{1,0:T(8,128)(2,1)S(1)}, bf16[1584,128]{1,0:T(8,128)(2,1)S(1)}, u32[]{:S(2)}, u32[]{:S(2)}) collective-permute-start(bf16[1584,128]{1,0:T(8,128)(2,1)S(1)} %get-tuple-element.56), channel_id=1, source_target_pairs={{0,1},{1,0},{2,3},{3,2},{4,5},{5,4},{6,7},{7,6},{8,9},{9,8},{10,11... | collective-permute-start | bytes 1216520 | tf_op jit(solution)/shard_map/ppermute | solution.py:474
  26.4 5.1 %collective-permute-start.12 = (bf16[864,128]{1,0:T(8,128)(2,1)S(1)}, bf16[864,128]{1,0:T(8,128)(2,1)S(1)}, u32[]{:S(2)}, u32[]{:S(2)}) collective-permute-start(bf16[864,128]{1,0:T(8,128)(2,1)S(1)} %get-tuple-element.60), channel_id=1, source_target_pairs={{0,8},{1,17},{2,10},{3,19},{4,12},{5,21},{6,14},{7,23},{8,0},{9,25... | collective-permute-start | bytes 663560 | tf_op jit(solution)/shard_map/ppermute | solution.py:527
  26.5 7.4 %collective-permute-start.11 = (bf16[864,128]{1,0:T(8,128)(2,1)S(1)}, bf16[864,128]{1,0:T(8,128)(2,1)S(1)}, u32[]{:S(2)}, u32[]{:S(2)}) collective-permute-start(bf16[864,128]{1,0:T(8,128)(2,1)S(1)} %get-tuple-element.73), channel_id=1, source_target_pairs={{0,8},{1,17},{2,10},{3,19},{4,12},{5,21},{6,14},{7,23},{8,0},{9,25... | collective-permute-start | bytes 663560 | tf_op jit(solution)/shard_map/ppermute | solution.py:527
  31.6 5.3 %collective-permute-start.13 = (bf16[864,128]{1,0:T(8,128)(2,1)S(1)}, bf16[864,128]{1,0:T(8,128)(2,1)S(1)}, u32[]{:S(2)}, u32[]{:S(2)}) collective-permute-start(bf16[864,128]{1,0:T(8,128)(2,1)S(1)} %add_convert_fusion), channel_id=1, source_target_pairs={{0,16},{1,9},{2,18},{3,11},{4,20},{5,13},{6,22},{7,15},{8,24},{9,1... | collective-permute-start | bytes 663560 | tf_op jit(solution)/shard_map/ppermute | solution.py:527
  37.0 5.8 %collective-permute-start.15 = (f32[216,128]{1,0:T(8,128)S(1)}, f32[216,128]{1,0:T(8,128)S(1)}, u32[]{:S(2)}, u32[]{:S(2)}) collective-permute-start(f32[216,128]{1,0:T(8,128)S(1)} %slice.24), channel_id=1, source_target_pairs={{0,2},{1,3},{2,0},{3,1},{4,6},{5,7},{6,4},{7,5},{8,10},{9,11},{10,... | collective-permute-start | bytes 331784 | tf_op jit(solution)/shard_map/ppermute | solution.py:527
  38.2 4.6 %collective-permute-start.14 = (bf16[216,128]{1,0:T(8,128)(2,1)S(1)}, bf16[216,128]{1,0:T(8,128)(2,1)S(1)}, u32[]{:S(2)}, u32[]{:S(2)}) collective-permute-start(bf16[216,128]{1,0:T(8,128)(2,1)S(1)} %get-tuple-element.84), channel_id=1, source_target_pairs={{0,4},{1,5},{2,6},{3,7},{4,0},{5,1},{6,2},{7,3},{8,12},{9,13},{10,... | collective-permute-start | bytes 165896 | tf_op jit(solution)/shard_map/ppermute | solution.py:527
  38.5 4.3 %collective-permute-start.16 = (bf16[216,128]{1,0:T(8,128)(2,1)S(1)}, bf16[216,128]{1,0:T(8,128)(2,1)S(1)}, u32[]{:S(2)}, u32[]{:S(2)}) collective-permute-start(bf16[216,128]{1,0:T(8,128)(2,1)S(1)} %get-tuple-element.85), channel_id=1, source_target_pairs={{0,6},{1,7},{2,4},{3,5},{4,2},{5,3},{6,0},{7,1},{8,14},{9,15},{10,... | collective-permute-start | bytes 165896 | tf_op jit(solution)/shard_map/ppermute | solution.py:527
  42.8 4.5 %collective-permute-start.19 = (bf16[224,128]{1,0:T(8,128)(2,1)S(1)}, bf16[224,128]{1,0:T(8,128)(2,1)S(1)}, u32[]{:S(2)}, u32[]{:S(2)}) collective-permute-start(bf16[224,128]{1,0:T(8,128)(2,1)S(1)} %shard_map.104.refs_0_), channel_id=1, source_target_pairs={{0,6},{1,7},{2,4},{3,5},{4,2},{5,3},{6,0},{7,1},{8,14},{9,15},{10,... | collective-permute-start | bytes 172040 | tf_op jit(solution)/shard_map/ppermute | solution.py:527
  43.4 6.1 %collective-permute-start.18 = (bf16[224,128]{1,0:T(8,128)(2,1)S(1)}, bf16[224,128]{1,0:T(8,128)(2,1)S(1)}, u32[]{:S(2)}, u32[]{:S(2)}) collective-permute-start(bf16[224,128]{1,0:T(8,128)(2,1)S(1)} %shard_map.104.refs_0_), channel_id=1, source_target_pairs={{0,2},{1,3},{2,0},{3,1},{4,6},{5,7},{6,4},{7,5},{8,10},{9,11},{10,... | collective-permute-start | bytes 172040 | tf_op jit(solution)/shard_map/ppermute | solution.py:527
  47.4 4.5 %collective-permute-start.17 = (bf16[224,128]{1,0:T(8,128)(2,1)S(1)}, bf16[224,128]{1,0:T(8,128)(2,1)S(1)}, u32[]{:S(2)}, u32[]{:S(2)}) collective-permute-start(bf16[224,128]{1,0:T(8,128)(2,1)S(1)} %shard_map.104.refs_0_), channel_id=1, source_target_pairs={{0,4},{1,5},{2,6},{3,7},{4,0},{5,1},{6,2},{7,3},{8,12},{9,13},{10,... | collective-permute-start | bytes 172040 | tf_op jit(solution)/shard_map/ppermute | solution.py:527
  51.8 4.9 %collective-permute-start.20 = (bf16[896,128]{1,0:T(8,128)(2,1)S(1)}, bf16[896,128]{1,0:T(8,128)(2,1)S(1)}, u32[]{:S(2)}, u32[]{:S(2)}) collective-permute-start(bf16[896,128]{1,0:T(8,128)(2,1)S(1)} %shard_map.105.o0), channel_id=1, source_target_pairs={{0,16},{1,9},{2,18},{3,11},{4,20},{5,13},{6,22},{7,15},{8,24},{9,1... | collective-permute-start | bytes 688136 | tf_op jit(solution)/shard_map/ppermute | solution.py:527
  51.9 14.9 %collective-permute-start.23 = (bf16[896,128]{1,0:T(8,128)(2,1)S(1)}, bf16[896,128]{1,0:T(8,128)(2,1)S(1)}, u32[]{:S(2)}, u32[]{:S(2)}) collective-permute-start(bf16[896,128]{1,0:T(8,128)(2,1)S(1)} %shard_map.105.o0), channel_id=1, source_target_pairs={{0,8},{1,17},{2,10},{3,19},{4,12},{5,21},{6,14},{7,23},{8,0},{9,25... | collective-permute-start | bytes 688136 | tf_op jit(solution)/shard_map/ppermute | solution.py:527
  56.8 10.6 %collective-permute-start.21 = (bf16[896,128]{1,0:T(8,128)(2,1)S(1)}, bf16[896,128]{1,0:T(8,128)(2,1)S(1)}, u32[]{:S(2)}, u32[]{:S(2)}) collective-permute-start(bf16[896,128]{1,0:T(8,128)(2,1)S(1)} %collective-permute-done.20.o1), channel_id=1, source_target_pairs={{0,8},{1,17},{2,10},{3,19},{4,12},{5,21},{6,14},{7,23},{8,0},{9,25... | collective-permute-start | bytes 688136 | tf_op jit(solution)/shard_map/ppermute | solution.py:527
  57.6 12.4 %collective-permute-start.7 = (bf16[2,128,128]{2,1,0:T(8,128)(2,1)S(1)}, bf16[2,128,128]{2,1,0:T(8,128)(2,1)S(1)}, u32[]{:S(2)}, u32[]{:S(2)}) collective-permute-start(bf16[2,128,128]{2,1,0:T(8,128)(2,1)S(1)} %get-tuple-element.62), channel_id=1, source_target_pairs={{0,8},{8,0},{16,24},{24,16},{1,9},{9,1},{17,25},{25,17},{2,10},{10... | collective-permute-start | bytes 196616 | tf_op jit(solution)/shard_map/ppermute | solution.py:385
  58.2 33.6 %collective-permute-start.24 = (bf16[896,128]{1,0:T(8,128)(2,1)S(1)}, bf16[896,128]{1,0:T(8,128)(2,1)S(1)}, u32[]{:S(2)}, u32[]{:S(2)}) collective-permute-start(bf16[896,128]{1,0:T(8,128)(2,1)S(1)} %shard_map.105.o0), channel_id=1, source_target_pairs={{0,1},{1,0},{2,3},{3,2},{4,5},{5,4},{6,7},{7,6},{8,9},{9,8},{10,11... | collective-permute-start | bytes 688136 | tf_op jit(solution)/shard_map/ppermute | solution.py:557
  66.8 24.9 %collective-permute-start.26 = (bf16[896,128]{1,0:T(8,128)(2,1)S(1)}, bf16[896,128]{1,0:T(8,128)(2,1)S(1)}, u32[]{:S(2)}, u32[]{:S(2)}) collective-permute-start(bf16[896,128]{1,0:T(8,128)(2,1)S(1)} %collective-permute-done.23.o2), channel_id=1, source_target_pairs={{0,1},{1,0},{2,3},{3,2},{4,5},{5,4},{6,7},{7,6},{8,9},{9,8},{10,11... | collective-permute-start | bytes 688136 | tf_op jit(solution)/shard_map/ppermute | solution.py:557
  66.9 24.9 %collective-permute-start.25 = (bf16[896,128]{1,0:T(8,128)(2,1)S(1)}, bf16[896,128]{1,0:T(8,128)(2,1)S(1)}, u32[]{:S(2)}, u32[]{:S(2)}) collective-permute-start(bf16[896,128]{1,0:T(8,128)(2,1)S(1)} %collective-permute-done.20.o1), channel_id=1, source_target_pairs={{0,1},{1,0},{2,3},{3,2},{4,5},{5,4},{6,7},{7,6},{8,9},{9,8},{10,11... | collective-permute-start | bytes 688136 | tf_op jit(solution)/shard_map/ppermute | solution.py:557
  67.4 25.2 %collective-permute-start.22 = (bf16[896,128]{1,0:T(8,128)(2,1)S(1)}, bf16[896,128]{1,0:T(8,128)(2,1)S(1)}, u32[]{:S(2)}, u32[]{:S(2)}) collective-permute-start(bf16[896,128]{1,0:T(8,128)(2,1)S(1)} %collective-permute-done.21.o3), channel_id=1, source_target_pairs={{0,1},{1,0},{2,3},{3,2},{4,5},{5,4},{6,7},{7,6},{8,9},{9,8},{10,11... | collective-permute-start | bytes 688136 | tf_op jit(solution)/shard_map/ppermute | solution.py:557
  70.0 5.9 %collective-permute-start.8 = (bf16[2,128,128]{2,1,0:T(8,128)(2,1)S(1)}, bf16[2,128,128]{2,1,0:T(8,128)(2,1)S(1)}, u32[]{:S(2)}, u32[]{:S(2)}) collective-permute-start(bf16[2,128,128]{2,1,0:T(8,128)(2,1)S(1)} %get-tuple-element.63), channel_id=1, source_target_pairs={{8,16},{16,8},{9,17},{17,9},{10,18},{18,10},{11,19},{19,11},{12,20... | collective-permute-start | bytes 196616 | tf_op jit(solution)/shard_map/ppermute | solution.py:384
  76.7 2.8 %collective-permute-start.9 = (bf16[2,144,128]{2,1,0:T(8,128)(2,1)S(1)}, bf16[2,144,128]{2,1,0:T(8,128)(2,1)S(1)}, u32[]{:S(2)}, u32[]{:S(2)}) collective-permute-start(bf16[2,144,128]{2,1,0:T(8,128)(2,1)S(1)} %get-tuple-element.64), channel_id=1, source_target_pairs={{0,1},{1,0},{2,3},{3,2},{4,5},{5,4},{6,7},{7,6},{8,9},{9,8},{10,11... | collective-permute-start | bytes 221192 | tf_op jit(solution)/shard_map/ppermute | solution.py:385
  79.5 5.7 %collective-permute-start.10 = (bf16[2,144,128]{2,1,0:T(8,128)(2,1)S(1)}, bf16[2,144,128]{2,1,0:T(8,128)(2,1)S(1)}, u32[]{:S(2)}, u32[]{:S(2)}) collective-permute-start(bf16[2,144,128]{2,1,0:T(8,128)(2,1)S(1)} %get-tuple-element.65), channel_id=1, source_target_pairs={{1,2},{2,1},{3,4},{4,3},{5,6},{6,5},{9,10},{10,9},{11,12},{12,11},... | collective-permute-start | bytes 221192 | tf_op jit(solution)/shard_map/ppermute | solution.py:384

commit v6 on v5

--- a/solution.py
+++ b/solution.py
@@ -214,20 +214,34 @@
         pt[i * C : (i + 1) * C, slot * 512 : (slot + 1) * 512] = t.reshape(512, C).T.astype(bf16)
 
 
-def product(grid, pos, pt, upper, cols):
+def product(core, grid, pos, pt, upper, cols):
     for s in range(2):
         _, bx, by = place(pos, s)
         for i in range(JS):
             sx = jnp.where(upper, (i + 9 - JS) // 3, i // 3)
             sy = jnp.where(upper, (i + 9 - JS) % 3, i % 3)
+            sx, sy = jnp.where(core == 0, sx, 2 - sx), jnp.where(core == 0, sy, 2 - sy)
             w = grid[pl.ds(bx * 8 + sx, 8), pl.ds(by * 8 + sy, 8)]
             cols[s * 512 : (s + 1) * 512, i * C : (i + 1) * C] = w.reshape(512, C).astype(bf16)
     return jnp.dot(pt[...], cols[...], preferred_element_type=f32)
 
 
-def pieces(y, acc, dsts, mine, upper, first, chunks):
-    for i in range(JS):
-        acc[i * 3 * C : (i + 1) * 3 * C] = y[:, i * C : (i + 1) * C]
+def pieces(core, sums, acc, dsts, mine, upper, first, chunks):
+    def block(i, oz):
+        return sums[oz * C : (oz + 1) * C, i * C : (i + 1) * C]
+
+    @pl.when(core == 0)
+    def _():
+        for i in range(JS):
+            for oz in range(3):
+                acc[(3 * i + oz) * C : (3 * i + oz + 1) * C] = block(i, oz).T
+
+    @pl.when(core != 0)
+    def _():
+        for i in range(JS):
+            for oz in range(3):
+                acc[(3 * i + oz) * C : (3 * i + oz + 1) * C] = block(i, 2 - oz)
+
     size = TAPS * C // chunks
     skip = jnp.where(upper, (9 - JS) * 3 * C, 0)
     p = first
@@ -253,11 +267,11 @@
 
     for s in range(2):
         shifted(pt, s, jnp.where(core == 0, pre[s], hid[s]))
-    part[...] = product(grid, pos, pt, sends_upper(meta[1], chunks), cols)
+    part[...] = product(core, grid, pos, pt, sends_upper(meta[1], chunks), cols)
 
 
 def send_body(
-    ppos, meta, other, msg, gain_part, part, grid, pt, out_b, out_a, gsum, cols, acc, *, chunks
+    ppos, meta, other, msg, gain_part, part, grid, pt, out_b, out_a, gsum, cols, sums, acc, *, chunks
 ):
     theirs, at = [], P_ROWS
     for rows in FACES:
@@ -267,17 +281,18 @@
     for s in range(2):
         shifted(pt, s, msg[s * 512 : (s + 1) * 512])
     upper = sends_upper(meta[1], chunks)
-    y = part[...] + product(grid, ppos, pt, upper, cols)
-    pieces(y, acc, (out_b, out_a), meta[1], upper, chunks // 2, chunks)
+    sums[...] = part[...] + product(meta[0], grid, ppos, pt, upper, cols)
+    pieces(meta[0], sums, acc, (out_b, out_a), meta[1], upper, chunks // 2, chunks)
     tile = msg[1024:P_ROWS].astype(f32)
     total = gain_part[0:1] + ((tile[2:3] + tile[1:2]) + tile[0:1])
     gsum[...] = jnp.broadcast_to(total, (8, C))
 
 
-def keep_body(pos, ppos, meta, grid_a, grid_b, pt_a, pt_b, keep_b, keep_a, cols_a, cols_b, acc, *, chunks):
+def keep_body(pos, ppos, meta, grid_a, grid_b, pt_a, pt_b, keep_b, keep_a, cols_a, cols_b, sums, acc, *, chunks):
     upper = jnp.logical_not(sends_upper(meta[1], chunks))
-    y = product(grid_a, pos, pt_a, upper, cols_a) + product(grid_b, ppos, pt_b, upper, cols_b)
-    pieces(y, acc, (keep_b, keep_a), meta[1], upper, 0, chunks)
+    sums[...] = product(meta[0], grid_a, pos, pt_a, upper, cols_a)
+    sums[...] += product(meta[0], grid_b, ppos, pt_b, upper, cols_b)
+    pieces(meta[0], sums, acc, (keep_b, keep_a), meta[1], upper, 0, chunks)
 
 
 def pack3(v):
@@ -287,10 +302,20 @@
 
 
 def seal_body(low, g, out):
-    hi, mid, rest = split3(g[0:1])
+    v = low[...].astype(bf16).astype(f32)
+    squares = jnp.sum(jnp.sum((v * v).reshape(-1, 8, C), axis=0), axis=0, keepdims=True)
     row = lax.broadcasted_iota(jnp.int32, (8, C), 0)
-    tile = jnp.where(row == 0, hi, jnp.where(row == 1, mid, jnp.where(row == 2, rest, 0.0)))
-    out[...] = jnp.concatenate([low[...], tile]).astype(bf16)
+    tile = jnp.zeros((8, C), f32)
+    for i, part in enumerate((*split3(g[0:1]), *split3(squares))):
+        tile = jnp.where(row == i, part, tile)
+    out[...] = jnp.concatenate([v, tile]).astype(bf16)
+
+
+def tiles_body(pieces, out):
+    n = out.shape[0] // 8
+    step = pieces.shape[0] // n
+    for i in range(n):
+        out[i * 8 : (i + 1) * 8] = pieces[(i + 1) * step - 8 : (i + 1) * step]
 
 
 def join_body(*refs):
@@ -306,74 +331,59 @@
     return out
 
 
-def collect(core, sources, mine, theirs, joined, squares, gains, first_piece, chunks):
-    size = TAPS * C // chunks
-    for own in (0, 1):
-
-        @pl.when(core == own)
-        def _():
-            for k in (0, 1):
-                srcs, me = (sources[0], mine) if k == own else (sources[1], theirs)
-                p = first_piece
-                for src in srcs:
-                    joined[k][p * (size + 8) : p * (size + 8) + src.shape[0]] = src[...]
-                    for q in range(src.shape[0] // (size + 8)):
-                        v = src[q * (size + 8) : (q + 1) * (size + 8)].astype(f32)
-                        cube = v[:size].reshape(size // 8, 8, C)
-                        squares[k, me ^ p] = jnp.sum(cube * cube, axis=0)
-                        if k == 0:
-                            t = v[size:]
-                            gains[me ^ p] = jnp.broadcast_to((t[2:3] + t[1:2]) + t[0:1], (8, C))
-                        p += 1
-
-
-def gathered_body(meta, o0, o1, o2, p0, p1, p2, first, second, squares, gains, *, chunks):
-    collect(
-        meta[0], ((o0, o1, o2), (p0, p1, p2)), meta[1], meta[2], (first, second), squares, gains, 0, chunks
-    )
-
-
-def final_body(
-    meta, o3, p3, first_in, second_in, squares_in, gains_in,
-    k_out, g_out, first, second, squares, gains, stage, sems, *, chunks
+def put(pieces, k, me, first, shrink, stage, sems, out, copies):
+    size = stage.shape[1]
+    for src in pieces:
+        for q in range(src.shape[0] // (size + 8)):
+            n = len(copies)
+            v = src[q * (size + 8) : (q + 1) * (size + 8)].astype(f32)
+            stage[n] = v[:size] * shrink
+            rows = pl.ds(pl.multiple_of((me ^ (first + q)) * size, 8), size)
+            copies.append(pltpu.make_async_copy(stage.at[n], out.at[k, rows], sems.at[n]))
+            copies[-1].start()
+        first += src.shape[0] // (size + 8)
+
+
+def gathered_body(
+    meta, o0, o1, o2, o3, p0, p1, p2, p3, k_out, g_out, shrink_out, gains, squares, stage, g_stage, sems, *, chunks
 ):
     core, mine, theirs = meta[0], meta[1], meta[2]
     n = TAPS * C
-    size = n // chunks
-    collect(
-        core, ((o3,), (p3,)), mine, theirs, (first, second), squares, gains, chunks // 4 * 3, chunks
-    )
-    g = jnp.sum(gains[...], axis=0)[0:1]
-    total = jnp.sum(g * g) + jnp.sum(jnp.sum(squares[...].reshape(2 * chunks, 8, C), axis=0))
+    step = n // chunks + 8
+    for k, me, pieces, tiles in (
+        (core, mine, (o0, o1, o2), o3), (1 - core, theirs, (p0, p1, p2), p3)
+    ):
+        quarter = chunks // 4
+        for p in range(chunks):
+            q = p % quarter
+            ref, at = (tiles, q * 8) if p >= 3 * quarter else (pieces[p // quarter], (q + 1) * step - 8)
+            t = ref[at : at + 8].astype(f32)
+            gains[k, me ^ p] = jnp.broadcast_to((t[2:3] + t[1:2]) + t[0:1], (8, C))
+            squares[k, me ^ p] = jnp.broadcast_to((t[5:6] + t[4:5]) + t[3:4], (8, C))
+    g = jnp.sum(gains[0], axis=0)[0:1]
+    total = jnp.sum(g * g) + jnp.sum(jnp.sum(squares[...].reshape(2 * chunks, 8, C), axis=0)[0:1])
     entries = 2.0 * n * C + C
     norm = jnp.full((8, C), total / entries + 1e-06, f32)
-    shrink = jnp.minimum(1.0, clip_level / jnp.sqrt(norm))[0:1]
-    g_out[...] = g * shrink
-
-    def tap(joined, me, t):
-        parts, row = [], t * C
-        while row < (t + 1) * C:
-            chunk, at = row // size, row % size
-            rows = min(size - at, (t + 1) * C - row)
-            start = pl.multiple_of((me ^ chunk) * (size + 8) + at, 8)
-            parts.append(joined[pl.ds(start, rows)].astype(f32))
-            row += rows
-        return jnp.concatenate(parts) if len(parts) > 1 else parts[0]
-
+    shrink = jnp.minimum(1.0, clip_level / jnp.sqrt(norm))
+    shrink_out[...] = shrink
+    g_stage[...] = g * shrink[0:1]
+    copy = pltpu.make_async_copy(g_stage, g_out, sems.at[stage.shape[0]])
+    copy.start()
     copies = []
-    for k, joined in ((1, second), (0, first)):
-        me = jnp.where(core == k, mine, theirs)
-        for part in range(3):
-            for t in range(part * 9, part * 9 + 9):
-                v = tap(joined, me, t if k == 0 else TAPS - 1 - t)
-                stage[k, t] = (v.T if k == 0 else v) * shrink
-            block = (k, pl.ds(part * 9, 9))
-            copies.append(
-                pltpu.make_async_copy(stage.at[block], k_out.at[block], sems.at[len(copies)])
-            )
-            copies[-1].start()
-    for copy in copies:
-        copy.wait()
+    put((o0, o1, o2), core, mine, 0, shrink[0:1], stage, sems, k_out, copies)
+    put((p0, p1, p2), 1 - core, theirs, 0, shrink[0:1], stage, sems, k_out, copies)
+    for c in (copy, *copies):
+        c.wait()
+
+
+def final_body(meta, o3, p3, shrink, k_in, k_out, stage, sems, *, chunks):
+    core, mine, theirs = meta[0], meta[1], meta[2]
+    first = chunks // 4 * 3
+    copies = []
+    put((o3,), core, mine, first, shrink[0:1], stage, sems, k_out, copies)
+    put((p3,), 1 - core, theirs, first, shrink[0:1], stage, sems, k_out, copies)
+    for c in copies:
+        c.wait()
 
 
 def across(a, b, axis):
@@ -487,7 +497,7 @@
     grid_b, pt_b, out_b, out_a, g = call(
         functools.partial(send_body, chunks=chunks),
         held + quarter + [sds((8, C), f32)],
-        [wide, acc],
+        [wide, pltpu.VMEM((3 * C, JS * C), f32), acc],
         (ppos, meta, other, pmsg, gain_part, part),
         2,
         10,
@@ -495,7 +505,7 @@
     keep_b, keep_a = call(
         functools.partial(keep_body, chunks=chunks),
         [sds((n // 4, C), f32)] * 2,
-        [wide, wide, acc],
+        [wide, wide, pltpu.VMEM((3 * C, JS * C), f32), acc],
         (brick_pos, ppos, meta, grid_a, grid_b, pt_a, pt_b),
         3,
         12,
@@ -553,29 +563,49 @@
     own = [full]
     own.append(swap(full, steps[1]))
     own.append(swap(full, steps[0]))
+    (tiles,) = call(tiles_body, [sds((chunks // 4 * 8, C), bf16)], [], (full,), 0)
+    far = swap(tiles, tuple(a ^ b for a, b in zip(*steps[:2])))
+    far_part = lax.ppermute(far, "gy", partner)
     own.append(swap(own[1], steps[0]))
     part = [lax.ppermute(v, "gy", partner) for v in own]
-    rows = chunks * (size + 8)
-    gathered = [
-        sds((rows, C), bf16), sds((rows, C), bf16), sds((2, chunks, 8, C), f32), sds((chunks, 8, C), f32)
-    ]
-    held = call(
-        functools.partial(gathered_body, chunks=chunks),
-        gathered,
+    any_space = pl.BlockSpec(memory_space=pl.ANY)
+
+    def pieces_call(body, count, outs, out_specs, scratch, args, in_specs, aliases):
+        return pl.pallas_call(
+            functools.partial(body, chunks=chunks),
+            out_shape=outs,
+            in_specs=[SMEM] + in_specs,
+            out_specs=out_specs,
+            scratch_shapes=scratch
+            + [pltpu.VMEM((count, size, C), f32)]
+            + ([pltpu.VMEM((1, C), f32)] if scratch else [])
+            + [pltpu.SemaphoreType.DMA((count + 1,))],
+            input_output_aliases=aliases,
+            compiler_params=pltpu.CompilerParams(vmem_limit_bytes=8 << 20),
+        )(meta, *args)
+
+    table = pltpu.VMEM((2, chunks, 8, C), f32)
+    k_up, g_up, shrink = pieces_call(
+        gathered_body,
+        chunks // 2 * 3,
+        [sds((2, n, C), f32), sds((1, C), f32), sds((8, C), f32)],
+        [any_space, any_space, VMEM],
+        [table, table],
+        (*own[:3], far, *part[:3], far_part),
+        [VMEM] * 8,
+        {},
+    )
+    (k_up,) = pieces_call(
+        final_body,
+        chunks // 2,
+        [sds((2, n, C), f32)],
+        [any_space],
         [],
-        (meta, *own[:3], *part[:3]),
-        1,
-    )
-    k_up, g_up = pl.pallas_call(
-        functools.partial(final_body, chunks=chunks),
-        out_shape=[sds((2, TAPS, C, C), f32), sds((1, C), f32), *gathered],
-        in_specs=[SMEM] + [VMEM] * 6,
-        out_specs=[pl.BlockSpec(memory_space=pl.ANY)] + [VMEM] * 5,
-        scratch_shapes=[pltpu.VMEM((2, TAPS, C, C), f32), pltpu.SemaphoreType.DMA((6,))],
-        input_output_aliases={3: 2, 4: 3, 5: 4, 6: 5},
-        compiler_params=pltpu.CompilerParams(vmem_limit_bytes=10 << 20),
-    )(meta, own[3], part[3], *held)[:2]
-    return (*results, k_up, g_up.reshape(C))
+        (own[3], part[3], shrink, k_up),
+        [VMEM] * 3 + [any_space],
+        {4: 0},
+    )
+    return (*results, k_up.reshape(2, TAPS, C, C), g_up.reshape(C))
 
 
 def solution(mesh):

time: 96.4 us -> 97.7 us (1.013)
  starting transfers between devices: 37.5 us -> 39.4 us
    ppermute x4, waiting for transfers between devices: 11.1 us -> 6.98 us  [across(): b = lax.ppermute(b, axis, odd)]
    ppermute x12 -> x13, waiting for transfers between devices: 18.3 us -> 21.8 us  [per_device(): swap = lambda v, dx, dy=0: lax.ppermute(v, both, pairs(dx, dy))]
    ppermute x4, starting transfers between devices: 11.8 us -> 8.44 us  [per_device(): part = [lax.ppermute(v, 'gy', partner) for v in own]]
    ppermute x4, starting transfers between devices: 11.2 us -> 13.5 us  [across(): b = lax.ppermute(b, axis, odd)]
    ppermute x0 -> x1, starting transfers between devices: none -> 1.5 us  [per_device(): far_part = lax.ppermute(far, 'gy', partner)]
    ppermute x4, starting transfers between devices: 3.76 us -> 5.1 us  [across(): a = lax.ppermute(a, axis, even)]
    pallas_call x1 -> x2, Pallas kernels: 3.27 us -> 4.03 us  [pieces_call(): pl.pallas_call(functools.partial(body, chunks=chunks), out_shape=outs, in...]
    ppermute x12 -> x13, starting transfers between devices: 9.49 us -> 9.66 us  [per_device(): swap = lambda v, dx, dy=0: lax.ppermute(v, both, pairs(dx, dy))]
  transfers between devices with their start and end apart: 27 -> 29, of which waited for: 12 -> 12; matrix products, arithmetic and copies ran while one was open for 0% -> 0% of each run, Pallas kernels for 17% -> 18%
where the time goes in v6:
time: 97.7 us; the launch traced here: 97.3 us
  starting transfers between devices  39.4 us (40%)
  waiting for transfers between devices  29.7 us (30%)
  Pallas kernels  26.9 us (28%)
  between operations  1.09 us (1%)
    pallas_call x14, Pallas kernels, call(): pl.pallas_call(body, out_shape=outs, in_specs=[SMEM] * n_smem + [VMEM] *...  22.8 us
    ppermute x13, waiting for transfers between devices, per_device(): swap = lambda v, dx, dy=0: lax.ppermute(v, both, pairs(dx, dy))  21.8 us
    ppermute x4, starting transfers between devices, across(): b = lax.ppermute(b, axis, odd)  13.5 us
    ppermute x13, starting transfers between devices, per_device(): swap = lambda v, dx, dy=0: lax.ppermute(v, both, pairs(dx, dy))  9.66 us
    ppermute x4, starting transfers between devices, per_device(): part = [lax.ppermute(v, 'gy', partner) for v in own]  8.44 us
    ppermute x4, waiting for transfers between devices, across(): b = lax.ppermute(b, axis, odd)  6.98 us
    ppermute x4, starting transfers between devices, across(): a = lax.ppermute(a, axis, even)  5.1 us
    pallas_call x2, Pallas kernels, pieces_call(): pl.pallas_call(functools.partial(body, chunks=chunks), out_shape=outs, in...  4.03 us
  transfers between devices with their start and end apart: 29, of which 12 were waited for; matrix products, arithmetic and copies ran while one was open for 0% of the time, Pallas kernels for 18%

profile of v6, /device:TPU:21, one launch (start us, length us, event | category | flops | bytes accessed | tf_op | source)
XLA Modules:
  0.0 97.3 jit_solution(687287906052702293)
XLA Ops:
  0.7 1.3 %shard_map.93 = (bf16[2,512,128]{2,1,0:T(8,128)(2,1)S(1)}, bf16[2,512,128]{2,1,0:T(8,128)(2,1)S(1)}, bf16[2,512,128]{2,1,0:T(8,128)(2,1)S(1)}, bf16[2,128,128]{2,1,0:T(8,128)(2,1)S(1)}, bf16[2,128,128]{2,1,0:T(8,128)(2,1)S(1)}) custom-call(s32[2]{0:T(128)} %pos.17, s32[1]{0:T(128)} %bitcast.core, s32[1]{0:T(128)} %bitcast.3.odd, bf16[2,512,128]{2,1,0:T(8,128)(2,1)} %a.1, ...), custom_call_target="tpu_custom_call" | custom-call | tf_op jit(solution)/shard_map/pallas_call | solution.py:34
  2.0 0.7 collective-permute-start.3
  2.8 1.2 %collective-permute-start = (bf16[2,128,128]{2,1,0:T(8,128)(2,1)S(1)}, bf16[2,128,128]{2,1,0:T(8,128)(2,1)S(1)}, u32[]{:S(2)}, u32[]{:S(2)}) collective-permute-start(bf16[2,128,128]{2,1,0:T(8,128)(2,1)S(1)} %get-tuple-element.42), channel_id=1, source_target_pairs={{0,8},{8,0},{16,24},{24,16},{1,9},{9,1},{17,25},{25,17},{2,10},{10... | collective-permute-start | bytes 196616 | tf_op jit(solution)/shard_map/ppermute | solution.py:395
  4.0 2.1 %collective-permute-start.1 = (bf16[2,128,128]{2,1,0:T(8,128)(2,1)S(1)}, bf16[2,128,128]{2,1,0:T(8,128)(2,1)S(1)}, u32[]{:S(2)}, u32[]{:S(2)}) collective-permute-start(bf16[2,128,128]{2,1,0:T(8,128)(2,1)S(1)} %get-tuple-element.43), channel_id=1, source_target_pairs={{8,16},{16,8},{9,17},{17,9},{10,18},{18,10},{11,19},{19,11},{12,20... | collective-permute-start | bytes 196616 | tf_op jit(solution)/shard_map/ppermute | solution.py:394
  6.1 2.0 %shard_map.94 = (bf16[1152,384]{1,0:T(8,128)(2,1)S(1)}, bf16[1152,384]{1,0:T(8,128)(2,1)S(1)}, bf16[384,1152]{1,0:T(8,128)(2,1)S(1)}, bf16[384,1152]{1,0:T(8,128)(2,1)S(1)}, f32[1,128]{1,0:T(1,128)S(1)}) custom-call(bf16[27,128,128]{2,1,0:T(8,128)(2,1)} %k1.1, bf16[27,128,128]{2,1,0:T(8,128)(2,1)} %k2.1, f32[1,128]{1,0:T(1,128)} %bitcast.8), custom_call_target="tpu_custom_call" | custom-call | tf_op jit(solution)/shard_map/pallas_call | solution.py:34
  8.1 0.1 pad_add_fusion.meta
  8.2 1.7 %collective-permute-done.1.xb = bf16[2,128,128]{2,1,0:T(8,128)(2,1)S(1)} collective-permute-done((bf16[2,128,128]{2,1,0:T(8,128)(2,1)S(1)}, bf16[2,128,128]{2,1,0:T(8,128)(2,1)S(1)}, u32[]{:S(2)}, u32[]{:S(2)}) %collective-permute-start.1) | collective-permute-done | bytes 65568 | tf_op jit(solution)/shard_map/ppermute | solution.py:394
  9.9 0.8 shard_map.95
  10.7 4.9 %collective-permute-start.5 = (bf16[2,144,128]{2,1,0:T(8,128)(2,1)S(1)}, bf16[2,144,128]{2,1,0:T(8,128)(2,1)S(1)}, u32[]{:S(2)}, u32[]{:S(2)}) collective-permute-start(bf16[2,144,128]{2,1,0:T(8,128)(2,1)S(1)} %get-tuple-element.49), channel_id=1, source_target_pairs={{1,2},{2,1},{3,4},{4,3},{5,6},{6,5},{9,10},{10,9},{11,12},{12,11},... | collective-permute-start | bytes 221192 | tf_op jit(solution)/shard_map/ppermute | solution.py:394
  15.8 2.1 %collective-permute-done.5.yb = bf16[2,144,128]{2,1,0:T(8,128)(2,1)S(1)} collective-permute-done((bf16[2,144,128]{2,1,0:T(8,128)(2,1)S(1)}, bf16[2,144,128]{2,1,0:T(8,128)(2,1)S(1)}, u32[]{:S(2)}, u32[]{:S(2)}) %collective-permute-start.5) | collective-permute-done | bytes 73760 | tf_op jit(solution)/shard_map/ppermute | solution.py:394
  17.9 4.6 %shard_map.96 = (bf16[2,512,128]{2,1,0:T(8,128)(2,1)S(1)}, bf16[2,512,128]{2,1,0:T(8,128)(2,1)S(1)}, bf16[1584,128]{1,0:T(8,128)(2,1)S(1)}, f32[8,128]{1,0:T(8,128)S(1)}) custom-call(s32[2]{0:T(128)} %pos.17, s32[4]{0:T(128)S(1)} %pad_add_fusion.meta, bf16[2,512,128]{2,1,0:T(8,128)(2,1)S(1)} %get-tuple-element.45.a.base, ...), custom_call_target="tpu_custom_call" | custom-call | tf_op jit(solution)/shard_map/pallas_call | solution.py:34
  22.4 0.4 collective-permute-start.6
  22.9 1.8 %shard_map.97 = (f32[18,18,8,128]{3,2,1,0:T(8,128)S(1)}, bf16[384,1024]{1,0:T(8,128)(2,1)S(1)}, f32[384,640]{1,0:T(8,128)S(1)}) custom-call(s32[2]{0:T(128)} %pos.17, s32[4]{0:T(128)S(1)} %pad_add_fusion.meta, bf16[2,512,128]{2,1,0:T(8,128)(2,1)S(1)} %get-tuple-element.45.a.base, bf16[2,512,128]{2,1,0:T(8,128)(2,1)S(1)} %get-tuple-element.41.b.base, ...), custom_call_target="tpu_custom_call" | custom-call | tf_op jit(solution)/shard_map/pallas_call | solution.py:34
  24.7 1.7 %shard_map.98 = (f32[18,18,8,128]{3,2,1,0:T(8,128)S(1)}, bf16[384,1024]{1,0:T(8,128)(2,1)S(1)}, bf16[864,128]{1,0:T(8,128)(2,1)S(1)}, bf16[864,128]{1,0:T(8,128)(2,1)S(1)}, f32[8,128]{1,0:T(8,128)S(1)}) custom-call(s32[2]{0:T(128)S(1)} %collective-permute-done.2.ppos, s32[4]{0:T(128)S(1)} %pad_add_fusion.meta, ...), custom_call_target="tpu_custom_call" | custom-call | tf_op jit(solution)/shard_map/pallas_call | solution.py:34
  26.5 1.5 %collective-permute-start.11 = (bf16[864,128]{1,0:T(8,128)(2,1)S(1)}, bf16[864,128]{1,0:T(8,128)(2,1)S(1)}, u32[]{:S(2)}, u32[]{:S(2)}) collective-permute-start(bf16[864,128]{1,0:T(8,128)(2,1)S(1)} %get-tuple-element.70), channel_id=1, source_target_pairs={{0,8},{1,17},{2,10},{3,19},{4,12},{5,21},{6,14},{7,23},{8,0},{9,25... | collective-permute-start | bytes 663560 | tf_op jit(solution)/shard_map/ppermute | solution.py:537
  28.0 2.4 %shard_map.103 = (f32[864,128]{1,0:T(8,128)S(1)}, f32[864,128]{1,0:T(8,128)S(1)}) custom-call(s32[2]{0:T(128)} %pos.17, s32[2]{0:T(128)S(1)} %collective-permute-done.2.ppos, s32[4]{0:T(128)S(1)} %pad_add_fusion.meta, f32[18,18,8,128]{3,2,1,0:T(8,128)S(1)} %get-tuple-element.65.grid_a, f32[18,18,8,128]{3,2,1,0:T(8,128)S(1)} %get-tuple-element.66.grid_b, ...), custom_call_target="tpu_custom_call" | custom-call | tf_op jit(solution)/shard_map/pallas_call | solution.py:34
  30.3 1.2 %collective-permute-done.12 = bf16[864,128]{1,0:T(8,128)(2,1)S(1)} collective-permute-done((bf16[864,128]{1,0:T(8,128)(2,1)S(1)}, bf16[864,128]{1,0:T(8,128)(2,1)S(1)}, u32[]{:S(2)}, u32[]{:S(2)}) %collective-permute-start.12) | collective-permute-done | bytes 221216 | tf_op jit(solution)/shard_map/ppermute | solution.py:537
  31.7 2.2 %collective-permute-done.11 = bf16[864,128]{1,0:T(8,128)(2,1)S(1)} collective-permute-done((bf16[864,128]{1,0:T(8,128)(2,1)S(1)}, bf16[864,128]{1,0:T(8,128)(2,1)S(1)}, u32[]{:S(2)}, u32[]{:S(2)}) %collective-permute-start.11) | collective-permute-done | bytes 221216 | tf_op jit(solution)/shard_map/ppermute | solution.py:537
  34.0 3.2 %collective-permute-done.13 = bf16[864,128]{1,0:T(8,128)(2,1)S(1)} collective-permute-done((bf16[864,128]{1,0:T(8,128)(2,1)S(1)}, bf16[864,128]{1,0:T(8,128)(2,1)S(1)}, u32[]{:S(2)}, u32[]{:S(2)}) %collective-permute-start.13) | collective-permute-done | bytes 221216 | tf_op jit(solution)/shard_map/ppermute | solution.py:537
  37.2 0.1 fusion.2
  37.3 1.2 %collective-permute-start.15 = (f32[216,128]{1,0:T(8,128)S(1)}, f32[216,128]{1,0:T(8,128)S(1)}, u32[]{:S(2)}, u32[]{:S(2)}) collective-permute-start(f32[216,128]{1,0:T(8,128)S(1)} %slice.24), channel_id=1, source_target_pairs={{0,2},{1,3},{2,0},{3,1},{4,6},{5,7},{6,4},{7,5},{8,10},{9,11},{10,... | collective-permute-start | bytes 331784 | tf_op jit(solution)/shard_map/ppermute | solution.py:537
  38.5 0.2 collective-permute-start.14
  38.8 1.3 %collective-permute-start.16 = (bf16[216,128]{1,0:T(8,128)(2,1)S(1)}, bf16[216,128]{1,0:T(8,128)(2,1)S(1)}, u32[]{:S(2)}, u32[]{:S(2)}) collective-permute-start(bf16[216,128]{1,0:T(8,128)(2,1)S(1)} %get-tuple-element.79), channel_id=1, source_target_pairs={{0,6},{1,7},{2,4},{3,5},{4,2},{5,3},{6,0},{7,1},{8,14},{9,15},{10,... | collective-permute-start | bytes 165896 | tf_op jit(solution)/shard_map/ppermute | solution.py:537
  40.1 3.0 %collective-permute-done.14 = bf16[216,128]{1,0:T(8,128)(2,1)S(1)} collective-permute-done((bf16[216,128]{1,0:T(8,128)(2,1)S(1)}, bf16[216,128]{1,0:T(8,128)(2,1)S(1)}, u32[]{:S(2)}, u32[]{:S(2)}) %collective-permute-start.14) | collective-permute-done | bytes 55328 | tf_op jit(solution)/shard_map/ppermute | solution.py:537
  43.2 0.6 collective-permute-start.19
  43.8 3.9 %collective-permute-start.18 = (bf16[224,128]{1,0:T(8,128)(2,1)S(1)}, bf16[224,128]{1,0:T(8,128)(2,1)S(1)}, u32[]{:S(2)}, u32[]{:S(2)}) collective-permute-start(bf16[224,128]{1,0:T(8,128)(2,1)S(1)} %shard_map.104.refs_0_), channel_id=1, source_target_pairs={{0,2},{1,3},{2,0},{3,1},{4,6},{5,7},{6,4},{7,5},{8,10},{9,11},{10,... | collective-permute-start | bytes 172040 | tf_op jit(solution)/shard_map/ppermute | solution.py:537
  47.7 2.2 %collective-permute-done.18.refs_2_ = bf16[224,128]{1,0:T(8,128)(2,1)S(1)} collective-permute-done((bf16[224,128]{1,0:T(8,128)(2,1)S(1)}, bf16[224,128]{1,0:T(8,128)(2,1)S(1)}, u32[]{:S(2)}, u32[]{:S(2)}) %collective-permute-start.18) | collective-permute-done | bytes 57376 | tf_op jit(solution)/shard_map/ppermute | solution.py:537
  49.9 2.3 %collective-permute-done.17.refs_1_ = bf16[224,128]{1,0:T(8,128)(2,1)S(1)} collective-permute-done((bf16[224,128]{1,0:T(8,128)(2,1)S(1)}, bf16[224,128]{1,0:T(8,128)(2,1)S(1)}, u32[]{:S(2)}, u32[]{:S(2)}) %collective-permute-start.17) | collective-permute-done | bytes 57376 | tf_op jit(solution)/shard_map/ppermute | solution.py:537
  52.3 0.5 collective-permute-start.23
  52.8 4.4 %collective-permute-done.20.o1 = bf16[896,128]{1,0:T(8,128)(2,1)S(1)} collective-permute-done((bf16[896,128]{1,0:T(8,128)(2,1)S(1)}, bf16[896,128]{1,0:T(8,128)(2,1)S(1)}, u32[]{:S(2)}, u32[]{:S(2)}) %collective-permute-start.20) | collective-permute-done | bytes 229408 | tf_op jit(solution)/shard_map/ppermute | solution.py:537
  57.1 0.8 shard_map.99
  57.9 0.6 collective-permute-start.7
  58.5 4.0 %collective-permute-start.8 = (bf16[2,128,128]{2,1,0:T(8,128)(2,1)S(1)}, bf16[2,128,128]{2,1,0:T(8,128)(2,1)S(1)}, u32[]{:S(2)}, u32[]{:S(2)}) collective-permute-start(bf16[2,128,128]{2,1,0:T(8,128)(2,1)S(1)} %get-tuple-element.60), channel_id=1, source_target_pairs={{8,16},{16,8},{9,17},{17,9},{10,18},{18,10},{11,19},{19,11},{12,20... | collective-permute-start | bytes 196616 | tf_op jit(solution)/shard_map/ppermute | solution.py:394
  62.6 7.0 %collective-permute-start.25 = (bf16[896,128]{1,0:T(8,128)(2,1)S(1)}, bf16[896,128]{1,0:T(8,128)(2,1)S(1)}, u32[]{:S(2)}, u32[]{:S(2)}) collective-permute-start(bf16[896,128]{1,0:T(8,128)(2,1)S(1)} %shard_map.105.pieces.o0), channel_id=1, source_target_pairs={{0,1},{1,0},{2,3},{3,2},{4,5},{5,4},{6,7},{7,6},{8,9},{9,8},{10,11... | collective-permute-start | bytes 688136 | tf_op jit(solution)/shard_map/ppermute | solution.py:570
  69.6 0.1 collective-permute-start.27
  69.7 1.3 %collective-permute-start.26 = (bf16[896,128]{1,0:T(8,128)(2,1)S(1)}, bf16[896,128]{1,0:T(8,128)(2,1)S(1)}, u32[]{:S(2)}, u32[]{:S(2)}) collective-permute-start(bf16[896,128]{1,0:T(8,128)(2,1)S(1)} %collective-permute-done.20.o1), channel_id=1, source_target_pairs={{0,1},{1,0},{2,3},{3,2},{4,5},{5,4},{6,7},{7,6},{8,9},{9,8},{10,11... | collective-permute-start | bytes 688136 | tf_op jit(solution)/shard_map/ppermute | solution.py:570
  71.0 0.8 shard_map.100
  71.9 3.2 %collective-permute-start.9 = (bf16[2,144,128]{2,1,0:T(8,128)(2,1)S(1)}, bf16[2,144,128]{2,1,0:T(8,128)(2,1)S(1)}, u32[]{:S(2)}, u32[]{:S(2)}) collective-permute-start(bf16[2,144,128]{2,1,0:T(8,128)(2,1)S(1)} %get-tuple-element.61), channel_id=1, source_target_pairs={{0,1},{1,0},{2,3},{3,2},{4,5},{5,4},{6,7},{7,6},{8,9},{9,8},{10,11... | collective-permute-start | bytes 221192 | tf_op jit(solution)/shard_map/ppermute | solution.py:395
  75.1 0.9 collective-permute-done.9.ya
  76.0 2.4 %collective-permute-start.10 = (bf16[2,144,128]{2,1,0:T(8,128)(2,1)S(1)}, bf16[2,144,128]{2,1,0:T(8,128)(2,1)S(1)}, u32[]{:S(2)}, u32[]{:S(2)}) collective-permute-start(bf16[2,144,128]{2,1,0:T(8,128)(2,1)S(1)} %get-tuple-element.62), channel_id=1, source_target_pairs={{1,2},{2,1},{3,4},{4,3},{5,6},{6,5},{9,10},{10,9},{11,12},{12,11},... | collective-permute-start | bytes 221192 | tf_op jit(solution)/shard_map/ppermute | solution.py:394
  78.5 3.2 %collective-permute-done.10.yb = bf16[2,144,128]{2,1,0:T(8,128)(2,1)S(1)} collective-permute-done((bf16[2,144,128]{2,1,0:T(8,128)(2,1)S(1)}, bf16[2,144,128]{2,1,0:T(8,128)(2,1)S(1)}, u32[]{:S(2)}, u32[]{:S(2)}) %collective-permute-start.10) | collective-permute-done | bytes 73760 | tf_op jit(solution)/shard_map/ppermute | solution.py:394
  81.7 0.2 collective-permute-start.24
  81.9 3.2 %collective-permute-done.24.o3 = bf16[32,128]{1,0:T(8,128)(2,1)S(1)} collective-permute-done((bf16[32,128]{1,0:T(8,128)(2,1)S(1)}, bf16[32,128]{1,0:T(8,128)(2,1)S(1)}, u32[]{:S(2)}, u32[]{:S(2)}) %collective-permute-start.24) | collective-permute-done | bytes 8224 | tf_op jit(solution)/shard_map/ppermute | solution.py:537
  85.1 1.5 %collective-permute-start.28 = (bf16[32,128]{1,0:T(8,128)(2,1)S(1)}, bf16[32,128]{1,0:T(8,128)(2,1)S(1)}, u32[]{:S(2)}, u32[]{:S(2)}) collective-permute-start(bf16[32,128]{1,0:T(8,128)(2,1)S(1)} %collective-permute-done.24.o3), channel_id=1, source_target_pairs={{0,1},{1,0},{2,3},{3,2},{4,5},{5,4},{6,7},{7,6},{8,9},{9,8},{10,11... | collective-permute-start | bytes 24584 | tf_op jit(solution)/shard_map/ppermute | solution.py:568
  86.6 3.4 %shard_map.102 = bf16[2,512,128]{2,1,0:T(8,128)(2,1)} custom-call(s32[2]{0:T(128)} %pos.17, s32[4]{0:T(128)S(1)} %pad_add_fusion.meta, bf16[2,512,128]{2,1,0:T(8,128)(2,1)S(1)} %get-tuple-element.55.pre.b.src, bf16[2,128,128]{2,1,0:T(8,128)(2,1)S(1)} %collective-permute-done.7.xa, bf16[2,128,128]{2,1,0:T(8,128)(2,1)S(1)} %collective-permute-done.8.xb, ...), custom_call_target="tpu_custom_call" | custom-call | tf_op jit(solution)/shard_map/pallas_call | solution.py:34
  90.0 3.2 %shard_map.101 = bf16[2,512,128]{2,1,0:T(8,128)(2,1)} custom-call(s32[2]{0:T(128)} %pos.17, s32[4]{0:T(128)S(1)} %pad_add_fusion.meta, bf16[2,512,128]{2,1,0:T(8,128)(2,1)S(1)} %get-tuple-element.58.hid.a.src, bf16[2,128,128]{2,1,0:T(8,128)(2,1)S(1)} %collective-permute-done.7.xa, bf16[2,128,128]{2,1,0:T(8,128)(2,1)S(1)} %collective-permute-done.8.xb, ...), custom_call_target="tpu_custom_call" | custom-call | tf_op jit(solution)/shard_map/pallas_call | solution.py:34
  93.1 2.5 %shard_map.107 = (f32[2,3456,128]{2,1,0:T(8,128)}, f32[1,128]{1,0:T(1,128)}, f32[8,128]{1,0:T(8,128)S(1)}) custom-call(s32[4]{0:T(128)S(1)} %pad_add_fusion.meta, bf16[896,128]{1,0:T(8,128)(2,1)S(1)} %shard_map.105.pieces.o0, bf16[896,128]{1,0:T(8,128)(2,1)S(1)} %collective-permute-done.20.o1, bf16[896,128]{1,0:T(8,128)(2,1)S(1)} %collective-permute-done.23.o2, ...), custom_call_target="tpu_custom_call" | custom-call | tf_op jit(solution)/shard_map/pallas_call | solution.py:574
  95.7 1.5 %shard_map.108 = f32[2,3456,128]{2,1,0:T(8,128)} custom-call(s32[4]{0:T(128)S(1)} %pad_add_fusion.meta, bf16[896,128]{1,0:T(8,128)(2,1)S(1)} %collective-permute-done.21.o3, bf16[896,128]{1,0:T(8,128)(2,1)S(1)} %collective-permute-done.22.p3, f32[8,128]{1,0:T(8,128)S(1)} %get-tuple-element.73.shrink, ...), custom_call_target="tpu_custom_call", output_to_operand_aliasing={{}: (4, {})} | custom-call | tf_op jit(solution)/shard_map/pallas_call | solution.py:574
  (33 shorter events, 0.6 us)
Async XLA Ops:
  2.0 13.7 %collective-permute-start.3 = (bf16[2,512,128]{2,1,0:T(8,128)(2,1)S(1)}, bf16[2,512,128]{2,1,0:T(8,128)(2,1)S(1)}, u32[]{:S(2)}, u32[]{:S(2)}) collective-permute-start(bf16[2,512,128]{2,1,0:T(8,128)(2,1)S(1)} %get-tuple-element.47), channel_id=1, source_target_pairs={{0,1},{1,0},{2,3},{3,2},{4,5},{5,4},{6,7},{7,6},{8,9},{9,8},{10,11... | collective-permute-start | bytes 786440 | tf_op jit(solution)/shard_map/ppermute | solution.py:462
  2.7 13.0 %collective-permute-start.2 = (s32[2]{0:T(128)}, s32[2]{0:T(128)S(1)}, u32[]{:S(2)}, u32[]{:S(2)}) collective-permute-start(s32[2]{0:T(128)} %pos.17), channel_id=1, source_target_pairs={{0,1},{1,0},{2,3},{3,2},{4,5},{5,4},{6,7},{7,6},{8,9},{9,8},{10,11... | collective-permute-start | bytes 32 | tf_op jit(solution)/shard_map/ppermute | solution.py:461
  2.8 5.4 %collective-permute-start = (bf16[2,128,128]{2,1,0:T(8,128)(2,1)S(1)}, bf16[2,128,128]{2,1,0:T(8,128)(2,1)S(1)}, u32[]{:S(2)}, u32[]{:S(2)}) collective-permute-start(bf16[2,128,128]{2,1,0:T(8,128)(2,1)S(1)} %get-tuple-element.42), channel_id=1, source_target_pairs={{0,8},{8,0},{16,24},{24,16},{1,9},{9,1},{17,25},{25,17},{2,10},{10... | collective-permute-start | bytes 196616 | tf_op jit(solution)/shard_map/ppermute | solution.py:395
  4.0 5.9 %collective-permute-start.1 = (bf16[2,128,128]{2,1,0:T(8,128)(2,1)S(1)}, bf16[2,128,128]{2,1,0:T(8,128)(2,1)S(1)}, u32[]{:S(2)}, u32[]{:S(2)}) collective-permute-start(bf16[2,128,128]{2,1,0:T(8,128)(2,1)S(1)} %get-tuple-element.43), channel_id=1, source_target_pairs={{8,16},{16,8},{9,17},{17,9},{10,18},{18,10},{11,19},{19,11},{12,20... | collective-permute-start | bytes 196616 | tf_op jit(solution)/shard_map/ppermute | solution.py:394
  10.7 7.1 %collective-permute-start.5 = (bf16[2,144,128]{2,1,0:T(8,128)(2,1)S(1)}, bf16[2,144,128]{2,1,0:T(8,128)(2,1)S(1)}, u32[]{:S(2)}, u32[]{:S(2)}) collective-permute-start(bf16[2,144,128]{2,1,0:T(8,128)(2,1)S(1)} %get-tuple-element.49), channel_id=1, source_target_pairs={{1,2},{2,1},{3,4},{4,3},{5,6},{6,5},{9,10},{10,9},{11,12},{12,11},... | collective-permute-start | bytes 221192 | tf_op jit(solution)/shard_map/ppermute | solution.py:394
  15.7 2.2 %collective-permute-start.4 = (bf16[2,144,128]{2,1,0:T(8,128)(2,1)S(1)}, bf16[2,144,128]{2,1,0:T(8,128)(2,1)S(1)}, u32[]{:S(2)}, u32[]{:S(2)}) collective-permute-start(bf16[2,144,128]{2,1,0:T(8,128)(2,1)S(1)} %get-tuple-element.48), channel_id=1, source_target_pairs={{0,1},{1,0},{2,3},{3,2},{4,5},{5,4},{6,7},{7,6},{8,9},{9,8},{10,11... | collective-permute-start | bytes 221192 | tf_op jit(solution)/shard_map/ppermute | solution.py:395
  22.4 2.3 %collective-permute-start.6 = (bf16[1584,128]{1,0:T(8,128)(2,1)S(1)}, bf16[1584,128]{1,0:T(8,128)(2,1)S(1)}, u32[]{:S(2)}, u32[]{:S(2)}) collective-permute-start(bf16[1584,128]{1,0:T(8,128)(2,1)S(1)} %get-tuple-element.53), channel_id=1, source_target_pairs={{0,1},{1,0},{2,3},{3,2},{4,5},{5,4},{6,7},{7,6},{8,9},{9,8},{10,11... | collective-permute-start | bytes 1216520 | tf_op jit(solution)/shard_map/ppermute | solution.py:484
  26.4 5.1 %collective-permute-start.12 = (bf16[864,128]{1,0:T(8,128)(2,1)S(1)}, bf16[864,128]{1,0:T(8,128)(2,1)S(1)}, u32[]{:S(2)}, u32[]{:S(2)}) collective-permute-start(bf16[864,128]{1,0:T(8,128)(2,1)S(1)} %get-tuple-element.57), channel_id=1, source_target_pairs={{0,8},{1,17},{2,10},{3,19},{4,12},{5,21},{6,14},{7,23},{8,0},{9,25... | collective-permute-start | bytes 663560 | tf_op jit(solution)/shard_map/ppermute | solution.py:537
  26.5 7.4 %collective-permute-start.11 = (bf16[864,128]{1,0:T(8,128)(2,1)S(1)}, bf16[864,128]{1,0:T(8,128)(2,1)S(1)}, u32[]{:S(2)}, u32[]{:S(2)}) collective-permute-start(bf16[864,128]{1,0:T(8,128)(2,1)S(1)} %get-tuple-element.70), channel_id=1, source_target_pairs={{0,8},{1,17},{2,10},{3,19},{4,12},{5,21},{6,14},{7,23},{8,0},{9,25... | collective-permute-start | bytes 663560 | tf_op jit(solution)/shard_map/ppermute | solution.py:537
  31.6 5.6 %collective-permute-start.13 = (bf16[864,128]{1,0:T(8,128)(2,1)S(1)}, bf16[864,128]{1,0:T(8,128)(2,1)S(1)}, u32[]{:S(2)}, u32[]{:S(2)}) collective-permute-start(bf16[864,128]{1,0:T(8,128)(2,1)S(1)} %add_convert_fusion), channel_id=1, source_target_pairs={{0,16},{1,9},{2,18},{3,11},{4,20},{5,13},{6,22},{7,15},{8,24},{9,1... | collective-permute-start | bytes 663560 | tf_op jit(solution)/shard_map/ppermute | solution.py:537
  37.3 5.8 %collective-permute-start.15 = (f32[216,128]{1,0:T(8,128)S(1)}, f32[216,128]{1,0:T(8,128)S(1)}, u32[]{:S(2)}, u32[]{:S(2)}) collective-permute-start(f32[216,128]{1,0:T(8,128)S(1)} %slice.24), channel_id=1, source_target_pairs={{0,2},{1,3},{2,0},{3,1},{4,6},{5,7},{6,4},{7,5},{8,10},{9,11},{10,... | collective-permute-start | bytes 331784 | tf_op jit(solution)/shard_map/ppermute | solution.py:537
  38.5 4.6 %collective-permute-start.14 = (bf16[216,128]{1,0:T(8,128)(2,1)S(1)}, bf16[216,128]{1,0:T(8,128)(2,1)S(1)}, u32[]{:S(2)}, u32[]{:S(2)}) collective-permute-start(bf16[216,128]{1,0:T(8,128)(2,1)S(1)} %get-tuple-element.78), channel_id=1, source_target_pairs={{0,4},{1,5},{2,6},{3,7},{4,0},{5,1},{6,2},{7,3},{8,12},{9,13},{10,... | collective-permute-start | bytes 165896 | tf_op jit(solution)/shard_map/ppermute | solution.py:537
  38.8 4.3 %collective-permute-start.16 = (bf16[216,128]{1,0:T(8,128)(2,1)S(1)}, bf16[216,128]{1,0:T(8,128)(2,1)S(1)}, u32[]{:S(2)}, u32[]{:S(2)}) collective-permute-start(bf16[216,128]{1,0:T(8,128)(2,1)S(1)} %get-tuple-element.79), channel_id=1, source_target_pairs={{0,6},{1,7},{2,4},{3,5},{4,2},{5,3},{6,0},{7,1},{8,14},{9,15},{10,... | collective-permute-start | bytes 165896 | tf_op jit(solution)/shard_map/ppermute | solution.py:537
  43.2 4.5 %collective-permute-start.19 = (bf16[224,128]{1,0:T(8,128)(2,1)S(1)}, bf16[224,128]{1,0:T(8,128)(2,1)S(1)}, u32[]{:S(2)}, u32[]{:S(2)}) collective-permute-start(bf16[224,128]{1,0:T(8,128)(2,1)S(1)} %shard_map.104.refs_0_), channel_id=1, source_target_pairs={{0,6},{1,7},{2,4},{3,5},{4,2},{5,3},{6,0},{7,1},{8,14},{9,15},{10,... | collective-permute-start | bytes 172040 | tf_op jit(solution)/shard_map/ppermute | solution.py:537
  43.8 6.1 %collective-permute-start.18 = (bf16[224,128]{1,0:T(8,128)(2,1)S(1)}, bf16[224,128]{1,0:T(8,128)(2,1)S(1)}, u32[]{:S(2)}, u32[]{:S(2)}) collective-permute-start(bf16[224,128]{1,0:T(8,128)(2,1)S(1)} %shard_map.104.refs_0_), channel_id=1, source_target_pairs={{0,2},{1,3},{2,0},{3,1},{4,6},{5,7},{6,4},{7,5},{8,10},{9,11},{10,... | collective-permute-start | bytes 172040 | tf_op jit(solution)/shard_map/ppermute | solution.py:537
  47.7 4.5 %collective-permute-start.17 = (bf16[224,128]{1,0:T(8,128)(2,1)S(1)}, bf16[224,128]{1,0:T(8,128)(2,1)S(1)}, u32[]{:S(2)}, u32[]{:S(2)}) collective-permute-start(bf16[224,128]{1,0:T(8,128)(2,1)S(1)} %shard_map.104.refs_0_), channel_id=1, source_target_pairs={{0,4},{1,5},{2,6},{3,7},{4,0},{5,1},{6,2},{7,3},{8,12},{9,13},{10,... | collective-permute-start | bytes 172040 | tf_op jit(solution)/shard_map/ppermute | solution.py:537
  52.2 4.9 %collective-permute-start.20 = (bf16[896,128]{1,0:T(8,128)(2,1)S(1)}, bf16[896,128]{1,0:T(8,128)(2,1)S(1)}, u32[]{:S(2)}, u32[]{:S(2)}) collective-permute-start(bf16[896,128]{1,0:T(8,128)(2,1)S(1)} %shard_map.105.pieces.o0), channel_id=1, source_target_pairs={{0,16},{1,9},{2,18},{3,11},{4,20},{5,13},{6,22},{7,15},{8,24},{9,1... | collective-permute-start | bytes 688136 | tf_op jit(solution)/shard_map/ppermute | solution.py:537
  52.3 17.3 %collective-permute-start.23 = (bf16[896,128]{1,0:T(8,128)(2,1)S(1)}, bf16[896,128]{1,0:T(8,128)(2,1)S(1)}, u32[]{:S(2)}, u32[]{:S(2)}) collective-permute-start(bf16[896,128]{1,0:T(8,128)(2,1)S(1)} %shard_map.105.pieces.o0), channel_id=1, source_target_pairs={{0,8},{1,17},{2,10},{3,19},{4,12},{5,21},{6,14},{7,23},{8,0},{9,25... | collective-permute-start | bytes 688136 | tf_op jit(solution)/shard_map/ppermute | solution.py:537
  57.1 13.9 %collective-permute-start.21 = (bf16[896,128]{1,0:T(8,128)(2,1)S(1)}, bf16[896,128]{1,0:T(8,128)(2,1)S(1)}, u32[]{:S(2)}, u32[]{:S(2)}) collective-permute-start(bf16[896,128]{1,0:T(8,128)(2,1)S(1)} %collective-permute-done.20.o1), channel_id=1, source_target_pairs={{0,8},{1,17},{2,10},{3,19},{4,12},{5,21},{6,14},{7,23},{8,0},{9,25... | collective-permute-start | bytes 688136 | tf_op jit(solution)/shard_map/ppermute | solution.py:537
  57.9 11.7 %collective-permute-start.7 = (bf16[2,128,128]{2,1,0:T(8,128)(2,1)S(1)}, bf16[2,128,128]{2,1,0:T(8,128)(2,1)S(1)}, u32[]{:S(2)}, u32[]{:S(2)}) collective-permute-start(bf16[2,128,128]{2,1,0:T(8,128)(2,1)S(1)} %get-tuple-element.59), channel_id=1, source_target_pairs={{0,8},{8,0},{16,24},{24,16},{1,9},{9,1},{17,25},{25,17},{2,10},{10... | collective-permute-start | bytes 196616 | tf_op jit(solution)/shard_map/ppermute | solution.py:395
  58.5 12.5 %collective-permute-start.8 = (bf16[2,128,128]{2,1,0:T(8,128)(2,1)S(1)}, bf16[2,128,128]{2,1,0:T(8,128)(2,1)S(1)}, u32[]{:S(2)}, u32[]{:S(2)}) collective-permute-start(bf16[2,128,128]{2,1,0:T(8,128)(2,1)S(1)} %get-tuple-element.60), channel_id=1, source_target_pairs={{8,16},{16,8},{9,17},{17,9},{10,18},{18,10},{11,19},{19,11},{12,20... | collective-permute-start | bytes 196616 | tf_op jit(solution)/shard_map/ppermute | solution.py:394
  62.6 30.6 %collective-permute-start.25 = (bf16[896,128]{1,0:T(8,128)(2,1)S(1)}, bf16[896,128]{1,0:T(8,128)(2,1)S(1)}, u32[]{:S(2)}, u32[]{:S(2)}) collective-permute-start(bf16[896,128]{1,0:T(8,128)(2,1)S(1)} %shard_map.105.pieces.o0), channel_id=1, source_target_pairs={{0,1},{1,0},{2,3},{3,2},{4,5},{5,4},{6,7},{7,6},{8,9},{9,8},{10,11... | collective-permute-start | bytes 688136 | tf_op jit(solution)/shard_map/ppermute | solution.py:570
  69.6 23.5 %collective-permute-start.27 = (bf16[896,128]{1,0:T(8,128)(2,1)S(1)}, bf16[896,128]{1,0:T(8,128)(2,1)S(1)}, u32[]{:S(2)}, u32[]{:S(2)}) collective-permute-start(bf16[896,128]{1,0:T(8,128)(2,1)S(1)} %collective-permute-done.23.o2), channel_id=1, source_target_pairs={{0,1},{1,0},{2,3},{3,2},{4,5},{5,4},{6,7},{7,6},{8,9},{9,8},{10,11... | collective-permute-start | bytes 688136 | tf_op jit(solution)/shard_map/ppermute | solution.py:570
  69.7 23.4 %collective-permute-start.26 = (bf16[896,128]{1,0:T(8,128)(2,1)S(1)}, bf16[896,128]{1,0:T(8,128)(2,1)S(1)}, u32[]{:S(2)}, u32[]{:S(2)}) collective-permute-start(bf16[896,128]{1,0:T(8,128)(2,1)S(1)} %collective-permute-done.20.o1), channel_id=1, source_target_pairs={{0,1},{1,0},{2,3},{3,2},{4,5},{5,4},{6,7},{7,6},{8,9},{9,8},{10,11... | collective-permute-start | bytes 688136 | tf_op jit(solution)/shard_map/ppermute | solution.py:570
  71.0 24.6 %collective-permute-start.22 = (bf16[896,128]{1,0:T(8,128)(2,1)S(1)}, bf16[896,128]{1,0:T(8,128)(2,1)S(1)}, u32[]{:S(2)}, u32[]{:S(2)}) collective-permute-start(bf16[896,128]{1,0:T(8,128)(2,1)S(1)} %collective-permute-done.21.o3), channel_id=1, source_target_pairs={{0,1},{1,0},{2,3},{3,2},{4,5},{5,4},{6,7},{7,6},{8,9},{9,8},{10,11... | collective-permute-start | bytes 688136 | tf_op jit(solution)/shard_map/ppermute | solution.py:570
  71.9 4.2 %collective-permute-start.9 = (bf16[2,144,128]{2,1,0:T(8,128)(2,1)S(1)}, bf16[2,144,128]{2,1,0:T(8,128)(2,1)S(1)}, u32[]{:S(2)}, u32[]{:S(2)}) collective-permute-start(bf16[2,144,128]{2,1,0:T(8,128)(2,1)S(1)} %get-tuple-element.61), channel_id=1, source_target_pairs={{0,1},{1,0},{2,3},{3,2},{4,5},{5,4},{6,7},{7,6},{8,9},{9,8},{10,11... | collective-permute-start | bytes 221192 | tf_op jit(solution)/shard_map/ppermute | solution.py:395
  76.0 5.7 %collective-permute-start.10 = (bf16[2,144,128]{2,1,0:T(8,128)(2,1)S(1)}, bf16[2,144,128]{2,1,0:T(8,128)(2,1)S(1)}, u32[]{:S(2)}, u32[]{:S(2)}) collective-permute-start(bf16[2,144,128]{2,1,0:T(8,128)(2,1)S(1)} %get-tuple-element.62), channel_id=1, source_target_pairs={{1,2},{2,1},{3,4},{4,3},{5,6},{6,5},{9,10},{10,9},{11,12},{12,11},... | collective-permute-start | bytes 221192 | tf_op jit(solution)/shard_map/ppermute | solution.py:394
  81.7 3.4 %collective-permute-start.24 = (bf16[32,128]{1,0:T(8,128)(2,1)S(1)}, bf16[32,128]{1,0:T(8,128)(2,1)S(1)}, u32[]{:S(2)}, u32[]{:S(2)}) collective-permute-start(bf16[32,128]{1,0:T(8,128)(2,1)S(1)} %shard_map.106), channel_id=1, source_target_pairs={{0,24},{1,25},{2,26},{3,27},{4,28},{5,29},{6,30},{7,31},{8,16},{9,... | collective-permute-start | bytes 24584 | tf_op jit(solution)/shard_map/ppermute | solution.py:537
  85.1 8.0 %collective-permute-start.28 = (bf16[32,128]{1,0:T(8,128)(2,1)S(1)}, bf16[32,128]{1,0:T(8,128)(2,1)S(1)}, u32[]{:S(2)}, u32[]{:S(2)}) collective-permute-start(bf16[32,128]{1,0:T(8,128)(2,1)S(1)} %collective-permute-done.24.o3), channel_id=1, source_target_pairs={{0,1},{1,0},{2,3},{3,2},{4,5},{5,4},{6,7},{7,6},{8,9},{9,8},{10,11... | collective-permute-start | bytes 24584 | tf_op jit(solution)/shard_map/ppermute | solution.py:568

commit v7 on v6

--- a/solution.py
+++ b/solution.py
@@ -30,9 +30,13 @@
     return p < POS, q // BY, q % BY
 
 
-def call(body, outs, scratch, args, n_smem, mib=4):
+def call(body, outs, scratch, args, n_smem, mib=4, who=None):
+    def kernel(*refs):
+        known = () if who is None else (who(),)
+        body(*refs[:n_smem], *known, *refs[n_smem:])
+
     return pl.pallas_call(
-        body,
+        kernel,
         out_shape=outs,
         in_specs=[SMEM] * n_smem + [VMEM] * (len(args) - n_smem),
         out_specs=[VMEM] * len(outs),
@@ -58,15 +62,15 @@
                     out[f, pl.ds(pl.multiple_of(by * 64, 64), 64)] = src[s, pl.ds(at, 64)]
 
 
-def pack_x_body(pos, odd, a, b, *outs):
-    pack_x(pos, odd[0], (a, b), outs)
-
-
-def load_body(pos, core, odd, a, b, a_out, b_out, sent, *outs):
-    pack_x(pos, odd[0], (a, b), outs)
+def pack_x_body(pos, meta, a, b, *outs):
+    pack_x(pos, meta[3], (a, b), outs)
+
+
+def load_body(pos, meta, a, b, a_out, b_out, sent, *outs):
+    pack_x(pos, meta[3], (a, b), outs)
     a_out[...] = a[...]
     b_out[...] = b[...]
-    sent[...] = jnp.where(core[0] == 0, b[...], a[...])
+    sent[...] = jnp.where(meta[0] == 0, b[...], a[...])
 
 
 def pack_y_body(pos, meta, a, b, xa, xb, ya, yb, tmp):
@@ -396,13 +400,14 @@
     return a, b
 
 
-def y_faces(pos, meta, a, b, xa, xb):
+def y_faces(pos, who, a, b, xa, xb):
     return call(
         pack_y_body,
         [sds((2, 144, C), bf16)] * 2,
         [pltpu.VMEM((18, 8, C), f32)],
-        (pos, meta, a, b, xa, xb),
-        2,
+        (pos, a, b, xa, xb),
+        1,
+        who=who,
     )
 
 
@@ -438,27 +443,31 @@
 def per_device(features, brick_pos, cotangent, first_kernel, second_kernel, norm_gain):
     both = ("gx", "gy")
     ny = lax.axis_size("gy")
-    ix, iy = lax.axis_index("gx"), lax.axis_index("gy")
-    core = iy % 2
     orders, halvings, group, copies = plan()
     chunks = 1 << len(orders[0])
-    me_a = chunk_index(orders[0], len(orders[0]), ix, iy)
-    me_b = chunk_index(orders[1], len(orders[1]), ix, iy)
-    meta = jnp.stack([core, jnp.where(core == 0, me_a, me_b), jnp.where(core == 0, me_b, me_a), ix % 2])
+
+    def who():
+        ix, iy = lax.axis_index("gx"), lax.axis_index("gy")
+        core = iy % 2
+        a, b = (chunk_index(o, len(o), ix, iy) for o in orders)
+        return core, jnp.where(core == 0, a, b), jnp.where(core == 0, b, a), ix % 2
+
     partner = [(i, i ^ 1) for i in range(ny)]
+    hbm = lambda v: pltpu.with_memory_space_constraint(v, pltpu.HBM)
+    slots, brick_pos = brick_pos, hbm(brick_pos)
     n = TAPS * C
     size = n // chunks
 
-    hbm = lambda v: pltpu.with_memory_space_constraint(v, pltpu.HBM)
     features, cotangent, sent, fa, fb = call(
         load_body,
         [sds((2, 512, C), bf16)] * 3 + [sds((2, 128, C), bf16)] * 2,
         [],
-        (brick_pos, core.reshape(1), (ix % 2).reshape(1), hbm(features), hbm(cotangent)),
-        3,
+        (brick_pos, hbm(features), hbm(cotangent)),
+        1,
+        who=who,
     )
     xa, xb = across(fa, fb, "gx")
-    ppos = lax.ppermute(brick_pos, "gy", partner)
+    ppos = lax.ppermute(slots, "gy", partner)
     other = lax.ppermute(sent, "gy", partner)
     straight, turned = sds((9 * C, 3 * C), bf16), sds((3 * C, 9 * C), bf16)
     w1, w2, t1, t2, gain = call(
@@ -468,7 +477,7 @@
         (hbm(first_kernel), hbm(second_kernel), hbm(norm_gain.reshape(1, C))),
         0,
     )
-    fa, fb = y_faces(brick_pos, meta, after(features, gain), cotangent, xa, xb)
+    fa, fb = y_faces(brick_pos, who, after(features, gain), cotangent, xa, xb)
     fa = after(fa, ppos, other)
     edge = xa, xb, *across(fa, fb, "gy")
     grid = pltpu.VMEM((2, 18, 18, 8, C), f32)
@@ -477,9 +486,10 @@
         main_body,
         [sds((2, 512, C), bf16)] * 2 + [sds((P_ROWS + sum(FACES), C), bf16), sds((8, C), f32)],
         [grid, cols, pltpu.VMEM((512, C), f32)],
-        (brick_pos, meta, features, cotangent, *edge, w1, t2, gain),
-        2,
+        (brick_pos, features, cotangent, *edge, w1, t2, gain),
+        1,
         14,
+        who,
     )
     pmsg = lax.ppermute(msg, "gy", partner)
     held = [sds((18, 18, 8, C), f32), sds((3 * C, 1024), bf16)]
@@ -489,26 +499,29 @@
         functools.partial(own_body, chunks=chunks),
         held + [sds((3 * C, JS * C), f32)],
         [wide],
-        (brick_pos, meta, features, cotangent, *edge, hid, pre),
-        2,
+        (brick_pos, features, cotangent, *edge, hid, pre),
+        1,
         10,
+        who,
     )
     quarter = [sds((n // 4, C), bf16)] * 2
     grid_b, pt_b, out_b, out_a, g = call(
         functools.partial(send_body, chunks=chunks),
         held + quarter + [sds((8, C), f32)],
         [wide, pltpu.VMEM((3 * C, JS * C), f32), acc],
-        (ppos, meta, other, pmsg, gain_part, part),
-        2,
+        (ppos, other, pmsg, gain_part, part),
+        1,
         10,
+        who,
     )
     keep_b, keep_a = call(
         functools.partial(keep_body, chunks=chunks),
         [sds((n // 4, C), f32)] * 2,
         [wide, wide, pltpu.VMEM((3 * C, JS * C), f32), acc],
-        (brick_pos, ppos, meta, grid_a, grid_b, pt_a, pt_b),
-        3,
+        (brick_pos, ppos, grid_a, grid_b, pt_a, pt_b),
+        2,
         12,
+        who,
     )
     g = g[0:1]
 
@@ -516,11 +529,12 @@
         pack_x_body,
         [sds((2, 128, C), bf16)] * 2,
         [],
-        (brick_pos, (ix % 2).reshape(1), after(hid, out_a), pre),
-        2,
+        (brick_pos, after(hid, out_a), pre),
+        1,
+        who=who,
     )
     xa, xb = across(fa, fb, "gx")
-    fa, fb = y_faces(brick_pos, meta, hid, pre, xa, xb)
+    fa, fb = y_faces(brick_pos, who, hid, pre, xa, xb)
     around = xa, xb, *across(fa, fb, "gy")
     results = []
     for f, (src, w, base) in enumerate(((hid, w2, features), (pre, t1, cotangent))):
@@ -528,9 +542,10 @@
             functools.partial(out_body, field=f),
             [sds((2, 512, C), bf16)],
             [pltpu.VMEM((1, 18, 18, 8, C), f32), cols],
-            (brick_pos, meta, src, *around, w, base),
-            2,
+            (brick_pos, src, *around, w, base),
+            1,
             10,
+            who,
         )
         results.append(res)
 
@@ -572,9 +587,9 @@
 
     def pieces_call(body, count, outs, out_specs, scratch, args, in_specs, aliases):
         return pl.pallas_call(
-            functools.partial(body, chunks=chunks),
+            lambda *refs: body(who(), *refs, chunks=chunks),
             out_shape=outs,
-            in_specs=[SMEM] + in_specs,
+            in_specs=in_specs,
             out_specs=out_specs,
             scratch_shapes=scratch
             + [pltpu.VMEM((count, size, C), f32)]
@@ -582,7 +597,7 @@
             + [pltpu.SemaphoreType.DMA((count + 1,))],
             input_output_aliases=aliases,
             compiler_params=pltpu.CompilerParams(vmem_limit_bytes=8 << 20),
-        )(meta, *args)
+        )(*args)
 
     table = pltpu.VMEM((2, chunks, 8, C), f32)
     k_up, g_up, shrink = pieces_call(
@@ -603,7 +618,7 @@
         [],
         (own[3], part[3], shrink, k_up),
         [VMEM] * 3 + [any_space],
-        {4: 0},
+        {3: 0},
     )
     return (*results, k_up.reshape(2, TAPS, C, C), g_up.reshape(C))
 

time: 97.7 us -> 96.2 us (0.985)
  Pallas kernels: 26.9 us -> 25.8 us
    pallas_call x16, Pallas kernels: 26.9 us -> 25.8 us  [the longest x14 22.8 us: call(): pl.pallas_call(kernel, out_shape=outs, in_specs=[SMEM] * n_smem + [VMEM]...]
where the time goes in v7:
time: 96.2 us; the launch traced here: 95.9 us
  starting transfers between devices  39.7 us (41%)
  waiting for transfers between devices  29.1 us (30%)
  Pallas kernels  25.8 us (27%)
  between operations  1.03 us (1%)
    pallas_call x14, Pallas kernels, call(): pl.pallas_call(kernel, out_shape=outs, in_specs=[SMEM] * n_smem + [VMEM]...  22.8 us
    ppermute x13, waiting for transfers between devices, per_device(): swap = lambda v, dx, dy=0: lax.ppermute(v, both, pairs(dx, dy))  21.8 us
    ppermute x4, starting transfers between devices, across(): b = lax.ppermute(b, axis, odd)  13.1 us
    ppermute x13, starting transfers between devices, per_device(): swap = lambda v, dx, dy=0: lax.ppermute(v, both, pairs(dx, dy))  9.64 us
    ppermute x4, starting transfers between devices, per_device(): part = [lax.ppermute(v, 'gy', partner) for v in own]  8.48 us
    ppermute x4, waiting for transfers between devices, across(): b = lax.ppermute(b, axis, odd)  6.41 us
    ppermute x4, starting transfers between devices, across(): a = lax.ppermute(a, axis, even)  5.1 us
    pallas_call x2, Pallas kernels, pieces_call(): pl.pallas_call(lambda *refs: body(who(), *refs, chunks=chunks), out_shape...  2.97 us
  transfers between devices with their start and end apart: 29, of which 12 were waited for; matrix products, arithmetic and copies ran while one was open for 0% of the time, Pallas kernels for 18%

profile of v7, /device:TPU:21, one launch (start us, length us, event | category | flops | bytes accessed | tf_op | source)
XLA Modules:
  0.0 95.9 jit_solution(2421728426113126375)
XLA Ops:
  0.6 1.3 %shard_map.93 = (bf16[2,512,128]{2,1,0:T(8,128)(2,1)S(1)}, bf16[2,512,128]{2,1,0:T(8,128)(2,1)S(1)}, bf16[2,512,128]{2,1,0:T(8,128)(2,1)S(1)}, bf16[2,128,128]{2,1,0:T(8,128)(2,1)S(1)}, bf16[2,128,128]{2,1,0:T(8,128)(2,1)S(1)}) custom-call(s32[2]{0:T(128)} %refs_0_.19, bf16[2,512,128]{2,1,0:T(8,128)(2,1)} %refs_1_.2, bf16[2,512,128]{2,1,0:T(8,128)(2,1)} %refs_2_.1), custom_call_target="tpu_custom_call" | custom-call | tf_op jit(solution)/shard_map/pallas_call | solution.py:38
  1.9 0.7 collective-permute-start.3
  2.7 1.2 %collective-permute-start = (bf16[2,128,128]{2,1,0:T(8,128)(2,1)S(1)}, bf16[2,128,128]{2,1,0:T(8,128)(2,1)S(1)}, u32[]{:S(2)}, u32[]{:S(2)}) collective-permute-start(bf16[2,128,128]{2,1,0:T(8,128)(2,1)S(1)} %get-tuple-element.42), channel_id=1, source_target_pairs={{0,8},{8,0},{16,24},{24,16},{1,9},{9,1},{17,25},{25,17},{2,10},{10... | collective-permute-start | bytes 196616 | tf_op jit(solution)/shard_map/ppermute | solution.py:399
  3.9 2.1 %collective-permute-start.1 = (bf16[2,128,128]{2,1,0:T(8,128)(2,1)S(1)}, bf16[2,128,128]{2,1,0:T(8,128)(2,1)S(1)}, u32[]{:S(2)}, u32[]{:S(2)}) collective-permute-start(bf16[2,128,128]{2,1,0:T(8,128)(2,1)S(1)} %get-tuple-element.43), channel_id=1, source_target_pairs={{8,16},{16,8},{9,17},{17,9},{10,18},{18,10},{11,19},{19,11},{12,20... | collective-permute-start | bytes 196616 | tf_op jit(solution)/shard_map/ppermute | solution.py:398
  6.0 0.7 collective-permute-start.2
  6.7 2.0 %shard_map.94 = (bf16[1152,384]{1,0:T(8,128)(2,1)S(1)}, bf16[1152,384]{1,0:T(8,128)(2,1)S(1)}, bf16[384,1152]{1,0:T(8,128)(2,1)S(1)}, bf16[384,1152]{1,0:T(8,128)(2,1)S(1)}, f32[1,128]{1,0:T(1,128)S(1)}) custom-call(bf16[27,128,128]{2,1,0:T(8,128)(2,1)} %refs_0_.11, bf16[27,128,128]{2,1,0:T(8,128)(2,1)} %refs_1_.3, f32[1,128]{1,0:T(1,128)} %bitcast.4), custom_call_target="tpu_custom_call" | custom-call | tf_op jit(solution)/shard_map/pallas_call | solution.py:38
  8.7 1.1 %collective-permute-done.1.refs_4_ = bf16[2,128,128]{2,1,0:T(8,128)(2,1)S(1)} collective-permute-done((bf16[2,128,128]{2,1,0:T(8,128)(2,1)S(1)}, bf16[2,128,128]{2,1,0:T(8,128)(2,1)S(1)}, u32[]{:S(2)}, u32[]{:S(2)}) %collective-permute-start.1) | collective-permute-done | bytes 65568 | tf_op jit(solution)/shard_map/ppermute | solution.py:398
  9.8 0.8 shard_map.95
  10.6 4.6 %collective-permute-start.5 = (bf16[2,144,128]{2,1,0:T(8,128)(2,1)S(1)}, bf16[2,144,128]{2,1,0:T(8,128)(2,1)S(1)}, u32[]{:S(2)}, u32[]{:S(2)}) collective-permute-start(bf16[2,144,128]{2,1,0:T(8,128)(2,1)S(1)} %get-tuple-element.49), channel_id=1, source_target_pairs={{1,2},{2,1},{3,4},{4,3},{5,6},{6,5},{9,10},{10,9},{11,12},{12,11},... | collective-permute-start | bytes 221192 | tf_op jit(solution)/shard_map/ppermute | solution.py:398
  15.3 2.1 %collective-permute-done.5.refs_6_ = bf16[2,144,128]{2,1,0:T(8,128)(2,1)S(1)} collective-permute-done((bf16[2,144,128]{2,1,0:T(8,128)(2,1)S(1)}, bf16[2,144,128]{2,1,0:T(8,128)(2,1)S(1)}, u32[]{:S(2)}, u32[]{:S(2)}) %collective-permute-start.5) | collective-permute-done | bytes 73760 | tf_op jit(solution)/shard_map/ppermute | solution.py:398
  17.4 4.5 %shard_map.96 = (bf16[2,512,128]{2,1,0:T(8,128)(2,1)S(1)}, bf16[2,512,128]{2,1,0:T(8,128)(2,1)S(1)}, bf16[1584,128]{1,0:T(8,128)(2,1)S(1)}, f32[8,128]{1,0:T(8,128)S(1)}) custom-call(s32[2]{0:T(128)} %refs_0_.19, bf16[2,512,128]{2,1,0:T(8,128)(2,1)S(1)} %get-tuple-element.45.refs_1_.refs_7_, bf16[2,512,128]{2,1,0:T(8,128)(2,1)S(1)} %get-tuple-element.41.refs_2_.refs_7_, ...), custom_call_target="tpu_custom_call" | custom-call | tf_op jit(solution)/shard_map/pallas_call | solution.py:38
  21.9 0.4 collective-permute-start.6
  22.4 1.9 %shard_map.97 = (f32[18,18,8,128]{3,2,1,0:T(8,128)S(1)}, bf16[384,1024]{1,0:T(8,128)(2,1)S(1)}, f32[384,640]{1,0:T(8,128)S(1)}) custom-call(s32[2]{0:T(128)} %refs_0_.19, bf16[2,512,128]{2,1,0:T(8,128)(2,1)S(1)} %get-tuple-element.45.refs_1_.refs_7_, bf16[2,512,128]{2,1,0:T(8,128)(2,1)S(1)} %get-tuple-element.41.refs_2_.refs_7_, ...), custom_call_target="tpu_custom_call" | custom-call | tf_op jit(solution)/shard_map/pallas_call | solution.py:38
  24.2 1.7 %shard_map.98 = (f32[18,18,8,128]{3,2,1,0:T(8,128)S(1)}, bf16[384,1024]{1,0:T(8,128)(2,1)S(1)}, bf16[864,128]{1,0:T(8,128)(2,1)S(1)}, bf16[864,128]{1,0:T(8,128)(2,1)S(1)}, f32[8,128]{1,0:T(8,128)S(1)}) custom-call(s32[2]{0:T(128)S(1)} %collective-permute-done.2.refs_0_.refs_1_, bf16[2,512,128]{2,1,0:T(8,128)(2,1)S(1)} %collective-permute-done.3.refs_1_, ...), custom_call_target="tpu_custom_call" | custom-call | tf_op jit(solution)/shard_map/pallas_call | solution.py:38
  26.0 1.5 %collective-permute-start.11 = (bf16[864,128]{1,0:T(8,128)(2,1)S(1)}, bf16[864,128]{1,0:T(8,128)(2,1)S(1)}, u32[]{:S(2)}, u32[]{:S(2)}) collective-permute-start(bf16[864,128]{1,0:T(8,128)(2,1)S(1)} %get-tuple-element.70), channel_id=1, source_target_pairs={{0,8},{1,17},{2,10},{3,19},{4,12},{5,21},{6,14},{7,23},{8,0},{9,25... | collective-permute-start | bytes 663560 | tf_op jit(solution)/shard_map/ppermute | solution.py:552
  27.5 2.4 %shard_map.103 = (f32[864,128]{1,0:T(8,128)S(1)}, f32[864,128]{1,0:T(8,128)S(1)}) custom-call(s32[2]{0:T(128)} %refs_0_.19, s32[2]{0:T(128)S(1)} %collective-permute-done.2.refs_0_.refs_1_, f32[18,18,8,128]{3,2,1,0:T(8,128)S(1)} %get-tuple-element.65.refs_2_, f32[18,18,8,128]{3,2,1,0:T(8,128)S(1)} %get-tuple-element.66.refs_3_, ...), custom_call_target="tpu_custom_call" | custom-call | tf_op jit(solution)/shard_map/pallas_call | solution.py:38
  29.9 1.2 %collective-permute-done.12 = bf16[864,128]{1,0:T(8,128)(2,1)S(1)} collective-permute-done((bf16[864,128]{1,0:T(8,128)(2,1)S(1)}, bf16[864,128]{1,0:T(8,128)(2,1)S(1)}, u32[]{:S(2)}, u32[]{:S(2)}) %collective-permute-start.12) | collective-permute-done | bytes 221216 | tf_op jit(solution)/shard_map/ppermute | solution.py:552
  31.2 2.2 %collective-permute-done.11 = bf16[864,128]{1,0:T(8,128)(2,1)S(1)} collective-permute-done((bf16[864,128]{1,0:T(8,128)(2,1)S(1)}, bf16[864,128]{1,0:T(8,128)(2,1)S(1)}, u32[]{:S(2)}, u32[]{:S(2)}) %collective-permute-start.11) | collective-permute-done | bytes 221216 | tf_op jit(solution)/shard_map/ppermute | solution.py:552
  33.5 3.3 %collective-permute-done.13 = bf16[864,128]{1,0:T(8,128)(2,1)S(1)} collective-permute-done((bf16[864,128]{1,0:T(8,128)(2,1)S(1)}, bf16[864,128]{1,0:T(8,128)(2,1)S(1)}, u32[]{:S(2)}, u32[]{:S(2)}) %collective-permute-start.13) | collective-permute-done | bytes 221216 | tf_op jit(solution)/shard_map/ppermute | solution.py:552
  36.7 0.1 fusion.2
  36.9 1.2 %collective-permute-start.15 = (f32[216,128]{1,0:T(8,128)S(1)}, f32[216,128]{1,0:T(8,128)S(1)}, u32[]{:S(2)}, u32[]{:S(2)}) collective-permute-start(f32[216,128]{1,0:T(8,128)S(1)} %slice.24), channel_id=1, source_target_pairs={{0,2},{1,3},{2,0},{3,1},{4,6},{5,7},{6,4},{7,5},{8,10},{9,11},{10,... | collective-permute-start | bytes 331784 | tf_op jit(solution)/shard_map/ppermute | solution.py:552
  38.1 0.3 collective-permute-start.14
  38.3 1.3 %collective-permute-start.16 = (bf16[216,128]{1,0:T(8,128)(2,1)S(1)}, bf16[216,128]{1,0:T(8,128)(2,1)S(1)}, u32[]{:S(2)}, u32[]{:S(2)}) collective-permute-start(bf16[216,128]{1,0:T(8,128)(2,1)S(1)} %get-tuple-element.79), channel_id=1, source_target_pairs={{0,6},{1,7},{2,4},{3,5},{4,2},{5,3},{6,0},{7,1},{8,14},{9,15},{10,... | collective-permute-start | bytes 165896 | tf_op jit(solution)/shard_map/ppermute | solution.py:552
  39.7 3.0 %collective-permute-done.14 = bf16[216,128]{1,0:T(8,128)(2,1)S(1)} collective-permute-done((bf16[216,128]{1,0:T(8,128)(2,1)S(1)}, bf16[216,128]{1,0:T(8,128)(2,1)S(1)}, u32[]{:S(2)}, u32[]{:S(2)}) %collective-permute-start.14) | collective-permute-done | bytes 55328 | tf_op jit(solution)/shard_map/ppermute | solution.py:552
  42.7 0.6 collective-permute-start.19
  43.3 3.9 %collective-permute-start.18 = (bf16[224,128]{1,0:T(8,128)(2,1)S(1)}, bf16[224,128]{1,0:T(8,128)(2,1)S(1)}, u32[]{:S(2)}, u32[]{:S(2)}) collective-permute-start(bf16[224,128]{1,0:T(8,128)(2,1)S(1)} %shard_map.104.refs_0_), channel_id=1, source_target_pairs={{0,2},{1,3},{2,0},{3,1},{4,6},{5,7},{6,4},{7,5},{8,10},{9,11},{10,... | collective-permute-start | bytes 172040 | tf_op jit(solution)/shard_map/ppermute | solution.py:552
  47.3 2.2 %collective-permute-done.18.refs_2_ = bf16[224,128]{1,0:T(8,128)(2,1)S(1)} collective-permute-done((bf16[224,128]{1,0:T(8,128)(2,1)S(1)}, bf16[224,128]{1,0:T(8,128)(2,1)S(1)}, u32[]{:S(2)}, u32[]{:S(2)}) %collective-permute-start.18) | collective-permute-done | bytes 57376 | tf_op jit(solution)/shard_map/ppermute | solution.py:552
  49.4 2.3 %collective-permute-done.17.refs_1_ = bf16[224,128]{1,0:T(8,128)(2,1)S(1)} collective-permute-done((bf16[224,128]{1,0:T(8,128)(2,1)S(1)}, bf16[224,128]{1,0:T(8,128)(2,1)S(1)}, u32[]{:S(2)}, u32[]{:S(2)}) %collective-permute-start.17) | collective-permute-done | bytes 57376 | tf_op jit(solution)/shard_map/ppermute | solution.py:552
  51.8 0.5 collective-permute-start.23
  52.3 4.4 %collective-permute-done.20.refs_1_ = bf16[896,128]{1,0:T(8,128)(2,1)S(1)} collective-permute-done((bf16[896,128]{1,0:T(8,128)(2,1)S(1)}, bf16[896,128]{1,0:T(8,128)(2,1)S(1)}, u32[]{:S(2)}, u32[]{:S(2)}) %collective-permute-start.20) | collective-permute-done | bytes 229408 | tf_op jit(solution)/shard_map/ppermute | solution.py:552
  56.7 0.8 shard_map.99
  57.5 0.6 collective-permute-start.7
  58.1 4.0 %collective-permute-start.8 = (bf16[2,128,128]{2,1,0:T(8,128)(2,1)S(1)}, bf16[2,128,128]{2,1,0:T(8,128)(2,1)S(1)}, u32[]{:S(2)}, u32[]{:S(2)}) collective-permute-start(bf16[2,128,128]{2,1,0:T(8,128)(2,1)S(1)} %get-tuple-element.60), channel_id=1, source_target_pairs={{8,16},{16,8},{9,17},{17,9},{10,18},{18,10},{11,19},{19,11},{12,20... | collective-permute-start | bytes 196616 | tf_op jit(solution)/shard_map/ppermute | solution.py:398
  62.1 7.1 %collective-permute-start.25 = (bf16[896,128]{1,0:T(8,128)(2,1)S(1)}, bf16[896,128]{1,0:T(8,128)(2,1)S(1)}, u32[]{:S(2)}, u32[]{:S(2)}) collective-permute-start(bf16[896,128]{1,0:T(8,128)(2,1)S(1)} %shard_map.105.refs_0_), channel_id=1, source_target_pairs={{0,1},{1,0},{2,3},{3,2},{4,5},{5,4},{6,7},{7,6},{8,9},{9,8},{10,11... | collective-permute-start | bytes 688136 | tf_op jit(solution)/shard_map/ppermute | solution.py:585
  69.2 0.1 collective-permute-start.27
  69.3 1.3 %collective-permute-start.26 = (bf16[896,128]{1,0:T(8,128)(2,1)S(1)}, bf16[896,128]{1,0:T(8,128)(2,1)S(1)}, u32[]{:S(2)}, u32[]{:S(2)}) collective-permute-start(bf16[896,128]{1,0:T(8,128)(2,1)S(1)} %collective-permute-done.20.refs_1_), channel_id=1, source_target_pairs={{0,1},{1,0},{2,3},{3,2},{4,5},{5,4},{6,7},{7,6},{8,9},{9,8},{10,11... | collective-permute-start | bytes 688136 | tf_op jit(solution)/shard_map/ppermute | solution.py:585
  70.6 0.8 shard_map.100
  71.5 3.3 %collective-permute-start.9 = (bf16[2,144,128]{2,1,0:T(8,128)(2,1)S(1)}, bf16[2,144,128]{2,1,0:T(8,128)(2,1)S(1)}, u32[]{:S(2)}, u32[]{:S(2)}) collective-permute-start(bf16[2,144,128]{2,1,0:T(8,128)(2,1)S(1)} %get-tuple-element.61), channel_id=1, source_target_pairs={{0,1},{1,0},{2,3},{3,2},{4,5},{5,4},{6,7},{7,6},{8,9},{9,8},{10,11... | collective-permute-start | bytes 221192 | tf_op jit(solution)/shard_map/ppermute | solution.py:399
  74.7 0.9 collective-permute-done.9.refs_4_
  75.6 2.4 %collective-permute-start.10 = (bf16[2,144,128]{2,1,0:T(8,128)(2,1)S(1)}, bf16[2,144,128]{2,1,0:T(8,128)(2,1)S(1)}, u32[]{:S(2)}, u32[]{:S(2)}) collective-permute-start(bf16[2,144,128]{2,1,0:T(8,128)(2,1)S(1)} %get-tuple-element.62), channel_id=1, source_target_pairs={{1,2},{2,1},{3,4},{4,3},{5,6},{6,5},{9,10},{10,9},{11,12},{12,11},... | collective-permute-start | bytes 221192 | tf_op jit(solution)/shard_map/ppermute | solution.py:398
  78.1 3.2 %collective-permute-done.10.refs_5_ = bf16[2,144,128]{2,1,0:T(8,128)(2,1)S(1)} collective-permute-done((bf16[2,144,128]{2,1,0:T(8,128)(2,1)S(1)}, bf16[2,144,128]{2,1,0:T(8,128)(2,1)S(1)}, u32[]{:S(2)}, u32[]{:S(2)}) %collective-permute-start.10) | collective-permute-done | bytes 73760 | tf_op jit(solution)/shard_map/ppermute | solution.py:398
  81.3 0.2 collective-permute-start.24
  81.5 3.2 %collective-permute-done.24.refs_3_ = bf16[32,128]{1,0:T(8,128)(2,1)S(1)} collective-permute-done((bf16[32,128]{1,0:T(8,128)(2,1)S(1)}, bf16[32,128]{1,0:T(8,128)(2,1)S(1)}, u32[]{:S(2)}, u32[]{:S(2)}) %collective-permute-start.24) | collective-permute-done | bytes 8224 | tf_op jit(solution)/shard_map/ppermute | solution.py:552
  84.7 1.5 %collective-permute-start.28 = (bf16[32,128]{1,0:T(8,128)(2,1)S(1)}, bf16[32,128]{1,0:T(8,128)(2,1)S(1)}, u32[]{:S(2)}, u32[]{:S(2)}) collective-permute-start(bf16[32,128]{1,0:T(8,128)(2,1)S(1)} %collective-permute-done.24.refs_3_), channel_id=1, source_target_pairs={{0,1},{1,0},{2,3},{3,2},{4,5},{5,4},{6,7},{7,6},{8,9},{9,8},{10,11... | collective-permute-start | bytes 24584 | tf_op jit(solution)/shard_map/ppermute | solution.py:583
  86.2 3.4 %shard_map.102 = bf16[2,512,128]{2,1,0:T(8,128)(2,1)} custom-call(s32[2]{0:T(128)} %refs_0_.19, bf16[2,512,128]{2,1,0:T(8,128)(2,1)S(1)} %get-tuple-element.55.refs_8_.refs_2_.refs_1_, bf16[2,128,128]{2,1,0:T(8,128)(2,1)S(1)} %collective-permute-done.7.refs_3_.refs_2_, bf16[2,128,128]{2,1,0:T(8,128)(2,1)S(1)} %collective-permute-done.8.refs_4_.refs_3_, ...), custom_call_target="tpu_custom_call" | custom-call | tf_op jit(solution)/shard_map/pallas_call | solution.py:38
  89.5 3.2 %shard_map.101 = bf16[2,512,128]{2,1,0:T(8,128)(2,1)} custom-call(s32[2]{0:T(128)} %refs_0_.19, bf16[2,512,128]{2,1,0:T(8,128)(2,1)S(1)} %get-tuple-element.58.refs_7_.refs_1_, bf16[2,128,128]{2,1,0:T(8,128)(2,1)S(1)} %collective-permute-done.7.refs_3_.refs_2_, bf16[2,128,128]{2,1,0:T(8,128)(2,1)S(1)} %collective-permute-done.8.refs_4_.refs_3_, ...), custom_call_target="tpu_custom_call" | custom-call | tf_op jit(solution)/shard_map/pallas_call | solution.py:38
  92.7 2.0 %shard_map.107 = (f32[2,3456,128]{2,1,0:T(8,128)}, f32[1,128]{1,0:T(1,128)}, f32[8,128]{1,0:T(8,128)S(1)}) custom-call(bf16[896,128]{1,0:T(8,128)(2,1)S(1)} %shard_map.105.refs_0_, bf16[896,128]{1,0:T(8,128)(2,1)S(1)} %collective-permute-done.20.refs_1_, bf16[896,128]{1,0:T(8,128)(2,1)S(1)} %collective-permute-done.23.refs_2_, ...), custom_call_target="tpu_custom_call" | custom-call | tf_op jit(solution)/shard_map/pallas_call | solution.py:589
  94.7 1.0 %shard_map.108 = f32[2,3456,128]{2,1,0:T(8,128)} custom-call(bf16[896,128]{1,0:T(8,128)(2,1)S(1)} %collective-permute-done.21.refs_0_, bf16[896,128]{1,0:T(8,128)(2,1)S(1)} %collective-permute-done.22.refs_1_, f32[8,128]{1,0:T(8,128)S(1)} %get-tuple-element.73.refs_2_, f32[2,3456,128]{2,1,0:T(8,128)} %get-tuple-element.74.refs_3_), custom_call_target="tpu_custom_call", output_to_operand_aliasing={{}: (3, {})} | custom-call | tf_op jit(solution)/shard_map/pallas_call | solution.py:589
  (32 shorter events, 0.5 us)
Async XLA Ops:
  1.9 13.3 %collective-permute-start.3 = (bf16[2,512,128]{2,1,0:T(8,128)(2,1)S(1)}, bf16[2,512,128]{2,1,0:T(8,128)(2,1)S(1)}, u32[]{:S(2)}, u32[]{:S(2)}) collective-permute-start(bf16[2,512,128]{2,1,0:T(8,128)(2,1)S(1)} %get-tuple-element.47), channel_id=1, source_target_pairs={{0,1},{1,0},{2,3},{3,2},{4,5},{5,4},{6,7},{7,6},{8,9},{9,8},{10,11... | collective-permute-start | bytes 786440 | tf_op jit(solution)/shard_map/ppermute | solution.py:471
  2.7 6.0 %collective-permute-start = (bf16[2,128,128]{2,1,0:T(8,128)(2,1)S(1)}, bf16[2,128,128]{2,1,0:T(8,128)(2,1)S(1)}, u32[]{:S(2)}, u32[]{:S(2)}) collective-permute-start(bf16[2,128,128]{2,1,0:T(8,128)(2,1)S(1)} %get-tuple-element.42), channel_id=1, source_target_pairs={{0,8},{8,0},{16,24},{24,16},{1,9},{9,1},{17,25},{25,17},{2,10},{10... | collective-permute-start | bytes 196616 | tf_op jit(solution)/shard_map/ppermute | solution.py:399
  3.9 5.9 %collective-permute-start.1 = (bf16[2,128,128]{2,1,0:T(8,128)(2,1)S(1)}, bf16[2,128,128]{2,1,0:T(8,128)(2,1)S(1)}, u32[]{:S(2)}, u32[]{:S(2)}) collective-permute-start(bf16[2,128,128]{2,1,0:T(8,128)(2,1)S(1)} %get-tuple-element.43), channel_id=1, source_target_pairs={{8,16},{16,8},{9,17},{17,9},{10,18},{18,10},{11,19},{19,11},{12,20... | collective-permute-start | bytes 196616 | tf_op jit(solution)/shard_map/ppermute | solution.py:398
  6.0 9.2 %collective-permute-start.2 = (s32[2]{0:T(128)}, s32[2]{0:T(128)S(1)}, u32[]{:S(2)}, u32[]{:S(2)}) collective-permute-start(s32[2]{0:T(128)} %refs_0_.19), channel_id=1, source_target_pairs={{0,1},{1,0},{2,3},{3,2},{4,5},{5,4},{6,7},{7,6},{8,9},{9,8},{10,11... | collective-permute-start | bytes 32 | tf_op jit(solution)/shard_map/ppermute | solution.py:470
  10.6 6.8 %collective-permute-start.5 = (bf16[2,144,128]{2,1,0:T(8,128)(2,1)S(1)}, bf16[2,144,128]{2,1,0:T(8,128)(2,1)S(1)}, u32[]{:S(2)}, u32[]{:S(2)}) collective-permute-start(bf16[2,144,128]{2,1,0:T(8,128)(2,1)S(1)} %get-tuple-element.49), channel_id=1, source_target_pairs={{1,2},{2,1},{3,4},{4,3},{5,6},{6,5},{9,10},{10,9},{11,12},{12,11},... | collective-permute-start | bytes 221192 | tf_op jit(solution)/shard_map/ppermute | solution.py:398
  15.3 2.2 %collective-permute-start.4 = (bf16[2,144,128]{2,1,0:T(8,128)(2,1)S(1)}, bf16[2,144,128]{2,1,0:T(8,128)(2,1)S(1)}, u32[]{:S(2)}, u32[]{:S(2)}) collective-permute-start(bf16[2,144,128]{2,1,0:T(8,128)(2,1)S(1)} %get-tuple-element.48), channel_id=1, source_target_pairs={{0,1},{1,0},{2,3},{3,2},{4,5},{5,4},{6,7},{7,6},{8,9},{9,8},{10,11... | collective-permute-start | bytes 221192 | tf_op jit(solution)/shard_map/ppermute | solution.py:399
  21.9 2.3 %collective-permute-start.6 = (bf16[1584,128]{1,0:T(8,128)(2,1)S(1)}, bf16[1584,128]{1,0:T(8,128)(2,1)S(1)}, u32[]{:S(2)}, u32[]{:S(2)}) collective-permute-start(bf16[1584,128]{1,0:T(8,128)(2,1)S(1)} %get-tuple-element.53), channel_id=1, source_target_pairs={{0,1},{1,0},{2,3},{3,2},{4,5},{5,4},{6,7},{7,6},{8,9},{9,8},{10,11... | collective-permute-start | bytes 1216520 | tf_op jit(solution)/shard_map/ppermute | solution.py:494
  26.0 5.1 %collective-permute-start.12 = (bf16[864,128]{1,0:T(8,128)(2,1)S(1)}, bf16[864,128]{1,0:T(8,128)(2,1)S(1)}, u32[]{:S(2)}, u32[]{:S(2)}) collective-permute-start(bf16[864,128]{1,0:T(8,128)(2,1)S(1)} %get-tuple-element.57), channel_id=1, source_target_pairs={{0,8},{1,17},{2,10},{3,19},{4,12},{5,21},{6,14},{7,23},{8,0},{9,25... | collective-permute-start | bytes 663560 | tf_op jit(solution)/shard_map/ppermute | solution.py:552
  26.0 7.4 %collective-permute-start.11 = (bf16[864,128]{1,0:T(8,128)(2,1)S(1)}, bf16[864,128]{1,0:T(8,128)(2,1)S(1)}, u32[]{:S(2)}, u32[]{:S(2)}) collective-permute-start(bf16[864,128]{1,0:T(8,128)(2,1)S(1)} %get-tuple-element.70), channel_id=1, source_target_pairs={{0,8},{1,17},{2,10},{3,19},{4,12},{5,21},{6,14},{7,23},{8,0},{9,25... | collective-permute-start | bytes 663560 | tf_op jit(solution)/shard_map/ppermute | solution.py:552
  31.2 5.6 %collective-permute-start.13 = (bf16[864,128]{1,0:T(8,128)(2,1)S(1)}, bf16[864,128]{1,0:T(8,128)(2,1)S(1)}, u32[]{:S(2)}, u32[]{:S(2)}) collective-permute-start(bf16[864,128]{1,0:T(8,128)(2,1)S(1)} %add_convert_fusion), channel_id=1, source_target_pairs={{0,16},{1,9},{2,18},{3,11},{4,20},{5,13},{6,22},{7,15},{8,24},{9,1... | collective-permute-start | bytes 663560 | tf_op jit(solution)/shard_map/ppermute | solution.py:552
  36.9 5.8 %collective-permute-start.15 = (f32[216,128]{1,0:T(8,128)S(1)}, f32[216,128]{1,0:T(8,128)S(1)}, u32[]{:S(2)}, u32[]{:S(2)}) collective-permute-start(f32[216,128]{1,0:T(8,128)S(1)} %slice.24), channel_id=1, source_target_pairs={{0,2},{1,3},{2,0},{3,1},{4,6},{5,7},{6,4},{7,5},{8,10},{9,11},{10,... | collective-permute-start | bytes 331784 | tf_op jit(solution)/shard_map/ppermute | solution.py:552
  38.1 4.6 %collective-permute-start.14 = (bf16[216,128]{1,0:T(8,128)(2,1)S(1)}, bf16[216,128]{1,0:T(8,128)(2,1)S(1)}, u32[]{:S(2)}, u32[]{:S(2)}) collective-permute-start(bf16[216,128]{1,0:T(8,128)(2,1)S(1)} %get-tuple-element.78), channel_id=1, source_target_pairs={{0,4},{1,5},{2,6},{3,7},{4,0},{5,1},{6,2},{7,3},{8,12},{9,13},{10,... | collective-permute-start | bytes 165896 | tf_op jit(solution)/shard_map/ppermute | solution.py:552
  38.3 4.3 %collective-permute-start.16 = (bf16[216,128]{1,0:T(8,128)(2,1)S(1)}, bf16[216,128]{1,0:T(8,128)(2,1)S(1)}, u32[]{:S(2)}, u32[]{:S(2)}) collective-permute-start(bf16[216,128]{1,0:T(8,128)(2,1)S(1)} %get-tuple-element.79), channel_id=1, source_target_pairs={{0,6},{1,7},{2,4},{3,5},{4,2},{5,3},{6,0},{7,1},{8,14},{9,15},{10,... | collective-permute-start | bytes 165896 | tf_op jit(solution)/shard_map/ppermute | solution.py:552
  42.7 4.5 %collective-permute-start.19 = (bf16[224,128]{1,0:T(8,128)(2,1)S(1)}, bf16[224,128]{1,0:T(8,128)(2,1)S(1)}, u32[]{:S(2)}, u32[]{:S(2)}) collective-permute-start(bf16[224,128]{1,0:T(8,128)(2,1)S(1)} %shard_map.104.refs_0_), channel_id=1, source_target_pairs={{0,6},{1,7},{2,4},{3,5},{4,2},{5,3},{6,0},{7,1},{8,14},{9,15},{10,... | collective-permute-start | bytes 172040 | tf_op jit(solution)/shard_map/ppermute | solution.py:552
  43.3 6.1 %collective-permute-start.18 = (bf16[224,128]{1,0:T(8,128)(2,1)S(1)}, bf16[224,128]{1,0:T(8,128)(2,1)S(1)}, u32[]{:S(2)}, u32[]{:S(2)}) collective-permute-start(bf16[224,128]{1,0:T(8,128)(2,1)S(1)} %shard_map.104.refs_0_), channel_id=1, source_target_pairs={{0,2},{1,3},{2,0},{3,1},{4,6},{5,7},{6,4},{7,5},{8,10},{9,11},{10,... | collective-permute-start | bytes 172040 | tf_op jit(solution)/shard_map/ppermute | solution.py:552
  47.3 4.5 %collective-permute-start.17 = (bf16[224,128]{1,0:T(8,128)(2,1)S(1)}, bf16[224,128]{1,0:T(8,128)(2,1)S(1)}, u32[]{:S(2)}, u32[]{:S(2)}) collective-permute-start(bf16[224,128]{1,0:T(8,128)(2,1)S(1)} %shard_map.104.refs_0_), channel_id=1, source_target_pairs={{0,4},{1,5},{2,6},{3,7},{4,0},{5,1},{6,2},{7,3},{8,12},{9,13},{10,... | collective-permute-start | bytes 172040 | tf_op jit(solution)/shard_map/ppermute | solution.py:552
  51.7 4.9 %collective-permute-start.20 = (bf16[896,128]{1,0:T(8,128)(2,1)S(1)}, bf16[896,128]{1,0:T(8,128)(2,1)S(1)}, u32[]{:S(2)}, u32[]{:S(2)}) collective-permute-start(bf16[896,128]{1,0:T(8,128)(2,1)S(1)} %shard_map.105.refs_0_), channel_id=1, source_target_pairs={{0,16},{1,9},{2,18},{3,11},{4,20},{5,13},{6,22},{7,15},{8,24},{9,1... | collective-permute-start | bytes 688136 | tf_op jit(solution)/shard_map/ppermute | solution.py:552
  51.8 17.3 %collective-permute-start.23 = (bf16[896,128]{1,0:T(8,128)(2,1)S(1)}, bf16[896,128]{1,0:T(8,128)(2,1)S(1)}, u32[]{:S(2)}, u32[]{:S(2)}) collective-permute-start(bf16[896,128]{1,0:T(8,128)(2,1)S(1)} %shard_map.105.refs_0_), channel_id=1, source_target_pairs={{0,8},{1,17},{2,10},{3,19},{4,12},{5,21},{6,14},{7,23},{8,0},{9,25... | collective-permute-start | bytes 688136 | tf_op jit(solution)/shard_map/ppermute | solution.py:552
  56.7 13.9 %collective-permute-start.21 = (bf16[896,128]{1,0:T(8,128)(2,1)S(1)}, bf16[896,128]{1,0:T(8,128)(2,1)S(1)}, u32[]{:S(2)}, u32[]{:S(2)}) collective-permute-start(bf16[896,128]{1,0:T(8,128)(2,1)S(1)} %collective-permute-done.20.refs_1_), channel_id=1, source_target_pairs={{0,8},{1,17},{2,10},{3,19},{4,12},{5,21},{6,14},{7,23},{8,0},{9,25... | collective-permute-start | bytes 688136 | tf_op jit(solution)/shard_map/ppermute | solution.py:552
  57.5 11.8 %collective-permute-start.7 = (bf16[2,128,128]{2,1,0:T(8,128)(2,1)S(1)}, bf16[2,128,128]{2,1,0:T(8,128)(2,1)S(1)}, u32[]{:S(2)}, u32[]{:S(2)}) collective-permute-start(bf16[2,128,128]{2,1,0:T(8,128)(2,1)S(1)} %get-tuple-element.59), channel_id=1, source_target_pairs={{0,8},{8,0},{16,24},{24,16},{1,9},{9,1},{17,25},{25,17},{2,10},{10... | collective-permute-start | bytes 196616 | tf_op jit(solution)/shard_map/ppermute | solution.py:399
  58.1 12.5 %collective-permute-start.8 = (bf16[2,128,128]{2,1,0:T(8,128)(2,1)S(1)}, bf16[2,128,128]{2,1,0:T(8,128)(2,1)S(1)}, u32[]{:S(2)}, u32[]{:S(2)}) collective-permute-start(bf16[2,128,128]{2,1,0:T(8,128)(2,1)S(1)} %get-tuple-element.60), channel_id=1, source_target_pairs={{8,16},{16,8},{9,17},{17,9},{10,18},{18,10},{11,19},{19,11},{12,20... | collective-permute-start | bytes 196616 | tf_op jit(solution)/shard_map/ppermute | solution.py:398
  62.1 30.6 %collective-permute-start.25 = (bf16[896,128]{1,0:T(8,128)(2,1)S(1)}, bf16[896,128]{1,0:T(8,128)(2,1)S(1)}, u32[]{:S(2)}, u32[]{:S(2)}) collective-permute-start(bf16[896,128]{1,0:T(8,128)(2,1)S(1)} %shard_map.105.refs_0_), channel_id=1, source_target_pairs={{0,1},{1,0},{2,3},{3,2},{4,5},{5,4},{6,7},{7,6},{8,9},{9,8},{10,11... | collective-permute-start | bytes 688136 | tf_op jit(solution)/shard_map/ppermute | solution.py:585
  69.2 23.6 %collective-permute-start.27 = (bf16[896,128]{1,0:T(8,128)(2,1)S(1)}, bf16[896,128]{1,0:T(8,128)(2,1)S(1)}, u32[]{:S(2)}, u32[]{:S(2)}) collective-permute-start(bf16[896,128]{1,0:T(8,128)(2,1)S(1)} %collective-permute-done.23.refs_2_), channel_id=1, source_target_pairs={{0,1},{1,0},{2,3},{3,2},{4,5},{5,4},{6,7},{7,6},{8,9},{9,8},{10,11... | collective-permute-start | bytes 688136 | tf_op jit(solution)/shard_map/ppermute | solution.py:585
  69.3 23.5 %collective-permute-start.26 = (bf16[896,128]{1,0:T(8,128)(2,1)S(1)}, bf16[896,128]{1,0:T(8,128)(2,1)S(1)}, u32[]{:S(2)}, u32[]{:S(2)}) collective-permute-start(bf16[896,128]{1,0:T(8,128)(2,1)S(1)} %collective-permute-done.20.refs_1_), channel_id=1, source_target_pairs={{0,1},{1,0},{2,3},{3,2},{4,5},{5,4},{6,7},{7,6},{8,9},{9,8},{10,11... | collective-permute-start | bytes 688136 | tf_op jit(solution)/shard_map/ppermute | solution.py:585
  70.6 24.1 %collective-permute-start.22 = (bf16[896,128]{1,0:T(8,128)(2,1)S(1)}, bf16[896,128]{1,0:T(8,128)(2,1)S(1)}, u32[]{:S(2)}, u32[]{:S(2)}) collective-permute-start(bf16[896,128]{1,0:T(8,128)(2,1)S(1)} %collective-permute-done.21.refs_0_), channel_id=1, source_target_pairs={{0,1},{1,0},{2,3},{3,2},{4,5},{5,4},{6,7},{7,6},{8,9},{9,8},{10,11... | collective-permute-start | bytes 688136 | tf_op jit(solution)/shard_map/ppermute | solution.py:585
  71.5 4.2 %collective-permute-start.9 = (bf16[2,144,128]{2,1,0:T(8,128)(2,1)S(1)}, bf16[2,144,128]{2,1,0:T(8,128)(2,1)S(1)}, u32[]{:S(2)}, u32[]{:S(2)}) collective-permute-start(bf16[2,144,128]{2,1,0:T(8,128)(2,1)S(1)} %get-tuple-element.61), channel_id=1, source_target_pairs={{0,1},{1,0},{2,3},{3,2},{4,5},{5,4},{6,7},{7,6},{8,9},{9,8},{10,11... | collective-permute-start | bytes 221192 | tf_op jit(solution)/shard_map/ppermute | solution.py:399
  75.6 5.7 %collective-permute-start.10 = (bf16[2,144,128]{2,1,0:T(8,128)(2,1)S(1)}, bf16[2,144,128]{2,1,0:T(8,128)(2,1)S(1)}, u32[]{:S(2)}, u32[]{:S(2)}) collective-permute-start(bf16[2,144,128]{2,1,0:T(8,128)(2,1)S(1)} %get-tuple-element.62), channel_id=1, source_target_pairs={{1,2},{2,1},{3,4},{4,3},{5,6},{6,5},{9,10},{10,9},{11,12},{12,11},... | collective-permute-start | bytes 221192 | tf_op jit(solution)/shard_map/ppermute | solution.py:398
  81.3 3.4 %collective-permute-start.24 = (bf16[32,128]{1,0:T(8,128)(2,1)S(1)}, bf16[32,128]{1,0:T(8,128)(2,1)S(1)}, u32[]{:S(2)}, u32[]{:S(2)}) collective-permute-start(bf16[32,128]{1,0:T(8,128)(2,1)S(1)} %shard_map.106), channel_id=1, source_target_pairs={{0,24},{1,25},{2,26},{3,27},{4,28},{5,29},{6,30},{7,31},{8,16},{9,... | collective-permute-start | bytes 24584 | tf_op jit(solution)/shard_map/ppermute | solution.py:552
  84.7 8.0 %collective-permute-start.28 = (bf16[32,128]{1,0:T(8,128)(2,1)S(1)}, bf16[32,128]{1,0:T(8,128)(2,1)S(1)}, u32[]{:S(2)}, u32[]{:S(2)}) collective-permute-start(bf16[32,128]{1,0:T(8,128)(2,1)S(1)} %collective-permute-done.24.refs_3_), channel_id=1, source_target_pairs={{0,1},{1,0},{2,3},{3,2},{4,5},{5,4},{6,7},{7,6},{8,9},{9,8},{10,11... | collective-permute-start | bytes 24584 | tf_op jit(solution)/shard_map/ppermute | solution.py:583

commit v8 on v7

--- a/solution.py
+++ b/solution.py
@@ -177,8 +177,8 @@
     total = jnp.zeros((1, C), f32)
     for s in range(2):
         live, bx, by = place(pos, s)
-        hg[...] = convolve(grid, 1, bx, by, cols, w2, True)
-        first = convolve(grid, 0, bx, by, cols, w1, False)
+        hg[...] = convolve(grid, 1, bx, by, cols.at[2 * s], w2, True)
+        first = convolve(grid, 0, bx, by, cols.at[2 * s + 1], w1, False)
         center = first - jnp.mean(first, axis=1, keepdims=True)
         spread = jnp.mean(center * center, axis=1, keepdims=True)
         inv = lax.rsqrt(spread + 1e-05)
@@ -485,7 +485,7 @@
     hid, pre, msg, gain_part = call(
         main_body,
         [sds((2, 512, C), bf16)] * 2 + [sds((P_ROWS + sum(FACES), C), bf16), sds((8, C), f32)],
-        [grid, cols, pltpu.VMEM((512, C), f32)],
+        [grid, pltpu.VMEM((4, 512, 9 * C), bf16), pltpu.VMEM((512, C), f32)],
         (brick_pos, features, cotangent, *edge, w1, t2, gain),
         1,
         14,

time: 96.2 us -> 95.9 us (level)
  no operation moved by 1% of the time
where the time goes in v8:
time: 95.9 us; the launch traced here: 95.6 us
  starting transfers between devices  39.7 us (41%)
  waiting for transfers between devices  29.1 us (30%)
  Pallas kernels  25.5 us (27%)
  between operations  1.03 us (1%)
    pallas_call x14, Pallas kernels, call(): pl.pallas_call(kernel, out_shape=outs, in_specs=[SMEM] * n_smem + [VMEM]...  22.6 us
    ppermute x13, waiting for transfers between devices, per_device(): swap = lambda v, dx, dy=0: lax.ppermute(v, both, pairs(dx, dy))  21.7 us
    ppermute x4, starting transfers between devices, across(): b = lax.ppermute(b, axis, odd)  13.1 us
    ppermute x13, starting transfers between devices, per_device(): swap = lambda v, dx, dy=0: lax.ppermute(v, both, pairs(dx, dy))  9.65 us
    ppermute x4, starting transfers between devices, per_device(): part = [lax.ppermute(v, 'gy', partner) for v in own]  8.51 us
    ppermute x4, waiting for transfers between devices, across(): b = lax.ppermute(b, axis, odd)  6.43 us
    ppermute x4, starting transfers between devices, across(): a = lax.ppermute(a, axis, even)  5.12 us
    pallas_call x2, Pallas kernels, pieces_call(): pl.pallas_call(lambda *refs: body(who(), *refs, chunks=chunks), out_shape...  2.97 us
  transfers between devices with their start and end apart: 29, of which 12 were waited for; matrix products, arithmetic and copies ran while one was open for 0% of the time, Pallas kernels for 18%

profile of v8, /device:TPU:21, one launch (start us, length us, event | category | flops | bytes accessed | tf_op | source)
XLA Modules:
  0.0 95.6 jit_solution(6016609801667891868)
XLA Ops:
  0.6 1.3 %shard_map.93 = (bf16[2,512,128]{2,1,0:T(8,128)(2,1)S(1)}, bf16[2,512,128]{2,1,0:T(8,128)(2,1)S(1)}, bf16[2,512,128]{2,1,0:T(8,128)(2,1)S(1)}, bf16[2,128,128]{2,1,0:T(8,128)(2,1)S(1)}, bf16[2,128,128]{2,1,0:T(8,128)(2,1)S(1)}) custom-call(s32[2]{0:T(128)} %refs_0_.19, bf16[2,512,128]{2,1,0:T(8,128)(2,1)} %refs_1_.2, bf16[2,512,128]{2,1,0:T(8,128)(2,1)} %refs_2_.1), custom_call_target="tpu_custom_call" | custom-call | tf_op jit(solution)/shard_map/pallas_call | solution.py:38
  1.9 0.7 collective-permute-start.3
  2.7 1.2 %collective-permute-start = (bf16[2,128,128]{2,1,0:T(8,128)(2,1)S(1)}, bf16[2,128,128]{2,1,0:T(8,128)(2,1)S(1)}, u32[]{:S(2)}, u32[]{:S(2)}) collective-permute-start(bf16[2,128,128]{2,1,0:T(8,128)(2,1)S(1)} %get-tuple-element.42), channel_id=1, source_target_pairs={{0,8},{8,0},{16,24},{24,16},{1,9},{9,1},{17,25},{25,17},{2,10},{10... | collective-permute-start | bytes 196616 | tf_op jit(solution)/shard_map/ppermute | solution.py:399
  3.9 2.1 %collective-permute-start.1 = (bf16[2,128,128]{2,1,0:T(8,128)(2,1)S(1)}, bf16[2,128,128]{2,1,0:T(8,128)(2,1)S(1)}, u32[]{:S(2)}, u32[]{:S(2)}) collective-permute-start(bf16[2,128,128]{2,1,0:T(8,128)(2,1)S(1)} %get-tuple-element.43), channel_id=1, source_target_pairs={{8,16},{16,8},{9,17},{17,9},{10,18},{18,10},{11,19},{19,11},{12,20... | collective-permute-start | bytes 196616 | tf_op jit(solution)/shard_map/ppermute | solution.py:398
  6.0 0.7 collective-permute-start.2
  6.7 2.0 %shard_map.94 = (bf16[1152,384]{1,0:T(8,128)(2,1)S(1)}, bf16[1152,384]{1,0:T(8,128)(2,1)S(1)}, bf16[384,1152]{1,0:T(8,128)(2,1)S(1)}, bf16[384,1152]{1,0:T(8,128)(2,1)S(1)}, f32[1,128]{1,0:T(1,128)S(1)}) custom-call(bf16[27,128,128]{2,1,0:T(8,128)(2,1)} %refs_0_.11, bf16[27,128,128]{2,1,0:T(8,128)(2,1)} %refs_1_.3, f32[1,128]{1,0:T(1,128)} %bitcast.4), custom_call_target="tpu_custom_call" | custom-call | tf_op jit(solution)/shard_map/pallas_call | solution.py:38
  8.7 1.1 %collective-permute-done.1.refs_4_ = bf16[2,128,128]{2,1,0:T(8,128)(2,1)S(1)} collective-permute-done((bf16[2,128,128]{2,1,0:T(8,128)(2,1)S(1)}, bf16[2,128,128]{2,1,0:T(8,128)(2,1)S(1)}, u32[]{:S(2)}, u32[]{:S(2)}) %collective-permute-start.1) | collective-permute-done | bytes 65568 | tf_op jit(solution)/shard_map/ppermute | solution.py:398
  9.8 0.8 shard_map.95
  10.6 4.6 %collective-permute-start.5 = (bf16[2,144,128]{2,1,0:T(8,128)(2,1)S(1)}, bf16[2,144,128]{2,1,0:T(8,128)(2,1)S(1)}, u32[]{:S(2)}, u32[]{:S(2)}) collective-permute-start(bf16[2,144,128]{2,1,0:T(8,128)(2,1)S(1)} %get-tuple-element.49), channel_id=1, source_target_pairs={{1,2},{2,1},{3,4},{4,3},{5,6},{6,5},{9,10},{10,9},{11,12},{12,11},... | collective-permute-start | bytes 221192 | tf_op jit(solution)/shard_map/ppermute | solution.py:398
  15.3 2.1 %collective-permute-done.5.refs_6_ = bf16[2,144,128]{2,1,0:T(8,128)(2,1)S(1)} collective-permute-done((bf16[2,144,128]{2,1,0:T(8,128)(2,1)S(1)}, bf16[2,144,128]{2,1,0:T(8,128)(2,1)S(1)}, u32[]{:S(2)}, u32[]{:S(2)}) %collective-permute-start.5) | collective-permute-done | bytes 73760 | tf_op jit(solution)/shard_map/ppermute | solution.py:398
  17.4 4.2 %shard_map.96 = (bf16[2,512,128]{2,1,0:T(8,128)(2,1)S(1)}, bf16[2,512,128]{2,1,0:T(8,128)(2,1)S(1)}, bf16[1584,128]{1,0:T(8,128)(2,1)S(1)}, f32[8,128]{1,0:T(8,128)S(1)}) custom-call(s32[2]{0:T(128)} %refs_0_.19, bf16[2,512,128]{2,1,0:T(8,128)(2,1)S(1)} %get-tuple-element.45.refs_1_.refs_7_, bf16[2,512,128]{2,1,0:T(8,128)(2,1)S(1)} %get-tuple-element.41.refs_2_.refs_7_, ...), custom_call_target="tpu_custom_call" | custom-call | tf_op jit(solution)/shard_map/pallas_call | solution.py:38
  21.7 0.4 collective-permute-start.6
  22.1 1.9 %shard_map.97 = (f32[18,18,8,128]{3,2,1,0:T(8,128)S(1)}, bf16[384,1024]{1,0:T(8,128)(2,1)S(1)}, f32[384,640]{1,0:T(8,128)S(1)}) custom-call(s32[2]{0:T(128)} %refs_0_.19, bf16[2,512,128]{2,1,0:T(8,128)(2,1)S(1)} %get-tuple-element.45.refs_1_.refs_7_, bf16[2,512,128]{2,1,0:T(8,128)(2,1)S(1)} %get-tuple-element.41.refs_2_.refs_7_, ...), custom_call_target="tpu_custom_call" | custom-call | tf_op jit(solution)/shard_map/pallas_call | solution.py:38
  24.0 1.7 %shard_map.98 = (f32[18,18,8,128]{3,2,1,0:T(8,128)S(1)}, bf16[384,1024]{1,0:T(8,128)(2,1)S(1)}, bf16[864,128]{1,0:T(8,128)(2,1)S(1)}, bf16[864,128]{1,0:T(8,128)(2,1)S(1)}, f32[8,128]{1,0:T(8,128)S(1)}) custom-call(s32[2]{0:T(128)S(1)} %collective-permute-done.2.refs_0_.refs_1_, bf16[2,512,128]{2,1,0:T(8,128)(2,1)S(1)} %collective-permute-done.3.refs_1_, ...), custom_call_target="tpu_custom_call" | custom-call | tf_op jit(solution)/shard_map/pallas_call | solution.py:38
  25.8 1.5 %collective-permute-start.11 = (bf16[864,128]{1,0:T(8,128)(2,1)S(1)}, bf16[864,128]{1,0:T(8,128)(2,1)S(1)}, u32[]{:S(2)}, u32[]{:S(2)}) collective-permute-start(bf16[864,128]{1,0:T(8,128)(2,1)S(1)} %get-tuple-element.70), channel_id=1, source_target_pairs={{0,8},{1,17},{2,10},{3,19},{4,12},{5,21},{6,14},{7,23},{8,0},{9,25... | collective-permute-start | bytes 663560 | tf_op jit(solution)/shard_map/ppermute | solution.py:552
  27.2 2.4 %shard_map.103 = (f32[864,128]{1,0:T(8,128)S(1)}, f32[864,128]{1,0:T(8,128)S(1)}) custom-call(s32[2]{0:T(128)} %refs_0_.19, s32[2]{0:T(128)S(1)} %collective-permute-done.2.refs_0_.refs_1_, f32[18,18,8,128]{3,2,1,0:T(8,128)S(1)} %get-tuple-element.65.refs_2_, f32[18,18,8,128]{3,2,1,0:T(8,128)S(1)} %get-tuple-element.66.refs_3_, ...), custom_call_target="tpu_custom_call" | custom-call | tf_op jit(solution)/shard_map/pallas_call | solution.py:38
  29.6 1.2 %collective-permute-done.12 = bf16[864,128]{1,0:T(8,128)(2,1)S(1)} collective-permute-done((bf16[864,128]{1,0:T(8,128)(2,1)S(1)}, bf16[864,128]{1,0:T(8,128)(2,1)S(1)}, u32[]{:S(2)}, u32[]{:S(2)}) %collective-permute-start.12) | collective-permute-done | bytes 221216 | tf_op jit(solution)/shard_map/ppermute | solution.py:552
  31.0 2.2 %collective-permute-done.11 = bf16[864,128]{1,0:T(8,128)(2,1)S(1)} collective-permute-done((bf16[864,128]{1,0:T(8,128)(2,1)S(1)}, bf16[864,128]{1,0:T(8,128)(2,1)S(1)}, u32[]{:S(2)}, u32[]{:S(2)}) %collective-permute-start.11) | collective-permute-done | bytes 221216 | tf_op jit(solution)/shard_map/ppermute | solution.py:552
  33.2 3.3 %collective-permute-done.13 = bf16[864,128]{1,0:T(8,128)(2,1)S(1)} collective-permute-done((bf16[864,128]{1,0:T(8,128)(2,1)S(1)}, bf16[864,128]{1,0:T(8,128)(2,1)S(1)}, u32[]{:S(2)}, u32[]{:S(2)}) %collective-permute-start.13) | collective-permute-done | bytes 221216 | tf_op jit(solution)/shard_map/ppermute | solution.py:552
  36.5 0.1 fusion.2
  36.6 1.2 %collective-permute-start.15 = (f32[216,128]{1,0:T(8,128)S(1)}, f32[216,128]{1,0:T(8,128)S(1)}, u32[]{:S(2)}, u32[]{:S(2)}) collective-permute-start(f32[216,128]{1,0:T(8,128)S(1)} %slice.24), channel_id=1, source_target_pairs={{0,2},{1,3},{2,0},{3,1},{4,6},{5,7},{6,4},{7,5},{8,10},{9,11},{10,... | collective-permute-start | bytes 331784 | tf_op jit(solution)/shard_map/ppermute | solution.py:552
  37.8 0.2 collective-permute-start.14
  38.1 1.3 %collective-permute-start.16 = (bf16[216,128]{1,0:T(8,128)(2,1)S(1)}, bf16[216,128]{1,0:T(8,128)(2,1)S(1)}, u32[]{:S(2)}, u32[]{:S(2)}) collective-permute-start(bf16[216,128]{1,0:T(8,128)(2,1)S(1)} %get-tuple-element.79), channel_id=1, source_target_pairs={{0,6},{1,7},{2,4},{3,5},{4,2},{5,3},{6,0},{7,1},{8,14},{9,15},{10,... | collective-permute-start | bytes 165896 | tf_op jit(solution)/shard_map/ppermute | solution.py:552
  39.4 3.0 %collective-permute-done.14 = bf16[216,128]{1,0:T(8,128)(2,1)S(1)} collective-permute-done((bf16[216,128]{1,0:T(8,128)(2,1)S(1)}, bf16[216,128]{1,0:T(8,128)(2,1)S(1)}, u32[]{:S(2)}, u32[]{:S(2)}) %collective-permute-start.14) | collective-permute-done | bytes 55328 | tf_op jit(solution)/shard_map/ppermute | solution.py:552
  42.5 0.6 collective-permute-start.19
  43.1 3.9 %collective-permute-start.18 = (bf16[224,128]{1,0:T(8,128)(2,1)S(1)}, bf16[224,128]{1,0:T(8,128)(2,1)S(1)}, u32[]{:S(2)}, u32[]{:S(2)}) collective-permute-start(bf16[224,128]{1,0:T(8,128)(2,1)S(1)} %shard_map.104.refs_0_), channel_id=1, source_target_pairs={{0,2},{1,3},{2,0},{3,1},{4,6},{5,7},{6,4},{7,5},{8,10},{9,11},{10,... | collective-permute-start | bytes 172040 | tf_op jit(solution)/shard_map/ppermute | solution.py:552
  47.0 2.2 %collective-permute-done.18.refs_2_ = bf16[224,128]{1,0:T(8,128)(2,1)S(1)} collective-permute-done((bf16[224,128]{1,0:T(8,128)(2,1)S(1)}, bf16[224,128]{1,0:T(8,128)(2,1)S(1)}, u32[]{:S(2)}, u32[]{:S(2)}) %collective-permute-start.18) | collective-permute-done | bytes 57376 | tf_op jit(solution)/shard_map/ppermute | solution.py:552
  49.2 2.3 %collective-permute-done.17.refs_1_ = bf16[224,128]{1,0:T(8,128)(2,1)S(1)} collective-permute-done((bf16[224,128]{1,0:T(8,128)(2,1)S(1)}, bf16[224,128]{1,0:T(8,128)(2,1)S(1)}, u32[]{:S(2)}, u32[]{:S(2)}) %collective-permute-start.17) | collective-permute-done | bytes 57376 | tf_op jit(solution)/shard_map/ppermute | solution.py:552
  51.5 0.5 collective-permute-start.23
  52.1 4.3 %collective-permute-done.20.refs_1_ = bf16[896,128]{1,0:T(8,128)(2,1)S(1)} collective-permute-done((bf16[896,128]{1,0:T(8,128)(2,1)S(1)}, bf16[896,128]{1,0:T(8,128)(2,1)S(1)}, u32[]{:S(2)}, u32[]{:S(2)}) %collective-permute-start.20) | collective-permute-done | bytes 229408 | tf_op jit(solution)/shard_map/ppermute | solution.py:552
  56.4 0.8 shard_map.99
  57.2 0.6 collective-permute-start.7
  57.8 4.0 %collective-permute-start.8 = (bf16[2,128,128]{2,1,0:T(8,128)(2,1)S(1)}, bf16[2,128,128]{2,1,0:T(8,128)(2,1)S(1)}, u32[]{:S(2)}, u32[]{:S(2)}) collective-permute-start(bf16[2,128,128]{2,1,0:T(8,128)(2,1)S(1)} %get-tuple-element.60), channel_id=1, source_target_pairs={{8,16},{16,8},{9,17},{17,9},{10,18},{18,10},{11,19},{19,11},{12,20... | collective-permute-start | bytes 196616 | tf_op jit(solution)/shard_map/ppermute | solution.py:398
  61.8 7.1 %collective-permute-start.25 = (bf16[896,128]{1,0:T(8,128)(2,1)S(1)}, bf16[896,128]{1,0:T(8,128)(2,1)S(1)}, u32[]{:S(2)}, u32[]{:S(2)}) collective-permute-start(bf16[896,128]{1,0:T(8,128)(2,1)S(1)} %shard_map.105.refs_0_), channel_id=1, source_target_pairs={{0,1},{1,0},{2,3},{3,2},{4,5},{5,4},{6,7},{7,6},{8,9},{9,8},{10,11... | collective-permute-start | bytes 688136 | tf_op jit(solution)/shard_map/ppermute | solution.py:585
  68.9 0.1 collective-permute-start.27
  69.0 1.3 %collective-permute-start.26 = (bf16[896,128]{1,0:T(8,128)(2,1)S(1)}, bf16[896,128]{1,0:T(8,128)(2,1)S(1)}, u32[]{:S(2)}, u32[]{:S(2)}) collective-permute-start(bf16[896,128]{1,0:T(8,128)(2,1)S(1)} %collective-permute-done.20.refs_1_), channel_id=1, source_target_pairs={{0,1},{1,0},{2,3},{3,2},{4,5},{5,4},{6,7},{7,6},{8,9},{9,8},{10,11... | collective-permute-start | bytes 688136 | tf_op jit(solution)/shard_map/ppermute | solution.py:585
  70.4 0.8 shard_map.100
  71.2 3.3 %collective-permute-start.9 = (bf16[2,144,128]{2,1,0:T(8,128)(2,1)S(1)}, bf16[2,144,128]{2,1,0:T(8,128)(2,1)S(1)}, u32[]{:S(2)}, u32[]{:S(2)}) collective-permute-start(bf16[2,144,128]{2,1,0:T(8,128)(2,1)S(1)} %get-tuple-element.61), channel_id=1, source_target_pairs={{0,1},{1,0},{2,3},{3,2},{4,5},{5,4},{6,7},{7,6},{8,9},{9,8},{10,11... | collective-permute-start | bytes 221192 | tf_op jit(solution)/shard_map/ppermute | solution.py:399
  74.5 0.9 collective-permute-done.9.refs_4_
  75.4 2.4 %collective-permute-start.10 = (bf16[2,144,128]{2,1,0:T(8,128)(2,1)S(1)}, bf16[2,144,128]{2,1,0:T(8,128)(2,1)S(1)}, u32[]{:S(2)}, u32[]{:S(2)}) collective-permute-start(bf16[2,144,128]{2,1,0:T(8,128)(2,1)S(1)} %get-tuple-element.62), channel_id=1, source_target_pairs={{1,2},{2,1},{3,4},{4,3},{5,6},{6,5},{9,10},{10,9},{11,12},{12,11},... | collective-permute-start | bytes 221192 | tf_op jit(solution)/shard_map/ppermute | solution.py:398
  77.8 3.3 %collective-permute-done.10.refs_5_ = bf16[2,144,128]{2,1,0:T(8,128)(2,1)S(1)} collective-permute-done((bf16[2,144,128]{2,1,0:T(8,128)(2,1)S(1)}, bf16[2,144,128]{2,1,0:T(8,128)(2,1)S(1)}, u32[]{:S(2)}, u32[]{:S(2)}) %collective-permute-start.10) | collective-permute-done | bytes 73760 | tf_op jit(solution)/shard_map/ppermute | solution.py:398
  81.0 0.2 collective-permute-start.24
  81.2 3.2 %collective-permute-done.24.refs_3_ = bf16[32,128]{1,0:T(8,128)(2,1)S(1)} collective-permute-done((bf16[32,128]{1,0:T(8,128)(2,1)S(1)}, bf16[32,128]{1,0:T(8,128)(2,1)S(1)}, u32[]{:S(2)}, u32[]{:S(2)}) %collective-permute-start.24) | collective-permute-done | bytes 8224 | tf_op jit(solution)/shard_map/ppermute | solution.py:552
  84.4 1.5 %collective-permute-start.28 = (bf16[32,128]{1,0:T(8,128)(2,1)S(1)}, bf16[32,128]{1,0:T(8,128)(2,1)S(1)}, u32[]{:S(2)}, u32[]{:S(2)}) collective-permute-start(bf16[32,128]{1,0:T(8,128)(2,1)S(1)} %collective-permute-done.24.refs_3_), channel_id=1, source_target_pairs={{0,1},{1,0},{2,3},{3,2},{4,5},{5,4},{6,7},{7,6},{8,9},{9,8},{10,11... | collective-permute-start | bytes 24584 | tf_op jit(solution)/shard_map/ppermute | solution.py:583
  85.9 3.4 %shard_map.102 = bf16[2,512,128]{2,1,0:T(8,128)(2,1)} custom-call(s32[2]{0:T(128)} %refs_0_.19, bf16[2,512,128]{2,1,0:T(8,128)(2,1)S(1)} %get-tuple-element.55.refs_8_.refs_2_.refs_1_, bf16[2,128,128]{2,1,0:T(8,128)(2,1)S(1)} %collective-permute-done.7.refs_3_.refs_2_, bf16[2,128,128]{2,1,0:T(8,128)(2,1)S(1)} %collective-permute-done.8.refs_4_.refs_3_, ...), custom_call_target="tpu_custom_call" | custom-call | tf_op jit(solution)/shard_map/pallas_call | solution.py:38
  89.3 3.2 %shard_map.101 = bf16[2,512,128]{2,1,0:T(8,128)(2,1)} custom-call(s32[2]{0:T(128)} %refs_0_.19, bf16[2,512,128]{2,1,0:T(8,128)(2,1)S(1)} %get-tuple-element.58.refs_7_.refs_1_, bf16[2,128,128]{2,1,0:T(8,128)(2,1)S(1)} %collective-permute-done.7.refs_3_.refs_2_, bf16[2,128,128]{2,1,0:T(8,128)(2,1)S(1)} %collective-permute-done.8.refs_4_.refs_3_, ...), custom_call_target="tpu_custom_call" | custom-call | tf_op jit(solution)/shard_map/pallas_call | solution.py:38
  92.5 2.0 %shard_map.107 = (f32[2,3456,128]{2,1,0:T(8,128)}, f32[1,128]{1,0:T(1,128)}, f32[8,128]{1,0:T(8,128)S(1)}) custom-call(bf16[896,128]{1,0:T(8,128)(2,1)S(1)} %shard_map.105.refs_0_, bf16[896,128]{1,0:T(8,128)(2,1)S(1)} %collective-permute-done.20.refs_1_, bf16[896,128]{1,0:T(8,128)(2,1)S(1)} %collective-permute-done.23.refs_2_, ...), custom_call_target="tpu_custom_call" | custom-call | tf_op jit(solution)/shard_map/pallas_call | solution.py:589
  94.5 1.0 %shard_map.108 = f32[2,3456,128]{2,1,0:T(8,128)} custom-call(bf16[896,128]{1,0:T(8,128)(2,1)S(1)} %collective-permute-done.21.refs_0_, bf16[896,128]{1,0:T(8,128)(2,1)S(1)} %collective-permute-done.22.refs_1_, f32[8,128]{1,0:T(8,128)S(1)} %get-tuple-element.73.refs_2_, f32[2,3456,128]{2,1,0:T(8,128)} %get-tuple-element.74.refs_3_), custom_call_target="tpu_custom_call", output_to_operand_aliasing={{}: (3, {})} | custom-call | tf_op jit(solution)/shard_map/pallas_call | solution.py:589
  (32 shorter events, 0.5 us)
Async XLA Ops:
  1.9 13.3 %collective-permute-start.3 = (bf16[2,512,128]{2,1,0:T(8,128)(2,1)S(1)}, bf16[2,512,128]{2,1,0:T(8,128)(2,1)S(1)}, u32[]{:S(2)}, u32[]{:S(2)}) collective-permute-start(bf16[2,512,128]{2,1,0:T(8,128)(2,1)S(1)} %get-tuple-element.47), channel_id=1, source_target_pairs={{0,1},{1,0},{2,3},{3,2},{4,5},{5,4},{6,7},{7,6},{8,9},{9,8},{10,11... | collective-permute-start | bytes 786440 | tf_op jit(solution)/shard_map/ppermute | solution.py:471
  2.7 6.0 %collective-permute-start = (bf16[2,128,128]{2,1,0:T(8,128)(2,1)S(1)}, bf16[2,128,128]{2,1,0:T(8,128)(2,1)S(1)}, u32[]{:S(2)}, u32[]{:S(2)}) collective-permute-start(bf16[2,128,128]{2,1,0:T(8,128)(2,1)S(1)} %get-tuple-element.42), channel_id=1, source_target_pairs={{0,8},{8,0},{16,24},{24,16},{1,9},{9,1},{17,25},{25,17},{2,10},{10... | collective-permute-start | bytes 196616 | tf_op jit(solution)/shard_map/ppermute | solution.py:399
  3.9 5.9 %collective-permute-start.1 = (bf16[2,128,128]{2,1,0:T(8,128)(2,1)S(1)}, bf16[2,128,128]{2,1,0:T(8,128)(2,1)S(1)}, u32[]{:S(2)}, u32[]{:S(2)}) collective-permute-start(bf16[2,128,128]{2,1,0:T(8,128)(2,1)S(1)} %get-tuple-element.43), channel_id=1, source_target_pairs={{8,16},{16,8},{9,17},{17,9},{10,18},{18,10},{11,19},{19,11},{12,20... | collective-permute-start | bytes 196616 | tf_op jit(solution)/shard_map/ppermute | solution.py:398
  6.0 9.2 %collective-permute-start.2 = (s32[2]{0:T(128)}, s32[2]{0:T(128)S(1)}, u32[]{:S(2)}, u32[]{:S(2)}) collective-permute-start(s32[2]{0:T(128)} %refs_0_.19), channel_id=1, source_target_pairs={{0,1},{1,0},{2,3},{3,2},{4,5},{5,4},{6,7},{7,6},{8,9},{9,8},{10,11... | collective-permute-start | bytes 32 | tf_op jit(solution)/shard_map/ppermute | solution.py:470
  10.6 6.8 %collective-permute-start.5 = (bf16[2,144,128]{2,1,0:T(8,128)(2,1)S(1)}, bf16[2,144,128]{2,1,0:T(8,128)(2,1)S(1)}, u32[]{:S(2)}, u32[]{:S(2)}) collective-permute-start(bf16[2,144,128]{2,1,0:T(8,128)(2,1)S(1)} %get-tuple-element.49), channel_id=1, source_target_pairs={{1,2},{2,1},{3,4},{4,3},{5,6},{6,5},{9,10},{10,9},{11,12},{12,11},... | collective-permute-start | bytes 221192 | tf_op jit(solution)/shard_map/ppermute | solution.py:398
  15.3 2.2 %collective-permute-start.4 = (bf16[2,144,128]{2,1,0:T(8,128)(2,1)S(1)}, bf16[2,144,128]{2,1,0:T(8,128)(2,1)S(1)}, u32[]{:S(2)}, u32[]{:S(2)}) collective-permute-start(bf16[2,144,128]{2,1,0:T(8,128)(2,1)S(1)} %get-tuple-element.48), channel_id=1, source_target_pairs={{0,1},{1,0},{2,3},{3,2},{4,5},{5,4},{6,7},{7,6},{8,9},{9,8},{10,11... | collective-permute-start | bytes 221192 | tf_op jit(solution)/shard_map/ppermute | solution.py:399
  21.7 2.3 %collective-permute-start.6 = (bf16[1584,128]{1,0:T(8,128)(2,1)S(1)}, bf16[1584,128]{1,0:T(8,128)(2,1)S(1)}, u32[]{:S(2)}, u32[]{:S(2)}) collective-permute-start(bf16[1584,128]{1,0:T(8,128)(2,1)S(1)} %get-tuple-element.53), channel_id=1, source_target_pairs={{0,1},{1,0},{2,3},{3,2},{4,5},{5,4},{6,7},{7,6},{8,9},{9,8},{10,11... | collective-permute-start | bytes 1216520 | tf_op jit(solution)/shard_map/ppermute | solution.py:494
  25.7 5.1 %collective-permute-start.12 = (bf16[864,128]{1,0:T(8,128)(2,1)S(1)}, bf16[864,128]{1,0:T(8,128)(2,1)S(1)}, u32[]{:S(2)}, u32[]{:S(2)}) collective-permute-start(bf16[864,128]{1,0:T(8,128)(2,1)S(1)} %get-tuple-element.57), channel_id=1, source_target_pairs={{0,8},{1,17},{2,10},{3,19},{4,12},{5,21},{6,14},{7,23},{8,0},{9,25... | collective-permute-start | bytes 663560 | tf_op jit(solution)/shard_map/ppermute | solution.py:552
  25.8 7.4 %collective-permute-start.11 = (bf16[864,128]{1,0:T(8,128)(2,1)S(1)}, bf16[864,128]{1,0:T(8,128)(2,1)S(1)}, u32[]{:S(2)}, u32[]{:S(2)}) collective-permute-start(bf16[864,128]{1,0:T(8,128)(2,1)S(1)} %get-tuple-element.70), channel_id=1, source_target_pairs={{0,8},{1,17},{2,10},{3,19},{4,12},{5,21},{6,14},{7,23},{8,0},{9,25... | collective-permute-start | bytes 663560 | tf_op jit(solution)/shard_map/ppermute | solution.py:552
  30.9 5.6 %collective-permute-start.13 = (bf16[864,128]{1,0:T(8,128)(2,1)S(1)}, bf16[864,128]{1,0:T(8,128)(2,1)S(1)}, u32[]{:S(2)}, u32[]{:S(2)}) collective-permute-start(bf16[864,128]{1,0:T(8,128)(2,1)S(1)} %add_convert_fusion), channel_id=1, source_target_pairs={{0,16},{1,9},{2,18},{3,11},{4,20},{5,13},{6,22},{7,15},{8,24},{9,1... | collective-permute-start | bytes 663560 | tf_op jit(solution)/shard_map/ppermute | solution.py:552
  36.6 5.8 %collective-permute-start.15 = (f32[216,128]{1,0:T(8,128)S(1)}, f32[216,128]{1,0:T(8,128)S(1)}, u32[]{:S(2)}, u32[]{:S(2)}) collective-permute-start(f32[216,128]{1,0:T(8,128)S(1)} %slice.24), channel_id=1, source_target_pairs={{0,2},{1,3},{2,0},{3,1},{4,6},{5,7},{6,4},{7,5},{8,10},{9,11},{10,... | collective-permute-start | bytes 331784 | tf_op jit(solution)/shard_map/ppermute | solution.py:552
  37.8 4.6 %collective-permute-start.14 = (bf16[216,128]{1,0:T(8,128)(2,1)S(1)}, bf16[216,128]{1,0:T(8,128)(2,1)S(1)}, u32[]{:S(2)}, u32[]{:S(2)}) collective-permute-start(bf16[216,128]{1,0:T(8,128)(2,1)S(1)} %get-tuple-element.78), channel_id=1, source_target_pairs={{0,4},{1,5},{2,6},{3,7},{4,0},{5,1},{6,2},{7,3},{8,12},{9,13},{10,... | collective-permute-start | bytes 165896 | tf_op jit(solution)/shard_map/ppermute | solution.py:552
  38.1 4.3 %collective-permute-start.16 = (bf16[216,128]{1,0:T(8,128)(2,1)S(1)}, bf16[216,128]{1,0:T(8,128)(2,1)S(1)}, u32[]{:S(2)}, u32[]{:S(2)}) collective-permute-start(bf16[216,128]{1,0:T(8,128)(2,1)S(1)} %get-tuple-element.79), channel_id=1, source_target_pairs={{0,6},{1,7},{2,4},{3,5},{4,2},{5,3},{6,0},{7,1},{8,14},{9,15},{10,... | collective-permute-start | bytes 165896 | tf_op jit(solution)/shard_map/ppermute | solution.py:552
  42.5 4.5 %collective-permute-start.19 = (bf16[224,128]{1,0:T(8,128)(2,1)S(1)}, bf16[224,128]{1,0:T(8,128)(2,1)S(1)}, u32[]{:S(2)}, u32[]{:S(2)}) collective-permute-start(bf16[224,128]{1,0:T(8,128)(2,1)S(1)} %shard_map.104.refs_0_), channel_id=1, source_target_pairs={{0,6},{1,7},{2,4},{3,5},{4,2},{5,3},{6,0},{7,1},{8,14},{9,15},{10,... | collective-permute-start | bytes 172040 | tf_op jit(solution)/shard_map/ppermute | solution.py:552
  43.1 6.1 %collective-permute-start.18 = (bf16[224,128]{1,0:T(8,128)(2,1)S(1)}, bf16[224,128]{1,0:T(8,128)(2,1)S(1)}, u32[]{:S(2)}, u32[]{:S(2)}) collective-permute-start(bf16[224,128]{1,0:T(8,128)(2,1)S(1)} %shard_map.104.refs_0_), channel_id=1, source_target_pairs={{0,2},{1,3},{2,0},{3,1},{4,6},{5,7},{6,4},{7,5},{8,10},{9,11},{10,... | collective-permute-start | bytes 172040 | tf_op jit(solution)/shard_map/ppermute | solution.py:552
  47.0 4.4 %collective-permute-start.17 = (bf16[224,128]{1,0:T(8,128)(2,1)S(1)}, bf16[224,128]{1,0:T(8,128)(2,1)S(1)}, u32[]{:S(2)}, u32[]{:S(2)}) collective-permute-start(bf16[224,128]{1,0:T(8,128)(2,1)S(1)} %shard_map.104.refs_0_), channel_id=1, source_target_pairs={{0,4},{1,5},{2,6},{3,7},{4,0},{5,1},{6,2},{7,3},{8,12},{9,13},{10,... | collective-permute-start | bytes 172040 | tf_op jit(solution)/shard_map/ppermute | solution.py:552
  51.5 4.9 %collective-permute-start.20 = (bf16[896,128]{1,0:T(8,128)(2,1)S(1)}, bf16[896,128]{1,0:T(8,128)(2,1)S(1)}, u32[]{:S(2)}, u32[]{:S(2)}) collective-permute-start(bf16[896,128]{1,0:T(8,128)(2,1)S(1)} %shard_map.105.refs_0_), channel_id=1, source_target_pairs={{0,16},{1,9},{2,18},{3,11},{4,20},{5,13},{6,22},{7,15},{8,24},{9,1... | collective-permute-start | bytes 688136 | tf_op jit(solution)/shard_map/ppermute | solution.py:552
  51.5 17.4 %collective-permute-start.23 = (bf16[896,128]{1,0:T(8,128)(2,1)S(1)}, bf16[896,128]{1,0:T(8,128)(2,1)S(1)}, u32[]{:S(2)}, u32[]{:S(2)}) collective-permute-start(bf16[896,128]{1,0:T(8,128)(2,1)S(1)} %shard_map.105.refs_0_), channel_id=1, source_target_pairs={{0,8},{1,17},{2,10},{3,19},{4,12},{5,21},{6,14},{7,23},{8,0},{9,25... | collective-permute-start | bytes 688136 | tf_op jit(solution)/shard_map/ppermute | solution.py:552
  56.4 13.9 %collective-permute-start.21 = (bf16[896,128]{1,0:T(8,128)(2,1)S(1)}, bf16[896,128]{1,0:T(8,128)(2,1)S(1)}, u32[]{:S(2)}, u32[]{:S(2)}) collective-permute-start(bf16[896,128]{1,0:T(8,128)(2,1)S(1)} %collective-permute-done.20.refs_1_), channel_id=1, source_target_pairs={{0,8},{1,17},{2,10},{3,19},{4,12},{5,21},{6,14},{7,23},{8,0},{9,25... | collective-permute-start | bytes 688136 | tf_op jit(solution)/shard_map/ppermute | solution.py:552
  57.2 11.8 %collective-permute-start.7 = (bf16[2,128,128]{2,1,0:T(8,128)(2,1)S(1)}, bf16[2,128,128]{2,1,0:T(8,128)(2,1)S(1)}, u32[]{:S(2)}, u32[]{:S(2)}) collective-permute-start(bf16[2,128,128]{2,1,0:T(8,128)(2,1)S(1)} %get-tuple-element.59), channel_id=1, source_target_pairs={{0,8},{8,0},{16,24},{24,16},{1,9},{9,1},{17,25},{25,17},{2,10},{10... | collective-permute-start | bytes 196616 | tf_op jit(solution)/shard_map/ppermute | solution.py:399
  57.8 12.6 %collective-permute-start.8 = (bf16[2,128,128]{2,1,0:T(8,128)(2,1)S(1)}, bf16[2,128,128]{2,1,0:T(8,128)(2,1)S(1)}, u32[]{:S(2)}, u32[]{:S(2)}) collective-permute-start(bf16[2,128,128]{2,1,0:T(8,128)(2,1)S(1)} %get-tuple-element.60), channel_id=1, source_target_pairs={{8,16},{16,8},{9,17},{17,9},{10,18},{18,10},{11,19},{19,11},{12,20... | collective-permute-start | bytes 196616 | tf_op jit(solution)/shard_map/ppermute | solution.py:398
  61.8 30.6 %collective-permute-start.25 = (bf16[896,128]{1,0:T(8,128)(2,1)S(1)}, bf16[896,128]{1,0:T(8,128)(2,1)S(1)}, u32[]{:S(2)}, u32[]{:S(2)}) collective-permute-start(bf16[896,128]{1,0:T(8,128)(2,1)S(1)} %shard_map.105.refs_0_), channel_id=1, source_target_pairs={{0,1},{1,0},{2,3},{3,2},{4,5},{5,4},{6,7},{7,6},{8,9},{9,8},{10,11... | collective-permute-start | bytes 688136 | tf_op jit(solution)/shard_map/ppermute | solution.py:585
  68.9 23.6 %collective-permute-start.27 = (bf16[896,128]{1,0:T(8,128)(2,1)S(1)}, bf16[896,128]{1,0:T(8,128)(2,1)S(1)}, u32[]{:S(2)}, u32[]{:S(2)}) collective-permute-start(bf16[896,128]{1,0:T(8,128)(2,1)S(1)} %collective-permute-done.23.refs_2_), channel_id=1, source_target_pairs={{0,1},{1,0},{2,3},{3,2},{4,5},{5,4},{6,7},{7,6},{8,9},{9,8},{10,11... | collective-permute-start | bytes 688136 | tf_op jit(solution)/shard_map/ppermute | solution.py:585
  69.0 23.5 %collective-permute-start.26 = (bf16[896,128]{1,0:T(8,128)(2,1)S(1)}, bf16[896,128]{1,0:T(8,128)(2,1)S(1)}, u32[]{:S(2)}, u32[]{:S(2)}) collective-permute-start(bf16[896,128]{1,0:T(8,128)(2,1)S(1)} %collective-permute-done.20.refs_1_), channel_id=1, source_target_pairs={{0,1},{1,0},{2,3},{3,2},{4,5},{5,4},{6,7},{7,6},{8,9},{9,8},{10,11... | collective-permute-start | bytes 688136 | tf_op jit(solution)/shard_map/ppermute | solution.py:585
  70.3 24.1 %collective-permute-start.22 = (bf16[896,128]{1,0:T(8,128)(2,1)S(1)}, bf16[896,128]{1,0:T(8,128)(2,1)S(1)}, u32[]{:S(2)}, u32[]{:S(2)}) collective-permute-start(bf16[896,128]{1,0:T(8,128)(2,1)S(1)} %collective-permute-done.21.refs_0_), channel_id=1, source_target_pairs={{0,1},{1,0},{2,3},{3,2},{4,5},{5,4},{6,7},{7,6},{8,9},{9,8},{10,11... | collective-permute-start | bytes 688136 | tf_op jit(solution)/shard_map/ppermute | solution.py:585
  71.2 4.2 %collective-permute-start.9 = (bf16[2,144,128]{2,1,0:T(8,128)(2,1)S(1)}, bf16[2,144,128]{2,1,0:T(8,128)(2,1)S(1)}, u32[]{:S(2)}, u32[]{:S(2)}) collective-permute-start(bf16[2,144,128]{2,1,0:T(8,128)(2,1)S(1)} %get-tuple-element.61), channel_id=1, source_target_pairs={{0,1},{1,0},{2,3},{3,2},{4,5},{5,4},{6,7},{7,6},{8,9},{9,8},{10,11... | collective-permute-start | bytes 221192 | tf_op jit(solution)/shard_map/ppermute | solution.py:399
  75.4 5.7 %collective-permute-start.10 = (bf16[2,144,128]{2,1,0:T(8,128)(2,1)S(1)}, bf16[2,144,128]{2,1,0:T(8,128)(2,1)S(1)}, u32[]{:S(2)}, u32[]{:S(2)}) collective-permute-start(bf16[2,144,128]{2,1,0:T(8,128)(2,1)S(1)} %get-tuple-element.62), channel_id=1, source_target_pairs={{1,2},{2,1},{3,4},{4,3},{5,6},{6,5},{9,10},{10,9},{11,12},{12,11},... | collective-permute-start | bytes 221192 | tf_op jit(solution)/shard_map/ppermute | solution.py:398
  81.0 3.4 %collective-permute-start.24 = (bf16[32,128]{1,0:T(8,128)(2,1)S(1)}, bf16[32,128]{1,0:T(8,128)(2,1)S(1)}, u32[]{:S(2)}, u32[]{:S(2)}) collective-permute-start(bf16[32,128]{1,0:T(8,128)(2,1)S(1)} %shard_map.106), channel_id=1, source_target_pairs={{0,24},{1,25},{2,26},{3,27},{4,28},{5,29},{6,30},{7,31},{8,16},{9,... | collective-permute-start | bytes 24584 | tf_op jit(solution)/shard_map/ppermute | solution.py:552
  84.4 8.0 %collective-permute-start.28 = (bf16[32,128]{1,0:T(8,128)(2,1)S(1)}, bf16[32,128]{1,0:T(8,128)(2,1)S(1)}, u32[]{:S(2)}, u32[]{:S(2)}) collective-permute-start(bf16[32,128]{1,0:T(8,128)(2,1)S(1)} %collective-permute-done.24.refs_3_), channel_id=1, source_target_pairs={{0,1},{1,0},{2,3},{3,2},{4,5},{5,4},{6,7},{7,6},{8,9},{9,8},{10,11... | collective-permute-start | bytes 24584 | tf_op jit(solution)/shard_map/ppermute | solution.py:583

commit v9 on v8

--- a/solution.py
+++ b/solution.py
@@ -177,7 +177,7 @@
     total = jnp.zeros((1, C), f32)
     for s in range(2):
         live, bx, by = place(pos, s)
-        hg[...] = convolve(grid, 1, bx, by, cols.at[2 * s], w2, True)
+        hg[s] = convolve(grid, 1, bx, by, cols.at[2 * s], w2, True)
         first = convolve(grid, 0, bx, by, cols.at[2 * s + 1], w1, False)
         center = first - jnp.mean(first, axis=1, keepdims=True)
         spread = jnp.mean(center * center, axis=1, keepdims=True)
@@ -187,7 +187,7 @@
         sig = jax.nn.sigmoid(v)
         on = jnp.where(live, 1.0, 0.0)
         h = jnp.where(live, v * sig, 0.0).astype(bf16)
-        grad = jnp.where(live, hg[...], 0.0)
+        grad = jnp.where(live, hg[s], 0.0)
         dv = grad * (sig * (1.0 + v * (1.0 - sig)))
         total = total + jnp.sum(dv * n, axis=0, keepdims=True)
         dn = dv * g
@@ -205,7 +205,7 @@
     build(grid, 0, pos, src, *faces(meta, field, xa, xb, ya, yb))
     for s in range(2):
         live, bx, by = place(pos, s)
-        y = convolve(grid, 0, bx, by, cols, w, field == 1)
+        y = convolve(grid, 0, bx, by, cols.at[s], w, field == 1)
         out[s] = jnp.where(live, base[s].astype(f32) + y, 0.0).astype(bf16)
 
 
@@ -481,11 +481,11 @@
     fa = after(fa, ppos, other)
     edge = xa, xb, *across(fa, fb, "gy")
     grid = pltpu.VMEM((2, 18, 18, 8, C), f32)
-    cols = pltpu.VMEM((512, 9 * C), bf16)
+    cols = pltpu.VMEM((2, 512, 9 * C), bf16)
     hid, pre, msg, gain_part = call(
         main_body,
         [sds((2, 512, C), bf16)] * 2 + [sds((P_ROWS + sum(FACES), C), bf16), sds((8, C), f32)],
-        [grid, pltpu.VMEM((4, 512, 9 * C), bf16), pltpu.VMEM((512, C), f32)],
+        [grid, pltpu.VMEM((4, 512, 9 * C), bf16), pltpu.VMEM((2, 512, C), f32)],
         (brick_pos, features, cotangent, *edge, w1, t2, gain),
         1,
         14,

time: 95.9 us -> 95.7 us (level)
  no operation moved by 1% of the time
where the time goes in v9:
time: 95.7 us; the launch traced here: 95.4 us
  starting transfers between devices  39.7 us (41%)
  waiting for transfers between devices  29.1 us (30%)
  Pallas kernels  25.3 us (26%)
  between operations  1.03 us (1%)
    pallas_call x14, Pallas kernels, call(): pl.pallas_call(kernel, out_shape=outs, in_specs=[SMEM] * n_smem + [VMEM]...  22.3 us
    ppermute x13, waiting for transfers between devices, per_device(): swap = lambda v, dx, dy=0: lax.ppermute(v, both, pairs(dx, dy))  21.7 us
    ppermute x4, starting transfers between devices, across(): b = lax.ppermute(b, axis, odd)  13.1 us
    ppermute x13, starting transfers between devices, per_device(): swap = lambda v, dx, dy=0: lax.ppermute(v, both, pairs(dx, dy))  9.65 us
    ppermute x4, starting transfers between devices, per_device(): part = [lax.ppermute(v, 'gy', partner) for v in own]  8.51 us
    ppermute x4, waiting for transfers between devices, across(): b = lax.ppermute(b, axis, odd)  6.43 us
    ppermute x4, starting transfers between devices, across(): a = lax.ppermute(a, axis, even)  5.12 us
    pallas_call x2, Pallas kernels, pieces_call(): pl.pallas_call(lambda *refs: body(who(), *refs, chunks=chunks), out_shape...  2.97 us
  transfers between devices with their start and end apart: 29, of which 12 were waited for; matrix products, arithmetic and copies ran while one was open for 0% of the time, Pallas kernels for 18%

profile of v9, /device:TPU:21, one launch (start us, length us, event | category | flops | bytes accessed | tf_op | source)
XLA Modules:
  0.0 95.4 jit_solution(8789235313364685035)
XLA Ops:
  0.6 1.3 %shard_map.93 = (bf16[2,512,128]{2,1,0:T(8,128)(2,1)S(1)}, bf16[2,512,128]{2,1,0:T(8,128)(2,1)S(1)}, bf16[2,512,128]{2,1,0:T(8,128)(2,1)S(1)}, bf16[2,128,128]{2,1,0:T(8,128)(2,1)S(1)}, bf16[2,128,128]{2,1,0:T(8,128)(2,1)S(1)}) custom-call(s32[2]{0:T(128)} %refs_0_.19, bf16[2,512,128]{2,1,0:T(8,128)(2,1)} %refs_1_.2, bf16[2,512,128]{2,1,0:T(8,128)(2,1)} %refs_2_.1), custom_call_target="tpu_custom_call" | custom-call | tf_op jit(solution)/shard_map/pallas_call | solution.py:38
  1.9 0.7 collective-permute-start.3
  2.7 1.2 %collective-permute-start = (bf16[2,128,128]{2,1,0:T(8,128)(2,1)S(1)}, bf16[2,128,128]{2,1,0:T(8,128)(2,1)S(1)}, u32[]{:S(2)}, u32[]{:S(2)}) collective-permute-start(bf16[2,128,128]{2,1,0:T(8,128)(2,1)S(1)} %get-tuple-element.42), channel_id=1, source_target_pairs={{0,8},{8,0},{16,24},{24,16},{1,9},{9,1},{17,25},{25,17},{2,10},{10... | collective-permute-start | bytes 196616 | tf_op jit(solution)/shard_map/ppermute | solution.py:399
  3.9 2.1 %collective-permute-start.1 = (bf16[2,128,128]{2,1,0:T(8,128)(2,1)S(1)}, bf16[2,128,128]{2,1,0:T(8,128)(2,1)S(1)}, u32[]{:S(2)}, u32[]{:S(2)}) collective-permute-start(bf16[2,128,128]{2,1,0:T(8,128)(2,1)S(1)} %get-tuple-element.43), channel_id=1, source_target_pairs={{8,16},{16,8},{9,17},{17,9},{10,18},{18,10},{11,19},{19,11},{12,20... | collective-permute-start | bytes 196616 | tf_op jit(solution)/shard_map/ppermute | solution.py:398
  6.0 0.7 collective-permute-start.2
  6.7 2.0 %shard_map.94 = (bf16[1152,384]{1,0:T(8,128)(2,1)S(1)}, bf16[1152,384]{1,0:T(8,128)(2,1)S(1)}, bf16[384,1152]{1,0:T(8,128)(2,1)S(1)}, bf16[384,1152]{1,0:T(8,128)(2,1)S(1)}, f32[1,128]{1,0:T(1,128)S(1)}) custom-call(bf16[27,128,128]{2,1,0:T(8,128)(2,1)} %refs_0_.11, bf16[27,128,128]{2,1,0:T(8,128)(2,1)} %refs_1_.3, f32[1,128]{1,0:T(1,128)} %bitcast.4), custom_call_target="tpu_custom_call" | custom-call | tf_op jit(solution)/shard_map/pallas_call | solution.py:38
  8.7 1.1 %collective-permute-done.1.refs_4_ = bf16[2,128,128]{2,1,0:T(8,128)(2,1)S(1)} collective-permute-done((bf16[2,128,128]{2,1,0:T(8,128)(2,1)S(1)}, bf16[2,128,128]{2,1,0:T(8,128)(2,1)S(1)}, u32[]{:S(2)}, u32[]{:S(2)}) %collective-permute-start.1) | collective-permute-done | bytes 65568 | tf_op jit(solution)/shard_map/ppermute | solution.py:398
  9.8 0.8 shard_map.95
  10.6 4.6 %collective-permute-start.5 = (bf16[2,144,128]{2,1,0:T(8,128)(2,1)S(1)}, bf16[2,144,128]{2,1,0:T(8,128)(2,1)S(1)}, u32[]{:S(2)}, u32[]{:S(2)}) collective-permute-start(bf16[2,144,128]{2,1,0:T(8,128)(2,1)S(1)} %get-tuple-element.49), channel_id=1, source_target_pairs={{1,2},{2,1},{3,4},{4,3},{5,6},{6,5},{9,10},{10,9},{11,12},{12,11},... | collective-permute-start | bytes 221192 | tf_op jit(solution)/shard_map/ppermute | solution.py:398
  15.3 2.1 %collective-permute-done.5.refs_6_ = bf16[2,144,128]{2,1,0:T(8,128)(2,1)S(1)} collective-permute-done((bf16[2,144,128]{2,1,0:T(8,128)(2,1)S(1)}, bf16[2,144,128]{2,1,0:T(8,128)(2,1)S(1)}, u32[]{:S(2)}, u32[]{:S(2)}) %collective-permute-start.5) | collective-permute-done | bytes 73760 | tf_op jit(solution)/shard_map/ppermute | solution.py:398
  17.4 4.2 %shard_map.96 = (bf16[2,512,128]{2,1,0:T(8,128)(2,1)S(1)}, bf16[2,512,128]{2,1,0:T(8,128)(2,1)S(1)}, bf16[1584,128]{1,0:T(8,128)(2,1)S(1)}, f32[8,128]{1,0:T(8,128)S(1)}) custom-call(s32[2]{0:T(128)} %refs_0_.19, bf16[2,512,128]{2,1,0:T(8,128)(2,1)S(1)} %get-tuple-element.45.refs_1_.refs_7_, bf16[2,512,128]{2,1,0:T(8,128)(2,1)S(1)} %get-tuple-element.41.refs_2_.refs_7_, ...), custom_call_target="tpu_custom_call" | custom-call | tf_op jit(solution)/shard_map/pallas_call | solution.py:38
  21.7 0.4 collective-permute-start.6
  22.1 1.9 %shard_map.97 = (f32[18,18,8,128]{3,2,1,0:T(8,128)S(1)}, bf16[384,1024]{1,0:T(8,128)(2,1)S(1)}, f32[384,640]{1,0:T(8,128)S(1)}) custom-call(s32[2]{0:T(128)} %refs_0_.19, bf16[2,512,128]{2,1,0:T(8,128)(2,1)S(1)} %get-tuple-element.45.refs_1_.refs_7_, bf16[2,512,128]{2,1,0:T(8,128)(2,1)S(1)} %get-tuple-element.41.refs_2_.refs_7_, ...), custom_call_target="tpu_custom_call" | custom-call | tf_op jit(solution)/shard_map/pallas_call | solution.py:38
  24.0 1.7 %shard_map.98 = (f32[18,18,8,128]{3,2,1,0:T(8,128)S(1)}, bf16[384,1024]{1,0:T(8,128)(2,1)S(1)}, bf16[864,128]{1,0:T(8,128)(2,1)S(1)}, bf16[864,128]{1,0:T(8,128)(2,1)S(1)}, f32[8,128]{1,0:T(8,128)S(1)}) custom-call(s32[2]{0:T(128)S(1)} %collective-permute-done.2.refs_0_.refs_1_, bf16[2,512,128]{2,1,0:T(8,128)(2,1)S(1)} %collective-permute-done.3.refs_1_, ...), custom_call_target="tpu_custom_call" | custom-call | tf_op jit(solution)/shard_map/pallas_call | solution.py:38
  25.8 1.5 %collective-permute-start.11 = (bf16[864,128]{1,0:T(8,128)(2,1)S(1)}, bf16[864,128]{1,0:T(8,128)(2,1)S(1)}, u32[]{:S(2)}, u32[]{:S(2)}) collective-permute-start(bf16[864,128]{1,0:T(8,128)(2,1)S(1)} %get-tuple-element.70), channel_id=1, source_target_pairs={{0,8},{1,17},{2,10},{3,19},{4,12},{5,21},{6,14},{7,23},{8,0},{9,25... | collective-permute-start | bytes 663560 | tf_op jit(solution)/shard_map/ppermute | solution.py:552
  27.2 2.4 %shard_map.103 = (f32[864,128]{1,0:T(8,128)S(1)}, f32[864,128]{1,0:T(8,128)S(1)}) custom-call(s32[2]{0:T(128)} %refs_0_.19, s32[2]{0:T(128)S(1)} %collective-permute-done.2.refs_0_.refs_1_, f32[18,18,8,128]{3,2,1,0:T(8,128)S(1)} %get-tuple-element.65.refs_2_, f32[18,18,8,128]{3,2,1,0:T(8,128)S(1)} %get-tuple-element.66.refs_3_, ...), custom_call_target="tpu_custom_call" | custom-call | tf_op jit(solution)/shard_map/pallas_call | solution.py:38
  29.6 1.2 %collective-permute-done.12 = bf16[864,128]{1,0:T(8,128)(2,1)S(1)} collective-permute-done((bf16[864,128]{1,0:T(8,128)(2,1)S(1)}, bf16[864,128]{1,0:T(8,128)(2,1)S(1)}, u32[]{:S(2)}, u32[]{:S(2)}) %collective-permute-start.12) | collective-permute-done | bytes 221216 | tf_op jit(solution)/shard_map/ppermute | solution.py:552
  31.0 2.2 %collective-permute-done.11 = bf16[864,128]{1,0:T(8,128)(2,1)S(1)} collective-permute-done((bf16[864,128]{1,0:T(8,128)(2,1)S(1)}, bf16[864,128]{1,0:T(8,128)(2,1)S(1)}, u32[]{:S(2)}, u32[]{:S(2)}) %collective-permute-start.11) | collective-permute-done | bytes 221216 | tf_op jit(solution)/shard_map/ppermute | solution.py:552
  33.2 3.3 %collective-permute-done.13 = bf16[864,128]{1,0:T(8,128)(2,1)S(1)} collective-permute-done((bf16[864,128]{1,0:T(8,128)(2,1)S(1)}, bf16[864,128]{1,0:T(8,128)(2,1)S(1)}, u32[]{:S(2)}, u32[]{:S(2)}) %collective-permute-start.13) | collective-permute-done | bytes 221216 | tf_op jit(solution)/shard_map/ppermute | solution.py:552
  36.5 0.1 fusion.2
  36.6 1.2 %collective-permute-start.15 = (f32[216,128]{1,0:T(8,128)S(1)}, f32[216,128]{1,0:T(8,128)S(1)}, u32[]{:S(2)}, u32[]{:S(2)}) collective-permute-start(f32[216,128]{1,0:T(8,128)S(1)} %slice.24), channel_id=1, source_target_pairs={{0,2},{1,3},{2,0},{3,1},{4,6},{5,7},{6,4},{7,5},{8,10},{9,11},{10,... | collective-permute-start | bytes 331784 | tf_op jit(solution)/shard_map/ppermute | solution.py:552
  37.8 0.2 collective-permute-start.14
  38.1 1.3 %collective-permute-start.16 = (bf16[216,128]{1,0:T(8,128)(2,1)S(1)}, bf16[216,128]{1,0:T(8,128)(2,1)S(1)}, u32[]{:S(2)}, u32[]{:S(2)}) collective-permute-start(bf16[216,128]{1,0:T(8,128)(2,1)S(1)} %get-tuple-element.79), channel_id=1, source_target_pairs={{0,6},{1,7},{2,4},{3,5},{4,2},{5,3},{6,0},{7,1},{8,14},{9,15},{10,... | collective-permute-start | bytes 165896 | tf_op jit(solution)/shard_map/ppermute | solution.py:552
  39.4 3.0 %collective-permute-done.14 = bf16[216,128]{1,0:T(8,128)(2,1)S(1)} collective-permute-done((bf16[216,128]{1,0:T(8,128)(2,1)S(1)}, bf16[216,128]{1,0:T(8,128)(2,1)S(1)}, u32[]{:S(2)}, u32[]{:S(2)}) %collective-permute-start.14) | collective-permute-done | bytes 55328 | tf_op jit(solution)/shard_map/ppermute | solution.py:552
  42.5 0.6 collective-permute-start.19
  43.1 3.9 %collective-permute-start.18 = (bf16[224,128]{1,0:T(8,128)(2,1)S(1)}, bf16[224,128]{1,0:T(8,128)(2,1)S(1)}, u32[]{:S(2)}, u32[]{:S(2)}) collective-permute-start(bf16[224,128]{1,0:T(8,128)(2,1)S(1)} %shard_map.104.refs_0_), channel_id=1, source_target_pairs={{0,2},{1,3},{2,0},{3,1},{4,6},{5,7},{6,4},{7,5},{8,10},{9,11},{10,... | collective-permute-start | bytes 172040 | tf_op jit(solution)/shard_map/ppermute | solution.py:552
  47.0 2.2 %collective-permute-done.18.refs_2_ = bf16[224,128]{1,0:T(8,128)(2,1)S(1)} collective-permute-done((bf16[224,128]{1,0:T(8,128)(2,1)S(1)}, bf16[224,128]{1,0:T(8,128)(2,1)S(1)}, u32[]{:S(2)}, u32[]{:S(2)}) %collective-permute-start.18) | collective-permute-done | bytes 57376 | tf_op jit(solution)/shard_map/ppermute | solution.py:552
  49.2 2.3 %collective-permute-done.17.refs_1_ = bf16[224,128]{1,0:T(8,128)(2,1)S(1)} collective-permute-done((bf16[224,128]{1,0:T(8,128)(2,1)S(1)}, bf16[224,128]{1,0:T(8,128)(2,1)S(1)}, u32[]{:S(2)}, u32[]{:S(2)}) %collective-permute-start.17) | collective-permute-done | bytes 57376 | tf_op jit(solution)/shard_map/ppermute | solution.py:552
  51.5 0.5 collective-permute-start.23
  52.1 4.3 %collective-permute-done.20.refs_1_ = bf16[896,128]{1,0:T(8,128)(2,1)S(1)} collective-permute-done((bf16[896,128]{1,0:T(8,128)(2,1)S(1)}, bf16[896,128]{1,0:T(8,128)(2,1)S(1)}, u32[]{:S(2)}, u32[]{:S(2)}) %collective-permute-start.20) | collective-permute-done | bytes 229408 | tf_op jit(solution)/shard_map/ppermute | solution.py:552
  56.4 0.8 shard_map.99
  57.2 0.6 collective-permute-start.7
  57.8 4.0 %collective-permute-start.8 = (bf16[2,128,128]{2,1,0:T(8,128)(2,1)S(1)}, bf16[2,128,128]{2,1,0:T(8,128)(2,1)S(1)}, u32[]{:S(2)}, u32[]{:S(2)}) collective-permute-start(bf16[2,128,128]{2,1,0:T(8,128)(2,1)S(1)} %get-tuple-element.60), channel_id=1, source_target_pairs={{8,16},{16,8},{9,17},{17,9},{10,18},{18,10},{11,19},{19,11},{12,20... | collective-permute-start | bytes 196616 | tf_op jit(solution)/shard_map/ppermute | solution.py:398
  61.8 7.1 %collective-permute-start.25 = (bf16[896,128]{1,0:T(8,128)(2,1)S(1)}, bf16[896,128]{1,0:T(8,128)(2,1)S(1)}, u32[]{:S(2)}, u32[]{:S(2)}) collective-permute-start(bf16[896,128]{1,0:T(8,128)(2,1)S(1)} %shard_map.105.refs_0_), channel_id=1, source_target_pairs={{0,1},{1,0},{2,3},{3,2},{4,5},{5,4},{6,7},{7,6},{8,9},{9,8},{10,11... | collective-permute-start | bytes 688136 | tf_op jit(solution)/shard_map/ppermute | solution.py:585
  68.9 0.1 collective-permute-start.27
  69.0 1.3 %collective-permute-start.26 = (bf16[896,128]{1,0:T(8,128)(2,1)S(1)}, bf16[896,128]{1,0:T(8,128)(2,1)S(1)}, u32[]{:S(2)}, u32[]{:S(2)}) collective-permute-start(bf16[896,128]{1,0:T(8,128)(2,1)S(1)} %collective-permute-done.20.refs_1_), channel_id=1, source_target_pairs={{0,1},{1,0},{2,3},{3,2},{4,5},{5,4},{6,7},{7,6},{8,9},{9,8},{10,11... | collective-permute-start | bytes 688136 | tf_op jit(solution)/shard_map/ppermute | solution.py:585
  70.4 0.8 shard_map.100
  71.2 3.3 %collective-permute-start.9 = (bf16[2,144,128]{2,1,0:T(8,128)(2,1)S(1)}, bf16[2,144,128]{2,1,0:T(8,128)(2,1)S(1)}, u32[]{:S(2)}, u32[]{:S(2)}) collective-permute-start(bf16[2,144,128]{2,1,0:T(8,128)(2,1)S(1)} %get-tuple-element.61), channel_id=1, source_target_pairs={{0,1},{1,0},{2,3},{3,2},{4,5},{5,4},{6,7},{7,6},{8,9},{9,8},{10,11... | collective-permute-start | bytes 221192 | tf_op jit(solution)/shard_map/ppermute | solution.py:399
  74.5 0.9 collective-permute-done.9.refs_4_
  75.4 2.4 %collective-permute-start.10 = (bf16[2,144,128]{2,1,0:T(8,128)(2,1)S(1)}, bf16[2,144,128]{2,1,0:T(8,128)(2,1)S(1)}, u32[]{:S(2)}, u32[]{:S(2)}) collective-permute-start(bf16[2,144,128]{2,1,0:T(8,128)(2,1)S(1)} %get-tuple-element.62), channel_id=1, source_target_pairs={{1,2},{2,1},{3,4},{4,3},{5,6},{6,5},{9,10},{10,9},{11,12},{12,11},... | collective-permute-start | bytes 221192 | tf_op jit(solution)/shard_map/ppermute | solution.py:398
  77.8 3.3 %collective-permute-done.10.refs_5_ = bf16[2,144,128]{2,1,0:T(8,128)(2,1)S(1)} collective-permute-done((bf16[2,144,128]{2,1,0:T(8,128)(2,1)S(1)}, bf16[2,144,128]{2,1,0:T(8,128)(2,1)S(1)}, u32[]{:S(2)}, u32[]{:S(2)}) %collective-permute-start.10) | collective-permute-done | bytes 73760 | tf_op jit(solution)/shard_map/ppermute | solution.py:398
  81.0 0.2 collective-permute-start.24
  81.2 3.2 %collective-permute-done.24.refs_3_ = bf16[32,128]{1,0:T(8,128)(2,1)S(1)} collective-permute-done((bf16[32,128]{1,0:T(8,128)(2,1)S(1)}, bf16[32,128]{1,0:T(8,128)(2,1)S(1)}, u32[]{:S(2)}, u32[]{:S(2)}) %collective-permute-start.24) | collective-permute-done | bytes 8224 | tf_op jit(solution)/shard_map/ppermute | solution.py:552
  84.4 1.5 %collective-permute-start.28 = (bf16[32,128]{1,0:T(8,128)(2,1)S(1)}, bf16[32,128]{1,0:T(8,128)(2,1)S(1)}, u32[]{:S(2)}, u32[]{:S(2)}) collective-permute-start(bf16[32,128]{1,0:T(8,128)(2,1)S(1)} %collective-permute-done.24.refs_3_), channel_id=1, source_target_pairs={{0,1},{1,0},{2,3},{3,2},{4,5},{5,4},{6,7},{7,6},{8,9},{9,8},{10,11... | collective-permute-start | bytes 24584 | tf_op jit(solution)/shard_map/ppermute | solution.py:583
  85.9 3.2 %shard_map.102 = bf16[2,512,128]{2,1,0:T(8,128)(2,1)} custom-call(s32[2]{0:T(128)} %refs_0_.19, bf16[2,512,128]{2,1,0:T(8,128)(2,1)S(1)} %get-tuple-element.55.refs_8_.refs_2_.refs_1_, bf16[2,128,128]{2,1,0:T(8,128)(2,1)S(1)} %collective-permute-done.7.refs_3_.refs_2_, bf16[2,128,128]{2,1,0:T(8,128)(2,1)S(1)} %collective-permute-done.8.refs_4_.refs_3_, ...), custom_call_target="tpu_custom_call" | custom-call | tf_op jit(solution)/shard_map/pallas_call | solution.py:38
  89.1 3.0 %shard_map.101 = bf16[2,512,128]{2,1,0:T(8,128)(2,1)} custom-call(s32[2]{0:T(128)} %refs_0_.19, bf16[2,512,128]{2,1,0:T(8,128)(2,1)S(1)} %get-tuple-element.58.refs_7_.refs_1_, bf16[2,128,128]{2,1,0:T(8,128)(2,1)S(1)} %collective-permute-done.7.refs_3_.refs_2_, bf16[2,128,128]{2,1,0:T(8,128)(2,1)S(1)} %collective-permute-done.8.refs_4_.refs_3_, ...), custom_call_target="tpu_custom_call" | custom-call | tf_op jit(solution)/shard_map/pallas_call | solution.py:38
  92.2 2.0 %shard_map.107 = (f32[2,3456,128]{2,1,0:T(8,128)}, f32[1,128]{1,0:T(1,128)}, f32[8,128]{1,0:T(8,128)S(1)}) custom-call(bf16[896,128]{1,0:T(8,128)(2,1)S(1)} %shard_map.105.refs_0_, bf16[896,128]{1,0:T(8,128)(2,1)S(1)} %collective-permute-done.20.refs_1_, bf16[896,128]{1,0:T(8,128)(2,1)S(1)} %collective-permute-done.23.refs_2_, ...), custom_call_target="tpu_custom_call" | custom-call | tf_op jit(solution)/shard_map/pallas_call | solution.py:589
  94.2 1.0 %shard_map.108 = f32[2,3456,128]{2,1,0:T(8,128)} custom-call(bf16[896,128]{1,0:T(8,128)(2,1)S(1)} %collective-permute-done.21.refs_0_, bf16[896,128]{1,0:T(8,128)(2,1)S(1)} %collective-permute-done.22.refs_1_, f32[8,128]{1,0:T(8,128)S(1)} %get-tuple-element.73.refs_2_, f32[2,3456,128]{2,1,0:T(8,128)} %get-tuple-element.74.refs_3_), custom_call_target="tpu_custom_call", output_to_operand_aliasing={{}: (3, {})} | custom-call | tf_op jit(solution)/shard_map/pallas_call | solution.py:589
  (32 shorter events, 0.5 us)
Async XLA Ops:
  1.9 13.3 %collective-permute-start.3 = (bf16[2,512,128]{2,1,0:T(8,128)(2,1)S(1)}, bf16[2,512,128]{2,1,0:T(8,128)(2,1)S(1)}, u32[]{:S(2)}, u32[]{:S(2)}) collective-permute-start(bf16[2,512,128]{2,1,0:T(8,128)(2,1)S(1)} %get-tuple-element.47), channel_id=1, source_target_pairs={{0,1},{1,0},{2,3},{3,2},{4,5},{5,4},{6,7},{7,6},{8,9},{9,8},{10,11... | collective-permute-start | bytes 786440 | tf_op jit(solution)/shard_map/ppermute | solution.py:471
  2.7 6.0 %collective-permute-start = (bf16[2,128,128]{2,1,0:T(8,128)(2,1)S(1)}, bf16[2,128,128]{2,1,0:T(8,128)(2,1)S(1)}, u32[]{:S(2)}, u32[]{:S(2)}) collective-permute-start(bf16[2,128,128]{2,1,0:T(8,128)(2,1)S(1)} %get-tuple-element.42), channel_id=1, source_target_pairs={{0,8},{8,0},{16,24},{24,16},{1,9},{9,1},{17,25},{25,17},{2,10},{10... | collective-permute-start | bytes 196616 | tf_op jit(solution)/shard_map/ppermute | solution.py:399
  3.9 5.9 %collective-permute-start.1 = (bf16[2,128,128]{2,1,0:T(8,128)(2,1)S(1)}, bf16[2,128,128]{2,1,0:T(8,128)(2,1)S(1)}, u32[]{:S(2)}, u32[]{:S(2)}) collective-permute-start(bf16[2,128,128]{2,1,0:T(8,128)(2,1)S(1)} %get-tuple-element.43), channel_id=1, source_target_pairs={{8,16},{16,8},{9,17},{17,9},{10,18},{18,10},{11,19},{19,11},{12,20... | collective-permute-start | bytes 196616 | tf_op jit(solution)/shard_map/ppermute | solution.py:398
  6.0 9.2 %collective-permute-start.2 = (s32[2]{0:T(128)}, s32[2]{0:T(128)S(1)}, u32[]{:S(2)}, u32[]{:S(2)}) collective-permute-start(s32[2]{0:T(128)} %refs_0_.19), channel_id=1, source_target_pairs={{0,1},{1,0},{2,3},{3,2},{4,5},{5,4},{6,7},{7,6},{8,9},{9,8},{10,11... | collective-permute-start | bytes 32 | tf_op jit(solution)/shard_map/ppermute | solution.py:470
  10.6 6.8 %collective-permute-start.5 = (bf16[2,144,128]{2,1,0:T(8,128)(2,1)S(1)}, bf16[2,144,128]{2,1,0:T(8,128)(2,1)S(1)}, u32[]{:S(2)}, u32[]{:S(2)}) collective-permute-start(bf16[2,144,128]{2,1,0:T(8,128)(2,1)S(1)} %get-tuple-element.49), channel_id=1, source_target_pairs={{1,2},{2,1},{3,4},{4,3},{5,6},{6,5},{9,10},{10,9},{11,12},{12,11},... | collective-permute-start | bytes 221192 | tf_op jit(solution)/shard_map/ppermute | solution.py:398
  15.3 2.2 %collective-permute-start.4 = (bf16[2,144,128]{2,1,0:T(8,128)(2,1)S(1)}, bf16[2,144,128]{2,1,0:T(8,128)(2,1)S(1)}, u32[]{:S(2)}, u32[]{:S(2)}) collective-permute-start(bf16[2,144,128]{2,1,0:T(8,128)(2,1)S(1)} %get-tuple-element.48), channel_id=1, source_target_pairs={{0,1},{1,0},{2,3},{3,2},{4,5},{5,4},{6,7},{7,6},{8,9},{9,8},{10,11... | collective-permute-start | bytes 221192 | tf_op jit(solution)/shard_map/ppermute | solution.py:399
  21.7 2.3 %collective-permute-start.6 = (bf16[1584,128]{1,0:T(8,128)(2,1)S(1)}, bf16[1584,128]{1,0:T(8,128)(2,1)S(1)}, u32[]{:S(2)}, u32[]{:S(2)}) collective-permute-start(bf16[1584,128]{1,0:T(8,128)(2,1)S(1)} %get-tuple-element.53), channel_id=1, source_target_pairs={{0,1},{1,0},{2,3},{3,2},{4,5},{5,4},{6,7},{7,6},{8,9},{9,8},{10,11... | collective-permute-start | bytes 1216520 | tf_op jit(solution)/shard_map/ppermute | solution.py:494
  25.7 5.1 %collective-permute-start.12 = (bf16[864,128]{1,0:T(8,128)(2,1)S(1)}, bf16[864,128]{1,0:T(8,128)(2,1)S(1)}, u32[]{:S(2)}, u32[]{:S(2)}) collective-permute-start(bf16[864,128]{1,0:T(8,128)(2,1)S(1)} %get-tuple-element.57), channel_id=1, source_target_pairs={{0,8},{1,17},{2,10},{3,19},{4,12},{5,21},{6,14},{7,23},{8,0},{9,25... | collective-permute-start | bytes 663560 | tf_op jit(solution)/shard_map/ppermute | solution.py:552
  25.8 7.4 %collective-permute-start.11 = (bf16[864,128]{1,0:T(8,128)(2,1)S(1)}, bf16[864,128]{1,0:T(8,128)(2,1)S(1)}, u32[]{:S(2)}, u32[]{:S(2)}) collective-permute-start(bf16[864,128]{1,0:T(8,128)(2,1)S(1)} %get-tuple-element.70), channel_id=1, source_target_pairs={{0,8},{1,17},{2,10},{3,19},{4,12},{5,21},{6,14},{7,23},{8,0},{9,25... | collective-permute-start | bytes 663560 | tf_op jit(solution)/shard_map/ppermute | solution.py:552
  30.9 5.6 %collective-permute-start.13 = (bf16[864,128]{1,0:T(8,128)(2,1)S(1)}, bf16[864,128]{1,0:T(8,128)(2,1)S(1)}, u32[]{:S(2)}, u32[]{:S(2)}) collective-permute-start(bf16[864,128]{1,0:T(8,128)(2,1)S(1)} %add_convert_fusion), channel_id=1, source_target_pairs={{0,16},{1,9},{2,18},{3,11},{4,20},{5,13},{6,22},{7,15},{8,24},{9,1... | collective-permute-start | bytes 663560 | tf_op jit(solution)/shard_map/ppermute | solution.py:552
  36.6 5.8 %collective-permute-start.15 = (f32[216,128]{1,0:T(8,128)S(1)}, f32[216,128]{1,0:T(8,128)S(1)}, u32[]{:S(2)}, u32[]{:S(2)}) collective-permute-start(f32[216,128]{1,0:T(8,128)S(1)} %slice.24), channel_id=1, source_target_pairs={{0,2},{1,3},{2,0},{3,1},{4,6},{5,7},{6,4},{7,5},{8,10},{9,11},{10,... | collective-permute-start | bytes 331784 | tf_op jit(solution)/shard_map/ppermute | solution.py:552
  37.8 4.6 %collective-permute-start.14 = (bf16[216,128]{1,0:T(8,128)(2,1)S(1)}, bf16[216,128]{1,0:T(8,128)(2,1)S(1)}, u32[]{:S(2)}, u32[]{:S(2)}) collective-permute-start(bf16[216,128]{1,0:T(8,128)(2,1)S(1)} %get-tuple-element.78), channel_id=1, source_target_pairs={{0,4},{1,5},{2,6},{3,7},{4,0},{5,1},{6,2},{7,3},{8,12},{9,13},{10,... | collective-permute-start | bytes 165896 | tf_op jit(solution)/shard_map/ppermute | solution.py:552
  38.1 4.3 %collective-permute-start.16 = (bf16[216,128]{1,0:T(8,128)(2,1)S(1)}, bf16[216,128]{1,0:T(8,128)(2,1)S(1)}, u32[]{:S(2)}, u32[]{:S(2)}) collective-permute-start(bf16[216,128]{1,0:T(8,128)(2,1)S(1)} %get-tuple-element.79), channel_id=1, source_target_pairs={{0,6},{1,7},{2,4},{3,5},{4,2},{5,3},{6,0},{7,1},{8,14},{9,15},{10,... | collective-permute-start | bytes 165896 | tf_op jit(solution)/shard_map/ppermute | solution.py:552
  42.5 4.5 %collective-permute-start.19 = (bf16[224,128]{1,0:T(8,128)(2,1)S(1)}, bf16[224,128]{1,0:T(8,128)(2,1)S(1)}, u32[]{:S(2)}, u32[]{:S(2)}) collective-permute-start(bf16[224,128]{1,0:T(8,128)(2,1)S(1)} %shard_map.104.refs_0_), channel_id=1, source_target_pairs={{0,6},{1,7},{2,4},{3,5},{4,2},{5,3},{6,0},{7,1},{8,14},{9,15},{10,... | collective-permute-start | bytes 172040 | tf_op jit(solution)/shard_map/ppermute | solution.py:552
  43.1 6.1 %collective-permute-start.18 = (bf16[224,128]{1,0:T(8,128)(2,1)S(1)}, bf16[224,128]{1,0:T(8,128)(2,1)S(1)}, u32[]{:S(2)}, u32[]{:S(2)}) collective-permute-start(bf16[224,128]{1,0:T(8,128)(2,1)S(1)} %shard_map.104.refs_0_), channel_id=1, source_target_pairs={{0,2},{1,3},{2,0},{3,1},{4,6},{5,7},{6,4},{7,5},{8,10},{9,11},{10,... | collective-permute-start | bytes 172040 | tf_op jit(solution)/shard_map/ppermute | solution.py:552
  47.0 4.4 %collective-permute-start.17 = (bf16[224,128]{1,0:T(8,128)(2,1)S(1)}, bf16[224,128]{1,0:T(8,128)(2,1)S(1)}, u32[]{:S(2)}, u32[]{:S(2)}) collective-permute-start(bf16[224,128]{1,0:T(8,128)(2,1)S(1)} %shard_map.104.refs_0_), channel_id=1, source_target_pairs={{0,4},{1,5},{2,6},{3,7},{4,0},{5,1},{6,2},{7,3},{8,12},{9,13},{10,... | collective-permute-start | bytes 172040 | tf_op jit(solution)/shard_map/ppermute | solution.py:552
  51.5 4.9 %collective-permute-start.20 = (bf16[896,128]{1,0:T(8,128)(2,1)S(1)}, bf16[896,128]{1,0:T(8,128)(2,1)S(1)}, u32[]{:S(2)}, u32[]{:S(2)}) collective-permute-start(bf16[896,128]{1,0:T(8,128)(2,1)S(1)} %shard_map.105.refs_0_), channel_id=1, source_target_pairs={{0,16},{1,9},{2,18},{3,11},{4,20},{5,13},{6,22},{7,15},{8,24},{9,1... | collective-permute-start | bytes 688136 | tf_op jit(solution)/shard_map/ppermute | solution.py:552
  51.5 17.4 %collective-permute-start.23 = (bf16[896,128]{1,0:T(8,128)(2,1)S(1)}, bf16[896,128]{1,0:T(8,128)(2,1)S(1)}, u32[]{:S(2)}, u32[]{:S(2)}) collective-permute-start(bf16[896,128]{1,0:T(8,128)(2,1)S(1)} %shard_map.105.refs_0_), channel_id=1, source_target_pairs={{0,8},{1,17},{2,10},{3,19},{4,12},{5,21},{6,14},{7,23},{8,0},{9,25... | collective-permute-start | bytes 688136 | tf_op jit(solution)/shard_map/ppermute | solution.py:552
  56.4 13.9 %collective-permute-start.21 = (bf16[896,128]{1,0:T(8,128)(2,1)S(1)}, bf16[896,128]{1,0:T(8,128)(2,1)S(1)}, u32[]{:S(2)}, u32[]{:S(2)}) collective-permute-start(bf16[896,128]{1,0:T(8,128)(2,1)S(1)} %collective-permute-done.20.refs_1_), channel_id=1, source_target_pairs={{0,8},{1,17},{2,10},{3,19},{4,12},{5,21},{6,14},{7,23},{8,0},{9,25... | collective-permute-start | bytes 688136 | tf_op jit(solution)/shard_map/ppermute | solution.py:552
  57.2 11.8 %collective-permute-start.7 = (bf16[2,128,128]{2,1,0:T(8,128)(2,1)S(1)}, bf16[2,128,128]{2,1,0:T(8,128)(2,1)S(1)}, u32[]{:S(2)}, u32[]{:S(2)}) collective-permute-start(bf16[2,128,128]{2,1,0:T(8,128)(2,1)S(1)} %get-tuple-element.59), channel_id=1, source_target_pairs={{0,8},{8,0},{16,24},{24,16},{1,9},{9,1},{17,25},{25,17},{2,10},{10... | collective-permute-start | bytes 196616 | tf_op jit(solution)/shard_map/ppermute | solution.py:399
  57.8 12.6 %collective-permute-start.8 = (bf16[2,128,128]{2,1,0:T(8,128)(2,1)S(1)}, bf16[2,128,128]{2,1,0:T(8,128)(2,1)S(1)}, u32[]{:S(2)}, u32[]{:S(2)}) collective-permute-start(bf16[2,128,128]{2,1,0:T(8,128)(2,1)S(1)} %get-tuple-element.60), channel_id=1, source_target_pairs={{8,16},{16,8},{9,17},{17,9},{10,18},{18,10},{11,19},{19,11},{12,20... | collective-permute-start | bytes 196616 | tf_op jit(solution)/shard_map/ppermute | solution.py:398
  61.8 30.4 %collective-permute-start.25 = (bf16[896,128]{1,0:T(8,128)(2,1)S(1)}, bf16[896,128]{1,0:T(8,128)(2,1)S(1)}, u32[]{:S(2)}, u32[]{:S(2)}) collective-permute-start(bf16[896,128]{1,0:T(8,128)(2,1)S(1)} %shard_map.105.refs_0_), channel_id=1, source_target_pairs={{0,1},{1,0},{2,3},{3,2},{4,5},{5,4},{6,7},{7,6},{8,9},{9,8},{10,11... | collective-permute-start | bytes 688136 | tf_op jit(solution)/shard_map/ppermute | solution.py:585
  68.9 23.3 %collective-permute-start.27 = (bf16[896,128]{1,0:T(8,128)(2,1)S(1)}, bf16[896,128]{1,0:T(8,128)(2,1)S(1)}, u32[]{:S(2)}, u32[]{:S(2)}) collective-permute-start(bf16[896,128]{1,0:T(8,128)(2,1)S(1)} %collective-permute-done.23.refs_2_), channel_id=1, source_target_pairs={{0,1},{1,0},{2,3},{3,2},{4,5},{5,4},{6,7},{7,6},{8,9},{9,8},{10,11... | collective-permute-start | bytes 688136 | tf_op jit(solution)/shard_map/ppermute | solution.py:585
  69.0 23.2 %collective-permute-start.26 = (bf16[896,128]{1,0:T(8,128)(2,1)S(1)}, bf16[896,128]{1,0:T(8,128)(2,1)S(1)}, u32[]{:S(2)}, u32[]{:S(2)}) collective-permute-start(bf16[896,128]{1,0:T(8,128)(2,1)S(1)} %collective-permute-done.20.refs_1_), channel_id=1, source_target_pairs={{0,1},{1,0},{2,3},{3,2},{4,5},{5,4},{6,7},{7,6},{8,9},{9,8},{10,11... | collective-permute-start | bytes 688136 | tf_op jit(solution)/shard_map/ppermute | solution.py:585
  70.3 23.8 %collective-permute-start.22 = (bf16[896,128]{1,0:T(8,128)(2,1)S(1)}, bf16[896,128]{1,0:T(8,128)(2,1)S(1)}, u32[]{:S(2)}, u32[]{:S(2)}) collective-permute-start(bf16[896,128]{1,0:T(8,128)(2,1)S(1)} %collective-permute-done.21.refs_0_), channel_id=1, source_target_pairs={{0,1},{1,0},{2,3},{3,2},{4,5},{5,4},{6,7},{7,6},{8,9},{9,8},{10,11... | collective-permute-start | bytes 688136 | tf_op jit(solution)/shard_map/ppermute | solution.py:585
  71.2 4.2 %collective-permute-start.9 = (bf16[2,144,128]{2,1,0:T(8,128)(2,1)S(1)}, bf16[2,144,128]{2,1,0:T(8,128)(2,1)S(1)}, u32[]{:S(2)}, u32[]{:S(2)}) collective-permute-start(bf16[2,144,128]{2,1,0:T(8,128)(2,1)S(1)} %get-tuple-element.61), channel_id=1, source_target_pairs={{0,1},{1,0},{2,3},{3,2},{4,5},{5,4},{6,7},{7,6},{8,9},{9,8},{10,11... | collective-permute-start | bytes 221192 | tf_op jit(solution)/shard_map/ppermute | solution.py:399
  75.4 5.7 %collective-permute-start.10 = (bf16[2,144,128]{2,1,0:T(8,128)(2,1)S(1)}, bf16[2,144,128]{2,1,0:T(8,128)(2,1)S(1)}, u32[]{:S(2)}, u32[]{:S(2)}) collective-permute-start(bf16[2,144,128]{2,1,0:T(8,128)(2,1)S(1)} %get-tuple-element.62), channel_id=1, source_target_pairs={{1,2},{2,1},{3,4},{4,3},{5,6},{6,5},{9,10},{10,9},{11,12},{12,11},... | collective-permute-start | bytes 221192 | tf_op jit(solution)/shard_map/ppermute | solution.py:398
  81.0 3.4 %collective-permute-start.24 = (bf16[32,128]{1,0:T(8,128)(2,1)S(1)}, bf16[32,128]{1,0:T(8,128)(2,1)S(1)}, u32[]{:S(2)}, u32[]{:S(2)}) collective-permute-start(bf16[32,128]{1,0:T(8,128)(2,1)S(1)} %shard_map.106), channel_id=1, source_target_pairs={{0,24},{1,25},{2,26},{3,27},{4,28},{5,29},{6,30},{7,31},{8,16},{9,... | collective-permute-start | bytes 24584 | tf_op jit(solution)/shard_map/ppermute | solution.py:552
  84.4 7.8 %collective-permute-start.28 = (bf16[32,128]{1,0:T(8,128)(2,1)S(1)}, bf16[32,128]{1,0:T(8,128)(2,1)S(1)}, u32[]{:S(2)}, u32[]{:S(2)}) collective-permute-start(bf16[32,128]{1,0:T(8,128)(2,1)S(1)} %collective-permute-done.24.refs_3_), channel_id=1, source_target_pairs={{0,1},{1,0},{2,3},{3,2},{4,5},{5,4},{6,7},{7,6},{8,9},{9,8},{10,11... | collective-permute-start | bytes 24584 | tf_op jit(solution)/shard_map/ppermute | solution.py:583
